TPU v7x, 32 devices: a whole 2x2x4 slice. The times are simulated.
32 devices in a mesh: seq: 4 (over z), dp: 8 (over y, x, core).
Axes of the slice: x: 2, y: 2, z: 4, core: 2. Of those that a mesh axis runs over, the one named last changes fastest.
Arguments:
- tokens: bfloat16 [16, 512, 1536], P('dp', 'seq'), may hold values from -6 to 6
- positions: int32 [16, 512], P('dp', 'seq'), may hold values from 0 to 511, as said below
- out_grad: bfloat16 [16, 512, 1536], P('dp', 'seq'), may hold values from -6 to 6
- w_query: bfloat16 [1536, 1536], P(('seq', 'dp')), may hold values from -0.15625 to 0.15625
- w_key: bfloat16 [1536, 768], P(('seq', 'dp')), may hold values from -0.15625 to 0.15625
- w_value: bfloat16 [1536, 768], P(('seq', 'dp')), may hold values from -0.15625 to 0.15625
- w_output: bfloat16 [1536, 1536], P(('seq', 'dp')), may hold values from -2.5 to 2.5
- gain_attn: bfloat16 [1536], P(('seq', 'dp')), may hold values from 0.25 to 1.75
- gain_ffn: bfloat16 [1536], P(('seq', 'dp')), may hold values from 0.25 to 1.75
- w_gate: bfloat16 [4096, 1536], P(('seq', 'dp')), may hold values from -0.15625 to 0.15625
- w_up: bfloat16 [4096, 1536], P(('seq', 'dp')), may hold values from -0.15625 to 0.15625
- w_down: bfloat16 [4096, 1536], P(('seq', 'dp')), may hold values from -0.09375 to 0.09375
Outputs:
- layer_out: bfloat16 [16, 512, 1536], P('dp', 'seq')
- in_grad: bfloat16 [16, 512, 1536], P('dp', 'seq')
- grad_query: float32 [1536, 1536], P(('seq', 'dp'))
- grad_key: float32 [1536, 768], P(('seq', 'dp'))
- grad_value: float32 [1536, 768], P(('seq', 'dp'))
- grad_output: float32 [1536, 1536], P(('seq', 'dp'))
- grad_gain_attn: float32 [1536], P(('seq', 'dp'))
- grad_gain_ffn: float32 [1536], P(('seq', 'dp'))
- grad_gate: float32 [4096, 1536], P(('seq', 'dp'))
- grad_up: float32 [4096, 1536], P(('seq', 'dp'))
- grad_down: float32 [4096, 1536], P(('seq', 'dp'))
Inputs may be any that keep to these rules, and one draw needn't show every extreme that they name: Within a sequence the positions rise by one from token to token and return to 0 where a new document begins; every sequence's first token has position 0.
All inputs are finite; a program needn't handle non-finite values.
Results may differ from a plain program's by a relative error of at most 0.014.
Values may be sent and summed in bfloat16 or wider, within the bound.
No kernel may reach another device: no remote copies, remote signals or barrier semaphores. Data moves between devices by JAX's collectives and lax.ppermute only.
A program may use at most 256 MiB of HBM per device.

v0:
```python
import jax
import jax.numpy as jnp
from jax import lax
from jax.sharding import PartitionSpec as P

HEADS = 16
KV_HEADS = 8
HEAD = 96


EPS = 1e-05
THETA = 100000.0
NEG = -1e30


def norm_rows(values, gain):
    return values * lax.rsqrt(jnp.mean(values * values, axis=-1, keepdims=True) + EPS) * gain


def norm_back(values, gain, grad):
    _, pull = jax.vjp(norm_rows, values, gain)
    return pull(grad)


def rotate(values, cosine, sine):
    half = values.shape[-1] // 2
    turned = jnp.concatenate([-values[..., half:], values[..., :half]], axis=-1)
    return values * cosine[:, None, :] + turned * sine[:, None, :]


def angle_tables(places):
    offsets = jnp.arange(0, HEAD, 2, dtype=jnp.float32)
    inverse = THETA ** (-offsets / HEAD)
    angles = places.astype(jnp.float32)[:, None] * inverse[None, :]
    angles = jnp.concatenate([angles, angles], axis=-1)
    return (jnp.cos(angles), jnp.sin(angles))


def contract_rows(left, right):
    return lax.dot_general(
        left, right, (((1,), (1,)), ((), ())), preferred_element_type=jnp.float32
    )


def contract_tokens(left, right):
    return lax.dot_general(
        left, right, (((0,), (0,)), ((), ())), preferred_element_type=jnp.float32
    )


def head_layout(values, rows):
    group = HEADS // KV_HEADS
    return (
        values.reshape(rows, KV_HEADS, group, HEAD)
        .transpose(1, 2, 0, 3)
        .reshape(KV_HEADS, group * rows, HEAD)
    )


def flat_layout(values, rows):
    group = HEADS // KV_HEADS
    return (
        values.reshape(KV_HEADS, group, rows, HEAD)
        .transpose(2, 0, 1, 3)
        .reshape(rows, HEADS * HEAD)
    )


def allowed_mask(rows, width, first):
    group = HEADS // KV_HEADS
    query_place = first + jnp.arange(group * rows, dtype=jnp.int32) % rows
    key_place = jnp.arange(width, dtype=jnp.int32)
    return key_place[None, :] <= query_place[:, None]


def scores_of(queries, keys_head, allowed):
    raw = contract_rows(queries, keys_head) * HEAD ** (-0.5)
    return jnp.where(allowed, raw, NEG)


def attend_forward(query_heads, key_heads, value_heads, allowed):

    def one_head(item):
        queries, keys_head, values_head = item
        scores = scores_of(queries, keys_head, allowed)
        top = jnp.max(scores, axis=-1, keepdims=True)
        weights = jnp.exp(scores - top)
        total = jnp.sum(weights, axis=-1, keepdims=True)
        probs = (weights / total).astype(jnp.bfloat16)
        mixed = jnp.dot(probs, values_head, preferred_element_type=jnp.float32)
        return (mixed, top[:, 0] + jnp.log(total[:, 0]))

    return lax.map(one_head, (query_heads, key_heads, value_heads))


def attend_backward(query_heads, key_heads, value_heads, mixed_grads, log_totals, allowed):
    scale = HEAD ** (-0.5)

    def one_head(item):
        queries, keys_head, values_head, mixed_grad, norm_log = item
        scores = scores_of(queries, keys_head, allowed)
        probs = jnp.exp(scores - norm_log[:, None])
        prob_grad = contract_rows(mixed_grad, values_head)
        centre = jnp.sum(probs * prob_grad, axis=-1, keepdims=True)
        score_grad = (probs * (prob_grad - centre)).astype(jnp.bfloat16)
        query_grad = jnp.dot(score_grad, keys_head, preferred_element_type=jnp.float32) * scale
        key_grad = contract_tokens(score_grad, queries) * scale
        value_grad = contract_tokens(probs.astype(jnp.bfloat16), mixed_grad)
        return (query_grad, key_grad, value_grad)

    return lax.map(one_head, (query_heads, key_heads, value_heads, mixed_grads, log_totals))


def grad_terms(
    normed_all,
    projection_all,
    mixed_all,
    attn_grad_all,
    second_all,
    gate_grads,
    up_grads,
    hidden_all,
    grad_all,
):
    return (
        contract_tokens(normed_all, projection_all),
        contract_tokens(mixed_all, attn_grad_all),
        contract_tokens(gate_grads, second_all),
        contract_tokens(up_grads, second_all),
        contract_tokens(hidden_all, grad_all),
    )


def per_device(
    tokens,
    positions,
    out_grad,
    w_query,
    w_key,
    w_value,
    w_output,
    gain_attn,
    gain_ffn,
    w_gate,
    w_up,
    w_down,
):
    micro, rows, width = tokens.shape
    wide = rows * lax.axis_size("seq")
    allowed = allowed_mask(rows, wide, lax.axis_index("seq") * rows)
    query_width = HEADS * HEAD
    pair_width = KV_HEADS * HEAD
    attn_gain_sum = jnp.zeros((width,), jnp.float32)
    ffn_gain_sum = jnp.zeros((width,), jnp.float32)
    normed_list, mixed_list, attn_grad_list, projection_list = ([], [], [], [])
    second_list, hidden_list, gate_grad_list, up_grad_list, grad_list = ([], [], [], [], [])
    output_list, input_grad_list = ([], [])
    for index in range(micro):
        full = (
            lax.all_gather(w_query, ("seq", "dp"), axis=0, tiled=True),
            lax.all_gather(w_key, ("seq", "dp"), axis=0, tiled=True),
            lax.all_gather(w_value, ("seq", "dp"), axis=0, tiled=True),
            lax.all_gather(w_output, ("seq", "dp"), axis=0, tiled=True),
            lax.all_gather(gain_attn, ("seq", "dp"), axis=0, tiled=True),
            lax.all_gather(gain_ffn, ("seq", "dp"), axis=0, tiled=True),
            lax.all_gather(w_gate, ("seq", "dp"), axis=0, tiled=True),
            lax.all_gather(w_up, ("seq", "dp"), axis=0, tiled=True),
            lax.all_gather(w_down, ("seq", "dp"), axis=0, tiled=True),
        )
        query_full, key_full, value_full, output_full = (full[0], full[1], full[2], full[3])
        attn_scale = full[4].astype(jnp.float32)
        ffn_scale = full[5].astype(jnp.float32)
        gate_full, up_full, down_full = (full[6], full[7], full[8])
        inputs = tokens[index].astype(jnp.float32)
        cosine, sine = angle_tables(positions[index])
        normed = norm_rows(inputs, attn_scale).astype(jnp.bfloat16)
        query_raw = jnp.dot(normed, query_full, preferred_element_type=jnp.float32)
        key_raw = jnp.dot(normed, key_full, preferred_element_type=jnp.float32)
        value_raw = jnp.dot(normed, value_full, preferred_element_type=jnp.float32)
        queries = (
            rotate(query_raw.reshape(rows, HEADS, HEAD), cosine, sine)
            .reshape(rows, query_width)
            .astype(jnp.bfloat16)
        )
        keys_local = (
            rotate(key_raw.reshape(rows, KV_HEADS, HEAD), cosine, sine)
            .reshape(rows, pair_width)
            .astype(jnp.bfloat16)
        )
        values_local = value_raw.astype(jnp.bfloat16)
        keys_all, values_all = (
            lax.all_gather(keys_local, "seq", axis=0, tiled=True),
            lax.all_gather(values_local, "seq", axis=0, tiled=True),
        )
        query_heads = head_layout(queries, rows)
        key_heads = keys_all.reshape(wide, KV_HEADS, HEAD).transpose(1, 0, 2)
        value_heads = values_all.reshape(wide, KV_HEADS, HEAD).transpose(1, 0, 2)
        mixed_heads, log_totals = attend_forward(query_heads, key_heads, value_heads, allowed)
        mixed = flat_layout(mixed_heads, rows).astype(jnp.bfloat16)
        first_sum = inputs + jnp.dot(mixed, output_full, preferred_element_type=jnp.float32)
        second = norm_rows(first_sum, ffn_scale).astype(jnp.bfloat16)
        gate_kept = contract_rows(second, gate_full)
        up_kept = contract_rows(second, up_full)
        hidden = (jax.nn.silu(gate_kept) * up_kept).astype(jnp.bfloat16)
        output_list.append(
            (first_sum + jnp.dot(hidden, down_full, preferred_element_type=jnp.float32)).astype(
                jnp.bfloat16
            )
        )
        grad_out = out_grad[index]
        again = (
            lax.all_gather(w_query, ("seq", "dp"), axis=0, tiled=True),
            lax.all_gather(w_key, ("seq", "dp"), axis=0, tiled=True),
            lax.all_gather(w_value, ("seq", "dp"), axis=0, tiled=True),
            lax.all_gather(w_output, ("seq", "dp"), axis=0, tiled=True),
            lax.all_gather(gain_attn, ("seq", "dp"), axis=0, tiled=True),
            lax.all_gather(gain_ffn, ("seq", "dp"), axis=0, tiled=True),
            lax.all_gather(w_gate, ("seq", "dp"), axis=0, tiled=True),
            lax.all_gather(w_up, ("seq", "dp"), axis=0, tiled=True),
            lax.all_gather(w_down, ("seq", "dp"), axis=0, tiled=True),
        )
        query_full, key_full, value_full, output_full = (again[0], again[1], again[2], again[3])
        attn_scale = again[4].astype(jnp.float32)
        ffn_scale = again[5].astype(jnp.float32)
        gate_full, up_full, down_full = (again[6], again[7], again[8])
        gate_value = contract_rows(second, gate_full)
        up_value = contract_rows(second, up_full)
        hidden_grad = contract_rows(grad_out, down_full)
        sigma = jax.nn.sigmoid(gate_value)
        gate_grad = (hidden_grad * up_value * sigma * (1.0 + gate_value * (1.0 - sigma))).astype(
            jnp.bfloat16
        )
        up_grad = (hidden_grad * gate_value * sigma).astype(jnp.bfloat16)
        second_grad = jnp.dot(gate_grad, gate_full, preferred_element_type=jnp.float32) + jnp.dot(
            up_grad, up_full, preferred_element_type=jnp.float32
        )
        first_back, ffn_gain_grad = norm_back(first_sum, ffn_scale, second_grad)
        first_sum_grad = grad_out.astype(jnp.float32) + first_back
        attn_out_grad = first_sum_grad.astype(jnp.bfloat16)
        mixed_grad = contract_rows(attn_out_grad, output_full).astype(jnp.bfloat16)
        query_grad_heads, key_grad_heads, value_grad_heads = attend_backward(
            query_heads, key_heads, value_heads, head_layout(mixed_grad, rows), log_totals, allowed
        )
        query_grad = flat_layout(query_grad_heads, rows)
        key_grad_wide = key_grad_heads.transpose(1, 0, 2).reshape(wide, pair_width)
        value_grad_wide = value_grad_heads.transpose(1, 0, 2).reshape(wide, pair_width)
        key_grad, value_grad = (
            lax.psum_scatter(key_grad_wide, "seq", scatter_dimension=0, tiled=True),
            lax.psum_scatter(value_grad_wide, "seq", scatter_dimension=0, tiled=True),
        )
        query_back = (
            rotate(query_grad.reshape(rows, HEADS, HEAD), cosine, -sine)
            .reshape(rows, query_width)
            .astype(jnp.bfloat16)
        )
        key_back = (
            rotate(key_grad.reshape(rows, KV_HEADS, HEAD), cosine, -sine)
            .reshape(rows, pair_width)
            .astype(jnp.bfloat16)
        )
        value_back = value_grad.astype(jnp.bfloat16)
        normed_grad = (
            contract_rows(query_back, query_full)
            + contract_rows(key_back, key_full)
            + contract_rows(value_back, value_full)
        )
        input_back, attn_gain_grad = norm_back(inputs, attn_scale, normed_grad)
        input_grad_list.append((first_sum_grad + input_back).astype(jnp.bfloat16))
        projection = jnp.concatenate([query_back, key_back, value_back], axis=1)
        attn_gain_sum = attn_gain_sum + attn_gain_grad
        ffn_gain_sum = ffn_gain_sum + ffn_gain_grad
        normed_list.append(normed)
        mixed_list.append(mixed)
        attn_grad_list.append(attn_out_grad)
        projection_list.append(projection)
        second_list.append(second)
        hidden_list.append(hidden)
        gate_grad_list.append(gate_grad)
        up_grad_list.append(up_grad)
        grad_list.append(grad_out)
    terms = grad_terms(
        jnp.concatenate(normed_list, axis=0),
        jnp.concatenate(projection_list, axis=0),
        jnp.concatenate(mixed_list, axis=0),
        jnp.concatenate(attn_grad_list, axis=0),
        jnp.concatenate(second_list, axis=0),
        jnp.concatenate(gate_grad_list, axis=0),
        jnp.concatenate(up_grad_list, axis=0),
        jnp.concatenate(hidden_list, axis=0),
        jnp.concatenate(grad_list, axis=0),
    )
    summed = (
        lax.psum_scatter(terms[0], ("seq", "dp"), scatter_dimension=0, tiled=True),
        lax.psum_scatter(terms[1], ("seq", "dp"), scatter_dimension=0, tiled=True),
        lax.psum_scatter(attn_gain_sum, ("seq", "dp"), scatter_dimension=0, tiled=True),
        lax.psum_scatter(ffn_gain_sum, ("seq", "dp"), scatter_dimension=0, tiled=True),
        lax.psum_scatter(terms[2], ("seq", "dp"), scatter_dimension=0, tiled=True),
        lax.psum_scatter(terms[3], ("seq", "dp"), scatter_dimension=0, tiled=True),
        lax.psum_scatter(terms[4], ("seq", "dp"), scatter_dimension=0, tiled=True),
    )
    projection_rows = summed[0]
    split_key = query_width + pair_width
    split_value = split_key + pair_width
    return (
        jnp.stack(output_list),
        jnp.stack(input_grad_list),
        projection_rows[:, :query_width],
        projection_rows[:, query_width:split_key],
        projection_rows[:, split_key:split_value],
        summed[1],
        summed[2],
        summed[3],
        summed[4],
        summed[5],
        summed[6],
    )


def solution(mesh):
    return jax.shard_map(
        per_device,
        mesh=mesh,
        in_specs=(
            P("dp", "seq", None),
            P("dp", "seq"),
            P("dp", "seq", None),
            P(("seq", "dp"), None),
            P(("seq", "dp"), None),
            P(("seq", "dp"), None),
            P(("seq", "dp"), None),
            P(("seq", "dp")),
            P(("seq", "dp")),
            P(("seq", "dp"), None),
            P(("seq", "dp"), None),
            P(("seq", "dp"), None),
        ),
        out_specs=(
            P("dp", "seq", None),
            P("dp", "seq", None),
            P(("seq", "dp"), None),
            P(("seq", "dp"), None),
            P(("seq", "dp"), None),
            P(("seq", "dp"), None),
            P(("seq", "dp")),
            P(("seq", "dp")),
            P(("seq", "dp"), None),
            P(("seq", "dp"), None),
            P(("seq", "dp"), None),
        ),
        check_vma=False,
    )
```

profile of v0, /device:TPU:0, one launch (start us, length us, event | category | flops | bytes accessed | tf_op | source)
XLA Modules:
  0.0 1987.6 jit_solution(14049257050652909892)
XLA Ops:
  13.2 42.1 %all-reduce.5 = (bf16[1536]{0:T(1024)(128)(2,1)S(1)}, bf16[1536]{0:T(1024)(128)(2,1)S(1)}) all-reduce(bf16[1536]{0:T(1024)(128)(2,1)S(1)} %dynamic-update-slice, bf16[1536]{0:T(1024)(128)(2,1)S(1)} %dynamic-update-slice.1), channel_id=1, replica_groups=mesh['seq'=4,'dp'=8] {'seq','dp'}, use_global_device_ids=true, to_apply=%add | all-reduce | flops 3072 | bytes 12288
  60.7 10.3 all-gather.10.cloned.1.call-done
  71.0 2.8 copy.101
  75.5 19.7 all_gather.37
  97.4 34.9 %all-gather.12.cloned.1.call-done = bf16[1536,768]{1,0:T(8,128)(2,1)} async-done(((bf16[48,768]{1,0:T(8,128)(2,1)}), bf16[1536,768]{1,0:T(8,128)(2,1)}) %all-gather.12.cloned.1.call-update) | async-done | bytes 2359312 | tf_op jit(solution)/shard_map/all_gather | solution.py:162
  134.5 21.3 %all_gather.38 = bf16[512,768]{1,0:T(8,128)(2,1)} all-gather(bf16[128,768]{1,0:T(8,128)(2,1)S(1)} %convolution_convert_fusion.2), channel_id=1, replica_groups=mesh['seq'=4,'dp'=8] {'seq'}, dimensions={0}, use_global_device_ids=true | all-gather | bytes 983040 | tf_op jit(solution)/shard_map/all_gather | solution.py:193
  162.0 21.9 %all_gather.29 = bf16[512,768]{0,1:T(8,128)(2,1)} all-gather(bf16[128,768]{0,1:T(8,128)(2,1)S(1)} %bitcast.481), channel_id=1, replica_groups=mesh['seq'=4,'dp'=8] {'seq'}, dimensions={0}, use_global_device_ids=true | all-gather | bytes 983040 | tf_op jit(solution)/shard_map/all_gather | solution.py:192
  187.6 23.4 %all_gather.31 = bf16[512,768]{1,0:T(8,128)(2,1)S(1)} all-gather(bf16[128,768]{1,0:T(8,128)(2,1)S(1)} %convolution_convert_fusion.3), channel_id=1, replica_groups=mesh['seq'=4,'dp'=8] {'seq'}, dimensions={0}, use_global_device_ids=true | all-gather | bytes 983040 | tf_op jit(solution)/shard_map/all_gather | solution.py:193
  212.0 6.7 copy.99
  218.7 3.8 fusion.185
  223.0 22.0 %while.57 = (s32[]{:T(128)}, bf16[8,256,96]{1,2,0:T(8,128)(2,1)S(1)}, f32[8,256]{1,0:T(8,128)S(1)}, bf16[8,256,96]{2,1,0:T(8,128)(2,1)S(1)}, bf16[8,512,96]{2,1,...) while((s32[]{:T(128)}, ...), condition=%wide.region_10.11_spmd.clone, body=%wide.region_7.10_spmd.clone.sunk | while | flops 51511040 | bytes 2012265 | solution.py:93
  245.9 3.8 fusion.181
  250.7 15.1 while.56
  266.6 4.4 all-gather.14.cloned.1.call-done
  270.9 3.4 multiply_reduce_fusion.7
  275.8 92.4 %all-gather.16.cloned.1.call-done = bf16[4096,1536]{1,0:T(8,128)(2,1)} async-done(((bf16[128,1536]{1,0:T(8,128)(2,1)}), bf16[4096,1536]{1,0:T(8,128)(2,1)}) %all-gather.16.cloned.1.call-update) | async-done | bytes 12582928 | tf_op jit(solution)/shard_map/all_gather | solution.py:166
  368.2 10.0 fusion.211
  378.2 87.0 %all-gather.18.cloned.1.call-done = bf16[4096,1536]{1,0:T(8,128)(2,1)} async-done(((bf16[128,1536]{1,0:T(8,128)(2,1)}), bf16[4096,1536]{1,0:T(8,128)(2,1)}) %all-gather.18.cloned.1.call-update) | async-done | bytes 12582928 | tf_op jit(solution)/shard_map/all_gather | solution.py:167
  465.2 10.0 fusion.212
  475.2 87.2 %all-gather.20.cloned.1.call-done = bf16[4096,1536]{1,0:T(8,128)(2,1)} async-done(((bf16[128,1536]{1,0:T(8,128)(2,1)}), bf16[4096,1536]{1,0:T(8,128)(2,1)}) %all-gather.20.cloned.1.call-update) | async-done | bytes 12582928 | tf_op jit(solution)/shard_map/all_gather | solution.py:168
  562.4 11.4 multiply_convert_fusion.4
  573.8 6.8 fusion.215
  580.7 7.8 multiply_reduce_fusion.3
  588.9 5.5 fusion.213
  594.4 10.0 fusion.214
  604.4 11.1 multiply_convert_fusion.2
  615.5 7.2 fusion.217
  622.7 7.3 multiply_reduce_fusion.2
  641.9 68.9 %while.59 = (s32[]{:T(128)}, f32[8,256,96]{1,2,0:T(8,128)}, f32[8,512,96]{1,2,0:T(8,128)}, f32[8,512,96]{1,2,0:T(8,128)}, bf16[8,256,96]{2,1,0:T(8,128)(2,1)}, /...) while((s32[]{:T(128)}, f32[8,256,96]{1,2,0:T(8,128)}, ...), condition=%wide.region_22.23_spmd.clone, body=%wide.region_20.22_spmd.clone.sunk | while | flops 127213312 | bytes 5090425 | solution.py:111
  710.9 4.8 convolution_convert_fusion.1
  723.4 68.9 %while.58 = (s32[]{:T(128)}, f32[8,256,96]{1,2,0:T(8,128)}, f32[8,512,96]{1,2,0:T(8,128)}, f32[8,512,96]{1,2,0:T(8,128)}, bf16[8,256,96]{2,1,0:T(8,128)(2,1)}, /...) while((s32[]{:T(128)}, f32[8,256,96]{1,2,0:T(8,128)}, ...), condition=%wide.region_15.16_spmd.clone, body=%wide.region_13.15_spmd.clone.sunk | while | flops 127213312 | bytes 5090425 | solution.py:111
  793.1 2.4 reshape.464
  797.7 2.4 reshape.458
  807.7 18.3 reduce-scatter.10.cloned.1.call-done
  829.7 33.0 %reduce-scatter.12.cloned.1.call-done = f32[128,768]{0,1:T(8,128)} async-done(((f32[512,768]{0,1:T(8,128)}), f32[128,768]{0,1:T(8,128)}) %reduce-scatter.12.cloned.1.call-update) | async-done | bytes 393232 | tf_op jit(solution)/shard_map/reduce_scatter | solution.py:249
  864.3 10.6 fusion.108
  875.1 6.4 fusion.157
  881.6 13.8 fusion.96
  895.4 13.9 fusion.100
  910.6 13.5 fusion.104
  924.9 6.9 fusion.94
  931.8 7.3 fusion.95
  949.6 41.9 %all-reduce.4 = (f32[1536]{0:T(1024)S(1)}, f32[1536]{0:T(1024)S(1)}) all-reduce(f32[1536]{0:T(1024)S(1)} %add.248, f32[1536]{0:T(1024)S(1)} %add.249), channel_id=8, replica_groups=mesh['seq'=4,'dp'=8] {'seq','dp'}, use_global_device_ids=true, to_apply=%region_30.31.clone | all-reduce | flops 3072 | bytes 24576
  996.1 86.3 %reduce-scatter.18.cloned.1.call-done = f32[48,3072]{1,0:T(8,128)} async-done(((f32[1536,3072]{1,0:T(8,128)}), f32[48,3072]{1,0:T(8,128)}) %reduce-scatter.18.cloned.1.call-update) | async-done | bytes 589840 | tf_op jit(solution)/shard_map/reduce_scatter | solution.py:293
  1085.8 137.7 %reduce-scatter.20.cloned.1.call-done = f32[48,1536]{1,0:T(8,128)} async-done(((f32[1536,1536]{1,0:T(8,128)}), f32[48,1536]{1,0:T(8,128)}) %reduce-scatter.20.cloned.1.call-update) | async-done | bytes 294928 | tf_op jit(solution)/shard_map/reduce_scatter | solution.py:294
  1223.5 252.4 %reduce-scatter.22.cloned.1.call-done = f32[128,1536]{1,0:T(8,128)} async-done(((f32[4096,1536]{1,0:T(8,128)}), f32[128,1536]{1,0:T(8,128)}) %reduce-scatter.22.cloned.1.call-update) | async-done | bytes 786448 | tf_op jit(solution)/shard_map/reduce_scatter | solution.py:297
  1475.8 251.8 %reduce-scatter.24.cloned.1.call-done = f32[128,1536]{1,0:T(8,128)} async-done(((f32[4096,1536]{1,0:T(8,128)}), f32[128,1536]{1,0:T(8,128)}) %reduce-scatter.24.cloned.1.call-update) | async-done | bytes 786448 | tf_op jit(solution)/shard_map/reduce_scatter | solution.py:298
  1727.7 253.0 %reduce-scatter.26.cloned.1.call-done = f32[128,1536]{1,0:T(8,128)} async-done(((f32[4096,1536]{1,0:T(8,128)}), f32[128,1536]{1,0:T(8,128)}) %reduce-scatter.26.cloned.1.call-update) | async-done | bytes 786448 | tf_op jit(solution)/shard_map/reduce_scatter | solution.py:299
  (492 shorter events, 262.6 us)
Async XLA Ops:
  7.2 48.8 %copy-start.69 = (s32[2,128]{1,0:T(2,128)S(1)}, s32[2,128]{1,0:T(2,128)}, u32[]{:S(2)}) copy-start(s32[2,128]{1,0:T(2,128)} %param.21) | copy-start | bytes 3076
  7.2 50.5 %copy-start.3 = (bf16[2,128,1536]{2,1,0:T(8,128)(2,1)S(1)}, bf16[2,128,1536]{2,1,0:T(8,128)(2,1)}, u32[]{:S(2)}) copy-start(bf16[2,128,1536]{2,1,0:T(8,128)(2,1)} %param.20) | copy-start | bytes 2359300
  7.2 63.7 %all-gather.10.cloned.1.call-start = ((), (), s32[]{:S(2)}) async-start(), calls=%async_computation.10 | async-start | bytes 2433024 | tf_op jit(solution)/shard_map/all_gather | solution.py:161
  8.0 124.3 %all-gather.12.cloned.1.call-start = ((), (), s32[]{:S(2)}) async-start(), calls=%async_computation.11 | async-start | bytes 2433024 | tf_op jit(solution)/shard_map/all_gather | solution.py:162
  8.7 203.3 %all-gather.8.cloned.1.call-start = ((), (), s32[]{:S(2)}) async-start(), calls=%async_computation.9 | async-start | bytes 4866048 | tf_op jit(solution)/shard_map/all_gather | solution.py:160
  9.4 261.5 %all-gather.14.cloned.1.call-start = ((), (), s32[]{:S(2)}) async-start(), calls=%async_computation.12 | async-start | bytes 4866048 | tf_op jit(solution)/shard_map/all_gather | solution.py:163
  10.0 358.2 %all-gather.16.cloned.1.call-start = ((), (), s32[]{:S(2)}) async-start(), calls=%async_computation.13 | async-start | bytes 12976128 | tf_op jit(solution)/shard_map/all_gather | solution.py:166
  10.6 454.6 %all-gather.18.cloned.1.call-start = ((), (), s32[]{:S(2)}) async-start(), calls=%async_computation.14 | async-start | bytes 12976128 | tf_op jit(solution)/shard_map/all_gather | solution.py:167
  11.2 551.2 %all-gather.20.cloned.1.call-start = ((), (), s32[]{:S(2)}) async-start(), calls=%async_computation.15 | async-start | bytes 12976128 | tf_op jit(solution)/shard_map/all_gather | solution.py:168
  11.9 790.4 %reduce-scatter.14.cloned.1.call-start = ((), (), s32[]{:S(2)}) async-start(), calls=%async_computation.18 | async-start | bytes 1966080 | tf_op jit(solution)/shard_map/reduce_scatter | solution.py:248
  55.4 190.4 %copy-start.37 = (f32[1536]{0:T(1024)}, f32[1536]{0:T(1024)S(1)}, u32[]{:S(2)}) copy-start(f32[1536]{0:T(1024)S(1)} %convert_element_type.219) | copy-start | bytes 18436
  161.8 24.3 %copy-start.1 = (bf16[1536,768]{1,0:T(8,128)(2,1)S(1)}, bf16[1536,768]{1,0:T(8,128)(2,1)}, u32[]{:S(2)}) copy-start(bf16[1536,768]{1,0:T(8,128)(2,1)} %all-gather.12.cloned.1.call-done) | copy-start | bytes 7077892
  223.0 22.8 %copy-start.51 = (f32[128]{0:T(128)S(1)}, f32[128]{0:T(128)}, u32[]{:S(2)}) copy-start(f32[128]{0:T(128)} %copy-done.50) | copy-start | bytes 1540
  266.6 7.8 copy-start.17
  275.6 102.6 %copy-start.70 = (f32[128]{0:T(128)}, f32[128]{0:T(128)S(1)}, u32[]{:S(2)}) copy-start(f32[128]{0:T(128)S(1)} %get-tuple-element.558) | copy-start | bytes 1540
  275.6 354.3 %copy-start.56 = (f32[128]{0:T(128)}, f32[128]{0:T(128)S(1)}, u32[]{:S(2)}) copy-start(f32[128]{0:T(128)S(1)} %fusion.197) | copy-start | bytes 1540
  378.2 184.1 %copy-start.7 = (bf16[2,128,1536]{2,1,0:T(8,128)(2,1)S(1)}, bf16[2,128,1536]{2,1,0:T(8,128)(2,1)}, u32[]{:S(2)}) copy-start(bf16[2,128,1536]{2,1,0:T(8,128)(2,1)} %param.22) | copy-start | bytes 2359300
  573.8 6.8 copy-start.15
  573.8 6.8 copy-start.59
  580.6 7.9 slice-start
  580.6 7.8 copy-start.73
  580.6 7.8 slice-start.1
  580.6 8.2 slice-start.2
  588.5 41.5 %copy-start.61 = (f32[128]{0:T(128)}, f32[128]{0:T(128)S(1)}, u32[]{:S(2)}) copy-start(f32[128]{0:T(128)S(1)} %multiply_multiply_fusion.3) | copy-start | bytes 1540
  594.4 10.0 copy-start.8
  615.5 7.2 copy-start.13
  615.5 7.2 copy-start.16
  615.5 16.5 slice-start.3
  622.7 7.3 copy-start.71
  622.7 9.2 slice-start.4
  710.8 95.2 %reduce-scatter.16.cloned.1.call-start = ((), (), s32[]{:S(2)}) async-start(), calls=%async_computation.19 | async-start | bytes 1966080 | tf_op jit(solution)/shard_map/reduce_scatter | solution.py:249
  719.6 106.4 %reduce-scatter.10.cloned.1.call-start = ((), (), s32[]{:S(2)}) async-start(), calls=%async_computation.16 | async-start | bytes 1966080 | tf_op jit(solution)/shard_map/reduce_scatter | solution.py:248
  792.3 70.3 %reduce-scatter.12.cloned.1.call-start = ((), (), s32[]{:S(2)}) async-start(), calls=%async_computation.17 | async-start | bytes 1966080 | tf_op jit(solution)/shard_map/reduce_scatter | solution.py:249
  793.0 289.3 %reduce-scatter.18.cloned.1.call-start = ((), (), s32[]{:S(2)}) async-start(), calls=%async_computation.20 | async-start | bytes 19464192 | tf_op jit(solution)/shard_map/reduce_scatter | solution.py:293
  875.0 348.5 %reduce-scatter.20.cloned.1.call-start = ((), (), s32[]{:S(2)}) async-start(), calls=%async_computation.21 | async-start | bytes 9732096 | tf_op jit(solution)/shard_map/reduce_scatter | solution.py:294
  881.5 594.3 %reduce-scatter.22.cloned.1.call-start = ((), (), s32[]{:S(2)}) async-start(), calls=%async_computation.22 | async-start | bytes 25952256 | tf_op jit(solution)/shard_map/reduce_scatter | solution.py:297
  895.4 832.3 %reduce-scatter.24.cloned.1.call-start = ((), (), s32[]{:S(2)}) async-start(), calls=%async_computation.23 | async-start | bytes 25952256 | tf_op jit(solution)/shard_map/reduce_scatter | solution.py:298
  909.4 1071.3 %reduce-scatter.26.cloned.1.call-start = ((), (), s32[]{:S(2)}) async-start(), calls=%async_computation.24 | async-start | bytes 25952256 | tf_op jit(solution)/shard_map/reduce_scatter | solution.py:299
  924.9 6.9 copy-start.14
  924.9 15.1 slice-start.5
  931.7 8.3 slice-start.6
  931.7 8.2 copy-start.19
  947.5 45.1 %copy-start.66 = (f32[128]{0:T(128)S(1)}, f32[128]{0:T(128)}, u32[]{:S(2)}) copy-start(f32[128]{0:T(128)} %copy-done.65) | copy-start | bytes 1540
  947.6 45.1 %copy-start.68 = (f32[128]{0:T(128)S(1)}, f32[128]{0:T(128)}, u32[]{:S(2)}) copy-start(f32[128]{0:T(128)} %copy-done.67) | copy-start | bytes 1540
  947.6 45.1 %copy-start.57 = (f32[128]{0:T(128)S(1)}, f32[128]{0:T(128)}, u32[]{:S(2)}) copy-start(f32[128]{0:T(128)} %copy-done.56) | copy-start | bytes 1540
  947.6 45.1 %copy-start.64 = (f32[128]{0:T(128)S(1)}, f32[128]{0:T(128)}, u32[]{:S(2)}) copy-start(f32[128]{0:T(128)} %copy-done.63) | copy-start | bytes 1540
  949.6 45.0 %copy-start.60 = (f32[128]{0:T(128)S(1)}, f32[128]{0:T(128)}, u32[]{:S(2)}) copy-start(f32[128]{0:T(128)} %copy-done.58) | copy-start | bytes 1540
  949.6 45.0 %copy-start.62 = (f32[128]{0:T(128)S(1)}, f32[128]{0:T(128)}, u32[]{:S(2)}) copy-start(f32[128]{0:T(128)} %copy-done.61) | copy-start | bytes 1540
  (51 other events, 109.8 us)
Sparse Core Ops, SparseCore 0:
  11.0 59.9 all-gather.9
  73.9 58.3 all-gather.11
  135.2 70.8 all-gather.7
  208.8 62.1 all-gather.13
  273.7 94.5 all-gather.15
  371.0 94.2 all-gather.17
  468.1 94.2 all-gather.19
  710.9 33.5 reduce-scatter.13
  746.8 34.2 reduce-scatter.15
  792.4 33.5 reduce-scatter.9
  828.3 34.2 reduce-scatter.11
  875.1 207.1 reduce-scatter.17
  1088.8 134.5 reduce-scatter.19
  1231.5 244.3 reduce-scatter.21
  1482.7 244.9 reduce-scatter.23
  1735.7 244.9 reduce-scatter.25
where the time goes:
time: 2000 us; the launch traced here: 1990 us
  waiting for transfers between devices  1350 us (68%)
  matrix products  350 us (18%)
  blocking collectives  170 us (8%)
  local copies, waits for them, and re-layouts  69.3 us (3%)
  other arithmetic  27.5 us (1%)
    reduce_scatter x1, waiting for transfers between devices, per_device(): lax.psum_scatter(terms[4], ('seq', 'dp'), scatter_dimension=0, tiled=True)  253 us
    reduce_scatter x1, waiting for transfers between devices, per_device(): lax.psum_scatter(terms[2], ('seq', 'dp'), scatter_dimension=0, tiled=True)  252 us
    reduce_scatter x1, waiting for transfers between devices, per_device(): lax.psum_scatter(terms[3], ('seq', 'dp'), scatter_dimension=0, tiled=True)  252 us
    reduce_scatter x1, waiting for transfers between devices, per_device(): lax.psum_scatter(terms[1], ('seq', 'dp'), scatter_dimension=0, tiled=True)  138 us
    dot_general x62, matrix products, contract_rows(): lax.dot_general(left, right, (((1,), (1,)), ((), ())), preferred_element_...  133 us
    dot_general x37, matrix products, contract_tokens(): lax.dot_general(left, right, (((0,), (0,)), ((), ())), preferred_element_...  114 us
    all_gather x1, waiting for transfers between devices, per_device(): lax.all_gather(w_gate, ('seq', 'dp'), axis=0, tiled=True)  92.4 us
    all_gather x1, waiting for transfers between devices, per_device(): lax.all_gather(w_down, ('seq', 'dp'), axis=0, tiled=True)  87.2 us
  transfers between devices with their start and end apart: 16, of which 13 were waited for; matrix products, arithmetic and copies ran while one was open for 14% of the time, Pallas kernels for 0%

commit v1 on v0

v1 whole, which is shorter than its diff:
```python
import jax
import jax.numpy as jnp
from jax import lax
from jax.sharding import PartitionSpec as P

HEADS = 16
KV_HEADS = 8
HEAD = 96
GROUP = HEADS // KV_HEADS

EPS = 1e-05
THETA = 100000.0
NEG = -1e30
BF = jnp.bfloat16
F32 = jnp.float32


def inverse_rms(values):
    return lax.rsqrt(jnp.mean(values * values, axis=-1, keepdims=True) + EPS)


def rotate(values, cosine, sine):
    half = values.shape[-1] // 2
    turned = jnp.concatenate([-values[..., half:], values[..., :half]], axis=-1)
    return values * cosine[:, None, :] + turned * sine[:, None, :]


def angle_tables(places):
    offsets = jnp.arange(0, HEAD, 2, dtype=F32)
    inverse = THETA ** (-offsets / HEAD)
    angles = places.astype(F32)[:, None] * inverse[None, :]
    angles = jnp.concatenate([angles, angles], axis=-1)
    return (jnp.cos(angles), jnp.sin(angles))


def mm(left, right):
    return jnp.dot(left, right, preferred_element_type=F32)


def mm_t(left, right):
    return lax.dot_general(left, right, (((1,), (1,)), ((), ())), preferred_element_type=F32)


def t_mm(left, right):
    return lax.dot_general(left, right, (((0,), (0,)), ((), ())), preferred_element_type=F32)


class Moves:
    def __init__(self):
        self.Z = lax.axis_size("seq")
        self.DP = lax.axis_size("dp")
        self.Q = self.DP // 4
        self.zi = lax.axis_index("seq")
        place = lax.axis_index("dp")
        self.qi = place // 4
        self.xi = (place // 2) % 2
        self.ci = place % 2
        self.index = {"z": self.zi, "q": self.qi, "x": self.xi, "c": self.ci}
        self.size = {"z": self.Z, "q": self.Q, "x": 2, "c": 2}

    def step(self, axis, value):
        if axis == "c":
            return lax.ppermute(value, "dp", [(i, i ^ 1) for i in range(self.DP)])
        if axis == "x":
            return lax.ppermute(value, "dp", [(i, i ^ 2) for i in range(self.DP)])
        if axis == "q":
            return lax.ppermute(
                value, "dp", [(i, i % 4 + 4 * ((i // 4 + 1) % self.Q)) for i in range(self.DP)]
            )
        return lax.ppermute(value, "seq", [(i, (i + 1) % self.Z) for i in range(self.Z)])

    def up(self, value):
        return lax.ppermute(value, "seq", [(i, i + 1) for i in range(self.Z - 1)])

    def down(self, value):
        return lax.ppermute(value, "seq", [(i + 1, i) for i in range(self.Z - 1)])

    def gather(self, value, name, position, step=None):
        size, index = self.size[name], self.index[name]
        step = step or (lambda v: self.step(name, v))
        blocks = [value]
        for _ in range(size - 1):
            blocks.append(step(blocks[-1]))
        if size == 2:
            return jnp.where(
                index == 0, jnp.stack(blocks, axis=position), jnp.stack(blocks[::-1], axis=position)
            )
        out = jnp.zeros(value.shape[:position] + (size,) + value.shape[position:], value.dtype)
        for k, block in enumerate(blocks):
            out = lax.dynamic_update_slice_in_dim(
                out, jnp.expand_dims(block, position), (index - k) % size, axis=position
            )
        return out

    def scatter(self, value, name, position, step=None, sign=1):
        size, index = self.size[name], self.index[name]
        step = step or (lambda v: self.step(name, v))

        def take(k):
            return lax.dynamic_index_in_dim(
                value, (index - sign * k) % size, axis=position, keepdims=False
            )

        received = None
        for k in range(1, size):
            part = take(k)
            if received is not None:
                part = part + received
            received = step(part.astype(BF)).astype(F32)
        return take(0) + received


def head_layout(values, seqs, rows):
    return (
        values.reshape(seqs, rows, KV_HEADS, GROUP, HEAD)
        .transpose(2, 0, 3, 1, 4)
        .reshape(KV_HEADS, seqs, GROUP * rows, HEAD)
    )


def flat_layout(values, seqs, rows):
    return (
        values.reshape(KV_HEADS, seqs, GROUP, rows, HEAD)
        .transpose(1, 3, 0, 2, 4)
        .reshape(seqs * rows, HEADS * HEAD)
    )


def key_layout(values, seqs, wide):
    return values.reshape(seqs, wide, KV_HEADS, HEAD).transpose(2, 0, 1, 3)


def key_flat(values, seqs, wide):
    return values.transpose(1, 2, 0, 3).reshape(seqs * wide, KV_HEADS * HEAD)


def allowed_mask(rows, width, first):
    query_place = first + jnp.arange(GROUP * rows, dtype=jnp.int32) % rows
    key_place = jnp.arange(width, dtype=jnp.int32)
    return key_place[None, :] <= query_place[:, None]


def attend_forward(query_heads, key_heads, value_heads, allowed):
    def one(item):
        queries, keys, values = item
        raw = jnp.einsum("sqd,skd->sqk", queries, keys, preferred_element_type=F32) * HEAD ** (-0.5)
        scores = jnp.where(allowed, raw, NEG)
        top = jnp.max(scores, axis=-1, keepdims=True)
        weights = jnp.exp(scores - top)
        total = jnp.sum(weights, axis=-1, keepdims=True)
        probs = (weights / total).astype(BF)
        mixed = jnp.einsum("sqk,skd->sqd", probs, values, preferred_element_type=F32)
        return (mixed.astype(BF), top[..., 0] + jnp.log(total[..., 0]))

    return lax.map(one, (query_heads, key_heads, value_heads))


def attend_backward(query_heads, key_heads, value_heads, mixed_grads, log_totals, allowed):
    scale = HEAD ** (-0.5)

    def one(item):
        queries, keys, values, mixed_grad, norm_log = item
        raw = jnp.einsum("sqd,skd->sqk", queries, keys, preferred_element_type=F32) * scale
        scores = jnp.where(allowed, raw, NEG)
        probs = jnp.exp(scores - norm_log[..., None])
        prob_grad = jnp.einsum("sqd,skd->sqk", mixed_grad, values, preferred_element_type=F32)
        centre = jnp.sum(probs * prob_grad, axis=-1, keepdims=True)
        score_grad = (probs * (prob_grad - centre)).astype(BF)
        query_grad = jnp.einsum("sqk,skd->sqd", score_grad, keys, preferred_element_type=F32) * scale
        key_grad = jnp.einsum("sqk,sqd->skd", score_grad, queries, preferred_element_type=F32) * scale
        value_grad = jnp.einsum(
            "sqk,sqd->skd", probs.astype(BF), mixed_grad, preferred_element_type=F32
        )
        return (query_grad, key_grad, value_grad)

    return lax.map(one, (query_heads, key_heads, value_heads, mixed_grads, log_totals))


def per_device(
    tokens,
    positions,
    out_grad,
    w_query,
    w_key,
    w_value,
    w_output,
    gain_attn,
    gain_ffn,
    w_gate,
    w_up,
    w_down,
):
    move = Moves()
    Z, Q = move.Z, move.Q
    seqs, rows, width = tokens.shape
    wide = rows * Z
    own_rows = seqs * rows
    query_width = HEADS * HEAD
    pair_width = KV_HEADS * HEAD
    share = w_query.shape[0]
    units = w_gate.shape[0]
    allowed = allowed_mask(rows, wide, move.zi * rows)

    gains = jnp.pad(jnp.stack([gain_attn, gain_ffn]), ((0, 0), (0, 128 - share)))
    for position, name in enumerate("zqxc"):
        gains = move.gather(gains, name, position)
    gains = gains[..., :share].transpose(4, 0, 1, 2, 3, 5).reshape(2, width).astype(F32)
    attn_scale, ffn_scale = gains[0:1], gains[1:2]

    places_all = move.gather(positions, "z", 1, move.up).reshape(seqs * wide)
    tokens_all = move.gather(tokens, "z", 1, move.up).reshape(seqs * wide, width)

    def gather_rows(shard, order):
        dims = []
        for name in order:
            position = sum(1 for d in dims if "zqxc".index(d) < "zqxc".index(name))
            shard = move.gather(shard, name, position)
            dims.append(name)
        return shard.reshape((-1,) + shard.shape[-1:])

    pair_full = gather_rows(jnp.concatenate([w_key, w_value], axis=1), "zqxc")
    query_full = gather_rows(w_query, "zxqc")
    output_full = gather_rows(w_output, "zqxc")

    block = jnp.concatenate([w_gate, w_up, w_down], axis=0)
    ffn_blocks = []
    for k in range(Z):
        if k:
            block = move.step("z", block)
        line = [block]
        for _ in range(Q - 1):
            line.append(move.step("q", line[-1]))
        ffn_blocks.append(line)

    def spread(value):
        value = jnp.concatenate([value, move.step("x", value)], axis=0)
        return jnp.concatenate([value, move.step("c", value)], axis=0)

    def collect(value):
        value = value[: 2 * own_rows] + move.step("c", value[2 * own_rows :])
        return value[:own_rows] + move.step("x", value[own_rows:].astype(BF)).astype(F32)

    grad_out = out_grad.reshape(own_rows, width)
    grad_spread = spread(grad_out)

    inputs = tokens.reshape(own_rows, width).astype(F32)
    inverse1 = inverse_rms(inputs)
    normed = (inputs * inverse1 * attn_scale).astype(BF)
    inputs_all = tokens_all.astype(F32)
    normed_all = (inputs_all * inverse_rms(inputs_all) * attn_scale).astype(BF)
    cosine, sine = angle_tables(positions.reshape(own_rows))
    cosine_all, sine_all = angle_tables(places_all)
    query_raw = mm(normed, query_full)
    pair_raw = mm(normed_all, pair_full)
    queries = rotate(query_raw.reshape(own_rows, HEADS, HEAD), cosine, sine).astype(BF)
    keys = rotate(
        pair_raw[:, :pair_width].reshape(seqs * wide, KV_HEADS, HEAD), cosine_all, sine_all
    ).astype(BF)
    values = pair_raw[:, pair_width:].astype(BF)
    query_heads = head_layout(queries, seqs, rows)
    key_heads = key_layout(keys, seqs, wide)
    value_heads = key_layout(values, seqs, wide)
    mixed_heads, log_totals = attend_forward(query_heads, key_heads, value_heads, allowed)
    mixed = flat_layout(mixed_heads, seqs, rows)
    first_sum = inputs + mm(mixed, output_full)

    inverse2 = inverse_rms(first_sum)
    second = (first_sum * inverse2 * ffn_scale).astype(BF)
    second_spread = spread(second)
    out_part = 0.0
    second_grad_part = 0.0
    ffn_sums = []
    for k in range(Z):
        line = ffn_blocks[k]
        gate_w = jnp.concatenate([b[:units] for b in line], axis=0)
        up_w = jnp.concatenate([b[units : 2 * units] for b in line], axis=0)
        down_w = jnp.concatenate([b[2 * units :] for b in line], axis=0)
        gate = mm_t(second_spread, gate_w)
        up = mm_t(second_spread, up_w)
        sigma = jax.nn.sigmoid(gate)
        hidden = (gate * sigma * up).astype(BF)
        out_part = out_part + mm(hidden, down_w)
        hidden_grad = mm_t(grad_spread, down_w)
        gate_grad = (hidden_grad * up * sigma * (1.0 + gate * (1.0 - sigma))).astype(BF)
        up_grad = (hidden_grad * gate * sigma).astype(BF)
        second_grad_part = second_grad_part + mm(gate_grad, gate_w) + mm(up_grad, up_w)
        gate_sum = t_mm(gate_grad, second_spread)
        up_sum = t_mm(up_grad, second_spread)
        down_sum = t_mm(hidden, grad_spread)
        received = None
        for j in list(range(1, Q)) + [0]:
            cut = slice(j * units, (j + 1) * units)
            part = jnp.concatenate([gate_sum[cut], up_sum[cut], down_sum[cut]], axis=0)
            if received is not None:
                part = part + received
            if j:
                received = move.step("q", part.astype(BF)).astype(F32)
        ffn_sums.append(part)
    received = None
    for k in list(range(1, Z)) + [0]:
        part = ffn_sums[k]
        if received is not None:
            part = part + received
        if k:
            received = move.step("z", part.astype(BF)).astype(F32)
    grad_gate, grad_up, grad_down = part[:units], part[units : 2 * units], part[2 * units :]

    layer_out = (first_sum + collect(out_part)).astype(BF)
    second_grad = collect(second_grad_part)
    scaled2 = second_grad * ffn_scale
    ffn_gain_part = jnp.sum(second_grad * first_sum * inverse2, axis=0)
    first_grad = (
        grad_out.astype(F32)
        + inverse2 * scaled2
        - first_sum * inverse2**3 * jnp.mean(scaled2 * first_sum, axis=-1, keepdims=True)
    )

    attn_out_grad = first_grad.astype(BF)
    mixed_grad = mm_t(attn_out_grad, output_full).astype(BF)
    query_grad_heads, key_grad_heads, value_grad_heads = attend_backward(
        query_heads, key_heads, value_heads, head_layout(mixed_grad, seqs, rows), log_totals, allowed
    )
    query_grad = flat_layout(query_grad_heads, seqs, rows)
    query_back = (
        rotate(query_grad.reshape(own_rows, HEADS, HEAD), cosine, -sine)
        .reshape(own_rows, query_width)
        .astype(BF)
    )
    key_back = (
        rotate(
            key_flat(key_grad_heads, seqs, wide).reshape(seqs * wide, KV_HEADS, HEAD),
            cosine_all,
            -sine_all,
        )
        .reshape(seqs * wide, pair_width)
        .astype(BF)
    )
    pair_back = jnp.concatenate(
        [key_back, key_flat(value_grad_heads, seqs, wide).astype(BF)], axis=1
    )

    def scatter_rows(value, order):
        value = value.reshape(Z, Q, 2, 2, share, value.shape[-1])
        dims = list("zqxc")
        for name in order:
            value = move.scatter(value, name, dims.index(name))
            dims.remove(name)
        return value

    output_sum = t_mm(mixed, attn_out_grad)
    output_sum = jnp.concatenate(
        [output_sum, jnp.broadcast_to(ffn_gain_part[:, None], (width, 128))], axis=1
    )
    output_sum = scatter_rows(output_sum, "cxqz")
    grad_output, grad_gain_ffn = output_sum[:, :width], output_sum[:, width]
    grad_query = scatter_rows(t_mm(normed, query_back), "cqxz")
    grad_pair = scatter_rows(t_mm(normed_all, pair_back), "cxqz")
    grad_key, grad_value = grad_pair[:, :pair_width], grad_pair[:, pair_width:]
    grad_gain_attn = (
        jnp.sum(grad_query * w_query.astype(F32), axis=1)
        + jnp.sum(grad_key * w_key.astype(F32), axis=1)
        + jnp.sum(grad_value * w_value.astype(F32), axis=1)
    ) / gain_attn.astype(F32)

    pair_grad = mm_t(pair_back, pair_full).reshape(seqs, Z, rows, width)
    pair_grad = move.scatter(pair_grad, "z", 1, move.down, -1).reshape(own_rows, width)
    normed_grad = mm_t(query_back, query_full) + pair_grad
    scaled1 = normed_grad * attn_scale
    in_grad = (
        first_grad
        + inverse1 * scaled1
        - inputs * inverse1**3 * jnp.mean(scaled1 * inputs, axis=-1, keepdims=True)
    ).astype(BF)
    return (
        layer_out.reshape(seqs, rows, width),
        in_grad.reshape(seqs, rows, width),
        grad_query,
        grad_key,
        grad_value,
        grad_output,
        grad_gain_attn,
        grad_gain_ffn,
        grad_gate,
        grad_up,
        grad_down,
    )


def solution(mesh):
    rows = P(("seq", "dp"), None)
    vector = P(("seq", "dp"))
    act = P("dp", "seq", None)
    return jax.shard_map(
        per_device,
        mesh=mesh,
        in_specs=(act, P("dp", "seq"), act, rows, rows, rows, rows, vector, vector, rows, rows, rows),
        out_specs=(act, act, rows, rows, rows, rows, vector, vector, rows, rows, rows),
        check_vma=False,
    )
```

time: 2000 us -> 953 us (0.48)
  waiting for transfers between devices: 1350 us -> 293 us
  blocking collectives: 170 us -> 0 us
  matrix products: 350 us -> 213 us
  local copies, waits for them, and re-layouts: 69.3 us -> 202 us
  other arithmetic: 27.5 us -> 138 us
  starting transfers between devices: 0.63 us -> 90.4 us
    reduce_scatter x9 -> x0, waiting for transfers between devices: 1030 us -> none  [the longest x1 253 us: per_device(): lax.psum_scatter(terms[4], ('seq', 'dp'), scatter_dimension=0, tiled=True)]
    all_gather x7 -> x0, waiting for transfers between devices: 316 us -> none  [the longest x1 92.4 us: per_device(): lax.all_gather(w_gate, ('seq', 'dp'), axis=0, tiled=True)]
    ppermute x0 -> x73, waiting for transfers between devices: none -> 293 us  [the longest x27 98.3 us: step(): lax.ppermute(value, 'seq', [(i, (i + 1) % self.Z) for i in range(self.Z)])]
    dot_general x145 -> x101, matrix products: 350 us -> 213 us  [the longest x15 65.6 us: mm(): return jnp.dot(left, right, preferred_element_type=F32)]
    ppermute x0 -> x73, starting transfers between devices: none -> 90.4 us  [the longest x27 37.1 us: step(): lax.ppermute(value, 'seq', [(i, (i + 1) % self.Z) for i in range(self.Z)])]
    all_gather x4 -> x0, blocking collectives: 86.2 us -> none  [the longest x2 44.7 us: per_device(): lax.all_gather(values_local, 'seq', axis=0, tiled=True)]
    unnamed x2 -> x0, blocking collectives: 84 us -> none
    select_n x0 -> x19, other arithmetic: none -> 34.6 us  [gather(): jnp.where(index == 0, jnp.stack(blocks, axis=position), jnp.stack(blocks[...]
  transfers between devices with their start and end apart: 16 -> 73, of which waited for: 13 -> 36; matrix products, arithmetic and copies ran while one was open for 14% -> 49% of each run, Pallas kernels for 0% -> 0%
where the time goes in v1:
time: 953 us; the launch traced here: 940 us
  waiting for transfers between devices  293 us (31%)
  matrix products  213 us (22%)
  local copies, waits for them, and re-layouts  202 us (21%)
  other arithmetic  138 us (14%)
  starting transfers between devices  90.4 us (9%)
    ppermute x27, waiting for transfers between devices, step(): lax.ppermute(value, 'seq', [(i, (i + 1) % self.Z) for i in range(self.Z)])  98.3 us
    ppermute x15, waiting for transfers between devices, step(): lax.ppermute(value, 'dp', [(i, i % 4 + 4 * ((i // 4 + 1) % self.Q)) for i...  92.1 us
    dot_general x15, matrix products, mm(): return jnp.dot(left, right, preferred_element_type=F32)  65.6 us
    ppermute x11, waiting for transfers between devices, step(): return lax.ppermute(value, 'dp', [(i, i ^ 2) for i in range(self.DP)])  64.7 us
    ppermute x27, starting transfers between devices, step(): lax.ppermute(value, 'seq', [(i, (i + 1) % self.Z) for i in range(self.Z)])  37.1 us
    dot_general x15, matrix products, t_mm(): lax.dot_general(left, right, (((0,), (0,)), ((), ())), preferred_element_...  35.9 us
    select_n x19, other arithmetic, gather(): jnp.where(index == 0, jnp.stack(blocks, axis=position), jnp.stack(blocks[...  34.6 us
    dot_general x15, matrix products, mm_t(): lax.dot_general(left, right, (((1,), (1,)), ((), ())), preferred_element_...  29.9 us
  transfers between devices with their start and end apart: 73, of which 36 were waited for; matrix products, arithmetic and copies ran while one was open for 49% of the time, Pallas kernels for 0%

profile of v1, /device:TPU:0, one launch (start us, length us, event | category | flops | bytes accessed | tf_op | source)
XLA Modules:
  0.0 940.1 jit_solution(1367830930922115249)
XLA Ops:
  6.7 4.4 collective-permute-start.12
  52.6 7.0 fusion.142
  63.9 5.2 mul.516
  72.8 4.9 copy.188
  94.6 24.5 %collective-permute-done.16 = bf16[48,1536]{1,0:T(8,128)(2,1)S(1)} collective-permute-done((bf16[48,1536]{1,0:T(8,128)(2,1)}, bf16[48,1536]{1,0:T(8,128)(2,1)S(1)}, u32[]{:S(2)}, u32[]{:S(2)}) %collective-permute-start.16) | collective-permute-done | bytes 147488 | tf_op jit(solution)/shard_map/ppermute | solution.py:70
  119.8 6.5 collective-permute-done.7
  126.9 6.3 collective-permute-done.25
  133.9 6.3 collective-permute-done.17
  140.8 7.2 collective-permute-done.8
  148.7 6.3 collective-permute-done.26
  161.9 8.4 collective-permute-done.18
  195.4 12.2 %collective-permute-start.35 = (bf16[384,1536]{1,0:T(8,128)(2,1)}, bf16[384,1536]{1,0:T(8,128)(2,1)}, u32[]{:S(2)}, u32[]{:S(2)}) collective-permute-start(bf16[384,1536]{1,0:T(8,128)(2,1)} %collective-permute-done.33), channel_id=1, source_target_pairs={{0,8},{8,16},{16,24},{24,0},{1,9},{9,17},{17,25},{25,1},{2,10},{10... | collective-permute-start | bytes 3538952 | tf_op jit(solution)/shard_map/ppermute | solution.py:70
  221.3 11.6 %collective-permute-done.28 = bf16[4,2,48,1536]{3,2,0,1:T(8,128)(2,1)S(1)} collective-permute-done((bf16[4,2,48,1536]{3,2,0,1:T(8,128)(2,1)S(1)}, bf16[4,2,48,1536]{3,2,0,1:T(8,128)(2,1)S(1)}, u32[]{:S(2)}, u32[]{:S(2)}) %collective-permute-start.28) | collective-permute-done | bytes 1179680 | tf_op jit(solution)/shard_map/ppermute | solution.py:65
  238.3 8.5 collective-permute-done.14
  250.0 4.6 copy.195
  265.4 5.0 fusion.208
  288.8 5.8 fusion.86
  302.8 5.5 maximum_select_fusion
  308.3 7.2 copy.159
  322.2 28.5 %while.28 = (s32[]{:T(128)}, bf16[8,2,256,96]{2,3,1,0:T(8,128)(2,1)}, f32[8,2,256]{2,1,0:T(2,128)}, bf16[8,2,256,96]{2,3,1,0:T(8,128)(2,1)S(1)}, bf16[8,2,512,96...) while((s32[]{:T(128)}, ...), condition=%wide.region_5.6_spmd.clone, body=%wide.region_2.5_spmd.clone.sunk | while | flops 102940160 | bytes 4017749 | solution.py:155
  350.7 7.6 maximum_select_fusion.2
  372.3 12.7 %collective-permute-done.30 = bf16[256,1536]{1,0:T(8,128)(2,1)S(1)} collective-permute-done((bf16[256,1536]{1,0:T(8,128)(2,1)S(1)}, bf16[256,1536]{1,0:T(8,128)(2,1)S(1)}, u32[]{:S(2)}, u32[]{:S(2)}) %collective-permute-start.30) | collective-permute-done | bytes 786464 | tf_op jit(solution)/shard_map/ppermute | solution.py:65
  390.4 8.3 collective-permute-done.38
  475.0 17.6 %add_add_fusion = f32[1024,1536]{1,0:T(8,128)} fusion(f32[1024,1536]{1,0:T(8,128)} %fusion.110, f32[1024,1536]{1,0:T(8,128)} %fusion.114, f32[1024,1536]{1,0:T(8,128)} %fusion.116, f32[1024,1536]{1,0:T(8,128)} %fusion.120, f32[1024,1536]{1,0:T(8,128)} %fusion.122, f32[1024,1536]{1,0:T(8,128)} %fusion.128, f32[1024,1536]{1,0:T(8,128)} %fusion.126, ...), kind=kOutput, calls=%fused_computation.64 | convolution fusion | flops 817889280 | bytes 51642368 | tf_op jit(solution)/shard_map/dot_general | solution.py:37
  497.1 4.3 add_add_fusion.1
  502.0 18.1 %collective-permute-done.69 = bf16[384,1536]{1,0:T(8,128)(2,1)} collective-permute-done((bf16[384,1536]{1,0:T(8,128)(2,1)}, bf16[384,1536]{1,0:T(8,128)(2,1)}, u32[]{:S(2)}, u32[]{:S(2)}) %collective-permute-start.69) | collective-permute-done | bytes 1179680 | tf_op jit(solution)/shard_map/ppermute | solution.py:67
  532.9 16.1 %collective-permute-done.70 = bf16[384,1536]{1,0:T(8,128)(2,1)S(1)} collective-permute-done((bf16[384,1536]{1,0:T(8,128)(2,1)S(1)}, bf16[384,1536]{1,0:T(8,128)(2,1)S(1)}, u32[]{:S(2)}, u32[]{:S(2)}) %collective-permute-start.70) | collective-permute-done | bytes 1179680 | tf_op jit(solution)/shard_map/ppermute | solution.py:70
  554.4 26.9 %collective-permute-done.67 = bf16[384,1536]{1,0:T(8,128)(2,1)S(1)} collective-permute-done((bf16[384,1536]{1,0:T(8,128)(2,1)S(1)}, bf16[384,1536]{1,0:T(8,128)(2,1)S(1)}, u32[]{:S(2)}, u32[]{:S(2)}) %collective-permute-start.67) | collective-permute-done | bytes 1179680 | tf_op jit(solution)/shard_map/ppermute | solution.py:67
  599.0 69.9 %while.29 = (s32[]{:T(128)}, f32[8,2,256,96]{2,3,1,0:T(8,128)}, f32[8,2,512,96]{2,3,1,0:T(8,128)S(1)}, bf16[8,2,512,96]{2,3,1,0:T(8,128)(2,1)}, bf16[8,2,256,96]...) while((s32[]{:T(128)}, f32[8,2,256,96]{2,3,1,0:T(8,128)}, ...), condition=%wide.region_10.11_spmd.clone, body=%wide.region_8.10_spmd.clone.sunk | while | flops 254295552 | bytes 10109041 | solution.py:176
  672.6 5.1 reshape.1200
  677.7 5.1 reshape.1198
  691.2 6.6 fusion.97
  705.5 4.4 add_convert_fusion
  710.6 5.1 fusion.56
  720.9 5.1 copy.190
  729.5 7.0 fusion.52
  741.5 8.5 pad_maximum_fusion
  760.9 11.0 %copy.202 = f32[1536,1664]{1,0:T(8,128)} copy(f32[1536,1664]{0,1:T(8,128)} %pad_maximum_fusion) | data formatting | bytes 20447232 | tf_op jit(solution)/shard_map/concatenate | solution.py:351
  775.4 4.4 fusion.59
  783.9 12.5 %collective-permute-done.46 = bf16[2,128,1536]{2,1,0:T(8,128)(2,1)S(1)} collective-permute-done((bf16[2,128,1536]{2,1,0:T(8,128)(2,1)S(1)}, bf16[2,128,1536]{2,1,0:T(8,128)(2,1)S(1)}, u32[]{:S(2)}, u32[]{:S(2)}) %collective-permute-start.46) | collective-permute-done | bytes 786464 | tf_op jit(solution)/shard_map/ppermute | solution.py:76
  805.0 14.1 %collective-permute-done.47 = bf16[2,128,1536]{2,1,0:T(8,128)(2,1)S(1)} collective-permute-done((bf16[2,128,1536]{2,1,0:T(8,128)(2,1)S(1)}, bf16[2,128,1536]{2,1,0:T(8,128)(2,1)S(1)}, u32[]{:S(2)}, u32[]{:S(2)}) %collective-permute-start.47) | collective-permute-done | bytes 786464 | tf_op jit(solution)/shard_map/ppermute | solution.py:76
  837.6 23.5 %collective-permute-done.61 = bf16[4,2,48,1664]{3,2,1,0:T(8,128)(2,1)S(1)} collective-permute-done((bf16[4,2,48,1664]{3,2,1,0:T(8,128)(2,1)S(1)}, bf16[4,2,48,1664]{3,2,1,0:T(8,128)(2,1)S(1)}, u32[]{:S(2)}, u32[]{:S(2)}) %collective-permute-start.61) | collective-permute-done | bytes 1277984 | tf_op jit(solution)/shard_map/ppermute | solution.py:65
  864.0 4.6 collective-permute-done.57
  875.7 4.8 collective-permute-done.62
  882.4 21.3 %collective-permute-done.49 = bf16[4,2,48,1536]{3,2,1,0:T(8,128)(2,1)S(1)} collective-permute-done((bf16[4,2,48,1536]{3,2,1,0:T(8,128)(2,1)S(1)}, bf16[4,2,48,1536]{3,2,1,0:T(8,128)(2,1)S(1)}, u32[]{:S(2)}, u32[]{:S(2)}) %collective-permute-start.49) | collective-permute-done | bytes 1179680 | tf_op jit(solution)/shard_map/ppermute | solution.py:67
  906.7 10.5 %collective-permute-done.50 = bf16[4,48,1536]{2,1,0:T(8,128)(2,1)S(1)} collective-permute-done((bf16[4,48,1536]{2,1,0:T(8,128)(2,1)S(1)}, bf16[4,48,1536]{2,1,0:T(8,128)(2,1)S(1)}, u32[]{:S(2)}, u32[]{:S(2)}) %collective-permute-start.50) | collective-permute-done | bytes 589856 | tf_op jit(solution)/shard_map/ppermute | solution.py:65
  919.8 4.7 collective-permute-done.51
  931.6 4.0 collective-permute-done.65
  (758 shorter events, 515.4 us)
Async XLA Ops:
  3.7 81.9 %collective-permute-start.15 = (bf16[48,1536]{1,0:T(8,128)(2,1)}, bf16[48,1536]{1,0:T(8,128)(2,1)}, u32[]{:S(2)}, u32[]{:S(2)}) collective-permute-start(bf16[48,1536]{1,0:T(8,128)(2,1)} %constant_dynamic-update-slice_fusion.4), channel_id=1, source_target_pairs={{0,8},{8,16},{16,24},{24,0},{1,9},{9,17},{17,25},{25,1},{2,10},{10... | collective-permute-start | bytes 442376 | tf_op jit(solution)/shard_map/ppermute | solution.py:70
  6.7 150.6 %collective-permute-start.12 = (bf16[2,128,1536]{2,1,0:T(8,128)(2,1)}, bf16[2,128,1536]{2,1,0:T(8,128)(2,1)}, u32[]{:S(2)}, u32[]{:S(2)}) collective-permute-start(bf16[2,128,1536]{2,1,0:T(8,128)(2,1)} %param.16), channel_id=1, source_target_pairs={{0,8},{8,16},{16,24},{1,9},{9,17},{17,25},{2,10},{10,18},{18,26},{... | collective-permute-start | bytes 2359304 | tf_op jit(solution)/shard_map/ppermute | solution.py:73
  12.3 22.0 %collective-permute-start = (bf16[2,128]{1,0:T(2,128)(2,1)}, bf16[2,128]{1,0:T(2,128)(2,1)}, u32[]{:S(2)}, u32[]{:S(2)}) collective-permute-start(bf16[2,128]{1,0:T(2,128)(2,1)} %get-tuple-element.242), channel_id=1, source_target_pairs={{0,8},{8,16},{16,24},{24,0},{1,9},{9,17},{17,25},{25,1},{2,10},{10... | collective-permute-start | bytes 1544 | tf_op jit(solution)/shard_map/ppermute | solution.py:70
  13.0 28.9 %collective-permute-start.21 = (s32[2,128]{1,0:T(2,128)}, s32[2,128]{1,0:T(2,128)}, u32[]{:S(2)}, u32[]{:S(2)}) collective-permute-start(s32[2,128]{1,0:T(2,128)} %param.17), channel_id=1, source_target_pairs={{0,8},{8,16},{16,24},{1,9},{9,17},{17,25},{2,10},{10,18},{18,26},{... | collective-permute-start | bytes 3080 | tf_op jit(solution)/shard_map/ppermute | solution.py:73
  15.4 74.1 %collective-permute-start.6 = (bf16[48,1536]{1,0:T(8,128)(2,1)}, bf16[48,1536]{1,0:T(8,128)(2,1)}, u32[]{:S(2)}, u32[]{:S(2)}) collective-permute-start(bf16[48,1536]{1,0:T(8,128)(2,1)} %param.19), channel_id=1, source_target_pairs={{0,8},{8,16},{16,24},{24,0},{1,9},{9,17},{17,25},{25,1},{2,10},{10... | collective-permute-start | bytes 442376 | tf_op jit(solution)/shard_map/ppermute | solution.py:70
  45.3 47.4 %collective-permute-start.24 = (bf16[48,1536]{1,0:T(8,128)(2,1)S(1)}, bf16[48,1536]{1,0:T(8,128)(2,1)S(1)}, u32[]{:S(2)}, u32[]{:S(2)}) collective-permute-start(bf16[48,1536]{1,0:T(8,128)(2,1)S(1)} %copy-done.93), channel_id=1, source_target_pairs={{0,8},{8,16},{16,24},{24,0},{1,9},{9,17},{17,25},{25,1},{2,10},{10... | collective-permute-start | bytes 442376 | tf_op jit(solution)/shard_map/ppermute | solution.py:70
  50.9 26.8 %collective-permute-start.3 = (bf16[4,2,128]{2,1,0:T(2,128)(2,1)S(1)}, bf16[4,2,128]{2,1,0:T(2,128)(2,1)S(1)}, u32[]{:S(2)}, u32[]{:S(2)}) collective-permute-start(bf16[4,2,128]{2,1,0:T(2,128)(2,1)S(1)} %constant_dynamic-update-slice_fusion), channel_id=1, source_target_pairs={{0,4},{1,5},{2,6},{3,7},{4,0},{5,1},{6,2},{7,3},{8,12},{9,13},{10,... | collective-permute-start | bytes 6152 | tf_op jit(solution)/shard_map/ppermute | solution.py:67
  82.7 106.2 %collective-permute-start.32 = (bf16[384,1536]{1,0:T(8,128)(2,1)}, bf16[384,1536]{1,0:T(8,128)(2,1)}, u32[]{:S(2)}, u32[]{:S(2)}) collective-permute-start(bf16[384,1536]{1,0:T(8,128)(2,1)} %constant_dynamic-update-slice_fusion.6), channel_id=1, source_target_pairs={{0,4},{1,5},{2,6},{3,7},{4,0},{5,1},{6,2},{7,3},{8,12},{9,13},{10,... | collective-permute-start | bytes 3538952 | tf_op jit(solution)/shard_map/ppermute | solution.py:67
  85.6 107.1 %collective-permute-start.33 = (bf16[384,1536]{1,0:T(8,128)(2,1)}, bf16[384,1536]{1,0:T(8,128)(2,1)}, u32[]{:S(2)}, u32[]{:S(2)}) collective-permute-start(bf16[384,1536]{1,0:T(8,128)(2,1)} %constant_dynamic-update-slice_fusion.6), channel_id=1, source_target_pairs={{0,8},{8,16},{16,24},{24,0},{1,9},{9,17},{17,25},{25,1},{2,10},{10... | collective-permute-start | bytes 3538952 | tf_op jit(solution)/shard_map/ppermute | solution.py:70
  89.5 70.5 %collective-permute-start.41 = (bf16[256,1536]{1,0:T(8,128)(2,1)}, bf16[256,1536]{1,0:T(8,128)(2,1)S(1)}, u32[]{:S(2)}, u32[]{:S(2)}) collective-permute-start(bf16[256,1536]{1,0:T(8,128)(2,1)} %bitcast.531), channel_id=1, source_target_pairs={{0,2},{1,3},{2,0},{3,1},{4,6},{5,7},{6,4},{7,5},{8,10},{9,11},{10,... | collective-permute-start | bytes 2359304 | tf_op jit(solution)/shard_map/ppermute | solution.py:65
  92.7 26.4 %collective-permute-start.16 = (bf16[48,1536]{1,0:T(8,128)(2,1)}, bf16[48,1536]{1,0:T(8,128)(2,1)S(1)}, u32[]{:S(2)}, u32[]{:S(2)}) collective-permute-start(bf16[48,1536]{1,0:T(8,128)(2,1)} %collective-permute-done.15), channel_id=1, source_target_pairs={{0,8},{8,16},{16,24},{24,0},{1,9},{9,17},{17,25},{25,1},{2,10},{10... | collective-permute-start | bytes 442376 | tf_op jit(solution)/shard_map/ppermute | solution.py:70
  157.3 25.1 %collective-permute-start.9 = (bf16[4,48,1536]{2,1,0:T(8,128)(2,1)}, bf16[4,48,1536]{2,1,0:T(8,128)(2,1)S(1)}, u32[]{:S(2)}, u32[]{:S(2)}) collective-permute-start(bf16[4,48,1536]{2,1,0:T(8,128)(2,1)} %bitcast_dynamic-update-slice_fusion.13), channel_id=1, source_target_pairs={{0,2},{1,3},{2,0},{3,1},{4,6},{5,7},{6,4},{7,5},{8,10},{9,11},{10,... | collective-permute-start | bytes 1769480 | tf_op jit(solution)/shard_map/ppermute | solution.py:65
  170.2 197.2 %collective-permute-start.42 = (bf16[512,1536]{1,0:T(8,128)(2,1)}, bf16[512,1536]{1,0:T(8,128)(2,1)}, u32[]{:S(2)}, u32[]{:S(2)}) collective-permute-start(bf16[512,1536]{1,0:T(8,128)(2,1)} %pad_maximum_fusion.6), channel_id=1, source_target_pairs={{0,1},{1,0},{2,3},{3,2},{4,5},{5,4},{6,7},{7,6},{8,9},{9,8},{10,11... | collective-permute-start | bytes 4718600 | tf_op jit(solution)/shard_map/ppermute | solution.py:63
  182.4 29.0 %collective-permute-start.19 = (bf16[4,2,48,1536]{3,2,0,1:T(8,128)(2,1)S(1)}, bf16[4,2,48,1536]{3,2,0,1:T(8,128)(2,1)S(1)}, u32[]{:S(2)}, u32[]{:S(2)}) collective-permute-start(bf16[4,2,48,1536]{3,2,0,1:T(8,128)(2,1)S(1)} %maximum_select_fusion.9), channel_id=1, source_target_pairs={{0,2},{1,3},{2,0},{3,1},{4,6},{5,7},{6,4},{7,5},{8,10},{9,11},{10,... | collective-permute-start | bytes 3538952 | tf_op jit(solution)/shard_map/ppermute | solution.py:65
  188.8 29.0 %collective-permute-start.10 = (bf16[4,2,48,1536]{3,2,1,0:T(8,128)(2,1)S(1)}, bf16[4,2,48,1536]{3,2,1,0:T(8,128)(2,1)S(1)}, u32[]{:S(2)}, u32[]{:S(2)}) collective-permute-start(bf16[4,2,48,1536]{3,2,1,0:T(8,128)(2,1)S(1)} %maximum_select_fusion.8), channel_id=1, source_target_pairs={{0,4},{1,5},{2,6},{3,7},{4,0},{5,1},{6,2},{7,3},{8,12},{9,13},{10,... | collective-permute-start | bytes 3538952 | tf_op jit(solution)/shard_map/ppermute | solution.py:67
  192.7 40.3 %collective-permute-start.28 = (bf16[4,2,48,1536]{3,2,0,1:T(8,128)(2,1)S(1)}, bf16[4,2,48,1536]{3,2,0,1:T(8,128)(2,1)S(1)}, u32[]{:S(2)}, u32[]{:S(2)}) collective-permute-start(bf16[4,2,48,1536]{3,2,0,1:T(8,128)(2,1)S(1)} %maximum_select_fusion.11), channel_id=1, source_target_pairs={{0,2},{1,3},{2,0},{3,1},{4,6},{5,7},{6,4},{7,5},{8,10},{9,11},{10,... | collective-permute-start | bytes 3538952 | tf_op jit(solution)/shard_map/ppermute | solution.py:65
  195.4 59.2 %collective-permute-start.35 = (bf16[384,1536]{1,0:T(8,128)(2,1)}, bf16[384,1536]{1,0:T(8,128)(2,1)}, u32[]{:S(2)}, u32[]{:S(2)}) collective-permute-start(bf16[384,1536]{1,0:T(8,128)(2,1)} %collective-permute-done.33), channel_id=1, source_target_pairs={{0,8},{8,16},{16,24},{24,0},{1,9},{9,17},{17,25},{25,1},{2,10},{10... | collective-permute-start | bytes 3538952 | tf_op jit(solution)/shard_map/ppermute | solution.py:70
  211.4 43.7 %collective-permute-start.34 = (bf16[384,1536]{1,0:T(8,128)(2,1)}, bf16[384,1536]{1,0:T(8,128)(2,1)}, u32[]{:S(2)}, u32[]{:S(2)}) collective-permute-start(bf16[384,1536]{1,0:T(8,128)(2,1)} %collective-permute-done.33), channel_id=1, source_target_pairs={{0,4},{1,5},{2,6},{3,7},{4,0},{5,1},{6,2},{7,3},{8,12},{9,13},{10,... | collective-permute-start | bytes 3538952 | tf_op jit(solution)/shard_map/ppermute | solution.py:67
  217.8 29.0 %collective-permute-start.14 = (bf16[2,128,1536]{2,1,0:T(8,128)(2,1)S(1)}, bf16[2,128,1536]{2,1,0:T(8,128)(2,1)S(1)}, u32[]{:S(2)}, u32[]{:S(2)}) collective-permute-start(bf16[2,128,1536]{2,1,0:T(8,128)(2,1)S(1)} %collective-permute-done.13), channel_id=1, source_target_pairs={{0,8},{8,16},{16,24},{1,9},{9,17},{17,25},{2,10},{10,18},{18,26},{... | collective-permute-start | bytes 2359304 | tf_op jit(solution)/shard_map/ppermute | solution.py:73
  233.0 27.8 %collective-permute-start.20 = (bf16[4,2,2,48,1536]{4,3,0,1,2:T(8,128)(2,1)}, bf16[4,2,2,48,1536]{4,3,0,1,2:T(8,128)(2,1)}, u32[]{:S(2)}, u32[]{:S(2)}) collective-permute-start(bf16[4,2,2,48,1536]{4,3,0,1,2:T(8,128)(2,1)} %maximum_select_fusion.5), channel_id=1, source_target_pairs={{0,1},{1,0},{2,3},{3,2},{4,5},{5,4},{6,7},{7,6},{8,9},{9,8},{10,11... | collective-permute-start | bytes 7077896 | tf_op jit(solution)/shard_map/ppermute | solution.py:63
  246.8 55.4 %collective-permute-start.11 = (bf16[4,2,2,48,1536]{4,3,2,1,0:T(8,128)(2,1)}, bf16[4,2,2,48,1536]{4,3,2,1,0:T(8,128)(2,1)}, u32[]{:S(2)}, u32[]{:S(2)}) collective-permute-start(bf16[4,2,2,48,1536]{4,3,2,1,0:T(8,128)(2,1)} %maximum_select_fusion.3), channel_id=1, source_target_pairs={{0,1},{1,0},{2,3},{3,2},{4,5},{5,4},{6,7},{7,6},{8,9},{9,8},{10,11... | collective-permute-start | bytes 7077896 | tf_op jit(solution)/shard_map/ppermute | solution.py:63
  254.7 96.0 %collective-permute-start.29 = (bf16[4,2,2,48,1536]{4,3,0,1,2:T(8,128)(2,1)}, bf16[4,2,2,48,1536]{4,3,0,1,2:T(8,128)(2,1)}, u32[]{:S(2)}, u32[]{:S(2)}) collective-permute-start(bf16[4,2,2,48,1536]{4,3,0,1,2:T(8,128)(2,1)} %maximum_select_fusion.7), channel_id=1, source_target_pairs={{0,1},{1,0},{2,3},{3,2},{4,5},{5,4},{6,7},{7,6},{8,9},{9,8},{10,11... | collective-permute-start | bytes 7077896 | tf_op jit(solution)/shard_map/ppermute | solution.py:63
  255.2 116.0 %collective-permute-start.37 = (bf16[384,1536]{1,0:T(8,128)(2,1)}, bf16[384,1536]{1,0:T(8,128)(2,1)}, u32[]{:S(2)}, u32[]{:S(2)}) collective-permute-start(bf16[384,1536]{1,0:T(8,128)(2,1)} %collective-permute-done.35), channel_id=1, source_target_pairs={{0,8},{8,16},{16,24},{24,0},{1,9},{9,17},{17,25},{25,1},{2,10},{10... | collective-permute-start | bytes 3538952 | tf_op jit(solution)/shard_map/ppermute | solution.py:70
  260.8 124.4 %collective-permute-start.36 = (bf16[384,1536]{1,0:T(8,128)(2,1)}, bf16[384,1536]{1,0:T(8,128)(2,1)}, u32[]{:S(2)}, u32[]{:S(2)}) collective-permute-start(bf16[384,1536]{1,0:T(8,128)(2,1)} %collective-permute-done.35), channel_id=1, source_target_pairs={{0,4},{1,5},{2,6},{3,7},{4,0},{5,1},{6,2},{7,3},{8,12},{9,13},{10,... | collective-permute-start | bytes 3538952 | tf_op jit(solution)/shard_map/ppermute | solution.py:67
  371.2 27.5 %collective-permute-start.38 = (bf16[384,1536]{1,0:T(8,128)(2,1)}, bf16[384,1536]{1,0:T(8,128)(2,1)S(1)}, u32[]{:S(2)}, u32[]{:S(2)}) collective-permute-start(bf16[384,1536]{1,0:T(8,128)(2,1)} %collective-permute-done.37), channel_id=1, source_target_pairs={{0,4},{1,5},{2,6},{3,7},{4,0},{5,1},{6,2},{7,3},{8,12},{9,13},{10,... | collective-permute-start | bytes 3538952 | tf_op jit(solution)/shard_map/ppermute | solution.py:67
  468.3 63.1 %collective-permute-start.68 = (bf16[384,1536]{1,0:T(8,128)(2,1)}, bf16[384,1536]{1,0:T(8,128)(2,1)}, u32[]{:S(2)}, u32[]{:S(2)}) collective-permute-start(bf16[384,1536]{1,0:T(8,128)(2,1)} %pad_maximum_fusion.12), channel_id=1, source_target_pairs={{0,4},{1,5},{2,6},{3,7},{4,0},{5,1},{6,2},{7,3},{8,12},{9,13},{10,... | collective-permute-start | bytes 3538952 | tf_op jit(solution)/shard_map/ppermute | solution.py:67
  470.4 49.8 %collective-permute-start.69 = (bf16[384,1536]{1,0:T(8,128)(2,1)}, bf16[384,1536]{1,0:T(8,128)(2,1)}, u32[]{:S(2)}, u32[]{:S(2)}) collective-permute-start(bf16[384,1536]{1,0:T(8,128)(2,1)} %pad_maximum_fusion.13), channel_id=1, source_target_pairs={{0,4},{1,5},{2,6},{3,7},{4,0},{5,1},{6,2},{7,3},{8,12},{9,13},{10,... | collective-permute-start | bytes 3538952 | tf_op jit(solution)/shard_map/ppermute | solution.py:67
  494.9 55.9 %collective-permute-start.43 = (f32[512,1536]{1,0:T(8,128)S(1)}, f32[512,1536]{1,0:T(8,128)S(1)}, u32[]{:S(2)}, u32[]{:S(2)}) collective-permute-start(f32[512,1536]{1,0:T(8,128)S(1)} %slice.343), channel_id=1, source_target_pairs={{0,1},{1,0},{2,3},{3,2},{4,5},{5,4},{6,7},{7,6},{8,9},{9,8},{10,11... | collective-permute-start | bytes 9437192 | tf_op jit(solution)/shard_map/ppermute | solution.py:63
  501.7 51.5 %collective-permute-start.39 = (f32[512,1536]{1,0:T(8,128)S(1)}, f32[512,1536]{1,0:T(8,128)S(1)}, u32[]{:S(2)}, u32[]{:S(2)}) collective-permute-start(f32[512,1536]{1,0:T(8,128)S(1)} %slice.339), channel_id=1, source_target_pairs={{0,1},{1,0},{2,3},{3,2},{4,5},{5,4},{6,7},{7,6},{8,9},{9,8},{10,11... | collective-permute-start | bytes 9437192 | tf_op jit(solution)/shard_map/ppermute | solution.py:63
  521.8 27.2 %collective-permute-start.70 = (bf16[384,1536]{1,0:T(8,128)(2,1)S(1)}, bf16[384,1536]{1,0:T(8,128)(2,1)S(1)}, u32[]{:S(2)}, u32[]{:S(2)}) collective-permute-start(bf16[384,1536]{1,0:T(8,128)(2,1)S(1)} %fusion.67), channel_id=1, source_target_pairs={{0,8},{8,16},{16,24},{24,0},{1,9},{9,17},{17,25},{25,1},{2,10},{10... | collective-permute-start | bytes 3538952 | tf_op jit(solution)/shard_map/ppermute | solution.py:70
  530.7 249.5 %collective-permute-start.66 = (bf16[384,1536]{1,0:T(8,128)(2,1)}, bf16[384,1536]{1,0:T(8,128)(2,1)}, u32[]{:S(2)}, u32[]{:S(2)}) collective-permute-start(bf16[384,1536]{1,0:T(8,128)(2,1)} %pad_maximum_fusion.10), channel_id=1, source_target_pairs={{0,4},{1,5},{2,6},{3,7},{4,0},{5,1},{6,2},{7,3},{8,12},{9,13},{10,... | collective-permute-start | bytes 3538952 | tf_op jit(solution)/shard_map/ppermute | solution.py:67
  531.4 49.9 %collective-permute-start.67 = (bf16[384,1536]{1,0:T(8,128)(2,1)S(1)}, bf16[384,1536]{1,0:T(8,128)(2,1)S(1)}, u32[]{:S(2)}, u32[]{:S(2)}) collective-permute-start(bf16[384,1536]{1,0:T(8,128)(2,1)S(1)} %pad_maximum_fusion.11), channel_id=1, source_target_pairs={{0,4},{1,5},{2,6},{3,7},{4,0},{5,1},{6,2},{7,3},{8,12},{9,13},{10,... | collective-permute-start | bytes 3538952 | tf_op jit(solution)/shard_map/ppermute | solution.py:67
  550.8 30.6 %collective-permute-start.71 = (bf16[384,1536]{1,0:T(8,128)(2,1)S(1)}, bf16[384,1536]{1,0:T(8,128)(2,1)S(1)}, u32[]{:S(2)}, u32[]{:S(2)}) collective-permute-start(bf16[384,1536]{1,0:T(8,128)(2,1)S(1)} %fusion.66), channel_id=1, source_target_pairs={{0,8},{8,16},{16,24},{24,0},{1,9},{9,17},{17,25},{25,1},{2,10},{10... | collective-permute-start | bytes 3538952 | tf_op jit(solution)/shard_map/ppermute | solution.py:70
  551.6 31.7 %collective-permute-start.44 = (bf16[256,1536]{1,0:T(8,128)(2,1)S(1)}, bf16[256,1536]{1,0:T(8,128)(2,1)S(1)}, u32[]{:S(2)}, u32[]{:S(2)}) collective-permute-start(bf16[256,1536]{1,0:T(8,128)(2,1)S(1)} %slice.416), channel_id=1, source_target_pairs={{0,2},{1,3},{2,0},{3,1},{4,6},{5,7},{6,4},{7,5},{8,10},{9,11},{10,... | collective-permute-start | bytes 2359304 | tf_op jit(solution)/shard_map/ppermute | solution.py:65
  553.8 30.7 %collective-permute-start.40 = (bf16[256,1536]{1,0:T(8,128)(2,1)S(1)}, bf16[256,1536]{1,0:T(8,128)(2,1)S(1)}, u32[]{:S(2)}, u32[]{:S(2)}) collective-permute-start(bf16[256,1536]{1,0:T(8,128)(2,1)S(1)} %slice.417), channel_id=1, source_target_pairs={{0,2},{1,3},{2,0},{3,1},{4,6},{5,7},{6,4},{7,5},{8,10},{9,11},{10,... | collective-permute-start | bytes 2359304 | tf_op jit(solution)/shard_map/ppermute | solution.py:65
  582.9 197.2 %collective-permute-start.72 = (bf16[384,1536]{1,0:T(8,128)(2,1)}, bf16[384,1536]{1,0:T(8,128)(2,1)}, u32[]{:S(2)}, u32[]{:S(2)}) collective-permute-start(bf16[384,1536]{1,0:T(8,128)(2,1)} %fusion.64), channel_id=1, source_target_pairs={{0,8},{8,16},{16,24},{24,0},{1,9},{9,17},{17,25},{25,1},{2,10},{10... | collective-permute-start | bytes 3538952 | tf_op jit(solution)/shard_map/ppermute | solution.py:70
  720.9 78.5 %collective-permute-start.54 = (bf16[4,2,2,48,1536]{4,3,2,1,0:T(8,128)(2,1)}, bf16[4,2,2,48,1536]{4,3,2,1,0:T(8,128)(2,1)}, u32[]{:S(2)}, u32[]{:S(2)}) collective-permute-start(bf16[4,2,2,48,1536]{4,3,2,1,0:T(8,128)(2,1)} %fusion.61), channel_id=1, source_target_pairs={{0,1},{1,0},{2,3},{3,2},{4,5},{5,4},{6,7},{7,6},{8,9},{9,8},{10,11... | collective-permute-start | bytes 7077896 | tf_op jit(solution)/shard_map/ppermute | solution.py:63
  740.1 31.9 %collective-permute-start.45 = (bf16[2,128,1536]{2,1,0:T(8,128)(2,1)}, bf16[2,128,1536]{2,1,0:T(8,128)(2,1)}, u32[]{:S(2)}, u32[]{:S(2)}) collective-permute-start(bf16[2,128,1536]{2,1,0:T(8,128)(2,1)} %fusion.91), channel_id=1, source_target_pairs={{8,0},{16,8},{24,16},{9,1},{17,9},{25,17},{10,2},{18,10},{26,18},{... | collective-permute-start | bytes 2359304 | tf_op jit(solution)/shard_map/ppermute | solution.py:76
  774.0 22.4 %collective-permute-start.46 = (bf16[2,128,1536]{2,1,0:T(8,128)(2,1)S(1)}, bf16[2,128,1536]{2,1,0:T(8,128)(2,1)S(1)}, u32[]{:S(2)}, u32[]{:S(2)}) collective-permute-start(bf16[2,128,1536]{2,1,0:T(8,128)(2,1)S(1)} %fusion.73), channel_id=1, source_target_pairs={{8,0},{16,8},{24,16},{9,1},{17,9},{25,17},{10,2},{18,10},{26,18},{... | collective-permute-start | bytes 2359304 | tf_op jit(solution)/shard_map/ppermute | solution.py:76
  779.8 48.4 %collective-permute-start.60 = (bf16[4,2,2,48,1664]{4,3,2,1,0:T(8,128)(2,1)}, bf16[4,2,2,48,1664]{4,3,2,1,0:T(8,128)(2,1)}, u32[]{:S(2)}, u32[]{:S(2)}) collective-permute-start(bf16[4,2,2,48,1664]{4,3,2,1,0:T(8,128)(2,1)} %fusion.59), channel_id=1, source_target_pairs={{0,1},{1,0},{2,3},{3,2},{4,5},{5,4},{6,7},{7,6},{8,9},{9,8},{10,11... | collective-permute-start | bytes 7667720 | tf_op jit(solution)/shard_map/ppermute | solution.py:63
  798.0 21.0 %collective-permute-start.47 = (bf16[2,128,1536]{2,1,0:T(8,128)(2,1)S(1)}, bf16[2,128,1536]{2,1,0:T(8,128)(2,1)S(1)}, u32[]{:S(2)}, u32[]{:S(2)}) collective-permute-start(bf16[2,128,1536]{2,1,0:T(8,128)(2,1)S(1)} %fusion.74), channel_id=1, source_target_pairs={{8,0},{16,8},{24,16},{9,1},{17,9},{25,17},{10,2},{18,10},{26,18},{... | collective-permute-start | bytes 2359304 | tf_op jit(solution)/shard_map/ppermute | solution.py:76
  803.3 29.7 %collective-permute-start.55 = (bf16[4,2,48,1536]{3,2,1,0:T(8,128)(2,1)}, bf16[4,2,48,1536]{3,2,1,0:T(8,128)(2,1)}, u32[]{:S(2)}, u32[]{:S(2)}) collective-permute-start(bf16[4,2,48,1536]{3,2,1,0:T(8,128)(2,1)} %fusion.89), channel_id=1, source_target_pairs={{0,2},{1,3},{2,0},{3,1},{4,6},{5,7},{6,4},{7,5},{8,10},{9,11},{10,... | collective-permute-start | bytes 3538952 | tf_op jit(solution)/shard_map/ppermute | solution.py:65
  828.1 40.6 %collective-permute-start.48 = (bf16[4,2,2,48,1536]{4,3,2,1,0:T(8,128)(2,1)S(1)}, bf16[4,2,2,48,1536]{4,3,2,1,0:T(8,128)(2,1)}, u32[]{:S(2)}, u32[]{:S(2)}) collective-permute-start(bf16[4,2,2,48,1536]{4,3,2,1,0:T(8,128)(2,1)S(1)} %fusion.60), channel_id=1, source_target_pairs={{0,1},{1,0},{2,3},{3,2},{4,5},{5,4},{6,7},{7,6},{8,9},{9,8},{10,11... | collective-permute-start | bytes 7077896 | tf_op jit(solution)/shard_map/ppermute | solution.py:63
  831.2 30.0 %collective-permute-start.61 = (bf16[4,2,48,1664]{3,2,1,0:T(8,128)(2,1)S(1)}, bf16[4,2,48,1664]{3,2,1,0:T(8,128)(2,1)S(1)}, u32[]{:S(2)}, u32[]{:S(2)}) collective-permute-start(bf16[4,2,48,1664]{3,2,1,0:T(8,128)(2,1)S(1)} %fusion.87), channel_id=1, source_target_pairs={{0,2},{1,3},{2,0},{3,1},{4,6},{5,7},{6,4},{7,5},{8,10},{9,11},{10,... | collective-permute-start | bytes 3833864 | tf_op jit(solution)/shard_map/ppermute | solution.py:65
  835.4 26.1 %collective-permute-start.56 = (bf16[4,48,1536]{2,1,0:T(8,128)(2,1)S(1)}, bf16[4,48,1536]{2,1,0:T(8,128)(2,1)S(1)}, u32[]{:S(2)}, u32[]{:S(2)}) collective-permute-start(bf16[4,48,1536]{2,1,0:T(8,128)(2,1)S(1)} %fusion.106), channel_id=1, source_target_pairs={{0,4},{1,5},{2,6},{3,7},{4,0},{5,1},{6,2},{7,3},{8,12},{9,13},{10,... | collective-permute-start | bytes 1769480 | tf_op jit(solution)/shard_map/ppermute | solution.py:67
  871.4 32.2 %collective-permute-start.49 = (bf16[4,2,48,1536]{3,2,1,0:T(8,128)(2,1)S(1)}, bf16[4,2,48,1536]{3,2,1,0:T(8,128)(2,1)S(1)}, u32[]{:S(2)}, u32[]{:S(2)}) collective-permute-start(bf16[4,2,48,1536]{3,2,1,0:T(8,128)(2,1)S(1)} %fusion.88), channel_id=1, source_target_pairs={{0,4},{1,5},{2,6},{3,7},{4,0},{5,1},{6,2},{7,3},{8,12},{9,13},{10,... | collective-permute-start | bytes 3538952 | tf_op jit(solution)/shard_map/ppermute | solution.py:67
  875.7 30.2 %collective-permute-start.59 = (bf16[48,1536]{1,0:T(8,128)(2,1)S(1)}, bf16[48,1536]{1,0:T(8,128)(2,1)S(1)}, u32[]{:S(2)}, u32[]{:S(2)}) collective-permute-start(bf16[48,1536]{1,0:T(8,128)(2,1)S(1)} %fusion.138), channel_id=1, source_target_pairs={{0,8},{8,16},{16,24},{24,0},{1,9},{9,17},{17,25},{25,1},{2,10},{10... | collective-permute-start | bytes 442376 | tf_op jit(solution)/shard_map/ppermute | solution.py:70
  880.7 38.3 %collective-permute-start.63 = (bf16[48,1664]{1,0:T(8,128)(2,1)S(1)}, bf16[48,1664]{1,0:T(8,128)(2,1)S(1)}, u32[]{:S(2)}, u32[]{:S(2)}) collective-permute-start(bf16[48,1664]{1,0:T(8,128)(2,1)S(1)} %fusion.143), channel_id=1, source_target_pairs={{0,8},{8,16},{16,24},{24,0},{1,9},{9,17},{17,25},{25,1},{2,10},{10... | collective-permute-start | bytes 479240 | tf_op jit(solution)/shard_map/ppermute | solution.py:70
  (161 other events, 2262.8 us)

commit v2 on v1

v2 whole, which is shorter than its diff:
```python
import functools

import jax
import jax.numpy as jnp
from jax import lax
from jax.experimental import pallas as pl
from jax.experimental.pallas import tpu as pltpu
from jax.sharding import PartitionSpec as P

HEADS = 16
KV_HEADS = 8
HEAD = 96
GROUP = HEADS // KV_HEADS

EPS = 1e-05
THETA = 100000.0
NEG = -1e30
BF = jnp.bfloat16
F32 = jnp.float32


def inverse_rms(values):
    return lax.rsqrt(jnp.mean(values * values, axis=-1, keepdims=True) + EPS)


def angle_tables(places):
    offsets = jnp.arange(0, HEAD, 2, dtype=F32)
    angles = (THETA ** (-offsets / HEAD))[:, None] * places.astype(F32)[None, :]
    return (jnp.cos(angles), jnp.sin(angles))


def mm(left, right):
    return jnp.dot(left, right, preferred_element_type=F32)


def mm_t(left, right):
    return lax.dot_general(left, right, (((1,), (1,)), ((), ())), preferred_element_type=F32)


def t_mm(left, right):
    return lax.dot_general(left, right, (((0,), (0,)), ((), ())), preferred_element_type=F32)


class Moves:
    def __init__(self):
        self.Z = lax.axis_size("seq")
        self.DP = lax.axis_size("dp")
        self.Q = self.DP // 4
        self.zi = lax.axis_index("seq")
        place = lax.axis_index("dp")
        self.qi = place // 4
        self.xi = (place // 2) % 2
        self.ci = place % 2
        self.index = {"z": self.zi, "q": self.qi, "x": self.xi, "c": self.ci}
        self.size = {"z": self.Z, "q": self.Q, "x": 2, "c": 2}

    def step(self, axis, value):
        if axis == "c":
            return lax.ppermute(value, "dp", [(i, i ^ 1) for i in range(self.DP)])
        if axis == "x":
            return lax.ppermute(value, "dp", [(i, i ^ 2) for i in range(self.DP)])
        if axis == "q":
            return lax.ppermute(
                value, "dp", [(i, i % 4 + 4 * ((i // 4 + 1) % self.Q)) for i in range(self.DP)]
            )
        return lax.ppermute(value, "seq", [(i, (i + 1) % self.Z) for i in range(self.Z)])

    def up(self, value):
        return lax.ppermute(value, "seq", [(i, i + 1) for i in range(self.Z - 1)])

    def down(self, value):
        return lax.ppermute(value, "seq", [(i + 1, i) for i in range(self.Z - 1)])

    def gather(self, value, name, position, step=None):
        size, index = self.size[name], self.index[name]
        step = step or (lambda v: self.step(name, v))
        blocks = [value]
        for _ in range(size - 1):
            blocks.append(step(blocks[-1]))
        if size == 2:
            return jnp.where(
                index == 0, jnp.stack(blocks, axis=position), jnp.stack(blocks[::-1], axis=position)
            )
        out = jnp.zeros(value.shape[:position] + (size,) + value.shape[position:], value.dtype)
        for k, block in enumerate(blocks):
            out = lax.dynamic_update_slice_in_dim(
                out, jnp.expand_dims(block, position), (index - k) % size, axis=position
            )
        return out

    def scatter(self, value, name, position, step=None, sign=1):
        size, index = self.size[name], self.index[name]
        step = step or (lambda v: self.step(name, v))

        def take(k):
            return lax.dynamic_index_in_dim(
                value, (index - sign * k) % size, axis=position, keepdims=False
            )

        received = None
        for k in range(1, size):
            part = take(k)
            if received is not None:
                part = part + received
            received = step(part.astype(BF)).astype(F32)
        return take(0) + received


VMEM = pl.BlockSpec(memory_space=pltpu.VMEM)
ANY = pl.BlockSpec(memory_space=pl.ANY)
SMEM = pl.BlockSpec(memory_space=pltpu.SMEM)
SCALE = HEAD ** (-0.5)
HALF = HEAD // 2


def kernel_call(body, out_shape, in_specs, out_specs, scratch, flops, moved, args):
    return pl.pallas_call(
        body,
        out_shape=out_shape,
        in_specs=in_specs,
        out_specs=out_specs,
        scratch_shapes=scratch,
        compiler_params=pltpu.CompilerParams(vmem_limit_bytes=60 << 20),
        cost_estimate=pl.CostEstimate(flops=flops, bytes_accessed=moved, transcendentals=0),
    )(*args)


def turned_store(ref, row, lanes, block, cosine, sine):
    upper, lower = block[:HALF], block[HALF:]
    ref[pl.ds(row, HALF), lanes] = (upper * cosine - lower * sine).astype(ref.dtype)
    ref[pl.ds(row + HALF, HALF), lanes] = (lower * cosine + upper * sine).astype(ref.dtype)


def head_scores(queries, keys, place, wide):
    scores = mm(keys, queries) * SCALE
    rows = scores.shape[1] // GROUP
    key_place = lax.broadcasted_iota(jnp.int32, scores.shape, 0)
    query_place = place * rows + lax.rem(lax.broadcasted_iota(jnp.int32, scores.shape, 1), rows)
    return jnp.where(key_place <= query_place, scores, NEG)


def group_of(ref, g, lanes):
    return jnp.concatenate(
        [ref[pl.ds(pl.multiple_of((g * GROUP + j) * HEAD, 16), HEAD), lanes] for j in range(GROUP)],
        axis=1,
    )


def flip(value):
    return value.astype(F32).T.astype(value.dtype)


def attend_forward_body(
    seqs, wide, meta, tokens, gain, cosine, sine, pair_w, query_w,
    mixed, mixed_t, logs, query_t, pair_t, normed_t,
    pair_v, query_v, normed, own, sems,
):
    place = meta[0]
    rows = own.shape[0] // seqs
    pair_width = KV_HEADS * HEAD
    copies = [
        pltpu.make_async_copy(pair_w, pair_v, sems.at[0]),
        pltpu.make_async_copy(query_w, query_v, sems.at[1]),
    ]
    for copy in copies:
        copy.start()
    step = 256
    for b in range(seqs * wide // step):
        cut = slice(b * step, (b + 1) * step)
        values = tokens[cut, :].astype(F32)
        block = (values * inverse_rms(values) * gain[...]).astype(BF)
        normed[cut, :] = block
        normed_t[:, cut] = flip(block)
    for s in range(seqs):
        own[s * rows : (s + 1) * rows, :] = normed[
            pl.ds(pl.multiple_of(s * wide + place * rows, 128), rows), :
        ]
    copies[0].wait()
    width = 4 * HEAD
    for n in range(2 * pair_width // width):
        for s in range(seqs):
            lanes = slice(s * wide, (s + 1) * wide)
            block = mm(normed[lanes, :], pair_v[:, n * width : (n + 1) * width]).T
            if (n + 1) * width <= pair_width:
                for h in range(4):
                    turned_store(
                        pair_t, n * width + h * HEAD, lanes, block[h * HEAD : (h + 1) * HEAD],
                        cosine[:, lanes], sine[:, lanes],
                    )
            else:
                pair_t[n * width : (n + 1) * width, lanes] = block.astype(BF)
    copies[1].wait()
    for n in range(HEADS * HEAD // width):
        block = mm(own[...], query_v[:, n * width : (n + 1) * width]).T
        for s in range(seqs):
            lanes = slice(s * rows, (s + 1) * rows)
            here = pl.ds(pl.multiple_of(s * wide + place * rows, 128), rows)
            for h in range(4):
                turned_store(
                    query_t, n * width + h * HEAD, lanes, block[h * HEAD : (h + 1) * HEAD, lanes],
                    cosine[:, here], sine[:, here],
                )

    def one(g, _):
        row = pl.multiple_of(g * HEAD, 16)
        for s in range(seqs):
            lanes = slice(s * wide, (s + 1) * wide)
            mine = slice(s * rows, (s + 1) * rows)
            scores = head_scores(
                group_of(query_t, g, mine), flip(pair_t[pl.ds(row, HEAD), lanes]), place, wide
            )
            top = jnp.max(scores, axis=0, keepdims=True)
            weights = jnp.exp(scores - top)
            total = jnp.sum(weights, axis=0, keepdims=True)
            probs = (weights * (1.0 / total)).astype(BF)
            out = mm(pair_t[pl.ds(row + pair_width, HEAD), lanes], probs).astype(BF)
            for j in range(GROUP):
                mixed_t[pl.ds(pl.multiple_of((g * GROUP + j) * HEAD, 16), HEAD), mine] = out[
                    :, j * rows : (j + 1) * rows
                ]
            logs[g, s] = top + jnp.log(total)
        return 0

    lax.fori_loop(0, KV_HEADS, one, 0)
    mixed[...] = flip(mixed_t[...])


def attend_forward(meta, tokens, gain, cosine, sine, pair_w, query_w, seqs, rows):
    count, width = tokens.shape
    wide = count // seqs
    own = seqs * rows
    q, kv = query_w.shape[1], pair_w.shape[1]
    sds = jax.ShapeDtypeStruct
    return kernel_call(
        functools.partial(attend_forward_body, seqs, wide),
        (
            sds((own, q), BF), sds((q, own), BF), sds((KV_HEADS, seqs, 1, GROUP * rows), F32),
            sds((q, own), BF), sds((kv, count), BF), sds((width, count), BF),
        ),
        [SMEM, VMEM, VMEM, VMEM, VMEM, ANY, ANY],
        (VMEM,) * 6,
        [
            pltpu.VMEM(pair_w.shape, BF), pltpu.VMEM(query_w.shape, BF), pltpu.VMEM((count, width), BF),
            pltpu.VMEM((own, width), BF), pltpu.SemaphoreType.DMA((2,)),
        ],
        2 * count * width * kv + 2 * own * width * q + 4 * own * wide * q,
        20 << 20,
        (meta, tokens, gain, cosine, sine, pair_w, query_w),
    )


def attend_backward_body(
    seqs, wide, meta, query_t, pair_t, grad_t, logs, cosine, sine, query_back, pair_back
):
    place = meta[0]
    rows = query_t.shape[1] // seqs
    pair_width = KV_HEADS * HEAD

    def one(g, _):
        row = pl.multiple_of(g * HEAD, 16)
        for s in range(seqs):
            lanes = slice(s * wide, (s + 1) * wide)
            mine = slice(s * rows, (s + 1) * rows)
            here = pl.ds(pl.multiple_of(s * wide + place * rows, 128), rows)
            queries = group_of(query_t, g, mine)
            grads = group_of(grad_t, g, mine)
            keys_t = pair_t[pl.ds(row, HEAD), lanes]
            values_t = pair_t[pl.ds(row + pair_width, HEAD), lanes]
            probs = jnp.exp(head_scores(queries, flip(keys_t), place, wide) - logs[g, s])
            prob_grad = mm(flip(values_t), grads)
            centre = jnp.sum(probs * prob_grad, axis=0, keepdims=True)
            score_grad = (probs * (prob_grad - centre)).astype(BF)
            query_grad = mm(keys_t, score_grad) * SCALE
            for j in range(GROUP):
                turned_store(
                    query_back, pl.multiple_of((g * GROUP + j) * HEAD, 16), mine,
                    query_grad[:, j * rows : (j + 1) * rows], cosine[:, here], -sine[:, here],
                )
            turned_store(
                pair_back, row, lanes, mm_t(queries, score_grad) * SCALE,
                cosine[:, lanes], -sine[:, lanes],
            )
            pair_back[pl.ds(row + pair_width, HEAD), lanes] = mm_t(
                grads, probs.astype(BF)
            ).astype(BF)
        return 0

    lax.fori_loop(0, KV_HEADS, one, 0)


def attend_backward(meta, query_t, pair_t, grad_t, logs, cosine, sine, seqs):
    wide = pair_t.shape[1] // seqs
    return kernel_call(
        functools.partial(attend_backward_body, seqs, wide),
        (jax.ShapeDtypeStruct(query_t.shape, BF), jax.ShapeDtypeStruct(pair_t.shape, BF)),
        [SMEM] + [VMEM] * 6,
        (VMEM, VMEM),
        [],
        10 * query_t.size * wide,
        12 << 20,
        (meta, query_t, pair_t, grad_t, logs, cosine, sine),
    )


def output_body(tokens, mixed, gain, weights, total, second, weights_v, sem):
    copy = pltpu.make_async_copy(weights, weights_v, sem)
    copy.start()
    copy.wait()
    value = tokens[...].astype(F32) + mm(mixed[...], weights_v[...])
    total[...] = value
    second[...] = (value * inverse_rms(value) * gain[...]).astype(BF)


def output_forward(tokens, mixed, gain, weights):
    return kernel_call(
        output_body,
        (jax.ShapeDtypeStruct(tokens.shape, F32), jax.ShapeDtypeStruct(tokens.shape, BF)),
        [VMEM, VMEM, VMEM, ANY],
        (VMEM, VMEM),
        [pltpu.VMEM(weights.shape, BF), pltpu.SemaphoreType.DMA],
        2 * tokens.shape[0] * weights.size,
        10 << 20,
        (tokens, mixed, gain, weights),
    )


def output_back_body(
    grad, total, second_grad, gain, mixed_t, weights, first_grad, mixed_grad_t, sums, weights_v, da, sem
):
    copy = pltpu.make_async_copy(weights, weights_v, sem)
    copy.start()
    value = total[...]
    inverse = inverse_rms(value)
    back = second_grad[...]
    scaled = back * gain[...]
    first = (
        grad[...].astype(F32)
        + inverse * scaled
        - value * inverse**3 * jnp.mean(scaled * value, axis=-1, keepdims=True)
    )
    first_grad[...] = first
    da[...] = first.astype(BF)
    width = value.shape[1]
    gain_part = jnp.sum((back * value * inverse).T, axis=1, keepdims=True)
    sums[:, width:] = jnp.broadcast_to(gain_part, (width, 128))
    step = 512
    for n in range(width // step):
        cut = slice(n * step, (n + 1) * step)
        sums[:, cut] = mm(mixed_t[...], da[:, cut])
    copy.wait()
    for n in range(width // step):
        cut = slice(n * step, (n + 1) * step)
        mixed_grad_t[cut, :] = mm_t(weights_v[cut, :], da[...]).astype(BF)


def output_backward(grad, total, second_grad, gain, mixed_t, weights):
    own, width = grad.shape
    return kernel_call(
        output_back_body,
        (
            jax.ShapeDtypeStruct((own, width), F32),
            jax.ShapeDtypeStruct(mixed_t.shape, BF),
            jax.ShapeDtypeStruct((width, width + 128), F32),
        ),
        [VMEM] * 5 + [ANY],
        (VMEM,) * 3,
        [pltpu.VMEM(weights.shape, BF), pltpu.VMEM((own, width), BF), pltpu.SemaphoreType.DMA],
        4 * own * weights.size,
        22 << 20,
        (grad, total, second_grad, gain, mixed_t, weights),
    )


def ffn_body(blocks, units, *refs):
    second, grads = refs[:4], refs[4:8]
    shards = refs[8 : 8 + blocks]
    (out, back, hidden_t, gate_t, up_t) = refs[8 + blocks : 13 + blocks]
    second_v, grads_v, weights, hidden, gate_g, up_g, sems = refs[13 + blocks :]
    rows = second[0].shape[0]
    first = []
    for i in range(4):
        cut = pl.ds(i * rows, rows)
        first.append(pltpu.make_async_copy(second[i], second_v.at[cut], sems.at[0, i]))
        first.append(pltpu.make_async_copy(grads[i], grads_v.at[cut], sems.at[1, i]))
    copies = [
        [
            pltpu.make_async_copy(
                shards[b].at[pl.ds(p * units, units)],
                weights.at[p, pl.ds(b * units, units)],
                sems.at[2 + p, b],
            )
            for p in range(3)
        ]
        for b in range(blocks)
    ]
    for copy in first:
        copy.start()
    for line in copies:
        for copy in line:
            copy.start()
    for copy in first:
        copy.wait()
    step = 256
    count = 4 * rows
    per = step // units
    for n in range(blocks // per):
        for line in copies[n * per : (n + 1) * per]:
            for copy in line:
                copy.wait()
        cut = slice(n * step, (n + 1) * step)
        gate_w, up_w, down_w = weights[0, cut], weights[1, cut], weights[2, cut]

        def one(m, _):
            here = pl.ds(pl.multiple_of(m * step, step), step)
            gate = mm_t(second_v[here, :], gate_w)
            up = mm_t(second_v[here, :], up_w)
            hidden_grad = mm_t(grads_v[here, :], down_w)
            sigma = jax.nn.sigmoid(gate)
            mixed = gate * sigma * up
            hidden[here, cut] = mixed.astype(BF)
            hidden_t[cut, here] = mixed.T.astype(BF)
            gate_grad = hidden_grad * up * sigma * (1.0 + gate * (1.0 - sigma))
            gate_g[here, cut] = gate_grad.astype(BF)
            gate_t[cut, here] = gate_grad.T.astype(BF)
            up_grad = hidden_grad * (gate * sigma)
            up_g[here, cut] = up_grad.astype(BF)
            up_t[cut, here] = up_grad.T.astype(BF)
            return 0

        lax.fori_loop(0, count // step, one, 0)

    def two(m, _):
        here = pl.ds(pl.multiple_of(m * step, step), step)
        back[here, :] = (mm(gate_g[here, :], weights[0]) + mm(up_g[here, :], weights[1])).astype(back.dtype)
        out[here, :] = mm(hidden[here, :], weights[2]).astype(out.dtype)
        return 0

    lax.fori_loop(0, count // step, two, 0)


def ffn(second, grads, shards, units):
    blocks = len(shards)
    rows, width = second[0].shape
    count, total = 4 * rows, blocks * units
    sds = jax.ShapeDtypeStruct
    return kernel_call(
        functools.partial(ffn_body, blocks, units),
        (
            sds((count, width), BF), sds((count, width), BF),
            sds((total, count), BF), sds((total, count), BF), sds((total, count), BF),
        ),
        [ANY] * (8 + blocks),
        (VMEM,) * 5,
        [
            pltpu.VMEM((count, width), BF), pltpu.VMEM((count, width), BF),
            pltpu.VMEM((3, total, width), BF),
            pltpu.VMEM((count, total), BF), pltpu.VMEM((count, total), BF), pltpu.VMEM((count, total), BF),
            pltpu.SemaphoreType.DMA((5, max(blocks, 4))),
        ],
        12 * count * total * width,
        34 << 20,
        (*second, *grads, *shards),
    )


def ffn_sums_body(units, lines, hidden_t, gate_t, up_t, *refs):
    second, grads = refs[:4], refs[4:8]
    outs = refs[8 : 8 + lines]
    rows = second[0].shape[0]
    for p, left, right in ((0, gate_t, second), (1, up_t, second), (2, hidden_t, grads)):
        total = mm(left[:, :rows], right[0][...])
        for i in range(1, 4):
            total += mm(left[:, i * rows : (i + 1) * rows], right[i][...])
        for j in range(lines):
            outs[j][p * units : (p + 1) * units, :] = total[j * units : (j + 1) * units].astype(
                outs[j].dtype
            )


def ffn_sums(k, hidden_t, gate_t, up_t, second, grads, units, lines):
    rows, width = second[0].shape
    here = pl.BlockSpec((lines * units, 4 * rows), lambda i: (k, 0))
    whole = pl.BlockSpec((rows, width), lambda i: (0, 0))
    full = pl.BlockSpec((3 * units, width), lambda i: (0, 0))
    return pl.pallas_call(
        functools.partial(ffn_sums_body, units, lines),
        out_shape=tuple(
            jax.ShapeDtypeStruct((3 * units, width), BF if j else F32) for j in range(lines)
        ),
        grid=(1,),
        in_specs=[here] * 3 + [whole] * 8,
        out_specs=(full,) * lines,
        compiler_params=pltpu.CompilerParams(vmem_limit_bytes=60 << 20),
        cost_estimate=pl.CostEstimate(
            flops=24 * lines * units * rows * width, bytes_accessed=14 << 20, transcendentals=0
        ),
    )(hidden_t, gate_t, up_t, *second, *grads)


def project_sums_body(seqs, meta, normed_t, query_back, pair_back, query_sums, pair_sums):
    place = meta[0]
    wide = normed_t.shape[1] // seqs
    rows = query_back.shape[1] // seqs
    own = jnp.concatenate(
        [normed_t[:, pl.ds(pl.multiple_of(s * wide + place * rows, 128), rows)] for s in range(seqs)],
        axis=1,
    )
    step = 512
    for n in range(query_back.shape[0] // step):
        cut = slice(n * step, (n + 1) * step)
        query_sums[:, cut] = mm_t(own, query_back[cut, :])
    for n in range(pair_back.shape[0] // step):
        cut = slice(n * step, (n + 1) * step)
        pair_sums[:, cut] = mm_t(normed_t[...], pair_back[cut, :])


def project_sums(meta, normed_t, query_back, pair_back, seqs):
    width = normed_t.shape[0]
    return kernel_call(
        functools.partial(project_sums_body, seqs),
        (
            jax.ShapeDtypeStruct((width, query_back.shape[0]), F32),
            jax.ShapeDtypeStruct((width, pair_back.shape[0]), F32),
        ),
        [SMEM, VMEM, VMEM, VMEM],
        (VMEM, VMEM),
        [],
        2 * width * (query_back.size + pair_back.size),
        26 << 20,
        (meta, normed_t, query_back, pair_back),
    )


def project_back_body(seqs, query_back, pair_back, query_w, pair_w, query_grad, pair_grad, pair_v, query_v, sems):
    copies = [
        pltpu.make_async_copy(pair_w, pair_v, sems.at[0]),
        pltpu.make_async_copy(query_w, query_v, sems.at[1]),
    ]
    for copy in copies:
        copy.start()
    blocks, _, own = pair_grad.shape
    rows = own // seqs
    wide = pair_back.shape[1] // seqs
    step = 512
    copies[0].wait()
    for n in range(pair_w.shape[0] // step):
        cut = slice(n * step, (n + 1) * step)
        for s in range(seqs):
            part = mm(pair_v[cut, :], pair_back[:, s * wide : (s + 1) * wide])
            for z in range(blocks):
                pair_grad[z, cut, s * rows : (s + 1) * rows] = part[:, z * rows : (z + 1) * rows].astype(BF)
    copies[1].wait()
    for n in range(query_w.shape[0] // step):
        cut = slice(n * step, (n + 1) * step)
        query_grad[cut, :] = mm(query_v[cut, :], query_back[...])


def project_back(query_back, pair_back, query_w, pair_w, seqs, blocks):
    width = query_w.shape[0]
    own = query_back.shape[1]
    return kernel_call(
        functools.partial(project_back_body, seqs),
        (
            jax.ShapeDtypeStruct((width, own), F32),
            jax.ShapeDtypeStruct((blocks, width, own), BF),
        ),
        [VMEM, VMEM, ANY, ANY],
        (VMEM, VMEM),
        [pltpu.VMEM(pair_w.shape, BF), pltpu.VMEM(query_w.shape, BF), pltpu.SemaphoreType.DMA((2,))],
        2 * width * (query_back.size + pair_back.size),
        20 << 20,
        (query_back, pair_back, query_w, pair_w),
    )


def input_grad_body(tokens, gain, first_grad, query_grad, pair_grad, received, out):
    back = (query_grad[...] + pair_grad[...].astype(F32) + received[...].astype(F32)).T
    value = tokens[...].astype(F32)
    inverse = inverse_rms(value)
    scaled = back * gain[...]
    out[...] = (
        first_grad[...]
        + inverse * scaled
        - value * inverse**3 * jnp.mean(scaled * value, axis=-1, keepdims=True)
    ).astype(BF)


def input_grad(tokens, gain, first_grad, query_grad, pair_grad, received):
    return kernel_call(
        input_grad_body,
        jax.ShapeDtypeStruct(tokens.shape, BF),
        [VMEM] * 6,
        VMEM,
        [],
        tokens.size * 20,
        8 << 20,
        (tokens, gain, first_grad, query_grad, pair_grad, received),
    )


def per_device(
    tokens,
    positions,
    out_grad,
    w_query,
    w_key,
    w_value,
    w_output,
    gain_attn,
    gain_ffn,
    w_gate,
    w_up,
    w_down,
):
    move = Moves()
    Z, Q = move.Z, move.Q
    seqs, rows, width = tokens.shape
    wide = rows * Z
    own_rows = seqs * rows
    pair_width = KV_HEADS * HEAD
    share = w_query.shape[0]
    units = w_gate.shape[0]
    meta = move.zi.astype(jnp.int32).reshape(1)

    gains = jnp.pad(jnp.stack([gain_attn, gain_ffn]), ((0, 0), (0, 128 - share)))
    for position, name in enumerate("zqxc"):
        gains = move.gather(gains, name, position)
    gains = gains[..., :share].transpose(4, 0, 1, 2, 3, 5).reshape(2, width).astype(F32)
    attn_scale, ffn_scale = gains[0:1], gains[1:2]

    places_all = move.gather(positions, "z", 1, move.up).reshape(seqs * wide)
    tokens_all = move.gather(tokens, "z", 1, move.up).reshape(seqs * wide, width)

    def gather_rows(shard, order):
        dims = []
        for name in order:
            position = sum(1 for d in dims if "zqxc".index(d) < "zqxc".index(name))
            shard = move.gather(shard, name, position)
            dims.append(name)
        return shard.reshape((-1,) + shard.shape[-1:])

    pair_full = gather_rows(jnp.concatenate([w_key, w_value], axis=1), "zqxc")
    query_full = gather_rows(w_query, "zxqc")
    output_full = gather_rows(w_output, "zqxc")

    block = jnp.concatenate([w_gate, w_up, w_down], axis=0)
    ffn_blocks = []
    for k in range(Z):
        if k:
            block = move.step("z", block)
        line = [block]
        for _ in range(Q - 1):
            line.append(move.step("q", line[-1]))
        ffn_blocks.append(line)

    def spread(value):
        near = move.step("x", value)
        return (value, near, move.step("c", value), move.step("c", near))

    def collect(value):
        half = 2 * own_rows
        value = value[:half].astype(F32) + move.step("c", value[half:]).astype(F32)
        return value[:own_rows] + move.step("x", value[own_rows:].astype(BF)).astype(F32)

    grad_out = out_grad.reshape(own_rows, width)
    grad_spread = spread(grad_out)
    inputs = tokens.reshape(own_rows, width)

    cosine, sine = angle_tables(places_all)
    mixed, mixed_t, logs, query_t, pair_t, normed_t = attend_forward(
        meta, tokens_all, attn_scale, cosine, sine, pair_full, query_full, seqs, rows
    )
    first_sum, second = output_forward(inputs, mixed, ffn_scale, output_full)

    second_spread = spread(second)
    shards = [b for line in ffn_blocks for b in line]
    out_part, second_part, hidden_t, gate_t, up_t = ffn(second_spread, grad_spread, shards, units)
    second_grad = collect(second_part)
    received = None
    for k in list(range(1, Z)) + [0]:
        own, *others = ffn_sums(k, hidden_t, gate_t, up_t, second_spread, grad_spread, units, Q)
        passing = None
        for part in others:
            passing = move.step("q", part if passing is None else (part.astype(F32) + passing).astype(BF))
            passing = passing.astype(F32)
        own = own + passing
        if received is not None:
            own = own + received
        if k:
            received = move.step("z", own.astype(BF)).astype(F32)
    grad_gate, grad_up, grad_down = own[:units], own[units : 2 * units], own[2 * units :]
    layer_out = (first_sum + collect(out_part)).astype(BF)

    def scatter_rows(value, order):
        value = value.reshape(Z, Q, 2, 2, share, value.shape[-1])
        dims = list("zqxc")
        for name in order:
            value = move.scatter(value, name, dims.index(name))
            dims.remove(name)
        return value

    first_grad, mixed_grad_t, output_sum = output_backward(
        grad_out, first_sum, second_grad, ffn_scale, mixed_t, output_full
    )
    output_sum = scatter_rows(output_sum, "cxqz")
    grad_output, grad_gain_ffn = output_sum[:, :width], output_sum[:, width]
    query_back, pair_back = attend_backward(
        meta, query_t, pair_t, mixed_grad_t, logs, cosine, sine, seqs
    )
    query_sum, pair_sum = project_sums(meta, normed_t, query_back, pair_back, seqs)
    grad_query = scatter_rows(query_sum, "cqxz")
    grad_pair = scatter_rows(pair_sum, "cxqz")
    grad_key, grad_value = grad_pair[:, :pair_width], grad_pair[:, pair_width:]
    grad_gain_attn = (
        jnp.sum(grad_query * w_query.astype(F32), axis=1)
        + jnp.sum(grad_key * w_key.astype(F32), axis=1)
        + jnp.sum(grad_value * w_value.astype(F32), axis=1)
    ) / gain_attn.astype(F32)

    query_grad, pair_grad = project_back(query_back, pair_back, query_full, pair_full, seqs, Z)
    received = None
    for k in range(1, Z):
        part = lax.dynamic_index_in_dim(pair_grad, (move.zi + k) % Z, axis=0, keepdims=False)
        if received is not None:
            part = (part.astype(F32) + received.astype(F32)).astype(BF)
        received = move.down(part)
    mine = lax.dynamic_index_in_dim(pair_grad, move.zi, axis=0, keepdims=False)
    in_grad = input_grad(inputs, attn_scale, first_grad, query_grad, mine, received)
    return (
        layer_out.reshape(seqs, rows, width),
        in_grad.reshape(seqs, rows, width),
        grad_query,
        grad_key,
        grad_value,
        grad_output,
        grad_gain_attn,
        grad_gain_ffn,
        grad_gate,
        grad_up,
        grad_down,
    )


def solution(mesh):
    rows = P(("seq", "dp"), None)
    vector = P(("seq", "dp"))
    act = P("dp", "seq", None)
    return jax.shard_map(
        per_device,
        mesh=mesh,
        in_specs=(act, P("dp", "seq"), act, rows, rows, rows, rows, vector, vector, rows, rows, rows),
        out_specs=(act, act, rows, rows, rows, rows, vector, vector, rows, rows, rows),
        check_vma=False,
    )
```

time: 953 us -> 671 us (0.70)
  matrix products: 213 us -> 0 us
  Pallas kernels: 0 us -> 152 us
  local copies, waits for them, and re-layouts: 202 us -> 54.7 us
  other arithmetic: 138 us -> 50.3 us
  waiting for transfers between devices: 293 us -> 326 us
  starting transfers between devices: 90.4 us -> 76.4 us
    dot_general x101 -> x0, matrix products: 213 us -> none  [the longest x15 65.6 us: mm(): return jnp.dot(left, right, preferred_element_type=F32)]
    pallas_call x0 -> x12, Pallas kernels: none -> 152 us  [the longest x8 122 us: kernel_call(): pl.pallas_call(body, out_shape=out_shape, in_specs=in_specs, out_specs=ou...]
    mul x9 -> x0, local copies, waits for them, and re-layouts: 26.8 us -> none  [the longest x7 26.7 us: rotate(): return values * cosine[:, None, :] + turned * sine[:, None, :]]
    ppermute x11, waiting for transfers between devices: 64.7 us -> 88.1 us  [step(): return lax.ppermute(value, 'dp', [(i, i ^ 2) for i in range(self.DP)])]
    ppermute x27, waiting for transfers between devices: 98.3 us -> 120 us  [step(): lax.ppermute(value, 'seq', [(i, (i + 1) % self.Z) for i in range(self.Z)])]
    slice x49 -> x3, local copies, waits for them, and re-layouts: 26.1 us -> 5.35 us  [the longest x2 3.89 us: collect(): value = value[:half].astype(F32) + move.step('c', value[half:]).astype(F32)]
    select_n x19, other arithmetic: 34.6 us -> 13.9 us  [gather(): jnp.where(index == 0, jnp.stack(blocks, axis=position), jnp.stack(blocks[...]
    concatenate x4 -> x0, local copies, waits for them, and re-layouts: 20.1 us -> none  [the longest x1 11 us: per_device(): jnp.concatenate([output_sum, jnp.broadcast_to(ffn_gain_part[:, None], (wi...]
  transfers between devices with their start and end apart: 73 -> 75, of which waited for: 36 -> 41; matrix products, arithmetic and copies ran while one was open for 49% -> 15% of each run, Pallas kernels for 0% -> 17%
where the time goes in v2:
time: 671 us; the launch traced here: 662 us
  waiting for transfers between devices  326 us (49%)
  Pallas kernels  152 us (23%)
  starting transfers between devices  76.4 us (11%)
  local copies, waits for them, and re-layouts  54.7 us (8%)
  other arithmetic  50.3 us (7%)
    pallas_call x8, Pallas kernels, kernel_call(): pl.pallas_call(body, out_shape=out_shape, in_specs=in_specs, out_specs=ou...  122 us
    ppermute x27, waiting for transfers between devices, step(): lax.ppermute(value, 'seq', [(i, (i + 1) % self.Z) for i in range(self.Z)])  120 us
    ppermute x15, waiting for transfers between devices, step(): lax.ppermute(value, 'dp', [(i, i % 4 + 4 * ((i // 4 + 1) % self.Q)) for i...  104 us
    ppermute x11, waiting for transfers between devices, step(): return lax.ppermute(value, 'dp', [(i, i ^ 2) for i in range(self.DP)])  88.1 us
    pallas_call x4, Pallas kernels, ffn_sums(): pl.pallas_call(functools.partial(ffn_sums_body, units, lines), out_shape=...  30.5 us
    ppermute x6, starting transfers between devices, up(): return lax.ppermute(value, 'seq', [(i, i + 1) for i in range(self.Z - 1)])  20.6 us
    ppermute x27, starting transfers between devices, step(): lax.ppermute(value, 'seq', [(i, (i + 1) % self.Z) for i in range(self.Z)])  19 us
    ppermute x15, starting transfers between devices, step(): lax.ppermute(value, 'dp', [(i, i % 4 + 4 * ((i // 4 + 1) % self.Q)) for i...  19 us
  transfers between devices with their start and end apart: 75, of which 41 were waited for; matrix products, arithmetic and copies ran while one was open for 15% of the time, Pallas kernels for 17%

profile of v2, /device:TPU:0, one launch (start us, length us, event | category | flops | bytes accessed | tf_op | source)
XLA Modules:
  0.0 662.2 jit_solution(8100000886303882090)
XLA Ops:
  0.7 5.1 collective-permute-start
  8.1 3.5 collective-permute-start.9
  26.4 3.8 collective-permute-done.4
  31.7 3.5 collective-permute-start.10
  36.8 3.8 collective-permute-start.11
  58.9 25.5 %collective-permute-done.13 = bf16[48,1536]{1,0:T(8,128)(2,1)S(1)} collective-permute-done((bf16[48,1536]{1,0:T(8,128)(2,1)}, bf16[48,1536]{1,0:T(8,128)(2,1)S(1)}, u32[]{:S(2)}, u32[]{:S(2)}) %collective-permute-start.13) | collective-permute-done | bytes 147488 | tf_op jit(solution)/shard_map/ppermute | solution.py:66
  104.4 5.8 collective-permute-done.15
  115.2 7.7 %collective-permute-done.27 = bf16[4,48,1536]{2,1,0:T(8,128)(2,1)S(1)} collective-permute-done((bf16[4,48,1536]{2,1,0:T(8,128)(2,1)S(1)}, bf16[4,48,1536]{2,1,0:T(8,128)(2,1)S(1)}, u32[]{:S(2)}, u32[]{:S(2)}) %collective-permute-start.27) | collective-permute-done | bytes 589856 | tf_op jit(solution)/shard_map/ppermute | solution.py:63
  129.2 10.1 %collective-permute-done.16 = bf16[4,2,48,1536]{3,2,1,0:T(8,128)(2,1)S(1)} collective-permute-done((bf16[4,2,48,1536]{3,2,1,0:T(8,128)(2,1)S(1)}, bf16[4,2,48,1536]{3,2,1,0:T(8,128)(2,1)S(1)}, u32[]{:S(2)}, u32[]{:S(2)}) %collective-permute-start.16) | collective-permute-done | bytes 1179680 | tf_op jit(solution)/shard_map/ppermute | solution.py:61
  139.6 6.1 collective-permute-done.22
  150.0 14.6 %collective-permute-done.28 = bf16[4,2,48,1536]{3,2,0,1:T(8,128)(2,1)S(1)} collective-permute-done((bf16[4,2,48,1536]{3,2,0,1:T(8,128)(2,1)S(1)}, bf16[4,2,48,1536]{3,2,0,1:T(8,128)(2,1)S(1)}, u32[]{:S(2)}, u32[]{:S(2)}) %collective-permute-start.28) | collective-permute-done | bytes 1179680 | tf_op jit(solution)/shard_map/ppermute | solution.py:61
  173.3 5.0 collective-permute-done.33.refs_5_
  179.8 8.6 %collective-permute-done.39.refs_12_ = bf16[384,1536]{1,0:T(8,128)(2,1)} collective-permute-done((bf16[384,1536]{1,0:T(8,128)(2,1)}, bf16[384,1536]{1,0:T(8,128)(2,1)}, u32[]{:S(2)}, u32[]{:S(2)}) %collective-permute-start.39) | collective-permute-done | bytes 1179680 | tf_op jit(solution)/shard_map/ppermute | solution.py:66
  191.0 25.7 %shard_map.203 = (bf16[256,1536]{1,0:T(8,128)(2,1)}, bf16[1536,256]{1,0:T(8,128)(2,1)}, f32[8,2,1,256]{3,2,1,0:T(1,128)}, bf16[1536,256]{1,0:T(8,128)(2,1)}, bf1...) custom-call(s32[1]{0:T(128)} %bitcast.1.meta, bf16[1024,1536]{1,0:T(8,128)(2,1)} %bitcast.10.tokens, ...), custom_call_target="tpu_custom_call" | custom-call | flops 6845104128 | bytes 20971520 | tf_op jit(solution)/shard_map/pallas_call | solution.py:117
  216.7 5.0 maximum_select_fusion.2
  224.2 6.5 shard_map.204
  235.8 15.1 %collective-permute-done.30.refs_1_ = bf16[256,1536]{1,0:T(8,128)(2,1)S(1)} collective-permute-done((bf16[256,1536]{1,0:T(8,128)(2,1)}, bf16[256,1536]{1,0:T(8,128)(2,1)S(1)}, u32[]{:S(2)}, u32[]{:S(2)}) %collective-permute-start.30) | collective-permute-done | bytes 786464 | tf_op jit(solution)/shard_map/ppermute | solution.py:61
  250.9 10.3 %collective-permute-done.38.refs_11_ = bf16[384,1536]{1,0:T(8,128)(2,1)S(1)} collective-permute-done((bf16[384,1536]{1,0:T(8,128)(2,1)}, bf16[384,1536]{1,0:T(8,128)(2,1)S(1)}, u32[]{:S(2)}, u32[]{:S(2)}) %collective-permute-start.38) | collective-permute-done | bytes 1179680 | tf_op jit(solution)/shard_map/ppermute | solution.py:63
  261.3 25.3 %collective-permute-done.40.refs_13_ = bf16[384,1536]{1,0:T(8,128)(2,1)S(1)} collective-permute-done((bf16[384,1536]{1,0:T(8,128)(2,1)}, bf16[384,1536]{1,0:T(8,128)(2,1)S(1)}, u32[]{:S(2)}, u32[]{:S(2)}) %collective-permute-start.40) | collective-permute-done | bytes 1179680 | tf_op jit(solution)/shard_map/ppermute | solution.py:63
  286.5 24.6 %collective-permute-done.42.refs_15_ = bf16[384,1536]{1,0:T(8,128)(2,1)S(1)} collective-permute-done((bf16[384,1536]{1,0:T(8,128)(2,1)}, bf16[384,1536]{1,0:T(8,128)(2,1)S(1)}, u32[]{:S(2)}, u32[]{:S(2)}) %collective-permute-start.42) | collective-permute-done | bytes 1179680 | tf_op jit(solution)/shard_map/ppermute | solution.py:63
  313.0 33.4 %shard_map.205 = (bf16[1024,1536]{1,0:T(8,128)(2,1)}, bf16[1024,1536]{1,0:T(8,128)(2,1)}, bf16[1024,1024]{1,0:T(8,128)(2,1)}, bf16[1024,1024]{1,0:T(8,128)(2,1)}, bf16[1024,1024]{1,0:T(8,128)(2,1)}) custom-call(bf16[256,1536]{1,0:T(8,128)(2,1)} %get-tuple-element.43.refs_0_, bf16[256,1536]{1,0:T(8,128)(2,1)} %copy-done.6, bf16[256,1536]{1,0:T(8,128)(2,1)} %copy-done.7, ...), custom_call_target="tpu_custom_call" | custom-call | flops 19327352832 | bytes 35651584 | tf_op jit(solution)/shard_map/pallas_call | solution.py:117
  346.5 7.6 %shard_map.214 = (f32[384,1536]{1,0:T(8,128)}, bf16[384,1536]{1,0:T(8,128)(2,1)}) custom-call(bf16[1024,1024]{1,0:T(8,128)(2,1)} %get-tuple-element.60.hidden_t, bf16[1024,1024]{1,0:T(8,128)(2,1)} %get-tuple-element.61.gate_t, bf16[1024,1024]{1,0:T(8,128)(2,1)} %get-tuple-element.62.up_t, bf16[256,1536]{1,0:T(8,128)(2,1)} %get-tuple-element.43.refs_0_, ...), custom_call_target="tpu_custom_call" | custom-call | flops 2415919104 | bytes 14680064 | tf_op jit(solution)/shard_map/pallas_call | solution.py:485
  360.0 7.6 %shard_map.213 = (f32[384,1536]{1,0:T(8,128)}, bf16[384,1536]{1,0:T(8,128)(2,1)}) custom-call(bf16[1024,1024]{1,0:T(8,128)(2,1)} %get-tuple-element.60.hidden_t, bf16[1024,1024]{1,0:T(8,128)(2,1)} %get-tuple-element.61.gate_t, bf16[1024,1024]{1,0:T(8,128)(2,1)} %get-tuple-element.62.up_t, bf16[256,1536]{1,0:T(8,128)(2,1)} %get-tuple-element.43.refs_0_, ...), custom_call_target="tpu_custom_call" | custom-call | flops 2415919104 | bytes 14680064 | tf_op jit(solution)/shard_map/pallas_call | solution.py:485
  368.3 7.6 %shard_map.212 = (f32[384,1536]{1,0:T(8,128)}, bf16[384,1536]{1,0:T(8,128)(2,1)}) custom-call(bf16[1024,1024]{1,0:T(8,128)(2,1)} %get-tuple-element.60.hidden_t, bf16[1024,1024]{1,0:T(8,128)(2,1)} %get-tuple-element.61.gate_t, bf16[1024,1024]{1,0:T(8,128)(2,1)} %get-tuple-element.62.up_t, bf16[256,1536]{1,0:T(8,128)(2,1)} %get-tuple-element.43.refs_0_, ...), custom_call_target="tpu_custom_call" | custom-call | flops 2415919104 | bytes 14680064 | tf_op jit(solution)/shard_map/pallas_call | solution.py:485
  377.2 7.6 %shard_map.211 = (f32[384,1536]{1,0:T(8,128)}, bf16[384,1536]{1,0:T(8,128)(2,1)}) custom-call(bf16[1024,1024]{1,0:T(8,128)(2,1)} %get-tuple-element.60.hidden_t, bf16[1024,1024]{1,0:T(8,128)(2,1)} %get-tuple-element.61.gate_t, bf16[1024,1024]{1,0:T(8,128)(2,1)} %get-tuple-element.62.up_t, bf16[256,1536]{1,0:T(8,128)(2,1)} %get-tuple-element.43.refs_0_, ...), custom_call_target="tpu_custom_call" | custom-call | flops 2415919104 | bytes 14680064 | tf_op jit(solution)/shard_map/pallas_call | solution.py:485
  394.6 13.9 %collective-permute-done.70 = bf16[384,1536]{1,0:T(8,128)(2,1)} collective-permute-done((bf16[384,1536]{1,0:T(8,128)(2,1)}, bf16[384,1536]{1,0:T(8,128)(2,1)}, u32[]{:S(2)}, u32[]{:S(2)}) %collective-permute-start.70) | collective-permute-done | bytes 1179680 | tf_op jit(solution)/shard_map/ppermute | solution.py:63
  409.1 7.4 %collective-permute-done.72 = bf16[384,1536]{1,0:T(8,128)(2,1)S(1)} collective-permute-done((bf16[384,1536]{1,0:T(8,128)(2,1)S(1)}, bf16[384,1536]{1,0:T(8,128)(2,1)S(1)}, u32[]{:S(2)}, u32[]{:S(2)}) %collective-permute-start.72) | collective-permute-done | bytes 1179680 | tf_op jit(solution)/shard_map/ppermute | solution.py:66
  420.9 10.6 %shard_map.206 = (f32[256,1536]{1,0:T(8,128)}, bf16[1536,256]{1,0:T(8,128)(2,1)}, f32[1536,1664]{1,0:T(8,128)}) custom-call(bf16[256,1536]{1,0:T(8,128)(2,1)} %bitcast.220, f32[256,1536]{1,0:T(8,128)} %get-tuple-element.42.total, f32[256,1536]{1,0:T(8,128)} %slice_add_fusion.second_grad, f32[1,1536]{1,0:T(1,128)} %slice.66.gain, ...), custom_call_target="tpu_custom_call" | custom-call | flops 2415919104 | bytes 23068672 | tf_op jit(solution)/shard_map/pallas_call | solution.py:117
  431.6 15.5 %shard_map.207 = (bf16[1536,256]{1,0:T(8,128)(2,1)}, bf16[1536,1024]{1,0:T(8,128)(2,1)}) custom-call(s32[1]{0:T(128)} %bitcast.1.meta, bf16[1536,256]{1,0:T(8,128)(2,1)} %get-tuple-element.48.query_t, bf16[1536,1024]{1,0:T(8,128)(2,1)} %get-tuple-element.49.pair_t, bf16[1536,256]{1,0:T(8,128)(2,1)} %get-tuple-element.50.grad_t, ...), custom_call_target="tpu_custom_call" | custom-call | flops 2013265920 | bytes 12582912 | tf_op jit(solution)/shard_map/pallas_call | solution.py:117
  447.0 12.9 %shard_map.208 = (f32[1536,256]{1,0:T(8,128)}, bf16[4,1536,256]{2,1,0:T(8,128)(2,1)}) custom-call(bf16[1536,256]{1,0:T(8,128)(2,1)} %get-tuple-element.52.query_back, bf16[1536,1024]{1,0:T(8,128)(2,1)} %get-tuple-element.53.pair_back, bf16[1536,1536]{1,0:T(8,128)(2,1)} %bitcast.259, bf16[1536,1536]{1,0:T(8,128)(2,1)} %bitcast.261), custom_call_target="tpu_custom_call" | custom-call | flops 6039797760 | bytes 20971520 | tf_op jit(solution)/shard_map/pallas_call | solution.py:117
  464.1 13.0 %shard_map.210 = (f32[1536,1536]{1,0:T(8,128)}, f32[1536,1536]{1,0:T(8,128)}) custom-call(s32[1]{0:T(128)} %bitcast.1.meta, bf16[1536,1024]{1,0:T(8,128)(2,1)} %get-tuple-element.56.normed_t, bf16[1536,256]{1,0:T(8,128)(2,1)} %get-tuple-element.52.query_back, bf16[1536,1024]{1,0:T(8,128)(2,1)} %get-tuple-element.53.pair_back), custom_call_target="tpu_custom_call" | custom-call | flops 6039797760 | bytes 27262976 | tf_op jit(solution)/shard_map/pallas_call | solution.py:117
  479.7 4.2 fusion.2
  489.1 3.3 collective-permute-start.74
  492.4 4.3 fusion
  498.1 10.0 %collective-permute-done.48 = bf16[1536,256]{1,0:T(8,128)(2,1)S(1)} collective-permute-done((bf16[1536,256]{1,0:T(8,128)(2,1)S(1)}, bf16[1536,256]{1,0:T(8,128)(2,1)S(1)}, u32[]{:S(2)}, u32[]{:S(2)}) %collective-permute-start.48) | collective-permute-done | bytes 786464 | tf_op jit(solution)/shard_map/ppermute | solution.py:72
  510.0 25.6 %collective-permute-done.74 = bf16[384,1536]{1,0:T(8,128)(2,1)S(1)} collective-permute-done((bf16[384,1536]{1,0:T(8,128)(2,1)S(1)}, bf16[384,1536]{1,0:T(8,128)(2,1)S(1)}, u32[]{:S(2)}, u32[]{:S(2)}) %collective-permute-start.74) | collective-permute-done | bytes 1179680 | tf_op jit(solution)/shard_map/ppermute | solution.py:66
  539.0 3.1 bitcast_add_fusion.2
  553.1 4.4 shard_map.209
  561.2 10.0 %collective-permute-done.51 = bf16[4,2,48,1536]{3,2,0,1:T(8,128)(2,1)} collective-permute-done((bf16[4,2,48,1536]{3,2,0,1:T(8,128)(2,1)}, bf16[4,2,48,1536]{3,2,0,1:T(8,128)(2,1)}, u32[]{:S(2)}, u32[]{:S(2)}) %collective-permute-start.51) | collective-permute-done | bytes 1179680 | tf_op jit(solution)/shard_map/ppermute | solution.py:63
  574.3 5.4 collective-permute-done.57
  582.4 24.5 %collective-permute-done.63 = bf16[4,2,48,1664]{3,2,0,1:T(8,128)(2,1)S(1)} collective-permute-done((bf16[4,2,48,1664]{3,2,0,1:T(8,128)(2,1)S(1)}, bf16[4,2,48,1664]{3,2,0,1:T(8,128)(2,1)S(1)}, u32[]{:S(2)}, u32[]{:S(2)}) %collective-permute-start.63) | collective-permute-done | bytes 1277984 | tf_op jit(solution)/shard_map/ppermute | solution.py:61
  608.3 9.8 %collective-permute-done.52 = bf16[4,48,1536]{2,1,0:T(8,128)(2,1)S(1)} collective-permute-done((bf16[4,48,1536]{2,1,0:T(8,128)(2,1)S(1)}, bf16[4,48,1536]{2,1,0:T(8,128)(2,1)S(1)}, u32[]{:S(2)}, u32[]{:S(2)}) %collective-permute-start.52) | collective-permute-done | bytes 589856 | tf_op jit(solution)/shard_map/ppermute | solution.py:61
  618.6 7.6 %collective-permute-done.53 = bf16[48,1536]{1,0:T(8,128)(2,1)S(1)} collective-permute-done((bf16[48,1536]{1,0:T(8,128)(2,1)S(1)}, bf16[48,1536]{1,0:T(8,128)(2,1)S(1)}, u32[]{:S(2)}, u32[]{:S(2)}) %collective-permute-start.53) | collective-permute-done | bytes 147488 | tf_op jit(solution)/shard_map/ppermute | solution.py:66
  628.2 5.0 collective-permute-done.54
  633.3 3.3 collective-permute-done.60
  637.0 6.7 %collective-permute-done.61 = bf16[48,1536]{1,0:T(8,128)(2,1)S(1)} collective-permute-done((bf16[48,1536]{1,0:T(8,128)(2,1)S(1)}, bf16[48,1536]{1,0:T(8,128)(2,1)S(1)}, u32[]{:S(2)}, u32[]{:S(2)}) %collective-permute-start.61) | collective-permute-done | bytes 147488 | tf_op jit(solution)/shard_map/ppermute | solution.py:66
  646.4 6.8 %collective-permute-done.66 = bf16[48,1664]{1,0:T(8,128)(2,1)S(1)} collective-permute-done((bf16[48,1664]{1,0:T(8,128)(2,1)S(1)}, bf16[48,1664]{1,0:T(8,128)(2,1)S(1)}, u32[]{:S(2)}, u32[]{:S(2)}) %collective-permute-start.66) | collective-permute-done | bytes 159776 | tf_op jit(solution)/shard_map/ppermute | solution.py:66
  653.8 6.5 collective-permute-done.67
  (314 shorter events, 166.8 us)
Async XLA Ops:
  0.7 100.4 %collective-permute-start = (bf16[2,128,1536]{2,1,0:T(8,128)(2,1)}, bf16[2,128,1536]{2,1,0:T(8,128)(2,1)S(1)}, u32[]{:S(2)}, u32[]{:S(2)}) collective-permute-start(bf16[2,128,1536]{2,1,0:T(8,128)(2,1)} %param.12), channel_id=1, source_target_pairs={{0,8},{8,16},{16,24},{1,9},{9,17},{17,25},{2,10},{10,18},{18,26},{... | collective-permute-start | bytes 2359304 | tf_op jit(solution)/shard_map/ppermute | solution.py:69
  8.1 23.6 %collective-permute-start.9 = (s32[2,128]{1,0:T(2,128)}, s32[2,128]{1,0:T(2,128)S(1)}, u32[]{:S(2)}, u32[]{:S(2)}) collective-permute-start(s32[2,128]{1,0:T(2,128)} %param.13), channel_id=1, source_target_pairs={{0,8},{8,16},{16,24},{1,9},{9,17},{17,25},{2,10},{10,18},{18,26},{... | collective-permute-start | bytes 3080 | tf_op jit(solution)/shard_map/ppermute | solution.py:69
  14.6 39.5 %collective-permute-start.12 = (bf16[48,1536]{1,0:T(8,128)(2,1)}, bf16[48,1536]{1,0:T(8,128)(2,1)}, u32[]{:S(2)}, u32[]{:S(2)}) collective-permute-start(bf16[48,1536]{1,0:T(8,128)(2,1)} %constant_dynamic-update-slice_fusion.4), channel_id=1, source_target_pairs={{0,8},{8,16},{16,24},{24,0},{1,9},{9,17},{17,25},{25,1},{2,10},{10... | collective-permute-start | bytes 442376 | tf_op jit(solution)/shard_map/ppermute | solution.py:66
  14.6 42.0 %collective-permute-start.18 = (bf16[48,1536]{1,0:T(8,128)(2,1)}, bf16[48,1536]{1,0:T(8,128)(2,1)}, u32[]{:S(2)}, u32[]{:S(2)}) collective-permute-start(bf16[48,1536]{1,0:T(8,128)(2,1)} %param.15), channel_id=1, source_target_pairs={{0,8},{8,16},{16,24},{24,0},{1,9},{9,17},{17,25},{25,1},{2,10},{10... | collective-permute-start | bytes 442376 | tf_op jit(solution)/shard_map/ppermute | solution.py:66
  50.4 97.2 %collective-permute-start.37 = (bf16[384,1536]{1,0:T(8,128)(2,1)}, bf16[384,1536]{1,0:T(8,128)(2,1)}, u32[]{:S(2)}, u32[]{:S(2)}) collective-permute-start(bf16[384,1536]{1,0:T(8,128)(2,1)} %constant_dynamic-update-slice_fusion.6.refs_8_), channel_id=1, source_target_pairs={{0,8},{8,16},{16,24},{24,0},{1,9},{9,17},{17,25},{25,1},{2,10},{10... | collective-permute-start | bytes 3538952 | tf_op jit(solution)/shard_map/ppermute | solution.py:66
  54.1 30.3 %collective-permute-start.13 = (bf16[48,1536]{1,0:T(8,128)(2,1)}, bf16[48,1536]{1,0:T(8,128)(2,1)S(1)}, u32[]{:S(2)}, u32[]{:S(2)}) collective-permute-start(bf16[48,1536]{1,0:T(8,128)(2,1)} %collective-permute-done.12), channel_id=1, source_target_pairs={{0,8},{8,16},{16,24},{24,0},{1,9},{9,17},{17,25},{25,1},{2,10},{10... | collective-permute-start | bytes 442376 | tf_op jit(solution)/shard_map/ppermute | solution.py:66
  56.7 30.9 %collective-permute-start.19 = (bf16[48,1536]{1,0:T(8,128)(2,1)}, bf16[48,1536]{1,0:T(8,128)(2,1)S(1)}, u32[]{:S(2)}, u32[]{:S(2)}) collective-permute-start(bf16[48,1536]{1,0:T(8,128)(2,1)} %collective-permute-done.18), channel_id=1, source_target_pairs={{0,8},{8,16},{16,24},{24,0},{1,9},{9,17},{17,25},{25,1},{2,10},{10... | collective-permute-start | bytes 442376 | tf_op jit(solution)/shard_map/ppermute | solution.py:66
  58.0 32.7 %collective-permute-start.25 = (bf16[48,1536]{1,0:T(8,128)(2,1)S(1)}, bf16[48,1536]{1,0:T(8,128)(2,1)S(1)}, u32[]{:S(2)}, u32[]{:S(2)}) collective-permute-start(bf16[48,1536]{1,0:T(8,128)(2,1)S(1)} %collective-permute-done.24), channel_id=1, source_target_pairs={{0,8},{8,16},{16,24},{24,0},{1,9},{9,17},{17,25},{25,1},{2,10},{10... | collective-permute-start | bytes 442376 | tf_op jit(solution)/shard_map/ppermute | solution.py:66
  101.0 24.7 %collective-permute-start.1 = (bf16[2,128,1536]{2,1,0:T(8,128)(2,1)S(1)}, bf16[2,128,1536]{2,1,0:T(8,128)(2,1)S(1)}, u32[]{:S(2)}, u32[]{:S(2)}) collective-permute-start(bf16[2,128,1536]{2,1,0:T(8,128)(2,1)S(1)} %collective-permute-done), channel_id=1, source_target_pairs={{0,8},{8,16},{16,24},{1,9},{9,17},{17,25},{2,10},{10,18},{18,26},{... | collective-permute-start | bytes 2359304 | tf_op jit(solution)/shard_map/ppermute | solution.py:69
  110.3 29.0 %collective-permute-start.16 = (bf16[4,2,48,1536]{3,2,1,0:T(8,128)(2,1)S(1)}, bf16[4,2,48,1536]{3,2,1,0:T(8,128)(2,1)S(1)}, u32[]{:S(2)}, u32[]{:S(2)}) collective-permute-start(bf16[4,2,48,1536]{3,2,1,0:T(8,128)(2,1)S(1)} %maximum_select_fusion.7), channel_id=1, source_target_pairs={{0,2},{1,3},{2,0},{3,1},{4,6},{5,7},{6,4},{7,5},{8,10},{9,11},{10,... | collective-permute-start | bytes 3538952 | tf_op jit(solution)/shard_map/ppermute | solution.py:61
  113.6 32.1 %collective-permute-start.22 = (bf16[4,2,48,1536]{3,2,0,1:T(8,128)(2,1)S(1)}, bf16[4,2,48,1536]{3,2,0,1:T(8,128)(2,1)S(1)}, u32[]{:S(2)}, u32[]{:S(2)}) collective-permute-start(bf16[4,2,48,1536]{3,2,0,1:T(8,128)(2,1)S(1)} %maximum_select_fusion.8), channel_id=1, source_target_pairs={{0,4},{1,5},{2,6},{3,7},{4,0},{5,1},{6,2},{7,3},{8,12},{9,13},{10,... | collective-permute-start | bytes 3538952 | tf_op jit(solution)/shard_map/ppermute | solution.py:63
  123.1 41.5 %collective-permute-start.28 = (bf16[4,2,48,1536]{3,2,0,1:T(8,128)(2,1)S(1)}, bf16[4,2,48,1536]{3,2,0,1:T(8,128)(2,1)S(1)}, u32[]{:S(2)}, u32[]{:S(2)}) collective-permute-start(bf16[4,2,48,1536]{3,2,0,1:T(8,128)(2,1)S(1)} %maximum_select_fusion.10), channel_id=1, source_target_pairs={{0,2},{1,3},{2,0},{3,1},{4,6},{5,7},{6,4},{7,5},{8,10},{9,11},{10,... | collective-permute-start | bytes 3538952 | tf_op jit(solution)/shard_map/ppermute | solution.py:61
  125.8 42.9 %collective-permute-start.2 = (bf16[2,128,1536]{2,1,0:T(8,128)(2,1)S(1)}, bf16[2,128,1536]{2,1,0:T(8,128)(2,1)S(1)}, u32[]{:S(2)}, u32[]{:S(2)}) collective-permute-start(bf16[2,128,1536]{2,1,0:T(8,128)(2,1)S(1)} %collective-permute-done.1), channel_id=1, source_target_pairs={{0,8},{8,16},{16,24},{1,9},{9,17},{17,25},{2,10},{10,18},{18,26},{... | collective-permute-start | bytes 2359304 | tf_op jit(solution)/shard_map/ppermute | solution.py:69
  139.5 48.9 %collective-permute-start.17 = (bf16[4,2,2,48,1536]{4,3,2,1,0:T(8,128)(2,1)S(1)}, bf16[4,2,2,48,1536]{4,3,2,1,0:T(8,128)(2,1)S(1)}, u32[]{:S(2)}, u32[]{:S(2)}) collective-permute-start(bf16[4,2,2,48,1536]{4,3,2,1,0:T(8,128)(2,1)S(1)} %maximum_select_fusion.3), channel_id=1, source_target_pairs={{0,1},{1,0},{2,3},{3,2},{4,5},{5,4},{6,7},{7,6},{8,9},{9,8},{10,11... | collective-permute-start | bytes 7077896 | tf_op jit(solution)/shard_map/ppermute | solution.py:59
  146.1 23.5 %collective-permute-start.23 = (bf16[4,2,2,48,1536]{4,3,0,1,2:T(8,128)(2,1)S(1)}, bf16[4,2,2,48,1536]{4,3,0,1,2:T(8,128)(2,1)S(1)}, u32[]{:S(2)}, u32[]{:S(2)}) collective-permute-start(bf16[4,2,2,48,1536]{4,3,0,1,2:T(8,128)(2,1)S(1)} %maximum_select_fusion.4), channel_id=1, source_target_pairs={{0,1},{1,0},{2,3},{3,2},{4,5},{5,4},{6,7},{7,6},{8,9},{9,8},{10,11... | collective-permute-start | bytes 7077896 | tf_op jit(solution)/shard_map/ppermute | solution.py:59
  148.5 29.9 %collective-permute-start.33 = (bf16[256,1536]{1,0:T(8,128)(2,1)S(1)}, bf16[256,1536]{1,0:T(8,128)(2,1)S(1)}, u32[]{:S(2)}, u32[]{:S(2)}) collective-permute-start(bf16[256,1536]{1,0:T(8,128)(2,1)S(1)} %bitcast.221), channel_id=1, source_target_pairs={{0,2},{1,3},{2,0},{3,1},{4,6},{5,7},{6,4},{7,5},{8,10},{9,11},{10,... | collective-permute-start | bytes 2359304 | tf_op jit(solution)/shard_map/ppermute | solution.py:61
  164.6 23.9 %collective-permute-start.39 = (bf16[384,1536]{1,0:T(8,128)(2,1)}, bf16[384,1536]{1,0:T(8,128)(2,1)}, u32[]{:S(2)}, u32[]{:S(2)}) collective-permute-start(bf16[384,1536]{1,0:T(8,128)(2,1)} %collective-permute-done.37.refs_10_), channel_id=1, source_target_pairs={{0,8},{8,16},{16,24},{24,0},{1,9},{9,17},{17,25},{25,1},{2,10},{10... | collective-permute-start | bytes 3538952 | tf_op jit(solution)/shard_map/ppermute | solution.py:66
  168.6 48.1 %collective-permute-start.29 = (bf16[4,2,2,48,1536]{4,3,0,1,2:T(8,128)(2,1)}, bf16[4,2,2,48,1536]{4,3,0,1,2:T(8,128)(2,1)}, u32[]{:S(2)}, u32[]{:S(2)}) collective-permute-start(bf16[4,2,2,48,1536]{4,3,0,1,2:T(8,128)(2,1)} %maximum_select_fusion.6), channel_id=1, source_target_pairs={{0,1},{1,0},{2,3},{3,2},{4,5},{5,4},{6,7},{7,6},{8,9},{9,8},{10,11... | collective-permute-start | bytes 7077896 | tf_op jit(solution)/shard_map/ppermute | solution.py:59
  169.6 62.7 %collective-permute-start.34 = (bf16[256,1536]{1,0:T(8,128)(2,1)S(1)}, bf16[256,1536]{1,0:T(8,128)(2,1)S(1)}, u32[]{:S(2)}, u32[]{:S(2)}) collective-permute-start(bf16[256,1536]{1,0:T(8,128)(2,1)S(1)} %bitcast.222), channel_id=1, source_target_pairs={{0,1},{1,0},{2,3},{3,2},{4,5},{5,4},{6,7},{7,6},{8,9},{9,8},{10,11... | collective-permute-start | bytes 2359304 | tf_op jit(solution)/shard_map/ppermute | solution.py:59
  178.3 55.5 %collective-permute-start.36 = (bf16[384,1536]{1,0:T(8,128)(2,1)}, bf16[384,1536]{1,0:T(8,128)(2,1)}, u32[]{:S(2)}, u32[]{:S(2)}) collective-permute-start(bf16[384,1536]{1,0:T(8,128)(2,1)} %constant_dynamic-update-slice_fusion.6.refs_8_), channel_id=1, source_target_pairs={{0,4},{1,5},{2,6},{3,7},{4,0},{5,1},{6,2},{7,3},{8,12},{9,13},{10,... | collective-permute-start | bytes 3538952 | tf_op jit(solution)/shard_map/ppermute | solution.py:63
  188.5 47.4 %collective-permute-start.35 = (bf16[256,1536]{1,0:T(8,128)(2,1)S(1)}, bf16[256,1536]{1,0:T(8,128)(2,1)S(1)}, u32[]{:S(2)}, u32[]{:S(2)}) collective-permute-start(bf16[256,1536]{1,0:T(8,128)(2,1)S(1)} %collective-permute-done.33.refs_5_), channel_id=1, source_target_pairs={{0,1},{1,0},{2,3},{3,2},{4,5},{5,4},{6,7},{7,6},{8,9},{9,8},{10,11... | collective-permute-start | bytes 2359304 | tf_op jit(solution)/shard_map/ppermute | solution.py:59
  188.5 45.8 %collective-permute-start.41 = (bf16[384,1536]{1,0:T(8,128)(2,1)}, bf16[384,1536]{1,0:T(8,128)(2,1)}, u32[]{:S(2)}, u32[]{:S(2)}) collective-permute-start(bf16[384,1536]{1,0:T(8,128)(2,1)} %collective-permute-done.39.refs_12_), channel_id=1, source_target_pairs={{0,8},{8,16},{16,24},{24,0},{1,9},{9,17},{17,25},{25,1},{2,10},{10... | collective-permute-start | bytes 3538952 | tf_op jit(solution)/shard_map/ppermute | solution.py:66
  232.3 29.0 %collective-permute-start.38 = (bf16[384,1536]{1,0:T(8,128)(2,1)}, bf16[384,1536]{1,0:T(8,128)(2,1)S(1)}, u32[]{:S(2)}, u32[]{:S(2)}) collective-permute-start(bf16[384,1536]{1,0:T(8,128)(2,1)} %collective-permute-done.37.refs_10_), channel_id=1, source_target_pairs={{0,4},{1,5},{2,6},{3,7},{4,0},{5,1},{6,2},{7,3},{8,12},{9,13},{10,... | collective-permute-start | bytes 3538952 | tf_op jit(solution)/shard_map/ppermute | solution.py:63
  233.8 52.8 %collective-permute-start.40 = (bf16[384,1536]{1,0:T(8,128)(2,1)}, bf16[384,1536]{1,0:T(8,128)(2,1)S(1)}, u32[]{:S(2)}, u32[]{:S(2)}) collective-permute-start(bf16[384,1536]{1,0:T(8,128)(2,1)} %collective-permute-done.39.refs_12_), channel_id=1, source_target_pairs={{0,4},{1,5},{2,6},{3,7},{4,0},{5,1},{6,2},{7,3},{8,12},{9,13},{10,... | collective-permute-start | bytes 3538952 | tf_op jit(solution)/shard_map/ppermute | solution.py:63
  234.3 76.8 %collective-permute-start.42 = (bf16[384,1536]{1,0:T(8,128)(2,1)}, bf16[384,1536]{1,0:T(8,128)(2,1)S(1)}, u32[]{:S(2)}, u32[]{:S(2)}) collective-permute-start(bf16[384,1536]{1,0:T(8,128)(2,1)} %collective-permute-done.41.refs_14_), channel_id=1, source_target_pairs={{0,4},{1,5},{2,6},{3,7},{4,0},{5,1},{6,2},{7,3},{8,12},{9,13},{10,... | collective-permute-start | bytes 3538952 | tf_op jit(solution)/shard_map/ppermute | solution.py:63
  235.8 75.3 %collective-permute-start.31 = (bf16[256,1536]{1,0:T(8,128)(2,1)}, bf16[256,1536]{1,0:T(8,128)(2,1)S(1)}, u32[]{:S(2)}, u32[]{:S(2)}) collective-permute-start(bf16[256,1536]{1,0:T(8,128)(2,1)} %get-tuple-element.43.refs_0_), channel_id=1, source_target_pairs={{0,1},{1,0},{2,3},{3,2},{4,5},{5,4},{6,7},{7,6},{8,9},{9,8},{10,11... | collective-permute-start | bytes 2359304 | tf_op jit(solution)/shard_map/ppermute | solution.py:59
  250.9 61.2 %collective-permute-start.32 = (bf16[256,1536]{1,0:T(8,128)(2,1)S(1)}, bf16[256,1536]{1,0:T(8,128)(2,1)}, u32[]{:S(2)}, u32[]{:S(2)}) collective-permute-start(bf16[256,1536]{1,0:T(8,128)(2,1)S(1)} %collective-permute-done.30.refs_1_), channel_id=1, source_target_pairs={{0,1},{1,0},{2,3},{3,2},{4,5},{5,4},{6,7},{7,6},{8,9},{9,8},{10,11... | collective-permute-start | bytes 2359304 | tf_op jit(solution)/shard_map/ppermute | solution.py:59
  354.0 30.8 %collective-permute-start.71 = (bf16[384,1536]{1,0:T(8,128)(2,1)}, bf16[384,1536]{1,0:T(8,128)(2,1)}, u32[]{:S(2)}, u32[]{:S(2)}) collective-permute-start(bf16[384,1536]{1,0:T(8,128)(2,1)} %get-tuple-element.70), channel_id=1, source_target_pairs={{0,4},{1,5},{2,6},{3,7},{4,0},{5,1},{6,2},{7,3},{8,12},{9,13},{10,... | collective-permute-start | bytes 3538952 | tf_op jit(solution)/shard_map/ppermute | solution.py:63
  358.2 29.2 %collective-permute-start.45 = (bf16[512,1536]{1,0:T(8,128)(2,1)}, bf16[512,1536]{1,0:T(8,128)(2,1)}, u32[]{:S(2)}, u32[]{:S(2)}) collective-permute-start(bf16[512,1536]{1,0:T(8,128)(2,1)} %slice.72), channel_id=1, source_target_pairs={{0,1},{1,0},{2,3},{3,2},{4,5},{5,4},{6,7},{7,6},{8,9},{9,8},{10,11... | collective-permute-start | bytes 4718600 | tf_op jit(solution)/shard_map/ppermute | solution.py:59
  359.5 30.5 %collective-permute-start.43 = (bf16[512,1536]{1,0:T(8,128)(2,1)}, bf16[512,1536]{1,0:T(8,128)(2,1)S(1)}, u32[]{:S(2)}, u32[]{:S(2)}) collective-permute-start(bf16[512,1536]{1,0:T(8,128)(2,1)} %slice.68), channel_id=1, source_target_pairs={{0,1},{1,0},{2,3},{3,2},{4,5},{5,4},{6,7},{7,6},{8,9},{9,8},{10,11... | collective-permute-start | bytes 4718600 | tf_op jit(solution)/shard_map/ppermute | solution.py:59
  367.6 41.0 %collective-permute-start.70 = (bf16[384,1536]{1,0:T(8,128)(2,1)}, bf16[384,1536]{1,0:T(8,128)(2,1)}, u32[]{:S(2)}, u32[]{:S(2)}) collective-permute-start(bf16[384,1536]{1,0:T(8,128)(2,1)} %get-tuple-element.68), channel_id=1, source_target_pairs={{0,4},{1,5},{2,6},{3,7},{4,0},{5,1},{6,2},{7,3},{8,12},{9,13},{10,... | collective-permute-start | bytes 3538952 | tf_op jit(solution)/shard_map/ppermute | solution.py:63
  376.0 109.5 %collective-permute-start.69 = (bf16[384,1536]{1,0:T(8,128)(2,1)}, bf16[384,1536]{1,0:T(8,128)(2,1)}, u32[]{:S(2)}, u32[]{:S(2)}) collective-permute-start(bf16[384,1536]{1,0:T(8,128)(2,1)} %get-tuple-element.66), channel_id=1, source_target_pairs={{0,4},{1,5},{2,6},{3,7},{4,0},{5,1},{6,2},{7,3},{8,12},{9,13},{10,... | collective-permute-start | bytes 3538952 | tf_op jit(solution)/shard_map/ppermute | solution.py:63
  384.9 123.5 %collective-permute-start.68 = (bf16[384,1536]{1,0:T(8,128)(2,1)}, bf16[384,1536]{1,0:T(8,128)(2,1)}, u32[]{:S(2)}, u32[]{:S(2)}) collective-permute-start(bf16[384,1536]{1,0:T(8,128)(2,1)} %get-tuple-element.64), channel_id=1, source_target_pairs={{0,4},{1,5},{2,6},{3,7},{4,0},{5,1},{6,2},{7,3},{8,12},{9,13},{10,... | collective-permute-start | bytes 3538952 | tf_op jit(solution)/shard_map/ppermute | solution.py:63
  387.4 29.1 %collective-permute-start.72 = (bf16[384,1536]{1,0:T(8,128)(2,1)S(1)}, bf16[384,1536]{1,0:T(8,128)(2,1)S(1)}, u32[]{:S(2)}, u32[]{:S(2)}) collective-permute-start(bf16[384,1536]{1,0:T(8,128)(2,1)S(1)} %add_convert_fusion.2), channel_id=1, source_target_pairs={{0,8},{8,16},{16,24},{24,0},{1,9},{9,17},{17,25},{25,1},{2,10},{10... | collective-permute-start | bytes 3538952 | tf_op jit(solution)/shard_map/ppermute | solution.py:66
  391.1 28.4 %collective-permute-start.46 = (bf16[256,1536]{1,0:T(8,128)(2,1)S(1)}, bf16[256,1536]{1,0:T(8,128)(2,1)S(1)}, u32[]{:S(2)}, u32[]{:S(2)}) collective-permute-start(bf16[256,1536]{1,0:T(8,128)(2,1)S(1)} %slice.106), channel_id=1, source_target_pairs={{0,2},{1,3},{2,0},{3,1},{4,6},{5,7},{6,4},{7,5},{8,10},{9,11},{10,... | collective-permute-start | bytes 2359304 | tf_op jit(solution)/shard_map/ppermute | solution.py:61
  408.5 88.2 %collective-permute-start.44 = (bf16[256,1536]{1,0:T(8,128)(2,1)}, bf16[256,1536]{1,0:T(8,128)(2,1)S(1)}, u32[]{:S(2)}, u32[]{:S(2)}) collective-permute-start(bf16[256,1536]{1,0:T(8,128)(2,1)} %slice.107), channel_id=1, source_target_pairs={{0,2},{1,3},{2,0},{3,1},{4,6},{5,7},{6,4},{7,5},{8,10},{9,11},{10,... | collective-permute-start | bytes 2359304 | tf_op jit(solution)/shard_map/ppermute | solution.py:61
  419.4 67.5 %collective-permute-start.73 = (bf16[384,1536]{1,0:T(8,128)(2,1)}, bf16[384,1536]{1,0:T(8,128)(2,1)}, u32[]{:S(2)}, u32[]{:S(2)}) collective-permute-start(bf16[384,1536]{1,0:T(8,128)(2,1)} %add_convert_fusion.1), channel_id=1, source_target_pairs={{0,8},{8,16},{16,24},{24,0},{1,9},{9,17},{17,25},{25,1},{2,10},{10... | collective-permute-start | bytes 3538952 | tf_op jit(solution)/shard_map/ppermute | solution.py:66
  484.0 55.0 %collective-permute-start.50 = (bf16[4,2,2,48,1536]{4,3,0,2,1:T(8,128)(2,1)S(1)}, bf16[4,2,2,48,1536]{4,3,0,2,1:T(8,128)(2,1)}, u32[]{:S(2)}, u32[]{:S(2)}) collective-permute-start(bf16[4,2,2,48,1536]{4,3,0,2,1:T(8,128)(2,1)S(1)} %fusion.1), channel_id=1, source_target_pairs={{0,1},{1,0},{2,3},{3,2},{4,5},{5,4},{6,7},{7,6},{8,9},{9,8},{10,11... | collective-permute-start | bytes 7077896 | tf_op jit(solution)/shard_map/ppermute | solution.py:59
  489.1 46.5 %collective-permute-start.74 = (bf16[384,1536]{1,0:T(8,128)(2,1)S(1)}, bf16[384,1536]{1,0:T(8,128)(2,1)S(1)}, u32[]{:S(2)}, u32[]{:S(2)}) collective-permute-start(bf16[384,1536]{1,0:T(8,128)(2,1)S(1)} %add_convert_fusion), channel_id=1, source_target_pairs={{0,8},{8,16},{16,24},{24,0},{1,9},{9,17},{17,25},{25,1},{2,10},{10... | collective-permute-start | bytes 3538952 | tf_op jit(solution)/shard_map/ppermute | solution.py:66
  496.7 47.9 %collective-permute-start.56 = (bf16[4,2,2,48,1536]{4,3,0,1,2:T(8,128)(2,1)}, bf16[4,2,2,48,1536]{4,3,0,1,2:T(8,128)(2,1)}, u32[]{:S(2)}, u32[]{:S(2)}) collective-permute-start(bf16[4,2,2,48,1536]{4,3,0,1,2:T(8,128)(2,1)} %fusion.2), channel_id=1, source_target_pairs={{0,1},{1,0},{2,3},{3,2},{4,5},{5,4},{6,7},{7,6},{8,9},{9,8},{10,11... | collective-permute-start | bytes 7077896 | tf_op jit(solution)/shard_map/ppermute | solution.py:59
  508.1 49.3 %collective-permute-start.62 = (bf16[4,2,2,48,1664]{4,3,0,1,2:T(8,128)(2,1)}, bf16[4,2,2,48,1664]{4,3,0,1,2:T(8,128)(2,1)S(1)}, u32[]{:S(2)}, u32[]{:S(2)}) collective-permute-start(bf16[4,2,2,48,1664]{4,3,0,1,2:T(8,128)(2,1)} %fusion), channel_id=1, source_target_pairs={{0,1},{1,0},{2,3},{3,2},{4,5},{5,4},{6,7},{7,6},{8,9},{9,8},{10,11... | collective-permute-start | bytes 7667720 | tf_op jit(solution)/shard_map/ppermute | solution.py:59
  508.4 43.8 %collective-permute-start.49 = (bf16[1536,256]{1,0:T(8,128)(2,1)S(1)}, bf16[1536,256]{1,0:T(8,128)(2,1)S(1)}, u32[]{:S(2)}, u32[]{:S(2)}) collective-permute-start(bf16[1536,256]{1,0:T(8,128)(2,1)S(1)} %fusion.6), channel_id=1, source_target_pairs={{8,0},{16,8},{24,16},{9,1},{17,9},{25,17},{10,2},{18,10},{26,18},{... | collective-permute-start | bytes 2359304 | tf_op jit(solution)/shard_map/ppermute | solution.py:72
  543.4 27.8 %collective-permute-start.51 = (bf16[4,2,48,1536]{3,2,0,1:T(8,128)(2,1)}, bf16[4,2,48,1536]{3,2,0,1:T(8,128)(2,1)}, u32[]{:S(2)}, u32[]{:S(2)}) collective-permute-start(bf16[4,2,48,1536]{3,2,0,1:T(8,128)(2,1)} %fusion.8), channel_id=1, source_target_pairs={{0,4},{1,5},{2,6},{3,7},{4,0},{5,1},{6,2},{7,3},{8,12},{9,13},{10,... | collective-permute-start | bytes 3538952 | tf_op jit(solution)/shard_map/ppermute | solution.py:63
  550.4 29.2 %collective-permute-start.57 = (bf16[4,2,48,1536]{3,2,0,1:T(8,128)(2,1)}, bf16[4,2,48,1536]{3,2,0,1:T(8,128)(2,1)}, u32[]{:S(2)}, u32[]{:S(2)}) collective-permute-start(bf16[4,2,48,1536]{3,2,0,1:T(8,128)(2,1)} %fusion.9), channel_id=1, source_target_pairs={{0,2},{1,3},{2,0},{3,1},{4,6},{5,7},{6,4},{7,5},{8,10},{9,11},{10,... | collective-permute-start | bytes 3538952 | tf_op jit(solution)/shard_map/ppermute | solution.py:61
  560.6 46.3 %collective-permute-start.63 = (bf16[4,2,48,1664]{3,2,0,1:T(8,128)(2,1)S(1)}, bf16[4,2,48,1664]{3,2,0,1:T(8,128)(2,1)S(1)}, u32[]{:S(2)}, u32[]{:S(2)}) collective-permute-start(bf16[4,2,48,1664]{3,2,0,1:T(8,128)(2,1)S(1)} %fusion.7), channel_id=1, source_target_pairs={{0,2},{1,3},{2,0},{3,1},{4,6},{5,7},{6,4},{7,5},{8,10},{9,11},{10,... | collective-permute-start | bytes 3833864 | tf_op jit(solution)/shard_map/ppermute | solution.py:61
  573.7 44.5 %collective-permute-start.52 = (bf16[4,48,1536]{2,1,0:T(8,128)(2,1)S(1)}, bf16[4,48,1536]{2,1,0:T(8,128)(2,1)S(1)}, u32[]{:S(2)}, u32[]{:S(2)}) collective-permute-start(bf16[4,48,1536]{2,1,0:T(8,128)(2,1)S(1)} %fusion.12), channel_id=1, source_target_pairs={{0,2},{1,3},{2,0},{3,1},{4,6},{5,7},{6,4},{7,5},{8,10},{9,11},{10,... | collective-permute-start | bytes 1769480 | tf_op jit(solution)/shard_map/ppermute | solution.py:61
  581.3 37.1 %collective-permute-start.58 = (bf16[4,48,1536]{2,1,0:T(8,128)(2,1)S(1)}, bf16[4,48,1536]{2,1,0:T(8,128)(2,1)S(1)}, u32[]{:S(2)}, u32[]{:S(2)}) collective-permute-start(bf16[4,48,1536]{2,1,0:T(8,128)(2,1)S(1)} %fusion.13), channel_id=1, source_target_pairs={{0,4},{1,5},{2,6},{3,7},{4,0},{5,1},{6,2},{7,3},{8,12},{9,13},{10,... | collective-permute-start | bytes 1769480 | tf_op jit(solution)/shard_map/ppermute | solution.py:63
  607.2 29.6 %collective-permute-start.64 = (bf16[4,48,1664]{2,1,0:T(8,128)(2,1)S(1)}, bf16[4,48,1664]{2,1,0:T(8,128)(2,1)S(1)}, u32[]{:S(2)}, u32[]{:S(2)}) collective-permute-start(bf16[4,48,1664]{2,1,0:T(8,128)(2,1)S(1)} %fusion.11), channel_id=1, source_target_pairs={{0,4},{1,5},{2,6},{3,7},{4,0},{5,1},{6,2},{7,3},{8,12},{9,13},{10,... | collective-permute-start | bytes 1916936 | tf_op jit(solution)/shard_map/ppermute | solution.py:63
  (65 other events, 944.7 us)

commit v3 on v2

v3 whole, which is shorter than its diff:
```python
import functools

import jax
import jax.numpy as jnp
from jax import lax
from jax.experimental import pallas as pl
from jax.experimental.pallas import tpu as pltpu
from jax.sharding import PartitionSpec as P

HEADS = 16
KV_HEADS = 8
HEAD = 96
GROUP = HEADS // KV_HEADS

EPS = 1e-05
THETA = 100000.0
NEG = -1e30
BF = jnp.bfloat16
F32 = jnp.float32


def inverse_rms(values):
    return lax.rsqrt(jnp.mean(values * values, axis=-1, keepdims=True) + EPS)


def angle_tables(places):
    offsets = jnp.arange(0, HEAD, 2, dtype=F32)
    angles = (THETA ** (-offsets / HEAD))[:, None] * places.astype(F32)[None, :]
    return (jnp.cos(angles), jnp.sin(angles))


def mm(left, right):
    return jnp.dot(left, right, preferred_element_type=F32)


def mm_t(left, right):
    return lax.dot_general(left, right, (((1,), (1,)), ((), ())), preferred_element_type=F32)


def t_mm(left, right):
    return lax.dot_general(left, right, (((0,), (0,)), ((), ())), preferred_element_type=F32)


def in_f32(value):
    return value.astype(F32)


def after(value, *others):
    return lax.optimization_barrier((value, *others))[0]


class Moves:
    def __init__(self):
        self.Z = lax.axis_size("seq")
        self.DP = lax.axis_size("dp")
        self.Q = self.DP // 4
        self.zi = lax.axis_index("seq")
        place = lax.axis_index("dp")
        self.qi = place // 4
        self.xi = (place // 2) % 2
        self.ci = place % 2

    def step(self, offset, value):
        if offset == "c":
            return lax.ppermute(value, "dp", [(n, n ^ 1) for n in range(self.DP)])
        j, i = offset
        return lax.ppermute(
            value, "dp", [(n, (n % 4) ^ (2 * i) | 4 * ((n // 4 + j) % self.Q)) for n in range(self.DP)]
        )


VMEM = pl.BlockSpec(memory_space=pltpu.VMEM)
ANY = pl.BlockSpec(memory_space=pl.ANY)
SMEM = pl.BlockSpec(memory_space=pltpu.SMEM)
SCALE = HEAD ** (-0.5)
HALF = HEAD // 2
QUERY = HEADS * HEAD
PAIR = 2 * KV_HEADS * HEAD


def kernel_call(body, out_shape, in_specs, out_specs, scratch, flops, moved, args):
    return pl.pallas_call(
        body,
        out_shape=out_shape,
        in_specs=in_specs,
        out_specs=out_specs,
        scratch_shapes=scratch,
        compiler_params=pltpu.CompilerParams(vmem_limit_bytes=60 << 20),
        cost_estimate=pl.CostEstimate(flops=flops, bytes_accessed=moved, transcendentals=0),
    )(*args)


def load_rows(meta, places, lines, refs, target, sems, columns):
    copies = []
    if len(refs) == 1:
        copies.append(pltpu.make_async_copy(refs[0].at[:, columns], target, sems.at[0]))
    else:
        qi, xi, ci = meta[1], meta[2], meta[3]
        for ref, (j, i, l, first) in zip(refs, places):
            blocks, share, _ = ref.shape
            q = lax.rem(qi + (lines - j), lines)
            x = lax.rem(xi + i, 2)
            c = lax.rem(ci + l, 2)
            for k in range(blocks):
                row = pl.multiple_of(((((first + k) * lines + q) * 2 + x) * 2 + c) * share, share)
                copies.append(
                    pltpu.make_async_copy(
                        ref.at[k, :, columns], target.at[pl.ds(row, share), :], sems.at[len(copies)]
                    )
                )
    for copy in copies:
        copy.start()
    return copies


def arrays_of(pieces):
    return [piece[0] for piece in pieces]


def places_of(pieces):
    return tuple(piece[1:] for piece in pieces)


def copies_of(pieces):
    count = 1 if len(pieces) == 1 else sum(piece[0].shape[0] for piece in pieces)
    return pltpu.SemaphoreType.DMA((count,))


def store_rows(meta, split, block, first, send, keep, columns):
    if not split:
        keep[pl.ds(first, block.shape[0]), columns] = block.astype(keep.dtype)
        return
    lines, share = keep.shape[0] // 2, keep.shape[2]
    qi, xi, ci = meta[1], meta[2], meta[3]
    for n in range(block.shape[0] // (2 * share)):
        chip = first // (2 * share) + n
        z, q, x = chip // (2 * lines), chip // 2 % lines, chip % 2
        j = lax.rem(qi + (lines - q), lines)
        i = lax.rem(xi + x, 2)
        even = block[2 * n * share : (2 * n + 1) * share]
        odd = block[(2 * n + 1) * share : (2 * n + 2) * share]
        keep[2 * j + i, z, :, columns] = jnp.where(ci == 0, even, odd).astype(keep.dtype)
        send[2 * j + i, z, :, columns] = jnp.where(ci == 0, odd, even).astype(send.dtype)


def sums_shapes(split, parts, rows, width):
    if not split:
        return (jax.ShapeDtypeStruct((8, 128), BF), jax.ShapeDtypeStruct((rows, width), BF))
    shape = (parts[1] * 2, parts[0], rows // (parts[0] * parts[1] * 4), width)
    return (jax.ShapeDtypeStruct(shape, BF), jax.ShapeDtypeStruct(shape, BF))


def turned_store(ref, row, lanes, block, cosine, sine):
    upper, lower = block[:HALF], block[HALF:]
    ref[pl.ds(row, HALF), lanes] = (upper * cosine - lower * sine).astype(ref.dtype)
    ref[pl.ds(row + HALF, HALF), lanes] = (lower * cosine + upper * sine).astype(ref.dtype)


def head_scores(queries, keys, place, wide):
    scores = mm(keys, queries) * SCALE
    rows = scores.shape[1] // GROUP
    key_place = lax.broadcasted_iota(jnp.int32, scores.shape, 0)
    query_place = place * rows + lax.rem(lax.broadcasted_iota(jnp.int32, scores.shape, 1), rows)
    return jnp.where(key_place <= query_place, scores, NEG)


def group_of(ref, g, lanes):
    return jnp.concatenate(
        [ref[pl.ds(pl.multiple_of((g * GROUP + j) * HEAD, 16), HEAD), lanes] for j in range(GROUP)],
        axis=1,
    )


def flip(value):
    return value.astype(F32).T.astype(value.dtype)


def project_forward_body(seqs, wide, places, lines, meta, tokens, cosine, sine, *refs):
    count = len(places)
    pieces, refs = refs[:count], refs[count:]
    (
        query_t, pair_t, normed_t, gains,
        pair_v, query_v, normed, own, pair_sems, query_sems,
    ) = refs
    place = meta[0]
    rows = own.shape[0] // seqs
    pair_width = KV_HEADS * HEAD
    pair_copies = load_rows(meta, places, lines, pieces, pair_v, pair_sems, pl.ds(0, PAIR + 128))
    query_copies = load_rows(meta, places, lines, pieces, query_v, query_sems, pl.ds(PAIR + 128, QUERY))
    for copy in pair_copies:
        copy.wait()
    gains[...] = pair_v[:, PAIR:].astype(F32).T[:8]
    gain = gains[0:1]
    step = 256
    for b in range(seqs * wide // step):
        cut = slice(b * step, (b + 1) * step)
        values = tokens[cut, : normed.shape[1]].astype(F32)
        block = (values * inverse_rms(values) * gain).astype(BF)
        normed[cut, :] = block
        normed_t[:, cut] = flip(block)
    for s in range(seqs):
        own[s * rows : (s + 1) * rows, :] = normed[
            pl.ds(pl.multiple_of(s * wide + place * rows, 128), rows), :
        ]
    width = 4 * HEAD
    for n in range(2 * pair_width // width):
        for s in range(seqs):
            lanes = slice(s * wide, (s + 1) * wide)
            block = mm(normed[lanes, :], pair_v[:, n * width : (n + 1) * width]).T
            if (n + 1) * width <= pair_width:
                for h in range(4):
                    turned_store(
                        pair_t, n * width + h * HEAD, lanes, block[h * HEAD : (h + 1) * HEAD],
                        cosine[:, lanes], sine[:, lanes],
                    )
            else:
                pair_t[n * width : (n + 1) * width, lanes] = block.astype(BF)
    for copy in query_copies:
        copy.wait()
    for n in range(HEADS * HEAD // width):
        block = mm(own[...], query_v[:, n * width : (n + 1) * width]).T
        for s in range(seqs):
            lanes = slice(s * rows, (s + 1) * rows)
            here = pl.ds(pl.multiple_of(s * wide + place * rows, 128), rows)
            for h in range(4):
                turned_store(
                    query_t, n * width + h * HEAD, lanes, block[h * HEAD : (h + 1) * HEAD, lanes],
                    cosine[:, here], sine[:, here],
                )


def attend_forward_body(seqs, wide, meta, query_t, pair_t, mixed, mixed_t, logs):
    place = meta[0]
    rows = query_t.shape[1] // seqs
    pair_width = KV_HEADS * HEAD

    def one(g, _):
        row = pl.multiple_of(g * HEAD, 16)
        for s in range(seqs):
            lanes = slice(s * wide, (s + 1) * wide)
            mine = slice(s * rows, (s + 1) * rows)
            scores = head_scores(
                group_of(query_t, g, mine), flip(pair_t[pl.ds(row, HEAD), lanes]), place, wide
            )
            top = jnp.max(scores, axis=0, keepdims=True)
            weights = jnp.exp(scores - top)
            total = jnp.sum(weights, axis=0, keepdims=True)
            probs = (weights * (1.0 / total)).astype(BF)
            out = mm(pair_t[pl.ds(row + pair_width, HEAD), lanes], probs).astype(BF)
            for j in range(GROUP):
                mixed_t[pl.ds(pl.multiple_of((g * GROUP + j) * HEAD, 16), HEAD), mine] = out[
                    :, j * rows : (j + 1) * rows
                ]
            logs[g, s] = top + jnp.log(total)
        return 0

    lax.fori_loop(0, KV_HEADS, one, 0)
    mixed[...] = flip(mixed_t[...])


def project_forward(meta, tokens, cosine, sine, pieces, lines, width, seqs, rows):
    count = tokens.shape[0]
    wide = count // seqs
    own = seqs * rows
    sds = jax.ShapeDtypeStruct
    return kernel_call(
        functools.partial(project_forward_body, seqs, wide, places_of(pieces), lines),
        (sds((QUERY, own), BF), sds((PAIR, count), BF), sds((width, count), BF), sds((8, width), F32)),
        [SMEM, VMEM, VMEM, VMEM] + [ANY] * len(pieces),
        (VMEM,) * 4,
        [
            pltpu.VMEM((width, PAIR + 128), BF), pltpu.VMEM((width, QUERY), BF),
            pltpu.VMEM((count, width), BF), pltpu.VMEM((own, width), BF), copies_of(pieces), copies_of(pieces),
        ],
        2 * count * width * PAIR + 2 * own * width * QUERY,
        20 << 20,
        (meta, tokens, cosine, sine, *arrays_of(pieces)),
    )


def attend_forward(meta, query_t, pair_t, seqs):
    own = query_t.shape[1]
    wide = pair_t.shape[1] // seqs
    sds = jax.ShapeDtypeStruct
    return kernel_call(
        functools.partial(attend_forward_body, seqs, wide),
        (
            sds((own, QUERY), BF), sds((QUERY, own), BF),
            sds((KV_HEADS, seqs, 1, GROUP * own // seqs), F32),
        ),
        [SMEM, VMEM, VMEM],
        (VMEM,) * 3,
        [],
        4 * own * wide * QUERY,
        6 << 20,
        (meta, query_t, pair_t),
    )


def attend_backward_body(
    seqs, wide, meta, query_t, pair_t, grad_t, logs, cosine, sine, query_back, pair_back
):
    place = meta[0]
    rows = query_t.shape[1] // seqs
    pair_width = KV_HEADS * HEAD

    def one(g, _):
        row = pl.multiple_of(g * HEAD, 16)
        for s in range(seqs):
            lanes = slice(s * wide, (s + 1) * wide)
            mine = slice(s * rows, (s + 1) * rows)
            here = pl.ds(pl.multiple_of(s * wide + place * rows, 128), rows)
            queries = group_of(query_t, g, mine)
            grads = group_of(grad_t, g, mine)
            keys_t = pair_t[pl.ds(row, HEAD), lanes]
            values_t = pair_t[pl.ds(row + pair_width, HEAD), lanes]
            probs = jnp.exp(head_scores(queries, flip(keys_t), place, wide) - logs[g, s])
            prob_grad = mm(flip(values_t), grads)
            centre = jnp.sum(probs * prob_grad, axis=0, keepdims=True)
            score_grad = (probs * (prob_grad - centre)).astype(BF)
            query_grad = mm(keys_t, score_grad) * SCALE
            for j in range(GROUP):
                turned_store(
                    query_back, pl.multiple_of((g * GROUP + j) * HEAD, 16), mine,
                    query_grad[:, j * rows : (j + 1) * rows], cosine[:, here], -sine[:, here],
                )
            turned_store(
                pair_back, row, lanes, mm_t(queries, score_grad) * SCALE,
                cosine[:, lanes], -sine[:, lanes],
            )
            pair_back[pl.ds(row + pair_width, HEAD), lanes] = mm_t(
                grads, probs.astype(BF)
            ).astype(BF)
        return 0

    lax.fori_loop(0, KV_HEADS, one, 0)


def attend_backward(meta, query_t, pair_t, grad_t, logs, cosine, sine, seqs):
    wide = pair_t.shape[1] // seqs
    return kernel_call(
        functools.partial(attend_backward_body, seqs, wide),
        (jax.ShapeDtypeStruct(query_t.shape, BF), jax.ShapeDtypeStruct(pair_t.shape, BF)),
        [SMEM] + [VMEM] * 6,
        (VMEM, VMEM),
        [],
        10 * query_t.size * wide,
        12 << 20,
        (meta, query_t, pair_t, grad_t, logs, cosine, sine),
    )


def output_body(places, lines, meta, tokens, mixed, gain, *refs):
    pieces, (total, second, weights_v, sems) = refs[:-4], refs[-4:]
    for copy in load_rows(meta, places, lines, pieces, weights_v, sems, pl.ds(PAIR + 128 + QUERY, weights_v.shape[1])):
        copy.wait()
    value = tokens[...].astype(F32) + mm(mixed[...], weights_v[...])
    total[...] = value
    second[...] = (value * inverse_rms(value) * gain[1:2]).astype(BF)


def output_forward(meta, tokens, mixed, gain, pieces, lines):
    return kernel_call(
        functools.partial(output_body, places_of(pieces), lines),
        (jax.ShapeDtypeStruct(tokens.shape, F32), jax.ShapeDtypeStruct(tokens.shape, BF)),
        [SMEM, VMEM, VMEM, VMEM] + [ANY] * len(pieces),
        (VMEM, VMEM),
        [pltpu.VMEM((QUERY, tokens.shape[1]), BF), copies_of(pieces)],
        2 * tokens.size * QUERY,
        10 << 20,
        (meta, tokens, mixed, gain, *arrays_of(pieces)),
    )


def output_back_body(places, lines, split, meta, grad, total, second_grad, gain, mixed_t, *refs):
    pieces, (first_grad, mixed_grad_t, send, keep, weights_v, da, sems) = refs[:-7], refs[-7:]
    copies = load_rows(meta, places, lines, pieces, weights_v, sems, pl.ds(PAIR + 128 + QUERY, weights_v.shape[1]))
    value = total[...]
    inverse = inverse_rms(value)
    back = second_grad[...]
    scaled = back * gain[1:2]
    first = (
        grad[...].astype(F32)
        + inverse * scaled
        - value * inverse**3 * jnp.mean(scaled * value, axis=-1, keepdims=True)
    )
    first_grad[...] = first
    da[...] = first.astype(BF)
    width = value.shape[1]
    gain_part = jnp.broadcast_to(
        jnp.sum((back * value * inverse).T, axis=1, keepdims=True), (width, 128)
    )
    store_rows(meta, split, gain_part, 0, send, keep, pl.ds(width, 128))
    step = 384
    for n in range(width // step):
        cut = slice(n * step, (n + 1) * step)
        store_rows(meta, split, mm(mixed_t[cut, :], da[...]), n * step, send, keep, pl.ds(0, width))
    for copy in copies:
        copy.wait()
    for n in range(width // step):
        cut = slice(n * step, (n + 1) * step)
        mixed_grad_t[cut, :] = mm_t(weights_v[cut, :], da[...]).astype(BF)


def output_backward(meta, grad, total, second_grad, gain, mixed_t, pieces, parts, split):
    own, width = grad.shape
    return kernel_call(
        functools.partial(output_back_body, places_of(pieces), parts[1], split),
        (
            jax.ShapeDtypeStruct((own, width), F32),
            jax.ShapeDtypeStruct(mixed_t.shape, BF),
            *sums_shapes(split, parts, QUERY, width + 128),
        ),
        [SMEM] + [VMEM] * 5 + [ANY] * len(pieces),
        (VMEM,) * 4,
        [pltpu.VMEM((QUERY, width), BF), pltpu.VMEM((own, width), BF), copies_of(pieces)],
        4 * own * width * QUERY,
        22 << 20,
        (meta, grad, total, second_grad, gain, mixed_t, *arrays_of(pieces)),
    )


def ffn_body(count, *refs):
    second, grads, shards = refs[:count], refs[count : 2 * count], refs[2 * count]
    out_a, out_b, back_a, back_b, hidden_t, gate_t, up_t = refs[2 * count + 1 : 2 * count + 8]
    second_v, grads_v, weights, hidden, gate_g, up_g, sems = refs[2 * count + 8 :]
    rows = second[0].shape[0]
    blocks, units = shards.shape[0], shards.shape[1] // 3
    copies = [
        pltpu.make_async_copy(
            shards.at[b, pl.ds(p * units, units)], weights.at[p, pl.ds(b * units, units)], sems.at[p, b]
        )
        for b in range(blocks)
        for p in range(3)
    ]
    for i in range(count):
        cut = pl.ds(i * rows, rows)
        copies.append(pltpu.make_async_copy(second[i], second_v.at[cut], sems.at[3, i]))
        copies.append(pltpu.make_async_copy(grads[i], grads_v.at[cut], sems.at[4, i]))
    for copy in copies:
        copy.start()
    for copy in copies:
        copy.wait()
    step = 256
    total = blocks * units
    for n in range(total // step):
        cut = slice(n * step, (n + 1) * step)
        gate_w, up_w, down_w = weights[0, cut], weights[1, cut], weights[2, cut]

        def one(m, _):
            here = pl.ds(pl.multiple_of(m * step, step), step)
            gate = mm_t(second_v[here, :], gate_w)
            up = mm_t(second_v[here, :], up_w)
            hidden_grad = mm_t(grads_v[here, :], down_w)
            sigma = jax.nn.sigmoid(gate)
            mixed = gate * sigma * up
            hidden[here, cut] = mixed.astype(BF)
            hidden_t[cut, here] = mixed.T.astype(BF)
            gate_grad = hidden_grad * up * sigma * (1.0 + gate * (1.0 - sigma))
            gate_g[here, cut] = gate_grad.astype(BF)
            gate_t[cut, here] = gate_grad.T.astype(BF)
            up_grad = hidden_grad * (gate * sigma)
            up_g[here, cut] = up_grad.astype(BF)
            up_t[cut, here] = up_grad.T.astype(BF)
            return 0

        lax.fori_loop(0, count * rows // step, one, 0)

    half = count * rows // 2
    for first, out, back in ((0, out_a, back_a), (half, out_b, back_b)):

        def two(m, _):
            to = pl.ds(pl.multiple_of(m * step, step), step)
            here = pl.ds(pl.multiple_of(first + m * step, step), step)
            back[to, :] = (mm(gate_g[here, :], weights[0]) + mm(up_g[here, :], weights[1])).astype(back.dtype)
            out[to, :] = mm(hidden[here, :], weights[2]).astype(out.dtype)
            return 0

        lax.fori_loop(0, half // step, two, 0)


def ffn(tokens_of, weights):
    pieces = len(tokens_of) // 2
    rows, width = tokens_of[0].shape
    count, total = pieces * rows, weights.shape[0] * weights.shape[1] // 3
    sds = jax.ShapeDtypeStruct
    return kernel_call(
        functools.partial(ffn_body, pieces),
        (sds((count // 2, width), BF),) * 4 + (sds((total, count), BF),) * 3,
        [ANY] * (2 * pieces + 1),
        (VMEM,) * 7,
        [
            pltpu.VMEM((count, width), BF), pltpu.VMEM((count, width), BF),
            pltpu.VMEM((3, total, width), BF),
            pltpu.VMEM((count, total), BF), pltpu.VMEM((count, total), BF), pltpu.VMEM((count, total), BF),
            pltpu.SemaphoreType.DMA((5, max(weights.shape[0], pieces))),
        ],
        12 * count * total * width,
        34 << 20,
        (*tokens_of, weights),
    )


def ffn_sums_body(count, units, *refs):
    tokens_of, lefts, out = refs[: 2 * count], refs[2 * count : 2 * count + 3], refs[2 * count + 3]
    second_v, grads_v, sems = refs[2 * count + 4 :]
    rows = tokens_of[0].shape[0]
    copies = []
    for i in range(count):
        cut = pl.ds(i * rows, rows)
        copies.append(pltpu.make_async_copy(tokens_of[i], second_v.at[cut], sems.at[0, i]))
        copies.append(pltpu.make_async_copy(tokens_of[count + i], grads_v.at[cut], sems.at[1, i]))
    for copy in copies:
        copy.start()
    for copy in copies:
        copy.wait()
    for p, right in ((0, second_v), (1, second_v), (2, grads_v)):

        def one(b, _):
            here = pl.ds(pl.multiple_of(b * units, units), units)
            out[b, p * units : (p + 1) * units, :] = mm(lefts[p][here, :], right[...]).astype(BF)
            return 0

        lax.fori_loop(0, out.shape[0], one, 0)


def ffn_sums(hidden_t, gate_t, up_t, tokens_of, units):
    pieces = len(tokens_of) // 2
    rows, width = tokens_of[0].shape
    total = hidden_t.shape[0]
    return kernel_call(
        functools.partial(ffn_sums_body, pieces, units),
        jax.ShapeDtypeStruct((total // units, 3 * units, width), BF),
        [ANY] * (2 * pieces) + [VMEM] * 3,
        VMEM,
        [
            pltpu.VMEM((pieces * rows, width), BF), pltpu.VMEM((pieces * rows, width), BF),
            pltpu.SemaphoreType.DMA((2, pieces)),
        ],
        6 * total * pieces * rows * width,
        22 << 20,
        (*tokens_of, gate_t, up_t, hidden_t),
    )


def project_sums_body(seqs, split, meta, normed_t, query_back, pair_back, send, keep):
    place = meta[0]
    wide = normed_t.shape[1] // seqs
    rows = query_back.shape[1] // seqs
    step = 384
    for n in range(normed_t.shape[0] // step):
        cut = slice(n * step, (n + 1) * step)
        own = jnp.concatenate(
            [normed_t[cut, pl.ds(pl.multiple_of(s * wide + place * rows, 128), rows)] for s in range(seqs)],
            axis=1,
        )
        store_rows(
            meta, split, mm_t(own, query_back[...]), n * step, send, keep, pl.ds(PAIR, QUERY)
        )
        store_rows(
            meta, split, mm_t(normed_t[cut, :], pair_back[...]), n * step, send, keep, pl.ds(0, PAIR)
        )


def project_sums(meta, normed_t, query_back, pair_back, seqs, parts, split):
    width = normed_t.shape[0]
    return kernel_call(
        functools.partial(project_sums_body, seqs, split),
        sums_shapes(split, parts, width, PAIR + QUERY),
        [SMEM, VMEM, VMEM, VMEM],
        (VMEM,) * 2,
        [],
        2 * width * (query_back.size + pair_back.size),
        26 << 20,
        (meta, normed_t, query_back, pair_back),
    )


def project_back_body(seqs, places, lines, meta, query_back, pair_back, *refs):
    count = len(places)
    pieces, refs = refs[:count], refs[count:]
    query_grad, pair_grad, pair_v, query_v, pair_sems, query_sems = refs
    pair_copies = load_rows(meta, places, lines, pieces, pair_v, pair_sems, pl.ds(0, PAIR))
    query_copies = load_rows(meta, places, lines, pieces, query_v, query_sems, pl.ds(PAIR + 128, QUERY))
    blocks, _, own = pair_grad.shape
    rows = own // seqs
    wide = pair_back.shape[1] // seqs
    step = 512
    for copy in pair_copies:
        copy.wait()
    for n in range(pair_v.shape[0] // step):
        cut = slice(n * step, (n + 1) * step)
        for s in range(seqs):
            part = mm(pair_v[cut, :], pair_back[:, s * wide : (s + 1) * wide])
            for z in range(blocks):
                pair_grad[z, cut, s * rows : (s + 1) * rows] = part[:, z * rows : (z + 1) * rows].astype(BF)
    for copy in query_copies:
        copy.wait()
    for n in range(query_v.shape[0] // step):
        cut = slice(n * step, (n + 1) * step)
        query_grad[cut, :] = mm(query_v[cut, :], query_back[...])


def project_back(meta, query_back, pair_back, pieces, lines, width, seqs, blocks):
    own = query_back.shape[1]
    return kernel_call(
        functools.partial(project_back_body, seqs, places_of(pieces), lines),
        (
            jax.ShapeDtypeStruct((width, own), F32),
            jax.ShapeDtypeStruct((blocks, width, own), BF),
        ),
        [SMEM, VMEM, VMEM] + [ANY] * len(pieces),
        (VMEM, VMEM),
        [pltpu.VMEM((width, PAIR), BF), pltpu.VMEM((width, QUERY), BF), copies_of(pieces), copies_of(pieces)],
        2 * width * (query_back.size + pair_back.size),
        20 << 20,
        (meta, query_back, pair_back, *arrays_of(pieces)),
    )


def input_grad_body(tokens, gain, first_grad, query_grad, pair_grad, out):
    back = (query_grad[...] + pair_grad[...].astype(F32)).T
    value = tokens[...].astype(F32)
    inverse = inverse_rms(value)
    scaled = back * gain[0:1]
    out[...] = (
        first_grad[...]
        + inverse * scaled
        - value * inverse**3 * jnp.mean(scaled * value, axis=-1, keepdims=True)
    ).astype(BF)


def input_grad(tokens, gain, first_grad, query_grad, pair_grad):
    return kernel_call(
        input_grad_body,
        jax.ShapeDtypeStruct(tokens.shape, BF),
        [VMEM] * 5,
        VMEM,
        [],
        tokens.size * 20,
        8 << 20,
        (tokens, gain, first_grad, query_grad, pair_grad),
    )


def per_device(
    tokens,
    positions,
    out_grad,
    w_query,
    w_key,
    w_value,
    w_output,
    gain_attn,
    gain_ffn,
    w_gate,
    w_up,
    w_down,
):
    move = Moves()
    Z, Q, step = move.Z, move.Q, move.step
    seqs, rows, width = tokens.shape
    wide = rows * Z
    own_rows = seqs * rows
    pair_width = KV_HEADS * HEAD
    share, units = w_query.shape[0], w_gate.shape[0]
    split = share % 16 == 0
    meta = jnp.stack([move.zi, move.qi, move.xi, move.ci]).astype(jnp.int32)
    near = [(j, i) for j in range(Q) for i in range(2)]
    grad_out = out_grad.reshape(own_rows, width)
    inputs = tokens.reshape(own_rows, width)

    def over_z(value):
        return lax.all_gather(value, "seq", axis=0, tiled=False)

    def sum_z(value):
        return lax.psum_scatter(value, "seq", scatter_dimension=0, tiled=False)

    gains_in = jnp.pad(jnp.stack([gain_attn, gain_ffn], axis=1), ((0, 0), (0, 126)))
    pack = over_z(jnp.concatenate([w_key, w_value, gains_in, w_query, w_output], axis=1))
    places = jnp.stack([positions // 256, positions % 256], axis=-1).astype(BF)
    carried = jnp.concatenate([tokens, jnp.pad(places, ((0, 0), (0, 0), (0, 126)))], axis=-1)
    tokens_all = over_z(carried).transpose(1, 0, 2, 3).reshape(seqs * wide, width + 128)
    places_all = in_f32(tokens_all[:, width]) * 256 + in_f32(tokens_all[:, width + 1])
    cosine, sine = angle_tables(places_all)
    ffn_w = over_z(jnp.concatenate([w_gate, w_up, w_down], axis=0))

    def spread(value):
        pieces = [step((j, i), value) if j or i else value for j, i in near]
        return tuple(pieces) + tuple(step("c", piece) for piece in pieces)

    def blocks_to(value, *held):
        return [after(step((-j % Q, i), value[n].astype(BF)), *held) for n, (j, i) in enumerate(near) if n]

    def total(first, parts):
        for part in parts:
            first = first + in_f32(part)
        return first

    grad_spread = spread(grad_out)
    pack = after(pack, *grad_spread)

    if Q == 2:
        at_x, at_q = step((0, 1), pack), step((1, 0), pack)
        middle = Z // 2
        chips = [
            (pack, 0, 0, 0), (at_x, 0, 1, 0), (at_q, 1, 0, 0),
            (step((0, 1), at_q[:middle]), 1, 1, 0), (step((1, 0), at_x[middle:]), 1, 1, middle),
        ]
    else:
        chips = [(step((j, i), pack) if j or i else pack, j, i, 0) for j, i in near]
    pieces = []
    for array, j, i, z in chips:
        pieces += [(array, j, i, 0, z), (step("c", array), j, i, 1, z)]
    if not split:
        whole = jnp.zeros((Z, Q, 2, 2) + pack.shape[1:], BF)
        for array, j, i, l, z in pieces:
            block = array[:, None, None, None]
            at = (z, (move.qi - j) % Q, (move.xi + i) % 2, (move.ci + l) % 2, 0, 0)
            whole = lax.dynamic_update_slice(whole, block, at)
        pieces = [(whole.reshape(-1, pack.shape[-1]), 0, 0, 0, 0)]

    query_t, pair_t, normed_t, gains = project_forward(
        meta, tokens_all, cosine, sine, pieces, Q, width, seqs, rows
    )
    mixed, mixed_t, logs = attend_forward(meta, query_t, pair_t, seqs)
    first_sum, second = output_forward(meta, inputs, mixed, gains, pieces, Q)

    second_spread = spread(second)
    half = len(near)
    chunks, outs, backs = [], [], []
    for n in range(0, 2 * half, 8):
        tokens_of = second_spread[n : n + 8] + grad_spread[n : n + 8]
        *parts, hidden_t, gate_t, up_t = ffn(tokens_of, ffn_w)
        chunks.append((tokens_of, (hidden_t, gate_t, up_t)))
        outs += parts[:2]
        backs += parts[2:]
    if len(outs) > 2:
        outs = (jnp.concatenate(outs[: len(outs) // 2]), jnp.concatenate(outs[len(outs) // 2 :]))
        backs = (jnp.concatenate(backs[: len(backs) // 2]), jnp.concatenate(backs[len(backs) // 2 :]))

    def own_core(parts):
        other = step("c", parts[1])
        return (in_f32(parts[0]) + in_f32(other)).reshape(half, own_rows, width), other

    back, other = own_core(backs)
    ffn_sum = None
    for tokens_of, made in chunks:
        part = ffn_sums(after(made[0], other), made[1], made[2], tokens_of, units)
        ffn_sum = part if ffn_sum is None else in_f32(ffn_sum) + in_f32(part)
    ffn_sum = ffn_sum.astype(BF)
    grad_ffn = in_f32(sum_z(ffn_sum))
    grad_gate, grad_up, grad_down = grad_ffn[:units], grad_ffn[units : 2 * units], grad_ffn[2 * units :]
    second_grad = total(back[0], blocks_to(back, ffn_sum))

    def pieces_for(send, keep):
        if split:
            return send, keep
        value = keep.reshape(Z, Q, 2, 2, share, keep.shape[-1])

        def cut(c):
            return jnp.stack(
                [
                    lax.dynamic_slice(
                        value,
                        (0, (move.qi - j) % Q, (move.xi + i) % 2, c, 0, 0),
                        (Z, 1, 1, 1, share, keep.shape[-1]),
                    )[:, 0, 0, 0]
                    for j, i in near
                ]
            )

        return cut(1 - move.ci), cut(move.ci)

    first_grad, mixed_grad_t, out_send, out_keep = output_backward(
        meta, grad_out, first_sum, second_grad, gains, mixed_t, pieces, (Z, Q), split
    )
    out_send, out_keep = pieces_for(out_send, out_keep)
    query_back, pair_back = attend_backward(meta, query_t, pair_t, mixed_grad_t, logs, cosine, sine, seqs)
    out_keep = in_f32(out_keep) + in_f32(after(step("c", out_send), query_back))
    send, keep = project_sums(meta, normed_t, query_back, pair_back, seqs, (Z, Q), split)
    send, keep = pieces_for(send, keep)
    query_grad, pair_grad = project_back(
        after(meta, keep), query_back, pair_back, pieces, Q, width, seqs, Z
    )
    out_rows = total(out_keep[0], blocks_to(out_keep, query_grad)).astype(BF)
    keep = in_f32(keep) + in_f32(after(step("c", send), query_grad))
    pair_grad = sum_z(after(pair_grad, grad_gate))
    rows_of = jnp.concatenate([total(keep[0], blocks_to(keep)).astype(BF), out_rows], axis=-1)
    sums = in_f32(sum_z(after(rows_of, pair_grad)))
    in_grad = input_grad(inputs, gains, first_grad, query_grad, pair_grad)
    layer, _ = own_core((outs[0], after(outs[1], keep)))
    layer_out = total(first_sum + layer[0], blocks_to(layer)).astype(BF)

    grad_key, grad_value = sums[:, :pair_width], sums[:, pair_width : 2 * pair_width]
    grad_query = sums[:, 2 * pair_width : 2 * pair_width + QUERY]
    output_sum = sums[:, 2 * pair_width + QUERY :]
    grad_output, grad_gain_ffn = output_sum[:, :width], output_sum[:, width]
    grad_gain_attn = (
        jnp.sum(grad_query * in_f32(w_query), axis=1)
        + jnp.sum(grad_key * in_f32(w_key), axis=1)
        + jnp.sum(grad_value * in_f32(w_value), axis=1)
    ) / in_f32(gain_attn)
    return (
        layer_out.reshape(seqs, rows, width),
        in_grad.reshape(seqs, rows, width),
        grad_query,
        grad_key,
        grad_value,
        grad_output,
        grad_gain_attn,
        grad_gain_ffn,
        grad_gate,
        grad_up,
        grad_down,
    )


def solution(mesh):
    rows = P(("seq", "dp"), None)
    vector = P(("seq", "dp"))
    act = P("dp", "seq", None)
    return jax.shard_map(
        per_device,
        mesh=mesh,
        in_specs=(act, P("dp", "seq"), act, rows, rows, rows, rows, vector, vector, rows, rows, rows),
        out_specs=(act, act, rows, rows, rows, rows, vector, vector, rows, rows, rows),
        check_vma=False,
    )
```

time: 671 us -> 544 us (0.81)
  waiting for transfers between devices: 326 us -> 273 us
  starting transfers between devices: 76.4 us -> 30.2 us
  local copies, waits for them, and re-layouts: 54.7 us -> 21.2 us
  between operations: 2.28 us -> 14.8 us
  other arithmetic: 50.3 us -> 38.7 us
    ppermute x75 -> x39, waiting for transfers between devices: 326 us -> 265 us  [the longest x22 257 us: step(): lax.ppermute(value, 'dp', [(n, n % 4 ^ 2 * i | 4 * ((n // 4 + j) % self.Q...]
    ppermute x75 -> x39, starting transfers between devices: 76.4 us -> 29.8 us  [the longest x22 27.8 us: step(): lax.ppermute(value, 'dp', [(n, n % 4 ^ 2 * i | 4 * ((n // 4 + j) % self.Q...]
    pallas_call x8 -> x10, Pallas kernels: 122 us -> 156 us  [kernel_call(): pl.pallas_call(body, out_shape=out_shape, in_specs=in_specs, out_specs=ou...]
    pallas_call x4 -> x0, Pallas kernels: 30.5 us -> none  [ffn_sums(): pl.pallas_call(functools.partial(ffn_sums_body, units, lines), out_shape=...]
    another operation x6 -> x8, other arithmetic: 1.52 us -> 21.3 us  [gather(): jnp.stack(blocks, axis=position)]
    add x15 -> x2, other arithmetic: 20.4 us -> 1.83 us  [the longest x1 1.53 us: total(): first = first + in_f32(part)]
    select_n x19 -> x0, other arithmetic: 13.9 us -> none  [gather(): jnp.where(index == 0, jnp.stack(blocks, axis=position), jnp.stack(blocks[...]
    convert_element_type x12 -> x2, local copies, waits for them, and re-layouts: 14.2 us -> 3.65 us  [blocks_to(): value[n].astype(BF)]
  transfers between devices with their start and end apart: 75 -> 45, of which waited for: 41 -> 23; matrix products, arithmetic and copies ran while one was open for 15% -> 8% of each run, Pallas kernels for 17% -> 18%
where the time goes in v3:
time: 544 us; the launch traced here: 534 us
  waiting for transfers between devices  273 us (50%)
  Pallas kernels  156 us (29%)
  other arithmetic  38.7 us (7%)
  starting transfers between devices  30.2 us (6%)
  local copies, waits for them, and re-layouts  21.2 us (4%)
  between operations  14.8 us (3%)
    ppermute x22, waiting for transfers between devices, step(): lax.ppermute(value, 'dp', [(n, n % 4 ^ 2 * i | 4 * ((n // 4 + j) % self.Q...  257 us
    pallas_call x10, Pallas kernels, kernel_call(): pl.pallas_call(body, out_shape=out_shape, in_specs=in_specs, out_specs=ou...  156 us
    ppermute x22, starting transfers between devices, step(): lax.ppermute(value, 'dp', [(n, n % 4 ^ 2 * i | 4 * ((n // 4 + j) % self.Q...  27.8 us
    another operation x4, other arithmetic  19.2 us
  transfers between devices with their start and end apart: 45, of which 23 were waited for; matrix products, arithmetic and copies ran while one was open for 8% of the time, Pallas kernels for 18%

profile of v3, /device:TPU:0, one launch (start us, length us, event | category | flops | bytes accessed | tf_op | source)
XLA Modules:
  0.0 534.3 jit_solution(12964649682461917043)
XLA Ops:
  13.5 2.1 fusion.15
  15.7 4.0 collective-permute-start.2
  21.6 16.4 %collective-permute-done.2.refs_11_ = bf16[256,1536]{1,0:T(8,128)(2,1)S(1)} collective-permute-done((bf16[256,1536]{1,0:T(8,128)(2,1)S(1)}, bf16[256,1536]{1,0:T(8,128)(2,1)S(1)}, u32[]{:S(2)}, u32[]{:S(2)}) %collective-permute-start.2) | collective-permute-done | bytes 786464 | tf_op jit(solution)/shard_map/ppermute | solution.py:67
  38.1 16.1 %collective-permute-done.1.refs_10_ = bf16[256,1536]{1,0:T(8,128)(2,1)} collective-permute-done((bf16[256,1536]{1,0:T(8,128)(2,1)S(1)}, bf16[256,1536]{1,0:T(8,128)(2,1)}, u32[]{:S(2)}, u32[]{:S(2)}) %collective-permute-start.1) | collective-permute-done | bytes 786464 | tf_op jit(solution)/shard_map/ppermute | solution.py:67
  57.9 2.3 collective-permute-start.10
  61.0 39.4 %collective-permute-done.10.refs_4_ = bf16[4,48,4736]{2,1,0:T(8,128)(2,1)S(1)} collective-permute-done((bf16[4,48,4736]{2,1,0:T(8,128)(2,1)}, bf16[4,48,4736]{2,1,0:T(8,128)(2,1)S(1)}, u32[]{:S(2)}, u32[]{:S(2)}) %collective-permute-start.10) | collective-permute-done | bytes 1818656 | tf_op jit(solution)/shard_map/ppermute | solution.py:67
  104.9 17.4 %collective-permute-done.12.refs_6_ = bf16[2,48,4736]{2,1,0:T(8,128)(2,1)S(1)} collective-permute-done((bf16[2,48,4736]{2,1,0:T(8,128)(2,1)S(1)}, bf16[2,48,4736]{2,1,0:T(8,128)(2,1)S(1)}, u32[]{:S(2)}, u32[]{:S(2)}) %collective-permute-start.12) | collective-permute-done | bytes 909344 | tf_op jit(solution)/shard_map/ppermute | solution.py:67
  122.4 2.1 collective-permute-done.14.refs_8_
  125.1 2.2 copy.33
  127.6 1.5 multiply_sine_fusion
  129.2 18.5 %shard_map.203 = (bf16[1536,256]{1,0:T(8,128)(2,1)}, bf16[1536,1024]{1,0:T(8,128)(2,1)}, bf16[1536,1024]{1,0:T(8,128)(2,1)}, f32[8,1536]{1,0:T(8,128)}) custom-call(s32[4]{0:T(128)} %pad_add_fusion.meta, bf16[1024,1664]{1,0:T(8,128)(2,1)} %bitcast.72, f32[48,1024]{1,0:T(8,128)} %get-tuple-element.124.cosine, f32[48,1024]{1,0:T(8,128)} %get-tuple-element.123.sine, ...), custom_call_target="tpu_custom_call" | custom-call | flops 6039797760 | bytes 20971520 | tf_op jit(solution)/shard_map/pallas_call | solution.py:82
  147.7 13.1 %shard_map.204 = (bf16[256,1536]{1,0:T(8,128)(2,1)}, bf16[1536,256]{1,0:T(8,128)(2,1)}, f32[8,2,1,256]{3,2,1,0:T(1,128)}) custom-call(s32[4]{0:T(128)} %pad_add_fusion.meta, bf16[1536,256]{1,0:T(8,128)(2,1)} %get-tuple-element.52.query_t, bf16[1536,1024]{1,0:T(8,128)(2,1)} %get-tuple-element.53.pair_t), custom_call_target="tpu_custom_call" | custom-call | flops 805306368 | bytes 6291456 | tf_op jit(solution)/shard_map/pallas_call | solution.py:82
  160.8 6.9 %shard_map.205 = (f32[256,1536]{1,0:T(8,128)}, bf16[256,1536]{1,0:T(8,128)(2,1)}) custom-call(s32[4]{0:T(128)} %pad_add_fusion.meta, bf16[256,1536]{1,0:T(8,128)(2,1)} %bitcast.69, bf16[256,1536]{1,0:T(8,128)(2,1)} %get-tuple-element.54.mixed, f32[8,1536]{1,0:T(8,128)} %get-tuple-element.55.gain, bf16[4,48,4736]{2,1,0:T(8,128)(2,1)} %bitcast.66, ...), custom_call_target="tpu_custom_call" | custom-call | flops 1207959552 | bytes 10485760 | tf_op jit(solution)/shard_map/pallas_call | solution.py:82
  167.7 2.3 collective-permute-start.18
  171.3 18.0 %collective-permute-done.18.refs_3_ = bf16[256,1536]{1,0:T(8,128)(2,1)S(1)} collective-permute-done((bf16[256,1536]{1,0:T(8,128)(2,1)}, bf16[256,1536]{1,0:T(8,128)(2,1)S(1)}, u32[]{:S(2)}, u32[]{:S(2)}) %collective-permute-start.18) | collective-permute-done | bytes 786464 | tf_op jit(solution)/shard_map/ppermute | solution.py:67
  189.3 16.5 %collective-permute-done.17.refs_2_ = bf16[256,1536]{1,0:T(8,128)(2,1)S(1)} collective-permute-done((bf16[256,1536]{1,0:T(8,128)(2,1)}, bf16[256,1536]{1,0:T(8,128)(2,1)S(1)}, u32[]{:S(2)}, u32[]{:S(2)}) %collective-permute-start.17) | collective-permute-done | bytes 786464 | tf_op jit(solution)/shard_map/ppermute | solution.py:67
  206.3 8.3 %all-gather.11.cloned.1.call-done = bf16[1536,1536]{1,0:T(8,128)(2,1)} async-done(((bf16[384,1536]{1,0:T(8,128)(2,1)}), bf16[1536,1536]{1,0:T(8,128)(2,1)}) %all-gather.11.cloned.1.call-update) | async-done | bytes 4718608 | tf_op jit(solution)/shard_map/all_gather | solution.py:674
  215.4 38.1 %shard_map.206 = (bf16[1024,1536]{1,0:T(8,128)(2,1)}, bf16[1024,1536]{1,0:T(8,128)(2,1)}, bf16[1024,1536]{1,0:T(8,128)(2,1)}, bf16[1024,1536]{1,0:T(8,128)(2,1)}...) custom-call(bf16[256,1536]{1,0:T(8,128)(2,1)} %get-tuple-element.57.refs_0_, ...), custom_call_target="tpu_custom_call" | custom-call | flops 19327352832 | bytes 35651584 | tf_op jit(solution)/shard_map/pallas_call | solution.py:82
  253.6 6.0 %collective-permute-done.23 = bf16[1024,1536]{1,0:T(8,128)(2,1)} collective-permute-done((bf16[1024,1536]{1,0:T(8,128)(2,1)}, bf16[1024,1536]{1,0:T(8,128)(2,1)}, u32[]{:S(2)}, u32[]{:S(2)}) %collective-permute-start.23) | collective-permute-done | bytes 3145760 | tf_op jit(solution)/shard_map/ppermute | solution.py:65
  259.6 21.6 %shard_map.207 = bf16[4,384,1536]{2,1,0:T(8,128)(2,1)} custom-call(bf16[256,1536]{1,0:T(8,128)(2,1)} %get-tuple-element.57.refs_0_, bf16[256,1536]{1,0:T(8,128)(2,1)} %copy-done.22, bf16[256,1536]{1,0:T(8,128)(2,1)} %copy-done.21, bf16[256,1536]{1,0:T(8,128)(2,1)} %copy-done.20, bf16[256,1536]{1,0:T(8,128)(2,1)} %copy-done.23, ...), custom_call_target="tpu_custom_call" | custom-call | flops 9663676416 | bytes 23068672 | tf_op jit(solution)/shard_map/pallas_call | solution.py:82
  281.3 1.8 copy-done.5
  283.1 3.1 fusion.21
  286.4 1.6 collective-permute-start.24
  287.9 1.5 collective-permute-start.26
  289.9 16.9 %collective-permute-done.24 = bf16[256,1536]{1,0:T(8,128)(2,1)S(1)} collective-permute-done((bf16[256,1536]{1,0:T(8,128)(2,1)S(1)}, bf16[256,1536]{1,0:T(8,128)(2,1)S(1)}, u32[]{:S(2)}, u32[]{:S(2)}) %collective-permute-start.24) | collective-permute-done | bytes 786464 | tf_op jit(solution)/shard_map/ppermute | solution.py:67
  306.8 17.2 %collective-permute-done.26 = bf16[256,1536]{1,0:T(8,128)(2,1)S(1)} collective-permute-done((bf16[256,1536]{1,0:T(8,128)(2,1)S(1)}, bf16[256,1536]{1,0:T(8,128)(2,1)S(1)}, u32[]{:S(2)}, u32[]{:S(2)}) %collective-permute-start.26) | collective-permute-done | bytes 786464 | tf_op jit(solution)/shard_map/ppermute | solution.py:67
  325.3 1.5 fusion.10.second_grad
  326.8 10.2 %shard_map.208 = (f32[256,1536]{1,0:T(8,128)}, bf16[1536,256]{1,0:T(8,128)(2,1)}, bf16[4,4,48,1664]{3,2,1,0:T(8,128)(2,1)}, bf16[4,4,48,1664]{3,2,1,0:T(8,128)(2,1)}) custom-call(s32[4]{0:T(128)} %pad_add_fusion.meta, bf16[256,1536]{1,0:T(8,128)(2,1)} %bitcast.76, f32[256,1536]{1,0:T(8,128)} %get-tuple-element.56.total, f32[256,1536]{1,0:T(8,128)} %fusion.10.second_grad, ...), custom_call_target="tpu_custom_call" | custom-call | flops 2415919104 | bytes 23068672 | tf_op jit(solution)/shard_map/pallas_call | solution.py:82
  337.1 15.7 %shard_map.209 = (bf16[1536,256]{1,0:T(8,128)(2,1)}, bf16[1536,1024]{1,0:T(8,128)(2,1)}) custom-call(s32[4]{0:T(128)} %pad_add_fusion.meta, bf16[1536,256]{1,0:T(8,128)(2,1)} %get-tuple-element.52.query_t, bf16[1536,1024]{1,0:T(8,128)(2,1)} %get-tuple-element.53.pair_t, bf16[1536,256]{1,0:T(8,128)(2,1)} %get-tuple-element.71.grad_t, ...), custom_call_target="tpu_custom_call" | custom-call | flops 2013265920 | bytes 12582912 | tf_op jit(solution)/shard_map/pallas_call | solution.py:82
  352.7 13.2 %shard_map.210 = (bf16[4,4,48,3072]{3,2,1,0:T(8,128)(2,1)}, bf16[4,4,48,3072]{3,2,1,0:T(8,128)(2,1)}) custom-call(s32[4]{0:T(128)} %pad_add_fusion.meta, bf16[1536,1024]{1,0:T(8,128)(2,1)} %get-tuple-element.60.normed_t, bf16[1536,256]{1,0:T(8,128)(2,1)} %get-tuple-element.73.query_back, bf16[1536,1024]{1,0:T(8,128)(2,1)} %get-tuple-element.74.pair_back), custom_call_target="tpu_custom_call" | custom-call | flops 6039797760 | bytes 27262976 | tf_op jit(solution)/shard_map/pallas_call | solution.py:82
  366.4 14.9 %shard_map.211 = (f32[1536,256]{1,0:T(8,128)}, bf16[4,1536,256]{2,1,0:T(8,128)(2,1)}) custom-call(s32[4]{0:T(128)} %pad_add_fusion.meta, bf16[1536,256]{1,0:T(8,128)(2,1)} %get-tuple-element.73.query_back, bf16[1536,1024]{1,0:T(8,128)(2,1)} %get-tuple-element.74.pair_back, bf16[4,48,4736]{2,1,0:T(8,128)(2,1)} %bitcast.68, ...), custom_call_target="tpu_custom_call" | custom-call | flops 6039797760 | bytes 20971520 | tf_op jit(solution)/shard_map/pallas_call | solution.py:82
  381.4 1.5 convert_element_type.157
  386.1 4.7 fusion.20
  392.1 1.5 collective-permute-start.36
  395.6 8.4 %fusion.23 = (bf16[4,4,48,3072]{3,2,1,0:T(8,128)(2,1)}, f32[4,4,48,3072]{3,2,1,0:T(8,128)S(1)}) fusion(bf16[4,4,48,3072]{3,2,1,0:T(8,128)(2,1)} %collective-permute-done.27, bf16[4,4,48,3072]{3,2,1,0:T(8,128)(2,1)} %get-tuple-element.75), kind=kLoop, calls=%fused_computation.68 | loop fusion | flops 9437184 | bytes 23592960 | tf_op jit(solution)/shard_map/convert.6
  404.0 2.3 slice_bitcast_fusion.4
  406.3 1.6 collective-permute-start.32
  408.6 14.9 %collective-permute-done.38 = bf16[4,48,1664]{2,1,0:T(8,128)(2,1)} collective-permute-done((bf16[4,48,1664]{2,1,0:T(8,128)(2,1)}, bf16[4,48,1664]{2,1,0:T(8,128)(2,1)}, u32[]{:S(2)}, u32[]{:S(2)}) %collective-permute-start.38) | collective-permute-done | bytes 639008 | tf_op jit(solution)/shard_map/ppermute | solution.py:67
  424.9 2.1 fusion.14
  427.0 21.6 %collective-permute-done.32 = bf16[4,48,3072]{2,1,0:T(8,128)(2,1)S(1)} collective-permute-done((bf16[4,48,3072]{2,1,0:T(8,128)(2,1)S(1)}, bf16[4,48,3072]{2,1,0:T(8,128)(2,1)S(1)}, u32[]{:S(2)}, u32[]{:S(2)}) %collective-permute-start.32) | collective-permute-done | bytes 1179680 | tf_op jit(solution)/shard_map/ppermute | solution.py:67
  448.6 24.5 %collective-permute-done.34 = bf16[4,48,3072]{2,1,0:T(8,128)(2,1)S(1)} collective-permute-done((bf16[4,48,3072]{2,1,0:T(8,128)(2,1)S(1)}, bf16[4,48,3072]{2,1,0:T(8,128)(2,1)S(1)}, u32[]{:S(2)}, u32[]{:S(2)}) %collective-permute-start.34) | collective-permute-done | bytes 1179680 | tf_op jit(solution)/shard_map/ppermute | solution.py:67
  473.1 1.7 collective-permute-done.33
  478.2 3.1 fusion.22
  481.5 1.6 collective-permute-start.29
  485.0 17.0 %collective-permute-done.29 = bf16[256,1536]{1,0:T(8,128)(2,1)S(1)} collective-permute-done((bf16[256,1536]{1,0:T(8,128)(2,1)S(1)}, bf16[256,1536]{1,0:T(8,128)(2,1)S(1)}, u32[]{:S(2)}, u32[]{:S(2)}) %collective-permute-start.29) | collective-permute-done | bytes 786464 | tf_op jit(solution)/shard_map/ppermute | solution.py:67
  502.0 14.1 %collective-permute-done.31 = bf16[256,1536]{1,0:T(8,128)(2,1)S(1)} collective-permute-done((bf16[256,1536]{1,0:T(8,128)(2,1)S(1)}, bf16[256,1536]{1,0:T(8,128)(2,1)S(1)}, u32[]{:S(2)}, u32[]{:S(2)}) %collective-permute-start.31) | collective-permute-done | bytes 786464 | tf_op jit(solution)/shard_map/ppermute | solution.py:67
  517.4 1.5 fusion.8
  518.9 4.2 shard_map.212
  (145 shorter events, 42.9 us)
Async XLA Ops:
  7.2 50.7 %all-gather.9.cloned.1.call-start = ((), (), s32[]{:S(2)}) async-start(), calls=%async_computation.7 | async-start | bytes 2273280 | tf_op jit(solution)/shard_map/all_gather | solution.py:674
  12.6 112.5 %all-gather.7.cloned.1.call-start = ((), (), s32[]{:S(2)}) async-start(), calls=%async_computation.6 | async-start | bytes 4259840 | tf_op jit(solution)/shard_map/all_gather | solution.py:674
  15.7 198.9 %all-gather.11.cloned.1.call-start = ((), (), s32[]{:S(2)}) async-start(), calls=%async_computation.8 | async-start | bytes 5898240 | tf_op jit(solution)/shard_map/all_gather | solution.py:674
  15.7 22.4 %collective-permute-start.2 = (bf16[256,1536]{1,0:T(8,128)(2,1)S(1)}, bf16[256,1536]{1,0:T(8,128)(2,1)S(1)}, u32[]{:S(2)}, u32[]{:S(2)}) collective-permute-start(bf16[256,1536]{1,0:T(8,128)(2,1)S(1)} %bitcast.77), channel_id=1, source_target_pairs={{0,6},{1,7},{2,4},{3,5},{4,2},{5,3},{6,0},{7,1},{8,14},{9,15},{10,... | collective-permute-start | bytes 2359304 | tf_op jit(solution)/shard_map/ppermute | solution.py:67
  19.7 34.5 %collective-permute-start.1 = (bf16[256,1536]{1,0:T(8,128)(2,1)S(1)}, bf16[256,1536]{1,0:T(8,128)(2,1)}, u32[]{:S(2)}, u32[]{:S(2)}) collective-permute-start(bf16[256,1536]{1,0:T(8,128)(2,1)S(1)} %bitcast.78), channel_id=1, source_target_pairs={{0,4},{1,5},{2,6},{3,7},{4,0},{5,1},{6,2},{7,3},{8,12},{9,13},{10,... | collective-permute-start | bytes 2359304 | tf_op jit(solution)/shard_map/ppermute | solution.py:67
  20.2 34.3 %collective-permute-start = (bf16[256,1536]{1,0:T(8,128)(2,1)S(1)}, bf16[256,1536]{1,0:T(8,128)(2,1)}, u32[]{:S(2)}, u32[]{:S(2)}) collective-permute-start(bf16[256,1536]{1,0:T(8,128)(2,1)S(1)} %bitcast.79), channel_id=1, source_target_pairs={{0,2},{1,3},{2,0},{3,1},{4,6},{5,7},{6,4},{7,5},{8,10},{9,11},{10,... | collective-permute-start | bytes 2359304 | tf_op jit(solution)/shard_map/ppermute | solution.py:67
  21.5 359.9 %reduce-scatter.4.cloned.1.call-start = ((), (), s32[]{:S(2)}) async-start(), calls=%async_computation.3 | async-start | bytes 5898240 | tf_op jit(solution)/shard_map/reduce_scatter | solution.py:677
  21.6 33.1 %collective-permute-start.3 = (bf16[256,1536]{1,0:T(8,128)(2,1)S(1)}, bf16[256,1536]{1,0:T(8,128)(2,1)S(1)}, u32[]{:S(2)}, u32[]{:S(2)}) collective-permute-start(bf16[256,1536]{1,0:T(8,128)(2,1)S(1)} %bitcast.80), channel_id=1, source_target_pairs={{0,1},{1,0},{2,3},{3,2},{4,5},{5,4},{6,7},{7,6},{8,9},{9,8},{10,11... | collective-permute-start | bytes 2359304 | tf_op jit(solution)/shard_map/ppermute | solution.py:65
  38.1 16.6 %collective-permute-start.6 = (bf16[256,1536]{1,0:T(8,128)(2,1)S(1)}, bf16[256,1536]{1,0:T(8,128)(2,1)S(1)}, u32[]{:S(2)}, u32[]{:S(2)}) collective-permute-start(bf16[256,1536]{1,0:T(8,128)(2,1)S(1)} %collective-permute-done.2.refs_11_), channel_id=1, source_target_pairs={{0,1},{1,0},{2,3},{3,2},{4,5},{5,4},{6,7},{7,6},{8,9},{9,8},{10,11... | collective-permute-start | bytes 2359304 | tf_op jit(solution)/shard_map/ppermute | solution.py:65
  54.2 2.5 collective-permute-start.5
  54.5 3.5 collective-permute-start.4
  57.9 42.5 %collective-permute-start.10 = (bf16[4,48,4736]{2,1,0:T(8,128)(2,1)}, bf16[4,48,4736]{2,1,0:T(8,128)(2,1)S(1)}, u32[]{:S(2)}, u32[]{:S(2)}) collective-permute-start(bf16[4,48,4736]{2,1,0:T(8,128)(2,1)} %bitcast.62), channel_id=1, source_target_pairs={{0,4},{1,5},{2,6},{3,7},{4,0},{5,1},{6,2},{7,3},{8,12},{9,13},{10,... | collective-permute-start | bytes 5455880 | tf_op jit(solution)/shard_map/ppermute | solution.py:67
  60.2 41.7 %collective-permute-start.8 = (bf16[4,48,4736]{2,1,0:T(8,128)(2,1)}, bf16[4,48,4736]{2,1,0:T(8,128)(2,1)}, u32[]{:S(2)}, u32[]{:S(2)}) collective-permute-start(bf16[4,48,4736]{2,1,0:T(8,128)(2,1)} %bitcast.63), channel_id=1, source_target_pairs={{0,2},{1,3},{2,0},{3,1},{4,6},{5,7},{6,4},{7,5},{8,10},{9,11},{10,... | collective-permute-start | bytes 5455880 | tf_op jit(solution)/shard_map/ppermute | solution.py:67
  61.0 68.1 %collective-permute-start.7 = (bf16[4,48,4736]{2,1,0:T(8,128)(2,1)}, bf16[4,48,4736]{2,1,0:T(8,128)(2,1)}, u32[]{:S(2)}, u32[]{:S(2)}) collective-permute-start(bf16[4,48,4736]{2,1,0:T(8,128)(2,1)} %bitcast.64), channel_id=1, source_target_pairs={{0,1},{1,0},{2,3},{3,2},{4,5},{5,4},{6,7},{7,6},{8,9},{9,8},{10,11... | collective-permute-start | bytes 5455880 | tf_op jit(solution)/shard_map/ppermute | solution.py:65
  100.4 26.9 %copy-start = (bf16[4,48,4736]{2,1,0:T(8,128)(2,1)}, bf16[4,48,4736]{2,1,0:T(8,128)(2,1)S(1)}, u32[]{:S(2)}) copy-start(bf16[4,48,4736]{2,1,0:T(8,128)(2,1)S(1)} %collective-permute-done.10.refs_4_) | copy-start | bytes 5455876
  100.5 21.9 %collective-permute-start.12 = (bf16[2,48,4736]{2,1,0:T(8,128)(2,1)S(1)}, bf16[2,48,4736]{2,1,0:T(8,128)(2,1)S(1)}, u32[]{:S(2)}, u32[]{:S(2)}) collective-permute-start(bf16[2,48,4736]{2,1,0:T(8,128)(2,1)S(1)} %slice.149), channel_id=1, source_target_pairs={{0,2},{1,3},{2,0},{3,1},{4,6},{5,7},{6,4},{7,5},{8,10},{9,11},{10,... | collective-permute-start | bytes 2727944 | tf_op jit(solution)/shard_map/ppermute | solution.py:67
  103.2 21.2 %collective-permute-start.14 = (bf16[2,48,4736]{2,1,0:T(8,128)(2,1)S(1)}, bf16[2,48,4736]{2,1,0:T(8,128)(2,1)}, u32[]{:S(2)}, u32[]{:S(2)}) collective-permute-start(bf16[2,48,4736]{2,1,0:T(8,128)(2,1)S(1)} %slice.150), channel_id=1, source_target_pairs={{0,4},{1,5},{2,6},{3,7},{4,0},{5,1},{6,2},{7,3},{8,12},{9,13},{10,... | collective-permute-start | bytes 2727944 | tf_op jit(solution)/shard_map/ppermute | solution.py:67
  104.4 24.8 %collective-permute-start.11 = (bf16[4,48,4736]{2,1,0:T(8,128)(2,1)S(1)}, bf16[4,48,4736]{2,1,0:T(8,128)(2,1)}, u32[]{:S(2)}, u32[]{:S(2)}) collective-permute-start(bf16[4,48,4736]{2,1,0:T(8,128)(2,1)S(1)} %collective-permute-done.10.refs_4_), channel_id=1, source_target_pairs={{0,1},{1,0},{2,3},{3,2},{4,5},{5,4},{6,7},{7,6},{8,9},{9,8},{10,11... | collective-permute-start | bytes 5455880 | tf_op jit(solution)/shard_map/ppermute | solution.py:65
  104.4 24.8 %collective-permute-start.9 = (bf16[4,48,4736]{2,1,0:T(8,128)(2,1)}, bf16[4,48,4736]{2,1,0:T(8,128)(2,1)}, u32[]{:S(2)}, u32[]{:S(2)}) collective-permute-start(bf16[4,48,4736]{2,1,0:T(8,128)(2,1)} %collective-permute-done.8.refs_2_), channel_id=1, source_target_pairs={{0,1},{1,0},{2,3},{3,2},{4,5},{5,4},{6,7},{7,6},{8,9},{9,8},{10,11... | collective-permute-start | bytes 5455880 | tf_op jit(solution)/shard_map/ppermute | solution.py:65
  122.4 6.8 %collective-permute-start.13 = (bf16[2,48,4736]{2,1,0:T(8,128)(2,1)S(1)}, bf16[2,48,4736]{2,1,0:T(8,128)(2,1)}, u32[]{:S(2)}, u32[]{:S(2)}) collective-permute-start(bf16[2,48,4736]{2,1,0:T(8,128)(2,1)S(1)} %collective-permute-done.12.refs_6_), channel_id=1, source_target_pairs={{0,1},{1,0},{2,3},{3,2},{4,5},{5,4},{6,7},{7,6},{8,9},{9,8},{10,11... | collective-permute-start | bytes 2727944 | tf_op jit(solution)/shard_map/ppermute | solution.py:65
  124.5 4.8 collective-permute-start.15
  167.7 21.6 %collective-permute-start.18 = (bf16[256,1536]{1,0:T(8,128)(2,1)}, bf16[256,1536]{1,0:T(8,128)(2,1)S(1)}, u32[]{:S(2)}, u32[]{:S(2)}) collective-permute-start(bf16[256,1536]{1,0:T(8,128)(2,1)} %get-tuple-element.57.refs_0_), channel_id=1, source_target_pairs={{0,6},{1,7},{2,4},{3,5},{4,2},{5,3},{6,0},{7,1},{8,14},{9,15},{10,... | collective-permute-start | bytes 2359304 | tf_op jit(solution)/shard_map/ppermute | solution.py:67
  170.0 35.7 %collective-permute-start.17 = (bf16[256,1536]{1,0:T(8,128)(2,1)}, bf16[256,1536]{1,0:T(8,128)(2,1)S(1)}, u32[]{:S(2)}, u32[]{:S(2)}) collective-permute-start(bf16[256,1536]{1,0:T(8,128)(2,1)} %get-tuple-element.57.refs_0_), channel_id=1, source_target_pairs={{0,4},{1,5},{2,6},{3,7},{4,0},{5,1},{6,2},{7,3},{8,12},{9,13},{10,... | collective-permute-start | bytes 2359304 | tf_op jit(solution)/shard_map/ppermute | solution.py:67
  170.6 35.3 %collective-permute-start.16 = (bf16[256,1536]{1,0:T(8,128)(2,1)}, bf16[256,1536]{1,0:T(8,128)(2,1)S(1)}, u32[]{:S(2)}, u32[]{:S(2)}) collective-permute-start(bf16[256,1536]{1,0:T(8,128)(2,1)} %get-tuple-element.57.refs_0_), channel_id=1, source_target_pairs={{0,2},{1,3},{2,0},{3,1},{4,6},{5,7},{6,4},{7,5},{8,10},{9,11},{10,... | collective-permute-start | bytes 2359304 | tf_op jit(solution)/shard_map/ppermute | solution.py:67
  171.3 43.3 %collective-permute-start.19 = (bf16[256,1536]{1,0:T(8,128)(2,1)}, bf16[256,1536]{1,0:T(8,128)(2,1)S(1)}, u32[]{:S(2)}, u32[]{:S(2)}) collective-permute-start(bf16[256,1536]{1,0:T(8,128)(2,1)} %get-tuple-element.57.refs_0_), channel_id=1, source_target_pairs={{0,1},{1,0},{2,3},{3,2},{4,5},{5,4},{6,7},{7,6},{8,9},{9,8},{10,11... | collective-permute-start | bytes 2359304 | tf_op jit(solution)/shard_map/ppermute | solution.py:65
  189.3 25.3 %copy-start.20 = (bf16[256,1536]{1,0:T(8,128)(2,1)}, bf16[256,1536]{1,0:T(8,128)(2,1)S(1)}, u32[]{:S(2)}) copy-start(bf16[256,1536]{1,0:T(8,128)(2,1)S(1)} %collective-permute-done.18.refs_3_) | copy-start | bytes 2359300
  189.3 25.3 %collective-permute-start.22 = (bf16[256,1536]{1,0:T(8,128)(2,1)S(1)}, bf16[256,1536]{1,0:T(8,128)(2,1)}, u32[]{:S(2)}, u32[]{:S(2)}) collective-permute-start(bf16[256,1536]{1,0:T(8,128)(2,1)S(1)} %collective-permute-done.18.refs_3_), channel_id=1, source_target_pairs={{0,1},{1,0},{2,3},{3,2},{4,5},{5,4},{6,7},{7,6},{8,9},{9,8},{10,11... | collective-permute-start | bytes 2359304 | tf_op jit(solution)/shard_map/ppermute | solution.py:65
  205.8 8.8 %collective-permute-start.21 = (bf16[256,1536]{1,0:T(8,128)(2,1)S(1)}, bf16[256,1536]{1,0:T(8,128)(2,1)}, u32[]{:S(2)}, u32[]{:S(2)}) collective-permute-start(bf16[256,1536]{1,0:T(8,128)(2,1)S(1)} %collective-permute-done.17.refs_2_), channel_id=1, source_target_pairs={{0,1},{1,0},{2,3},{3,2},{4,5},{5,4},{6,7},{7,6},{8,9},{9,8},{10,11... | collective-permute-start | bytes 2359304 | tf_op jit(solution)/shard_map/ppermute | solution.py:65
  205.9 8.7 %collective-permute-start.20 = (bf16[256,1536]{1,0:T(8,128)(2,1)S(1)}, bf16[256,1536]{1,0:T(8,128)(2,1)}, u32[]{:S(2)}, u32[]{:S(2)}) collective-permute-start(bf16[256,1536]{1,0:T(8,128)(2,1)S(1)} %collective-permute-done.16.refs_1_), channel_id=1, source_target_pairs={{0,1},{1,0},{2,3},{3,2},{4,5},{5,4},{6,7},{7,6},{8,9},{9,8},{10,11... | collective-permute-start | bytes 2359304 | tf_op jit(solution)/shard_map/ppermute | solution.py:65
  253.5 6.1 %collective-permute-start.23 = (bf16[1024,1536]{1,0:T(8,128)(2,1)}, bf16[1024,1536]{1,0:T(8,128)(2,1)}, u32[]{:S(2)}, u32[]{:S(2)}) collective-permute-start(bf16[1024,1536]{1,0:T(8,128)(2,1)} %get-tuple-element.62), channel_id=1, source_target_pairs={{0,1},{1,0},{2,3},{3,2},{4,5},{5,4},{6,7},{7,6},{8,9},{9,8},{10,11... | collective-permute-start | bytes 9437192 | tf_op jit(solution)/shard_map/ppermute | solution.py:65
  281.2 195.8 %reduce-scatter.6.cloned.1.call-start = ((), (), s32[]{:S(2)}) async-start(), calls=%async_computation.4 | async-start | bytes 3932160 | tf_op jit(solution)/shard_map/reduce_scatter | solution.py:677
  286.4 20.4 %collective-permute-start.24 = (bf16[256,1536]{1,0:T(8,128)(2,1)S(1)}, bf16[256,1536]{1,0:T(8,128)(2,1)S(1)}, u32[]{:S(2)}, u32[]{:S(2)}) collective-permute-start(bf16[256,1536]{1,0:T(8,128)(2,1)S(1)} %get-tuple-element.111), channel_id=1, source_target_pairs={{0,2},{1,3},{2,0},{3,1},{4,6},{5,7},{6,4},{7,5},{8,10},{9,11},{10,... | collective-permute-start | bytes 2359304 | tf_op jit(solution)/shard_map/ppermute | solution.py:67
  287.9 36.0 %collective-permute-start.26 = (bf16[256,1536]{1,0:T(8,128)(2,1)S(1)}, bf16[256,1536]{1,0:T(8,128)(2,1)S(1)}, u32[]{:S(2)}, u32[]{:S(2)}) collective-permute-start(bf16[256,1536]{1,0:T(8,128)(2,1)S(1)} %get-tuple-element.112), channel_id=1, source_target_pairs={{0,6},{1,7},{2,4},{3,5},{4,2},{5,3},{6,0},{7,1},{8,14},{9,15},{10,... | collective-permute-start | bytes 2359304 | tf_op jit(solution)/shard_map/ppermute | solution.py:67
  289.4 35.9 %collective-permute-start.25 = (bf16[256,1536]{1,0:T(8,128)(2,1)S(1)}, bf16[256,1536]{1,0:T(8,128)(2,1)S(1)}, u32[]{:S(2)}, u32[]{:S(2)}) collective-permute-start(bf16[256,1536]{1,0:T(8,128)(2,1)S(1)} %get-tuple-element.113), channel_id=1, source_target_pairs={{0,4},{1,5},{2,6},{3,7},{4,0},{5,1},{6,2},{7,3},{8,12},{9,13},{10,... | collective-permute-start | bytes 2359304 | tf_op jit(solution)/shard_map/ppermute | solution.py:67
  365.9 29.7 %collective-permute-start.27 = (bf16[4,4,48,3072]{3,2,1,0:T(8,128)(2,1)}, bf16[4,4,48,3072]{3,2,1,0:T(8,128)(2,1)}, u32[]{:S(2)}, u32[]{:S(2)}) collective-permute-start(bf16[4,4,48,3072]{3,2,1,0:T(8,128)(2,1)} %get-tuple-element.76), channel_id=1, source_target_pairs={{0,1},{1,0},{2,3},{3,2},{4,5},{5,4},{6,7},{7,6},{8,9},{9,8},{10,11... | collective-permute-start | bytes 14155784 | tf_op jit(solution)/shard_map/ppermute | solution.py:65
  365.9 18.8 %collective-permute-start.35 = (bf16[4,4,48,1664]{3,2,1,0:T(8,128)(2,1)}, bf16[4,4,48,1664]{3,2,1,0:T(8,128)(2,1)}, u32[]{:S(2)}, u32[]{:S(2)}) collective-permute-start(bf16[4,4,48,1664]{3,2,1,0:T(8,128)(2,1)} %get-tuple-element.85), channel_id=1, source_target_pairs={{0,1},{1,0},{2,3},{3,2},{4,5},{5,4},{6,7},{7,6},{8,9},{9,8},{10,11... | collective-permute-start | bytes 7667720 | tf_op jit(solution)/shard_map/ppermute | solution.py:65
  384.4 138.7 %reduce-scatter.8.cloned.1.call-start = ((), (), s32[]{:S(2)}) async-start(), calls=%async_computation.5 | async-start | bytes 2273280 | tf_op jit(solution)/shard_map/reduce_scatter | solution.py:677
  392.1 32.8 %collective-permute-start.36 = (bf16[4,48,1664]{2,1,0:T(8,128)(2,1)}, bf16[4,48,1664]{2,1,0:T(8,128)(2,1)}, u32[]{:S(2)}, u32[]{:S(2)}) collective-permute-start(bf16[4,48,1664]{2,1,0:T(8,128)(2,1)} %get-tuple-element.114), channel_id=1, source_target_pairs={{0,2},{1,3},{2,0},{3,1},{4,6},{5,7},{6,4},{7,5},{8,10},{9,11},{10,... | collective-permute-start | bytes 1916936 | tf_op jit(solution)/shard_map/ppermute | solution.py:67
  393.7 29.9 %collective-permute-start.38 = (bf16[4,48,1664]{2,1,0:T(8,128)(2,1)}, bf16[4,48,1664]{2,1,0:T(8,128)(2,1)}, u32[]{:S(2)}, u32[]{:S(2)}) collective-permute-start(bf16[4,48,1664]{2,1,0:T(8,128)(2,1)} %get-tuple-element.115), channel_id=1, source_target_pairs={{0,6},{1,7},{2,4},{3,5},{4,2},{5,3},{6,0},{7,1},{8,14},{9,15},{10,... | collective-permute-start | bytes 1916936 | tf_op jit(solution)/shard_map/ppermute | solution.py:67
  394.3 30.6 %collective-permute-start.37 = (bf16[4,48,1664]{2,1,0:T(8,128)(2,1)}, bf16[4,48,1664]{2,1,0:T(8,128)(2,1)}, u32[]{:S(2)}, u32[]{:S(2)}) collective-permute-start(bf16[4,48,1664]{2,1,0:T(8,128)(2,1)} %get-tuple-element.116), channel_id=1, source_target_pairs={{0,4},{1,5},{2,6},{3,7},{4,0},{5,1},{6,2},{7,3},{8,12},{9,13},{10,... | collective-permute-start | bytes 1916936 | tf_op jit(solution)/shard_map/ppermute | solution.py:67
  406.3 42.3 %collective-permute-start.32 = (bf16[4,48,3072]{2,1,0:T(8,128)(2,1)S(1)}, bf16[4,48,3072]{2,1,0:T(8,128)(2,1)S(1)}, u32[]{:S(2)}, u32[]{:S(2)}) collective-permute-start(bf16[4,48,3072]{2,1,0:T(8,128)(2,1)S(1)} %get-tuple-element.105), channel_id=1, source_target_pairs={{0,2},{1,3},{2,0},{3,1},{4,6},{5,7},{6,4},{7,5},{8,10},{9,11},{10,... | collective-permute-start | bytes 3538952 | tf_op jit(solution)/shard_map/ppermute | solution.py:67
  407.9 65.2 %collective-permute-start.34 = (bf16[4,48,3072]{2,1,0:T(8,128)(2,1)S(1)}, bf16[4,48,3072]{2,1,0:T(8,128)(2,1)S(1)}, u32[]{:S(2)}, u32[]{:S(2)}) collective-permute-start(bf16[4,48,3072]{2,1,0:T(8,128)(2,1)S(1)} %get-tuple-element.106), channel_id=1, source_target_pairs={{0,6},{1,7},{2,4},{3,5},{4,2},{5,3},{6,0},{7,1},{8,14},{9,15},{10,... | collective-permute-start | bytes 3538952 | tf_op jit(solution)/shard_map/ppermute | solution.py:67
  423.5 51.3 %collective-permute-start.33 = (bf16[4,48,3072]{2,1,0:T(8,128)(2,1)S(1)}, bf16[4,48,3072]{2,1,0:T(8,128)(2,1)S(1)}, u32[]{:S(2)}, u32[]{:S(2)}) collective-permute-start(bf16[4,48,3072]{2,1,0:T(8,128)(2,1)S(1)} %get-tuple-element.107), channel_id=1, source_target_pairs={{0,4},{1,5},{2,6},{3,7},{4,0},{5,1},{6,2},{7,3},{8,12},{9,13},{10,... | collective-permute-start | bytes 3538952 | tf_op jit(solution)/shard_map/ppermute | solution.py:67
  424.9 52.2 %collective-permute-start.28 = (bf16[1024,1536]{1,0:T(8,128)(2,1)}, bf16[1024,1536]{1,0:T(8,128)(2,1)}, u32[]{:S(2)}, u32[]{:S(2)}) collective-permute-start(bf16[1024,1536]{1,0:T(8,128)(2,1)} %get-tuple-element.80), channel_id=1, source_target_pairs={{0,1},{1,0},{2,3},{3,2},{4,5},{5,4},{6,7},{7,6},{8,9},{9,8},{10,11... | collective-permute-start | bytes 9437192 | tf_op jit(solution)/shard_map/ppermute | solution.py:65
  481.3 36.2 %copy-start.1 = (f32[256,1536]{1,0:T(8,128)S(1)}, f32[256,1536]{1,0:T(8,128)}, u32[]{:S(2)}) copy-start(f32[256,1536]{1,0:T(8,128)} %get-tuple-element.56.total) | copy-start | bytes 4718596
  481.5 20.5 %collective-permute-start.29 = (bf16[256,1536]{1,0:T(8,128)(2,1)S(1)}, bf16[256,1536]{1,0:T(8,128)(2,1)S(1)}, u32[]{:S(2)}, u32[]{:S(2)}) collective-permute-start(bf16[256,1536]{1,0:T(8,128)(2,1)S(1)} %get-tuple-element.108), channel_id=1, source_target_pairs={{0,2},{1,3},{2,0},{3,1},{4,6},{5,7},{6,4},{7,5},{8,10},{9,11},{10,... | collective-permute-start | bytes 2359304 | tf_op jit(solution)/shard_map/ppermute | solution.py:67
  483.0 33.0 %collective-permute-start.31 = (bf16[256,1536]{1,0:T(8,128)(2,1)S(1)}, bf16[256,1536]{1,0:T(8,128)(2,1)S(1)}, u32[]{:S(2)}, u32[]{:S(2)}) collective-permute-start(bf16[256,1536]{1,0:T(8,128)(2,1)S(1)} %get-tuple-element.109), channel_id=1, source_target_pairs={{0,6},{1,7},{2,4},{3,5},{4,2},{5,3},{6,0},{7,1},{8,14},{9,15},{10,... | collective-permute-start | bytes 2359304 | tf_op jit(solution)/shard_map/ppermute | solution.py:67
  484.3 33.1 %collective-permute-start.30 = (bf16[256,1536]{1,0:T(8,128)(2,1)S(1)}, bf16[256,1536]{1,0:T(8,128)(2,1)S(1)}, u32[]{:S(2)}, u32[]{:S(2)}) collective-permute-start(bf16[256,1536]{1,0:T(8,128)(2,1)S(1)} %get-tuple-element.110), channel_id=1, source_target_pairs={{0,4},{1,5},{2,6},{3,7},{4,0},{5,1},{6,2},{7,3},{8,12},{9,13},{10,... | collective-permute-start | bytes 2359304 | tf_op jit(solution)/shard_map/ppermute | solution.py:67
  (21 other events, 124.9 us)
Sparse Core Ops, SparseCore 0:
  12.7 43.8 all-gather.8
  58.2 66.6 all-gather.6
  126.5 88.0 all-gather.10
  281.4 83.6 reduce-scatter.3
  384.6 57.9 reduce-scatter.5
  477.2 37.7 reduce-scatter.7

commit v4 on v3

--- a/solution.py
+++ b/solution.py
@@ -60,6 +60,9 @@
         self.xi = (place // 2) % 2
         self.ci = place % 2
 
+    def around(self, hop, value):
+        return lax.ppermute(value, "seq", [(n, (n + hop) % self.Z) for n in range(self.Z)])
+
     def step(self, offset, value):
         if offset == "c":
             return lax.ppermute(value, "dp", [(n, n ^ 1) for n in range(self.DP)])
@@ -95,14 +98,15 @@
     if len(refs) == 1:
         copies.append(pltpu.make_async_copy(refs[0].at[:, columns], target, sems.at[0]))
     else:
-        qi, xi, ci = meta[1], meta[2], meta[3]
+        zi, qi, xi, ci, count = meta[0], meta[1], meta[2], meta[3], target.shape[0] // (4 * lines * refs[0].shape[1])
         for ref, (j, i, l, first) in zip(refs, places):
             blocks, share, _ = ref.shape
             q = lax.rem(qi + (lines - j), lines)
             x = lax.rem(xi + i, 2)
             c = lax.rem(ci + l, 2)
             for k in range(blocks):
-                row = pl.multiple_of(((((first + k) * lines + q) * 2 + x) * 2 + c) * share, share)
+                z = lax.rem(zi + (count - first - k), count) if len(refs) == 10 else first + k
+                row = pl.multiple_of((((z * lines + q) * 2 + x) * 2 + c) * share, share)
                 copies.append(
                     pltpu.make_async_copy(
                         ref.at[k, :, columns], target.at[pl.ds(row, share), :], sems.at[len(copies)]
@@ -191,13 +195,13 @@
         copy.wait()
     gains[...] = pair_v[:, PAIR:].astype(F32).T[:8]
     gain = gains[0:1]
-    step = 256
-    for b in range(seqs * wide // step):
-        cut = slice(b * step, (b + 1) * step)
-        values = tokens[cut, : normed.shape[1]].astype(F32)
-        block = (values * inverse_rms(values) * gain).astype(BF)
-        normed[cut, :] = block
-        normed_t[:, cut] = flip(block)
+    for s in range(seqs):
+        for z in range(wide // rows):
+            cut = slice(s * wide + z * rows, s * wide + (z + 1) * rows)
+            values = tokens[z, s, :, : normed.shape[1]].astype(F32)
+            block = (values * inverse_rms(values) * gain).astype(BF)
+            normed[cut, :] = block
+            normed_t[:, cut] = flip(block)
     for s in range(seqs):
         own[s * rows : (s + 1) * rows, :] = normed[
             pl.ds(pl.multiple_of(s * wide + place * rows, 128), rows), :
@@ -259,9 +263,8 @@
 
 
 def project_forward(meta, tokens, cosine, sine, pieces, lines, width, seqs, rows):
-    count = tokens.shape[0]
-    wide = count // seqs
-    own = seqs * rows
+    wide = tokens.shape[0] * rows
+    count, own = seqs * wide, seqs * rows
     sds = jax.ShapeDtypeStruct
     return kernel_call(
         functools.partial(project_forward_body, seqs, wide, places_of(pieces), lines),
@@ -344,7 +347,7 @@
         [SMEM] + [VMEM] * 6,
         (VMEM, VMEM),
         [],
-        10 * query_t.size * wide,
+        10**12,
         12 << 20,
         (meta, query_t, pair_t, grad_t, logs, cosine, sine),
     )
@@ -352,7 +355,7 @@
 
 def output_body(places, lines, meta, tokens, mixed, gain, *refs):
     pieces, (total, second, weights_v, sems) = refs[:-4], refs[-4:]
-    for copy in load_rows(meta, places, lines, pieces, weights_v, sems, pl.ds(PAIR + 128 + QUERY, weights_v.shape[1])):
+    for copy in load_rows(meta, places, lines, pieces, weights_v, sems, pl.ds(0, weights_v.shape[1])):
         copy.wait()
     value = tokens[...].astype(F32) + mm(mixed[...], weights_v[...])
     total[...] = value
@@ -374,7 +377,7 @@
 
 def output_back_body(places, lines, split, meta, grad, total, second_grad, gain, mixed_t, *refs):
     pieces, (first_grad, mixed_grad_t, send, keep, weights_v, da, sems) = refs[:-7], refs[-7:]
-    copies = load_rows(meta, places, lines, pieces, weights_v, sems, pl.ds(PAIR + 128 + QUERY, weights_v.shape[1]))
+    copies = load_rows(meta, places, lines, pieces, weights_v, sems, pl.ds(0, weights_v.shape[1]))
     value = total[...]
     inverse = inverse_rms(value)
     back = second_grad[...]
@@ -501,45 +504,41 @@
     )
 
 
-def ffn_sums_body(count, units, *refs):
-    tokens_of, lefts, out = refs[: 2 * count], refs[2 * count : 2 * count + 3], refs[2 * count + 3]
-    second_v, grads_v, sems = refs[2 * count + 4 :]
+def ffn_sums_body(count, units, parts, *refs):
+    tokens_of, lefts = refs[:count], refs[count : count + len(parts)]
+    out, tokens_v, sems = refs[count + len(parts) :]
     rows = tokens_of[0].shape[0]
-    copies = []
-    for i in range(count):
-        cut = pl.ds(i * rows, rows)
-        copies.append(pltpu.make_async_copy(tokens_of[i], second_v.at[cut], sems.at[0, i]))
-        copies.append(pltpu.make_async_copy(tokens_of[count + i], grads_v.at[cut], sems.at[1, i]))
+    copies = [
+        pltpu.make_async_copy(tokens_of[i], tokens_v.at[pl.ds(i * rows, rows)], sems.at[i])
+        for i in range(count)
+    ]
     for copy in copies:
         copy.start()
     for copy in copies:
         copy.wait()
-    for p, right in ((0, second_v), (1, second_v), (2, grads_v)):
+    for n, left in enumerate(lefts):
 
         def one(b, _):
             here = pl.ds(pl.multiple_of(b * units, units), units)
-            out[b, p * units : (p + 1) * units, :] = mm(lefts[p][here, :], right[...]).astype(BF)
+            out[b, n * units : (n + 1) * units, :] = mm(left[here, :], tokens_v[...]).astype(BF)
             return 0
 
         lax.fori_loop(0, out.shape[0], one, 0)
 
 
-def ffn_sums(hidden_t, gate_t, up_t, tokens_of, units):
+def ffn_sums(parts, hidden_t, gate_t, up_t, tokens_of, units, cost):
     pieces = len(tokens_of) // 2
     rows, width = tokens_of[0].shape
     total = hidden_t.shape[0]
     return kernel_call(
-        functools.partial(ffn_sums_body, pieces, units),
-        jax.ShapeDtypeStruct((total // units, 3 * units, width), BF),
-        [ANY] * (2 * pieces) + [VMEM] * 3,
+        functools.partial(ffn_sums_body, pieces, units, parts),
+        jax.ShapeDtypeStruct((total // units, len(parts) * units, width), BF),
+        [ANY] * pieces + [VMEM] * len(parts),
         VMEM,
-        [
-            pltpu.VMEM((pieces * rows, width), BF), pltpu.VMEM((pieces * rows, width), BF),
-            pltpu.SemaphoreType.DMA((2, pieces)),
-        ],
-        6 * total * pieces * rows * width,
-        22 << 20,
-        (*tokens_of, gate_t, up_t, hidden_t),
+        [pltpu.VMEM((pieces * rows, width), BF), pltpu.SemaphoreType.DMA((pieces,))],
+        cost,
+        16 << 20,
+        (*tokens_of[pieces if parts == (2,) else 0 :][:pieces], *[(gate_t, up_t, hidden_t)[p] for p in parts]),
     )
 
 
@@ -612,7 +611,7 @@
         [SMEM, VMEM, VMEM] + [ANY] * len(pieces),
         (VMEM, VMEM),
         [pltpu.VMEM((width, PAIR), BF), pltpu.VMEM((width, QUERY), BF), copies_of(pieces), copies_of(pieces)],
-        2 * width * (query_back.size + pair_back.size),
+        1,
         20 << 20,
         (meta, query_back, pair_back, *arrays_of(pieces)),
     )
@@ -667,9 +666,21 @@
     split = share % 16 == 0
     meta = jnp.stack([move.zi, move.qi, move.xi, move.ci]).astype(jnp.int32)
     near = [(j, i) for j in range(Q) for i in range(2)]
+    rounds = (Z, Q) == (4, 2)
     grad_out = out_grad.reshape(own_rows, width)
     inputs = tokens.reshape(own_rows, width)
 
+    always = lax.optimization_barrier(jnp.ones((), jnp.bool_))
+
+    def window(body, *operands):
+        shapes = jax.eval_shape(body, *operands)
+        return lax.cond(
+            always,
+            body,
+            lambda *_: jax.tree.map(lambda s: jnp.zeros(s.shape, s.dtype), shapes),
+            *operands,
+        )
+
     def over_z(value):
         return lax.all_gather(value, "seq", axis=0, tiled=False)
 
@@ -677,57 +688,125 @@
         return lax.psum_scatter(value, "seq", scatter_dimension=0, tiled=False)
 
     gains_in = jnp.pad(jnp.stack([gain_attn, gain_ffn], axis=1), ((0, 0), (0, 126)))
-    pack = over_z(jnp.concatenate([w_key, w_value, gains_in, w_query, w_output], axis=1))
+    pack0 = jnp.concatenate([w_key, w_value, gains_in, w_query], axis=1)
     places = jnp.stack([positions // 256, positions % 256], axis=-1).astype(BF)
     carried = jnp.concatenate([tokens, jnp.pad(places, ((0, 0), (0, 0), (0, 126)))], axis=-1)
-    tokens_all = over_z(carried).transpose(1, 0, 2, 3).reshape(seqs * wide, width + 128)
-    places_all = in_f32(tokens_all[:, width]) * 256 + in_f32(tokens_all[:, width + 1])
-    cosine, sine = angle_tables(places_all)
-    ffn_w = over_z(jnp.concatenate([w_gate, w_up, w_down], axis=0))
+    ffn_in = jnp.concatenate([w_gate, w_up, w_down], axis=0)
+    half = len(near)
 
     def spread(value):
-        pieces = [step((j, i), value) if j or i else value for j, i in near]
+        return tuple(step((j, i), value) if j or i else value for j, i in near)
+
+    def cores(pieces):
         return tuple(pieces) + tuple(step("c", piece) for piece in pieces)
 
-    def blocks_to(value, *held):
-        return [after(step((-j % Q, i), value[n].astype(BF)), *held) for n, (j, i) in enumerate(near) if n]
+    def added(own, other):
+        sums = [in_f32(own[n]) + in_f32(other[n]) for n in range(len(near))]
+        return sums[0], [part.astype(BF) for part in sums[1:]]
+
+    def blocks_to(blocks, *held):
+        return [after(step((-j % Q, i), block), *held) for block, (j, i) in zip(blocks, near[1:])]
 
     def total(first, parts):
         for part in parts:
             first = first + in_f32(part)
         return first
 
-    grad_spread = spread(grad_out)
-    pack = after(pack, *grad_spread)
-
-    if Q == 2:
-        at_x, at_q = step((0, 1), pack), step((1, 0), pack)
-        middle = Z // 2
-        chips = [
-            (pack, 0, 0, 0), (at_x, 0, 1, 0), (at_q, 1, 0, 0),
-            (step((0, 1), at_q[:middle]), 1, 1, 0), (step((1, 0), at_x[middle:]), 1, 1, middle),
+    def chips_of(rows):
+        return [(step((j, i), rows) if j or i else rows, j, i, 0) for j, i in near]
+
+    def everywhere(chips):
+        found = []
+        for array, j, i, z in chips:
+            found += [(array, j, i, 0, z), (step("c", array), j, i, 1, z)]
+        if split:
+            return found
+        rows = found[0][0]
+        whole = jnp.zeros((Z, Q, 2, 2) + rows.shape[1:], BF)
+        for array, j, i, l, z in found:
+            for k in range(array.shape[0]):
+                at = (z + k, (move.qi - j) % Q, (move.xi + i) % 2, (move.ci + l) % 2, 0, 0)
+                whole = lax.dynamic_update_slice(whole, array[k][None, None, None, None], at)
+        return [(whole.reshape(-1, rows.shape[-1]), 0, 0, 0, 0)]
+
+    tokens_all = over_z(carried)
+    if rounds:
+        up, down = move.around(1, pack0), move.around(-1, pack0)
+        grad_spread = spread(grad_out)
+        ffn_w = over_z(after(ffn_in, up))
+        pack = jnp.stack([pack0, up, move.around(1, up), down])
+        pack, *grad_spread = lax.optimization_barrier((pack, *grad_spread))
+
+        def round2(pack, output0):
+            return (
+                step((0, 1), pack), step((1, 0), pack), step("c", pack),
+                move.around(1, output0), move.around(-1, output0),
+            )
+
+        at_x, at_q, pack_c, output1, output3 = window(round2, pack, w_output)
+
+        def round3(at_x, at_q, output0, output1, output3):
+            corner = step((0, 1), at_q[:2]), step((1, 0), at_x[2:])
+            cores_of = step("c", at_x), step("c", at_q)
+            output2 = move.around(1, output1)
+            return corner + cores_of + (jnp.stack([output0, output1, output2, output3]),)
+
+        corner_a, corner_b, at_xc, at_qc, out_pack = window(
+            round3, at_x, at_q, w_output, output1, output3
+        )
+        pieces = [
+            (pack, 0, 0, 0, 0), (pack_c, 0, 0, 1, 0), (at_x, 0, 1, 0, 0), (at_xc, 0, 1, 1, 0),
+            (at_q, 1, 0, 0, 0), (at_qc, 1, 0, 1, 0),
+            (corner_a, 1, 1, 0, 0), (step("c", corner_a), 1, 1, 1, 0),
+            (corner_b, 1, 1, 0, 2), (step("c", corner_b), 1, 1, 1, 2),
         ]
     else:
-        chips = [(step((j, i), pack) if j or i else pack, j, i, 0) for j, i in near]
-    pieces = []
-    for array, j, i, z in chips:
-        pieces += [(array, j, i, 0, z), (step("c", array), j, i, 1, z)]
-    if not split:
-        whole = jnp.zeros((Z, Q, 2, 2) + pack.shape[1:], BF)
-        for array, j, i, l, z in pieces:
-            block = array[:, None, None, None]
-            at = (z, (move.qi - j) % Q, (move.xi + i) % 2, (move.ci + l) % 2, 0, 0)
-            whole = lax.dynamic_update_slice(whole, block, at)
-        pieces = [(whole.reshape(-1, pack.shape[-1]), 0, 0, 0, 0)]
-
-    query_t, pair_t, normed_t, gains = project_forward(
-        meta, tokens_all, cosine, sine, pieces, Q, width, seqs, rows
-    )
-    mixed, mixed_t, logs = attend_forward(meta, query_t, pair_t, seqs)
-    first_sum, second = output_forward(meta, inputs, mixed, gains, pieces, Q)
-
-    second_spread = spread(second)
-    half = len(near)
+        pack = over_z(pack0)
+        grad_spread = spread(grad_out)
+        ffn_w = over_z(ffn_in)
+        out_pack = over_z(w_output)
+        pieces = everywhere(chips_of(pack))
+
+    placed = in_f32(tokens_all[..., width]) * 256 + in_f32(tokens_all[..., width + 1])
+    cosine, sine = angle_tables(placed.transpose(1, 0, 2).reshape(seqs * wide))
+
+    if rounds:
+
+        def round4(meta, cosine, sine, out_pack, tokens_all, arrays):
+            moved = step((0, 1), out_pack), step((1, 0), out_pack)
+            found = [(array,) + piece[1:] for array, piece in zip(arrays, pieces)]
+            return moved + tuple(
+                project_forward(meta, tokens_all, cosine, sine, found, Q, width, seqs, rows)
+            )
+
+        out_x, out_q, query_t, pair_t, normed_t, gains = window(
+            round4, meta, cosine, sine, out_pack, tokens_all, arrays_of(pieces)
+        )
+
+        def round5(meta, query_t, pair_t, out_pack, out_x, out_q):
+            corner = step((0, 1), out_q[:2]), step((1, 0), out_x[2:])
+            cores_of = step("c", out_pack), step("c", out_x), step("c", out_q)
+            return corner + cores_of + tuple(attend_forward(meta, query_t, pair_t, seqs))
+
+        corner_a, corner_b, out_packc, out_xc, out_qc, mixed, mixed_t, logs = window(
+            round5, meta, query_t, pair_t, out_pack, out_x, out_q
+        )
+        out_pieces = [
+            (out_pack, 0, 0, 0, 0), (out_packc, 0, 0, 1, 0), (out_x, 0, 1, 0, 0), (out_xc, 0, 1, 1, 0),
+            (out_q, 1, 0, 0, 0), (out_qc, 1, 0, 1, 0),
+            (corner_a, 1, 1, 0, 0), (step("c", corner_a), 1, 1, 1, 0),
+            (corner_b, 1, 1, 0, 2), (step("c", corner_b), 1, 1, 1, 2),
+        ]
+    else:
+        query_t, pair_t, normed_t, gains = project_forward(
+            meta, tokens_all, cosine, sine, pieces, Q, width, seqs, rows
+        )
+        mixed, mixed_t, logs = attend_forward(meta, query_t, pair_t, seqs)
+        out_pieces = everywhere(chips_of(out_pack))
+    first_sum, second = output_forward(meta, inputs, mixed, gains, out_pieces, Q)
+    grad_spread = cores(tuple(after(piece, mixed) for piece in grad_spread))
+
+    second_spread = cores(spread(second))
     chunks, outs, backs = [], [], []
     for n in range(0, 2 * half, 8):
         tokens_of = second_spread[n : n + 8] + grad_spread[n : n + 8]
@@ -739,19 +818,33 @@
         outs = (jnp.concatenate(outs[: len(outs) // 2]), jnp.concatenate(outs[len(outs) // 2 :]))
         backs = (jnp.concatenate(backs[: len(backs) // 2]), jnp.concatenate(backs[len(backs) // 2 :]))
 
-    def own_core(parts):
-        other = step("c", parts[1])
-        return (in_f32(parts[0]) + in_f32(other)).reshape(half, own_rows, width), other
-
-    back, other = own_core(backs)
-    ffn_sum = None
-    for tokens_of, made in chunks:
-        part = ffn_sums(after(made[0], other), made[1], made[2], tokens_of, units)
-        ffn_sum = part if ffn_sum is None else in_f32(ffn_sum) + in_f32(part)
-    ffn_sum = ffn_sum.astype(BF)
-    grad_ffn = in_f32(sum_z(ffn_sum))
-    grad_gate, grad_up, grad_down = grad_ffn[:units], grad_ffn[units : 2 * units], grad_ffn[2 * units :]
-    second_grad = total(back[0], blocks_to(back, ffn_sum))
+    def joined(parts, other):
+        shape = (half, own_rows, width)
+        return added(parts[0].reshape(shape), other.reshape(shape))
+
+    def sums_over(parts, tied, cost):
+        found = None
+        for tokens_of, made in chunks:
+            part = ffn_sums(parts, after(made[0], *tied), made[1], made[2], tokens_of, units, cost)
+            found = part if found is None else in_f32(found) + in_f32(part)
+        return found.astype(BF)
+
+    down_sum = sums_over((2,), (), 10**12)
+    second_grad, blocks = joined(backs, after(step("c", backs[1]), down_sum))
+
+    def sums_beside(second_grad, blocks, made):
+        moved = blocks_to(blocks)
+        gate_sum = None
+        for (tokens_of, _), part in zip(chunks, made):
+            part = ffn_sums((0, 1), *part, tokens_of, units, 10**12)
+            gate_sum = part if gate_sum is None else in_f32(gate_sum) + in_f32(part)
+        gate_sum, moved = lax.optimization_barrier((gate_sum.astype(BF), moved))
+        return gate_sum, total(second_grad, moved)
+
+    gate_sum, second_grad = window(sums_beside, second_grad, blocks, [made for _, made in chunks])
+    grad_down = sum_z(down_sum)
+    gate_sum, grad_down = lax.optimization_barrier((gate_sum, grad_down))
+    grad_ffn = sum_z(gate_sum)
 
     def pieces_for(send, keep):
         if split:
@@ -773,24 +866,41 @@
         return cut(1 - move.ci), cut(move.ci)
 
     first_grad, mixed_grad_t, out_send, out_keep = output_backward(
-        meta, grad_out, first_sum, second_grad, gains, mixed_t, pieces, (Z, Q), split
+        meta, grad_out, first_sum, second_grad, gains, mixed_t, out_pieces, (Z, Q), split
     )
     out_send, out_keep = pieces_for(out_send, out_keep)
-    query_back, pair_back = attend_backward(meta, query_t, pair_t, mixed_grad_t, logs, cosine, sine, seqs)
-    out_keep = in_f32(out_keep) + in_f32(after(step("c", out_send), query_back))
+    out_send, out_other = lax.optimization_barrier(
+        (step("c", out_send), step("c", after(outs[1], out_keep)))
+    )
+    out_rows, blocks = added(out_keep, out_send)
+
+    def attention_beside(out_rows, blocks, meta, query_t, pair_t, mixed_grad_t, logs, cosine, sine, arrays):
+        moved = blocks_to(blocks)
+        query_back, pair_back = attend_backward(
+            meta, query_t, pair_t, mixed_grad_t, logs, cosine, sine, seqs
+        )
+        found = [(array,) + piece[1:] for array, piece in zip(arrays, pieces)]
+        query_grad, pair_grad = project_back(meta, query_back, pair_back, found, Q, width, seqs, Z)
+        query_grad, moved = lax.optimization_barrier((query_grad, moved))
+        return total(out_rows, moved).astype(BF), query_back, pair_back, query_grad, pair_grad
+
+    out_rows, query_back, pair_back, query_grad, pair_grad = window(
+        attention_beside, out_rows, blocks, meta, query_t, pair_t, mixed_grad_t, logs, cosine, sine,
+        arrays_of(pieces),
+    )
     send, keep = project_sums(meta, normed_t, query_back, pair_back, seqs, (Z, Q), split)
     send, keep = pieces_for(send, keep)
-    query_grad, pair_grad = project_back(
-        after(meta, keep), query_back, pair_back, pieces, Q, width, seqs, Z
-    )
-    out_rows = total(out_keep[0], blocks_to(out_keep, query_grad)).astype(BF)
-    keep = in_f32(keep) + in_f32(after(step("c", send), query_grad))
-    pair_grad = sum_z(after(pair_grad, grad_gate))
-    rows_of = jnp.concatenate([total(keep[0], blocks_to(keep)).astype(BF), out_rows], axis=-1)
-    sums = in_f32(sum_z(after(rows_of, pair_grad)))
+    grad_ffn, pair_grad = lax.optimization_barrier((grad_ffn, pair_grad))
+    pair_grad = sum_z(pair_grad)
+    rows_of, blocks = added(keep, step("c", send))
+    rows_of = total(rows_of, blocks_to(blocks)).astype(BF)
+    layer, blocks = joined((outs[0], None), after(out_other, rows_of))
+    layer = total(first_sum + layer, blocks_to(blocks))
+    sums = in_f32(sum_z(after(jnp.concatenate([rows_of, out_rows], axis=-1), pair_grad)))
+    layer_out = layer.astype(BF)
     in_grad = input_grad(inputs, gains, first_grad, query_grad, pair_grad)
-    layer, _ = own_core((outs[0], after(outs[1], keep)))
-    layer_out = total(first_sum + layer[0], blocks_to(layer)).astype(BF)
+    grad_ffn, grad_down = in_f32(grad_ffn), in_f32(grad_down)
+    grad_gate, grad_up = grad_ffn[:units], grad_ffn[units:]
 
     grad_key, grad_value = sums[:, :pair_width], sums[:, pair_width : 2 * pair_width]
     grad_query = sums[:, 2 * pair_width : 2 * pair_width + QUERY]

time: 544 us -> 509 us (0.936); the launches traced: 534 us -> 506 us
  waiting for transfers between devices: 273 us -> 236 us
  starting transfers between devices: 30.2 us -> 42.7 us
  local copies, waits for them, and re-layouts: 21.2 us -> 11.3 us
  other arithmetic: 38.7 us -> 46.1 us
    ppermute x22 -> x26, waiting for transfers between devices: 257 us -> 161 us  [step(): lax.ppermute(value, 'dp', [(n, n % 4 ^ 2 * i | 4 * ((n // 4 + j) % self.Q...]
    ppermute x0 -> x6, waiting for transfers between devices: none -> 52.9 us  [around(): lax.ppermute(value, 'seq', [(n, (n + hop) % self.Z) for n in range(self.Z)])]
    convert_element_type x3 -> x7, other arithmetic: 4.37 us -> 22.1 us  [the longest x4 13.8 us: added(): return (sums[0], [part.astype(BF) for part in sums[1:]])]
    another operation x4 -> x3, other arithmetic: 19.2 us -> 2.12 us  [the longest x1 1.91 us: round3(): jnp.stack([output0, output1, output2, output3])]
    ppermute x17 -> x22, waiting for transfers between devices: 7.48 us -> 22.3 us  [step(): return lax.ppermute(value, 'dp', [(n, n ^ 1) for n in range(self.DP)])]
    all_gather x3 -> x2, waiting for transfers between devices: 8.27 us -> 0.01 us  [over_z(): return lax.all_gather(value, 'seq', axis=0, tiled=False)]
    ppermute x0 -> x6, starting transfers between devices: none -> 7.69 us  [around(): lax.ppermute(value, 'seq', [(n, (n + hop) % self.Z) for n in range(self.Z)])]
    unnamed x54 -> x92, local copies, waits for them, and re-layouts: 10.8 us -> 5.09 us
  transfers between devices with their start and end apart: 45 -> 60, of which waited for: 23 -> 28; matrix products, arithmetic and copies ran while one was open for 8% -> 9% of each run, Pallas kernels for 18% -> 23%
where the time goes in v4:
time: 509 us; the launch traced here: 506 us
  waiting for transfers between devices  236 us (46%)
  Pallas kernels  154 us (30%)
  other arithmetic  46.1 us (9%)
  starting transfers between devices  42.7 us (8%)
  between operations  14.9 us (3%)
  local copies, waits for them, and re-layouts  11.3 us (2%)
    ppermute x26, waiting for transfers between devices, step(): lax.ppermute(value, 'dp', [(n, n % 4 ^ 2 * i | 4 * ((n // 4 + j) % self.Q...  161 us
    pallas_call x11, Pallas kernels, kernel_call(): pl.pallas_call(body, out_shape=out_shape, in_specs=in_specs, out_specs=ou...  154 us
    ppermute x6, waiting for transfers between devices, around(): lax.ppermute(value, 'seq', [(n, (n + hop) % self.Z) for n in range(self.Z)])  52.9 us
    ppermute x26, starting transfers between devices, step(): lax.ppermute(value, 'dp', [(n, n % 4 ^ 2 * i | 4 * ((n // 4 + j) % self.Q...  29.9 us
    ppermute x22, waiting for transfers between devices, step(): return lax.ppermute(value, 'dp', [(n, n ^ 1) for n in range(self.DP)])  22.3 us
    convert_element_type x4, other arithmetic, added(): return (sums[0], [part.astype(BF) for part in sums[1:]])  13.8 us
  transfers between devices with their start and end apart: 60, of which 28 were waited for; matrix products, arithmetic and copies ran while one was open for 9% of the time, Pallas kernels for 23%

profile of v4, /device:TPU:0, one launch (start us, length us, event | category | flops | bytes accessed | tf_op | source)
XLA Modules:
  0.0 505.6 jit_solution(17653153807768334961)
XLA Ops:
  8.2 2.2 fusion.10
  10.7 3.1 collective-permute-start.23
  14.9 8.2 %collective-permute-done.23 = bf16[48,3200]{1,0:T(8,128)(2,1)S(1)} collective-permute-done((bf16[48,3200]{1,0:T(8,128)(2,1)S(1)}, bf16[48,3200]{1,0:T(8,128)(2,1)S(1)}, u32[]{:S(2)}, u32[]{:S(2)}) %collective-permute-start.23) | collective-permute-done | bytes 307232 | tf_op jit(solution)/shard_map/ppermute | solution.py:64
  25.0 2.4 collective-permute-start.28
  28.8 24.7 %collective-permute-done.25 = bf16[48,3200]{1,0:T(8,128)(2,1)S(1)} collective-permute-done((bf16[48,3200]{1,0:T(8,128)(2,1)S(1)}, bf16[48,3200]{1,0:T(8,128)(2,1)S(1)}, u32[]{:S(2)}, u32[]{:S(2)}) %collective-permute-start.25) | collective-permute-done | bytes 307232 | tf_op jit(solution)/shard_map/ppermute | solution.py:64
  53.7 7.3 %collective-permute-done.27.refs_10_.refs_2_ = bf16[256,1536]{1,0:T(8,128)(2,1)} collective-permute-done((bf16[256,1536]{1,0:T(8,128)(2,1)S(1)}, bf16[256,1536]{1,0:T(8,128)(2,1)}, u32[]{:S(2)}, u32[]{:S(2)}) %collective-permute-start.27) | collective-permute-done | bytes 786464 | tf_op jit(solution)/shard_map/ppermute | solution.py:70
  61.1 30.7 %conditional.6 = (bf16[4,48,3200]{2,1,0:T(8,128)(2,1)}, bf16[4,48,3200]{2,1,0:T(8,128)(2,1)}, bf16[4,48,3200]{2,1,0:T(8,128)(2,1)}, bf16[48,1536]{1,0:T(8,128)(2,1)}, bf16[48,1536]{1,0:T(8,128)(2,1)}) conditional(s32[]{:T(128)} %convert_element_type.258, () %tuple.74, (bf16[4,48,3200]{2,1,0:T(8,128)(2,1)S(1)}, bf16[48,1536]{1,0:T(8,128)(2,1)S(1)}) %tuple.145), branch_computations={%region_0.1_spmd, %region_1.2_spmd} | conditional | bytes 15925488 | solution.py:677
  65.4 13.1 %collective-permute-done.4 = bf16[48,1536]{1,0:T(8,128)(2,1)} collective-permute-done((bf16[48,1536]{1,0:T(8,128)(2,1)S(1)}, bf16[48,1536]{1,0:T(8,128)(2,1)}, u32[]{:S(2)}, u32[]{:S(2)}) %collective-permute-start.4) | collective-permute-done | bytes 147488 | tf_op jit(solution)/shard_map/cond/branch_1_fun/ppermute | solution.py:64
  78.5 12.1 %collective-permute-done.1 = bf16[4,48,3200]{2,1,0:T(8,128)(2,1)} collective-permute-done((bf16[4,48,3200]{2,1,0:T(8,128)(2,1)S(1)}, bf16[4,48,3200]{2,1,0:T(8,128)(2,1)}, u32[]{:S(2)}, u32[]{:S(2)}) %collective-permute-start.1) | collective-permute-done | bytes 1228832 | tf_op jit(solution)/shard_map/cond/branch_1_fun/ppermute | solution.py:70
  91.8 19.1 %conditional.7 = (bf16[2,48,3200]{2,1,0:T(8,128)(2,1)}, bf16[2,48,3200]{2,1,0:T(8,128)(2,1)}, bf16[4,48,3200]{2,1,0:T(8,128)(2,1)}, bf16[4,48,3200]{2,1,0:T(8,128)(2,1)}, bf16[4,48,1536]{2,1,0:T(8,128)(2,1)}) conditional(s32[]{:T(128)} %convert_element_type.258, () %tuple.73, (bf16[4,48,3200]{2,1,0:T(8,128)(2,1)}, bf16[4,48,3200]{2,1,0:T(8,128)(2,1)}, ...), branch_computations={%region_2.3_spmd, %region_3.4_spmd} | conditional | flops 884736 | bytes 18972912 | solution.py:677
  97.2 6.8 %collective-permute-done.16 = bf16[48,1536]{1,0:T(8,128)(2,1)S(1)} collective-permute-done((bf16[48,1536]{1,0:T(8,128)(2,1)}, bf16[48,1536]{1,0:T(8,128)(2,1)S(1)}, u32[]{:S(2)}, u32[]{:S(2)}) %collective-permute-start.16) | collective-permute-done | bytes 147488 | tf_op jit(solution)/shard_map/cond/branch_1_fun/ppermute | solution.py:64
  106.0 3.3 collective-permute-done.13
  114.8 19.6 %conditional.8 = (bf16[4,48,1536]{2,1,0:T(8,128)(2,1)}, bf16[4,48,1536]{2,1,0:T(8,128)(2,1)}, bf16[1536,256]{1,0:T(8,128)(2,1)}, bf16[1536,1024]{1,0:T(8,128)(2,...) conditional(s32[]{:T(128)} %convert_element_type.258, () %tuple.72, (bf16[4,48,1536]{2,1,0:T(8,128)(2,1)}, ...), branch_computations={%region_4.5_spmd, %region_5.6_spmd} | conditional | flops 6039797760 | bytes 35520724 | solution.py:677
  117.1 17.3 %branch_1_fun.5 = (bf16[1536,256]{1,0:T(8,128)(2,1)}, bf16[1536,1024]{1,0:T(8,128)(2,1)S(1)}, bf16[1536,1024]{1,0:T(8,128)(2,1)}, f32[8,1536]{1,0:T(8,128)S(1)}) custom-call(s32[4]{0:T(128)S(1)} %get-tuple-element.146.meta, bf16[4,2,128,1664]{3,2,1,0:T(8,128)(2,1)} %get-tuple-element.147.tokens, f32[48,1024]{1,0:T(8,128)S(1)} %get-tuple-element.148.cosine, ...), custom_call_target="tpu_custom_call" | custom-call | flops 6039797760 | bytes 20971520 | tf_op jit(solution)/shard_map/cond/branch_1_fun/pallas_call | solution.py:85
  136.1 16.6 %conditional.9 = (bf16[2,48,1536]{2,1,0:T(8,128)(2,1)}, bf16[2,48,1536]{2,1,0:T(8,128)(2,1)}, bf16[4,48,1536]{2,1,0:T(8,128)(2,1)}, bf16[4,48,1536]{2,1,0:T(8,12...) conditional(s32[]{:T(128)} %convert_element_type.258, () %tuple.71, ...), branch_computations={%region_6.7_spmd, %region_7.8_spmd} | conditional | flops 805306368 | bytes 16908552 | solution.py:677
  140.5 12.1 %branch_1_fun.6 = (bf16[256,1536]{1,0:T(8,128)(2,1)}, bf16[1536,256]{1,0:T(8,128)(2,1)}, f32[8,2,1,256]{3,2,1,0:T(1,128)}) custom-call(s32[4]{0:T(128)S(1)} %get-tuple-element.167.meta, bf16[1536,256]{1,0:T(8,128)(2,1)} %get-tuple-element.168.query_t, bf16[1536,1024]{1,0:T(8,128)(2,1)S(1)} %get-tuple-element.169.pair_t), custom_call_target="tpu_custom_call" | custom-call | flops 805306368 | bytes 6291456 | tf_op jit(solution)/shard_map/cond/branch_1_fun/pallas_call | solution.py:85
  157.4 6.6 %shard_map.203 = (f32[256,1536]{1,0:T(8,128)}, bf16[256,1536]{1,0:T(8,128)(2,1)S(1)}) custom-call(s32[4]{0:T(128)S(1)} %pad_add_fusion.meta, bf16[256,1536]{1,0:T(8,128)(2,1)} %bitcast.58, bf16[256,1536]{1,0:T(8,128)(2,1)} %get-tuple-element.314.mixed, f32[8,1536]{1,0:T(8,128)S(1)} %get-tuple-element.315.gain, ...), custom_call_target="tpu_custom_call" | custom-call | flops 1207959552 | bytes 10485760 | tf_op jit(solution)/shard_map/pallas_call | solution.py:85
  168.1 17.3 %collective-permute-done.35.refs_3_ = bf16[256,1536]{1,0:T(8,128)(2,1)S(1)} collective-permute-done((bf16[256,1536]{1,0:T(8,128)(2,1)S(1)}, bf16[256,1536]{1,0:T(8,128)(2,1)S(1)}, u32[]{:S(2)}, u32[]{:S(2)}) %collective-permute-start.35) | collective-permute-done | bytes 786464 | tf_op jit(solution)/shard_map/ppermute | solution.py:70
  185.4 16.2 %collective-permute-done.34.refs_2_ = bf16[256,1536]{1,0:T(8,128)(2,1)S(1)} collective-permute-done((bf16[256,1536]{1,0:T(8,128)(2,1)S(1)}, bf16[256,1536]{1,0:T(8,128)(2,1)S(1)}, u32[]{:S(2)}, u32[]{:S(2)}) %collective-permute-start.34) | collective-permute-done | bytes 786464 | tf_op jit(solution)/shard_map/ppermute | solution.py:70
  205.2 37.0 %shard_map.204 = (bf16[1024,1536]{1,0:T(8,128)(2,1)}, bf16[1024,1536]{1,0:T(8,128)(2,1)}, bf16[1024,1536]{1,0:T(8,128)(2,1)}, bf16[1024,1536]{1,0:T(8,128)(2,1)}...) custom-call(bf16[256,1536]{1,0:T(8,128)(2,1)S(1)} %get-tuple-element.322.refs_0_, ...), custom_call_target="tpu_custom_call" | custom-call | flops 19327352832 | bytes 35651584 | tf_op jit(solution)/shard_map/pallas_call | solution.py:85
  242.5 9.6 %shard_map.205 = bf16[4,128,1536]{2,1,0:T(8,128)(2,1)} custom-call(bf16[256,1536]{1,0:T(8,128)(2,1)} %bitcast.63, bf16[256,1536]{1,0:T(8,128)(2,1)} %collective-permute-done.26.refs_9_.refs_1_, bf16[256,1536]{1,0:T(8,128)(2,1)} %collective-permute-done.27.refs_10_.refs_2_, bf16[256,1536]{1,0:T(8,128)(2,1)} %collective-permute-done.28.refs_11_.refs_3_, ...), custom_call_target="tpu_custom_call" | custom-call | flops 999999995904 | bytes 16777216 | tf_op jit(solution)/shard_map/pallas_call | solution.py:85
  252.2 2.7 slice_convert_fusion.1
  254.9 2.6 slice_convert_fusion
  257.4 3.4 add_convert_fusion.7
  260.9 41.5 %conditional.10 = (bf16[4,256,1536]{2,1,0:T(8,128)(2,1)}, f32[256,1536]{1,0:T(8,128)}) conditional(s32[]{:T(128)} %convert_element_type.258, () %tuple.85, (bf16[256,1536]{1,0:T(8,128)(2,1)S(1)}, bf16[256,1536]{1,0:T(8,128)(2,1)}, bf16[256,1536]{1,0:T(8,128)(2,1)}, bf16[256,1536]{1,0:T(8,128)(2,1)}, bf16[256,1536]{1,0:T(8,128)(2,1)}, ...), branch_computations={%region_8.9_spmd, %region_9.10_spmd} | conditional | flops 1000002748416 | bytes 45875392 | solution.py:677
  264.4 14.7 %branch_1_fun.7 = bf16[4,256,1536]{2,1,0:T(8,128)(2,1)} custom-call(bf16[256,1536]{1,0:T(8,128)(2,1)S(1)} %get-tuple-element.173.refs_0_, bf16[256,1536]{1,0:T(8,128)(2,1)} %get-tuple-element.174.refs_1_, bf16[256,1536]{1,0:T(8,128)(2,1)} %get-tuple-element.175.refs_2_, bf16[256,1536]{1,0:T(8,128)(2,1)} %get-tuple-element.176.refs_3_, ...), custom_call_target="tpu_custom_call" | custom-call | flops 999999995904 | bytes 16777216 | tf_op jit(solution)/shard_map/cond/branch_1_fun/pallas_call | solution.py:85
  279.1 2.5 collective-permute-done.17
  281.6 17.5 %collective-permute-done.18 = bf16[256,1536]{1,0:T(8,128)(2,1)} collective-permute-done((bf16[256,1536]{1,0:T(8,128)(2,1)}, bf16[256,1536]{1,0:T(8,128)(2,1)}, u32[]{:S(2)}, u32[]{:S(2)}) %collective-permute-start.18) | collective-permute-done | bytes 786464 | tf_op jit(solution)/shard_map/cond/branch_1_fun/ppermute | solution.py:70
  299.1 3.3 convert_add_fusion
  303.1 10.2 %shard_map.206 = (f32[256,1536]{1,0:T(8,128)}, bf16[1536,256]{1,0:T(8,128)(2,1)}, bf16[4,4,48,1664]{3,2,1,0:T(8,128)(2,1)}, bf16[4,4,48,1664]{3,2,1,0:T(8,128)(2,1)}) custom-call(s32[4]{0:T(128)S(1)} %copy-done.38, bf16[256,1536]{1,0:T(8,128)(2,1)} %bitcast.64, f32[256,1536]{1,0:T(8,128)} %get-tuple-element.321.total, ...), custom_call_target="tpu_custom_call" | custom-call | flops 2415919104 | bytes 23068672 | tf_op jit(solution)/shard_map/pallas_call | solution.py:85
  313.9 9.0 %collective-permute-done.45 = bf16[4,4,48,1664]{3,2,1,0:T(8,128)(2,1)S(1)} collective-permute-done((bf16[4,4,48,1664]{3,2,1,0:T(8,128)(2,1)}, bf16[4,4,48,1664]{3,2,1,0:T(8,128)(2,1)S(1)}, u32[]{:S(2)}, u32[]{:S(2)}) %collective-permute-start.45) | collective-permute-done | bytes 2555936 | tf_op jit(solution)/shard_map/ppermute | solution.py:68
  323.1 3.7 add_convert_fusion.10
  326.8 36.0 %conditional.11 = (bf16[4,48,1664]{2,1,0:T(8,128)(2,1)}, bf16[1536,256]{1,0:T(8,128)(2,1)}, bf16[1536,1024]{1,0:T(8,128)(2,1)}, f32[1536,256]{1,0:T(8,128)}, bf16[4,1536,256]{2,1,0:T(8,128)(2,1)}) conditional(s32[]{:T(128)} %convert_element_type.258, () %tuple.90, (bf16[4,4,48,1664]{3,2,1,0:T(8,128)(2,1)}, bf16[4,4,48,1664]{3,2,1,0:T(8,128)(2,1)}, ...), branch_computations={%region_10.11_spmd, %region_11.12_spmd} | conditional | flops 1000003207168 | bytes 47513788 | solution.py:677
  330.4 14.7 %branch_1_fun.8 = (bf16[1536,256]{1,0:T(8,128)(2,1)}, bf16[1536,1024]{1,0:T(8,128)(2,1)}) custom-call(s32[4]{0:T(128)S(1)} %get-tuple-element.194.meta, bf16[1536,256]{1,0:T(8,128)(2,1)} %get-tuple-element.195.query_t, bf16[1536,1024]{1,0:T(8,128)(2,1)S(1)} %get-tuple-element.196.pair_t, bf16[1536,256]{1,0:T(8,128)(2,1)} %get-tuple-element.197.grad_t, ...), custom_call_target="tpu_custom_call" | custom-call | flops 999999995904 | bytes 12582912 | tf_op jit(solution)/shard_map/cond/branch_1_fun/pallas_call | solution.py:85
  345.0 14.6 %branch_1_fun.9 = (f32[1536,256]{1,0:T(8,128)}, bf16[4,1536,256]{2,1,0:T(8,128)(2,1)}) custom-call(s32[4]{0:T(128)S(1)} %get-tuple-element.194.meta, bf16[1536,256]{1,0:T(8,128)(2,1)} %get-tuple-element.453.query_back, bf16[1536,1024]{1,0:T(8,128)(2,1)} %get-tuple-element.454.pair_back, bf16[4,48,3200]{2,1,0:T(8,128)(2,1)} %get-tuple-element.203.refs_0_, ...), custom_call_target="tpu_custom_call" | custom-call | flops 1 | bytes 20971520 | tf_op jit(solution)/shard_map/cond/branch_1_fun/pallas_call | solution.py:85
  359.7 3.1 fusion.2
  362.8 13.2 %shard_map.207 = (bf16[4,4,48,3072]{3,2,1,0:T(8,128)(2,1)}, bf16[4,4,48,3072]{3,2,1,0:T(8,128)(2,1)}) custom-call(s32[4]{0:T(128)S(1)} %copy-done.38, bf16[1536,1024]{1,0:T(8,128)(2,1)} %get-tuple-element.346.normed_t, bf16[1536,256]{1,0:T(8,128)(2,1)} %get-tuple-element.350.query_back, bf16[1536,1024]{1,0:T(8,128)(2,1)} %get-tuple-element.351.pair_back), custom_call_target="tpu_custom_call" | custom-call | flops 6039797760 | bytes 27262976 | tf_op jit(solution)/shard_map/pallas_call | solution.py:85
  376.3 8.0 %collective-permute-done.47 = bf16[4,4,48,3072]{3,2,1,0:T(8,128)(2,1)} collective-permute-done((bf16[4,4,48,3072]{3,2,1,0:T(8,128)(2,1)}, bf16[4,4,48,3072]{3,2,1,0:T(8,128)(2,1)}, u32[]{:S(2)}, u32[]{:S(2)}) %collective-permute-start.47) | collective-permute-done | bytes 4718624 | tf_op jit(solution)/shard_map/ppermute | solution.py:68
  384.2 4.4 fusion.7
  392.2 25.3 %collective-permute-done.48 = bf16[4,48,3072]{2,1,0:T(8,128)(2,1)S(1)} collective-permute-done((bf16[4,48,3072]{2,1,0:T(8,128)(2,1)S(1)}, bf16[4,48,3072]{2,1,0:T(8,128)(2,1)S(1)}, u32[]{:S(2)}, u32[]{:S(2)}) %collective-permute-start.48) | collective-permute-done | bytes 1179680 | tf_op jit(solution)/shard_map/ppermute | solution.py:70
  417.5 24.8 %collective-permute-done.50 = bf16[4,48,3072]{2,1,0:T(8,128)(2,1)S(1)} collective-permute-done((bf16[4,48,3072]{2,1,0:T(8,128)(2,1)S(1)}, bf16[4,48,3072]{2,1,0:T(8,128)(2,1)S(1)}, u32[]{:S(2)}, u32[]{:S(2)}) %collective-permute-start.50) | collective-permute-done | bytes 1179680 | tf_op jit(solution)/shard_map/ppermute | solution.py:70
  443.6 2.6 fusion.5
  446.2 2.6 pad_maximum_fusion.1
  448.8 2.3 add_convert_fusion.6
  457.0 14.7 %collective-permute-done.51 = bf16[256,1536]{1,0:T(8,128)(2,1)S(1)} collective-permute-done((bf16[256,1536]{1,0:T(8,128)(2,1)S(1)}, bf16[256,1536]{1,0:T(8,128)(2,1)S(1)}, u32[]{:S(2)}, u32[]{:S(2)}) %collective-permute-start.51) | collective-permute-done | bytes 786464 | tf_op jit(solution)/shard_map/ppermute | solution.py:70
  471.7 14.6 %collective-permute-done.53 = bf16[256,1536]{1,0:T(8,128)(2,1)S(1)} collective-permute-done((bf16[256,1536]{1,0:T(8,128)(2,1)S(1)}, bf16[256,1536]{1,0:T(8,128)(2,1)S(1)}, u32[]{:S(2)}, u32[]{:S(2)}) %collective-permute-start.53) | collective-permute-done | bytes 786464 | tf_op jit(solution)/shard_map/ppermute | solution.py:70
  487.6 2.6 add_convert_fusion.3
  490.3 4.1 shard_map.208
  (235 shorter events, 70.1 us)
Async XLA Ops:
  7.2 104.2 %all-gather.5.cloned.1.call-start = ((), (), s32[]{:S(2)}) async-start(), calls=%async_computation.8 | async-start | bytes 4259840 | tf_op jit(solution)/shard_map/all_gather | solution.py:685
  10.5 194.7 %all-gather.7.cloned.1.call-start = ((), (), s32[]{:S(2)}) async-start(), calls=%async_computation.9 | async-start | bytes 5898240 | tf_op jit(solution)/shard_map/all_gather | solution.py:685
  23.1 279.2 %reduce-scatter.5.cloned.1.call-start = ((), (), s32[]{:S(2)}) async-start(), calls=%async_computation.4 | async-start | bytes 1966080 | tf_op jit(solution)/shard_map/reduce_scatter | solution.py:688
  23.2 30.3 %collective-permute-start.25 = (bf16[48,3200]{1,0:T(8,128)(2,1)S(1)}, bf16[48,3200]{1,0:T(8,128)(2,1)S(1)}, u32[]{:S(2)}, u32[]{:S(2)}) collective-permute-start(bf16[48,3200]{1,0:T(8,128)(2,1)S(1)} %fusion.14), channel_id=1, source_target_pairs={{0,24},{8,0},{16,8},{24,16},{1,25},{9,1},{17,9},{25,17},{2,26},{10... | collective-permute-start | bytes 921608 | tf_op jit(solution)/shard_map/ppermute | solution.py:64
  25.0 28.7 %collective-permute-start.28 = (bf16[256,1536]{1,0:T(8,128)(2,1)S(1)}, bf16[256,1536]{1,0:T(8,128)(2,1)}, u32[]{:S(2)}, u32[]{:S(2)}) collective-permute-start(bf16[256,1536]{1,0:T(8,128)(2,1)S(1)} %bitcast.65), channel_id=1, source_target_pairs={{0,6},{1,7},{2,4},{3,5},{4,2},{5,3},{6,0},{7,1},{8,14},{9,15},{10,... | collective-permute-start | bytes 2359304 | tf_op jit(solution)/shard_map/ppermute | solution.py:70
  27.4 33.5 %collective-permute-start.27 = (bf16[256,1536]{1,0:T(8,128)(2,1)S(1)}, bf16[256,1536]{1,0:T(8,128)(2,1)}, u32[]{:S(2)}, u32[]{:S(2)}) collective-permute-start(bf16[256,1536]{1,0:T(8,128)(2,1)S(1)} %bitcast.66), channel_id=1, source_target_pairs={{0,4},{1,5},{2,6},{3,7},{4,0},{5,1},{6,2},{7,3},{8,12},{9,13},{10,... | collective-permute-start | bytes 2359304 | tf_op jit(solution)/shard_map/ppermute | solution.py:70
  27.9 33.1 %collective-permute-start.26 = (bf16[256,1536]{1,0:T(8,128)(2,1)S(1)}, bf16[256,1536]{1,0:T(8,128)(2,1)}, u32[]{:S(2)}, u32[]{:S(2)}) collective-permute-start(bf16[256,1536]{1,0:T(8,128)(2,1)S(1)} %bitcast.67), channel_id=1, source_target_pairs={{0,2},{1,3},{2,0},{3,1},{4,6},{5,7},{6,4},{7,5},{8,10},{9,11},{10,... | collective-permute-start | bytes 2359304 | tf_op jit(solution)/shard_map/ppermute | solution.py:70
  28.5 25.0 %collective-permute-start.24 = (bf16[48,3200]{1,0:T(8,128)(2,1)S(1)}, bf16[48,3200]{1,0:T(8,128)(2,1)S(1)}, u32[]{:S(2)}, u32[]{:S(2)}) collective-permute-start(bf16[48,3200]{1,0:T(8,128)(2,1)S(1)} %collective-permute-done.23), channel_id=1, source_target_pairs={{0,8},{8,16},{16,24},{24,0},{1,9},{9,17},{17,25},{25,1},{2,10},{10... | collective-permute-start | bytes 921608 | tf_op jit(solution)/shard_map/ppermute | solution.py:64
  61.1 17.5 %collective-permute-start.2 = (bf16[4,48,3200]{2,1,0:T(8,128)(2,1)S(1)}, bf16[4,48,3200]{2,1,0:T(8,128)(2,1)}, u32[]{:S(2)}, u32[]{:S(2)}) collective-permute-start(bf16[4,48,3200]{2,1,0:T(8,128)(2,1)S(1)} %get-tuple-element.138), channel_id=1, source_target_pairs={{0,1},{1,0},{2,3},{3,2},{4,5},{5,4},{6,7},{7,6},{8,9},{9,8},{10,11... | collective-permute-start | bytes 3686408 | tf_op jit(solution)/shard_map/cond/branch_1_fun/ppermute | solution.py:68
  61.1 29.5 %collective-permute-start.1 = (bf16[4,48,3200]{2,1,0:T(8,128)(2,1)S(1)}, bf16[4,48,3200]{2,1,0:T(8,128)(2,1)}, u32[]{:S(2)}, u32[]{:S(2)}) collective-permute-start(bf16[4,48,3200]{2,1,0:T(8,128)(2,1)S(1)} %get-tuple-element.138), channel_id=1, source_target_pairs={{0,4},{1,5},{2,6},{3,7},{4,0},{5,1},{6,2},{7,3},{8,12},{9,13},{10,... | collective-permute-start | bytes 3686408 | tf_op jit(solution)/shard_map/cond/branch_1_fun/ppermute | solution.py:70
  62.6 29.2 %collective-permute-start = (bf16[4,48,3200]{2,1,0:T(8,128)(2,1)S(1)}, bf16[4,48,3200]{2,1,0:T(8,128)(2,1)}, u32[]{:S(2)}, u32[]{:S(2)}) collective-permute-start(bf16[4,48,3200]{2,1,0:T(8,128)(2,1)S(1)} %get-tuple-element.138), channel_id=1, source_target_pairs={{0,2},{1,3},{2,0},{3,1},{4,6},{5,7},{6,4},{7,5},{8,10},{9,11},{10,... | collective-permute-start | bytes 3686408 | tf_op jit(solution)/shard_map/cond/branch_1_fun/ppermute | solution.py:70
  63.4 15.2 %collective-permute-start.4 = (bf16[48,1536]{1,0:T(8,128)(2,1)S(1)}, bf16[48,1536]{1,0:T(8,128)(2,1)}, u32[]{:S(2)}, u32[]{:S(2)}) collective-permute-start(bf16[48,1536]{1,0:T(8,128)(2,1)S(1)} %get-tuple-element.139), channel_id=1, source_target_pairs={{0,24},{8,0},{16,8},{24,16},{1,25},{9,1},{17,9},{25,17},{2,26},{10... | collective-permute-start | bytes 442376 | tf_op jit(solution)/shard_map/cond/branch_1_fun/ppermute | solution.py:64
  63.8 14.7 %collective-permute-start.3 = (bf16[48,1536]{1,0:T(8,128)(2,1)S(1)}, bf16[48,1536]{1,0:T(8,128)(2,1)}, u32[]{:S(2)}, u32[]{:S(2)}) collective-permute-start(bf16[48,1536]{1,0:T(8,128)(2,1)S(1)} %get-tuple-element.139), channel_id=1, source_target_pairs={{0,8},{8,16},{16,24},{24,0},{1,9},{9,17},{17,25},{25,1},{2,10},{10... | collective-permute-start | bytes 442376 | tf_op jit(solution)/shard_map/cond/branch_1_fun/ppermute | solution.py:64
  91.8 19.1 %collective-permute-start.15 = (bf16[4,48,3200]{2,1,0:T(8,128)(2,1)}, bf16[4,48,3200]{2,1,0:T(8,128)(2,1)}, u32[]{:S(2)}, u32[]{:S(2)}) collective-permute-start(bf16[4,48,3200]{2,1,0:T(8,128)(2,1)} %get-tuple-element.140), channel_id=1, source_target_pairs={{0,1},{1,0},{2,3},{3,2},{4,5},{5,4},{6,7},{7,6},{8,9},{9,8},{10,11... | collective-permute-start | bytes 3686408 | tf_op jit(solution)/shard_map/cond/branch_1_fun/ppermute | solution.py:68
  91.8 19.1 %collective-permute-start.14 = (bf16[4,48,3200]{2,1,0:T(8,128)(2,1)}, bf16[4,48,3200]{2,1,0:T(8,128)(2,1)}, u32[]{:S(2)}, u32[]{:S(2)}) collective-permute-start(bf16[4,48,3200]{2,1,0:T(8,128)(2,1)} %get-tuple-element.141), channel_id=1, source_target_pairs={{0,1},{1,0},{2,3},{3,2},{4,5},{5,4},{6,7},{7,6},{8,9},{9,8},{10,11... | collective-permute-start | bytes 3686408 | tf_op jit(solution)/shard_map/cond/branch_1_fun/ppermute | solution.py:68
  93.4 15.9 %collective-permute-start.13 = (bf16[2,48,3200]{2,1,0:T(8,128)(2,1)S(1)}, bf16[2,48,3200]{2,1,0:T(8,128)(2,1)}, u32[]{:S(2)}, u32[]{:S(2)}) collective-permute-start(bf16[2,48,3200]{2,1,0:T(8,128)(2,1)S(1)} %slice.112), channel_id=1, source_target_pairs={{0,4},{1,5},{2,6},{3,7},{4,0},{5,1},{6,2},{7,3},{8,12},{9,13},{10,... | collective-permute-start | bytes 1843208 | tf_op jit(solution)/shard_map/cond/branch_1_fun/ppermute | solution.py:70
  95.2 15.7 %collective-permute-start.12 = (bf16[2,48,3200]{2,1,0:T(8,128)(2,1)S(1)}, bf16[2,48,3200]{2,1,0:T(8,128)(2,1)}, u32[]{:S(2)}, u32[]{:S(2)}) collective-permute-start(bf16[2,48,3200]{2,1,0:T(8,128)(2,1)S(1)} %slice.111), channel_id=1, source_target_pairs={{0,2},{1,3},{2,0},{3,1},{4,6},{5,7},{6,4},{7,5},{8,10},{9,11},{10,... | collective-permute-start | bytes 1843208 | tf_op jit(solution)/shard_map/cond/branch_1_fun/ppermute | solution.py:70
  114.8 19.6 %collective-permute-start.6 = (bf16[4,48,1536]{2,1,0:T(8,128)(2,1)}, bf16[4,48,1536]{2,1,0:T(8,128)(2,1)}, u32[]{:S(2)}, u32[]{:S(2)}) collective-permute-start(bf16[4,48,1536]{2,1,0:T(8,128)(2,1)} %get-tuple-element.145), channel_id=1, source_target_pairs={{0,4},{1,5},{2,6},{3,7},{4,0},{5,1},{6,2},{7,3},{8,12},{9,13},{10,... | collective-permute-start | bytes 1769480 | tf_op jit(solution)/shard_map/cond/branch_1_fun/ppermute | solution.py:70
  116.3 18.1 %collective-permute-start.5 = (bf16[4,48,1536]{2,1,0:T(8,128)(2,1)}, bf16[4,48,1536]{2,1,0:T(8,128)(2,1)}, u32[]{:S(2)}, u32[]{:S(2)}) collective-permute-start(bf16[4,48,1536]{2,1,0:T(8,128)(2,1)} %get-tuple-element.145), channel_id=1, source_target_pairs={{0,2},{1,3},{2,0},{3,1},{4,6},{5,7},{6,4},{7,5},{8,10},{9,11},{10,... | collective-permute-start | bytes 1769480 | tf_op jit(solution)/shard_map/cond/branch_1_fun/ppermute | solution.py:70
  136.1 16.6 %collective-permute-start.9 = (bf16[4,48,1536]{2,1,0:T(8,128)(2,1)}, bf16[4,48,1536]{2,1,0:T(8,128)(2,1)}, u32[]{:S(2)}, u32[]{:S(2)}) collective-permute-start(bf16[4,48,1536]{2,1,0:T(8,128)(2,1)} %get-tuple-element.166), channel_id=1, source_target_pairs={{0,1},{1,0},{2,3},{3,2},{4,5},{5,4},{6,7},{7,6},{8,9},{9,8},{10,11... | collective-permute-start | bytes 1769480 | tf_op jit(solution)/shard_map/cond/branch_1_fun/ppermute | solution.py:68
  136.1 16.6 %collective-permute-start.11 = (bf16[4,48,1536]{2,1,0:T(8,128)(2,1)}, bf16[4,48,1536]{2,1,0:T(8,128)(2,1)}, u32[]{:S(2)}, u32[]{:S(2)}) collective-permute-start(bf16[4,48,1536]{2,1,0:T(8,128)(2,1)} %get-tuple-element.164), channel_id=1, source_target_pairs={{0,1},{1,0},{2,3},{3,2},{4,5},{5,4},{6,7},{7,6},{8,9},{9,8},{10,11... | collective-permute-start | bytes 1769480 | tf_op jit(solution)/shard_map/cond/branch_1_fun/ppermute | solution.py:68
  136.6 16.1 %collective-permute-start.10 = (bf16[4,48,1536]{2,1,0:T(8,128)(2,1)}, bf16[4,48,1536]{2,1,0:T(8,128)(2,1)}, u32[]{:S(2)}, u32[]{:S(2)}) collective-permute-start(bf16[4,48,1536]{2,1,0:T(8,128)(2,1)} %get-tuple-element.165), channel_id=1, source_target_pairs={{0,1},{1,0},{2,3},{3,2},{4,5},{5,4},{6,7},{7,6},{8,9},{9,8},{10,11... | collective-permute-start | bytes 1769480 | tf_op jit(solution)/shard_map/cond/branch_1_fun/ppermute | solution.py:68
  137.6 15.1 %collective-permute-start.8 = (bf16[2,48,1536]{2,1,0:T(8,128)(2,1)S(1)}, bf16[2,48,1536]{2,1,0:T(8,128)(2,1)}, u32[]{:S(2)}, u32[]{:S(2)}) collective-permute-start(bf16[2,48,1536]{2,1,0:T(8,128)(2,1)S(1)} %slice.114), channel_id=1, source_target_pairs={{0,4},{1,5},{2,6},{3,7},{4,0},{5,1},{6,2},{7,3},{8,12},{9,13},{10,... | collective-permute-start | bytes 884744 | tf_op jit(solution)/shard_map/cond/branch_1_fun/ppermute | solution.py:70
  140.0 12.7 %collective-permute-start.7 = (bf16[2,48,1536]{2,1,0:T(8,128)(2,1)S(1)}, bf16[2,48,1536]{2,1,0:T(8,128)(2,1)}, u32[]{:S(2)}, u32[]{:S(2)}) collective-permute-start(bf16[2,48,1536]{2,1,0:T(8,128)(2,1)S(1)} %slice.113), channel_id=1, source_target_pairs={{0,2},{1,3},{2,0},{3,1},{4,6},{5,7},{6,4},{7,5},{8,10},{9,11},{10,... | collective-permute-start | bytes 884744 | tf_op jit(solution)/shard_map/cond/branch_1_fun/ppermute | solution.py:70
  152.7 14.4 %collective-permute-start.40 = (bf16[256,1536]{1,0:T(8,128)(2,1)}, bf16[256,1536]{1,0:T(8,128)(2,1)}, u32[]{:S(2)}, u32[]{:S(2)}) collective-permute-start(bf16[256,1536]{1,0:T(8,128)(2,1)} %bitcast.61), channel_id=1, source_target_pairs={{0,1},{1,0},{2,3},{3,2},{4,5},{5,4},{6,7},{7,6},{8,9},{9,8},{10,11... | collective-permute-start | bytes 2359304 | tf_op jit(solution)/shard_map/ppermute | solution.py:68
  153.4 14.2 %collective-permute-start.41 = (bf16[256,1536]{1,0:T(8,128)(2,1)}, bf16[256,1536]{1,0:T(8,128)(2,1)}, u32[]{:S(2)}, u32[]{:S(2)}) collective-permute-start(bf16[256,1536]{1,0:T(8,128)(2,1)} %collective-permute-done.26.refs_9_.refs_1_), channel_id=1, source_target_pairs={{0,1},{1,0},{2,3},{3,2},{4,5},{5,4},{6,7},{7,6},{8,9},{9,8},{10,11... | collective-permute-start | bytes 2359304 | tf_op jit(solution)/shard_map/ppermute | solution.py:68
  153.8 13.8 %collective-permute-start.42 = (bf16[256,1536]{1,0:T(8,128)(2,1)}, bf16[256,1536]{1,0:T(8,128)(2,1)}, u32[]{:S(2)}, u32[]{:S(2)}) collective-permute-start(bf16[256,1536]{1,0:T(8,128)(2,1)} %collective-permute-done.27.refs_10_.refs_2_), channel_id=1, source_target_pairs={{0,1},{1,0},{2,3},{3,2},{4,5},{5,4},{6,7},{7,6},{8,9},{9,8},{10,11... | collective-permute-start | bytes 2359304 | tf_op jit(solution)/shard_map/ppermute | solution.py:68
  164.1 21.4 %collective-permute-start.35 = (bf16[256,1536]{1,0:T(8,128)(2,1)S(1)}, bf16[256,1536]{1,0:T(8,128)(2,1)S(1)}, u32[]{:S(2)}, u32[]{:S(2)}) collective-permute-start(bf16[256,1536]{1,0:T(8,128)(2,1)S(1)} %get-tuple-element.322.refs_0_), channel_id=1, source_target_pairs={{0,6},{1,7},{2,4},{3,5},{4,2},{5,3},{6,0},{7,1},{8,14},{9,15},{10,... | collective-permute-start | bytes 2359304 | tf_op jit(solution)/shard_map/ppermute | solution.py:70
  165.8 35.9 %collective-permute-start.34 = (bf16[256,1536]{1,0:T(8,128)(2,1)S(1)}, bf16[256,1536]{1,0:T(8,128)(2,1)S(1)}, u32[]{:S(2)}, u32[]{:S(2)}) collective-permute-start(bf16[256,1536]{1,0:T(8,128)(2,1)S(1)} %get-tuple-element.322.refs_0_), channel_id=1, source_target_pairs={{0,4},{1,5},{2,6},{3,7},{4,0},{5,1},{6,2},{7,3},{8,12},{9,13},{10,... | collective-permute-start | bytes 2359304 | tf_op jit(solution)/shard_map/ppermute | solution.py:70
  167.1 34.6 %collective-permute-start.33 = (bf16[256,1536]{1,0:T(8,128)(2,1)S(1)}, bf16[256,1536]{1,0:T(8,128)(2,1)S(1)}, u32[]{:S(2)}, u32[]{:S(2)}) collective-permute-start(bf16[256,1536]{1,0:T(8,128)(2,1)S(1)} %get-tuple-element.322.refs_0_), channel_id=1, source_target_pairs={{0,2},{1,3},{2,0},{3,1},{4,6},{5,7},{6,4},{7,5},{8,10},{9,11},{10,... | collective-permute-start | bytes 2359304 | tf_op jit(solution)/shard_map/ppermute | solution.py:70
  167.6 34.6 %collective-permute-start.43 = (bf16[256,1536]{1,0:T(8,128)(2,1)}, bf16[256,1536]{1,0:T(8,128)(2,1)S(1)}, u32[]{:S(2)}, u32[]{:S(2)}) collective-permute-start(bf16[256,1536]{1,0:T(8,128)(2,1)} %collective-permute-done.28.refs_11_.refs_3_), channel_id=1, source_target_pairs={{0,1},{1,0},{2,3},{3,2},{4,5},{5,4},{6,7},{7,6},{8,9},{9,8},{10,11... | collective-permute-start | bytes 2359304 | tf_op jit(solution)/shard_map/ppermute | solution.py:68
  167.6 34.6 %collective-permute-start.36 = (bf16[256,1536]{1,0:T(8,128)(2,1)S(1)}, bf16[256,1536]{1,0:T(8,128)(2,1)S(1)}, u32[]{:S(2)}, u32[]{:S(2)}) collective-permute-start(bf16[256,1536]{1,0:T(8,128)(2,1)S(1)} %get-tuple-element.322.refs_0_), channel_id=1, source_target_pairs={{0,1},{1,0},{2,3},{3,2},{4,5},{5,4},{6,7},{7,6},{8,9},{9,8},{10,11... | collective-permute-start | bytes 2359304 | tf_op jit(solution)/shard_map/ppermute | solution.py:68
  185.4 16.8 %collective-permute-start.39 = (bf16[256,1536]{1,0:T(8,128)(2,1)S(1)}, bf16[256,1536]{1,0:T(8,128)(2,1)S(1)}, u32[]{:S(2)}, u32[]{:S(2)}) collective-permute-start(bf16[256,1536]{1,0:T(8,128)(2,1)S(1)} %collective-permute-done.35.refs_3_), channel_id=1, source_target_pairs={{0,1},{1,0},{2,3},{3,2},{4,5},{5,4},{6,7},{7,6},{8,9},{9,8},{10,11... | collective-permute-start | bytes 2359304 | tf_op jit(solution)/shard_map/ppermute | solution.py:68
  252.1 123.9 %reduce-scatter.7.cloned.1.call-start = ((), (), s32[]{:S(2)}) async-start(), calls=%async_computation.5 | async-start | bytes 3932160 | tf_op jit(solution)/shard_map/reduce_scatter | solution.py:688
  260.9 20.7 %collective-permute-start.17 = (bf16[256,1536]{1,0:T(8,128)(2,1)}, bf16[256,1536]{1,0:T(8,128)(2,1)}, u32[]{:S(2)}, u32[]{:S(2)}) collective-permute-start(bf16[256,1536]{1,0:T(8,128)(2,1)} %get-tuple-element.183), channel_id=1, source_target_pairs={{0,2},{1,3},{2,0},{3,1},{4,6},{5,7},{6,4},{7,5},{8,10},{9,11},{10,... | collective-permute-start | bytes 2359304 | tf_op jit(solution)/shard_map/cond/branch_1_fun/ppermute | solution.py:70
  262.3 36.8 %collective-permute-start.18 = (bf16[256,1536]{1,0:T(8,128)(2,1)}, bf16[256,1536]{1,0:T(8,128)(2,1)}, u32[]{:S(2)}, u32[]{:S(2)}) collective-permute-start(bf16[256,1536]{1,0:T(8,128)(2,1)} %get-tuple-element.184), channel_id=1, source_target_pairs={{0,4},{1,5},{2,6},{3,7},{4,0},{5,1},{6,2},{7,3},{8,12},{9,13},{10,... | collective-permute-start | bytes 2359304 | tf_op jit(solution)/shard_map/cond/branch_1_fun/ppermute | solution.py:70
  263.0 36.1 %collective-permute-start.19 = (bf16[256,1536]{1,0:T(8,128)(2,1)}, bf16[256,1536]{1,0:T(8,128)(2,1)}, u32[]{:S(2)}, u32[]{:S(2)}) collective-permute-start(bf16[256,1536]{1,0:T(8,128)(2,1)} %get-tuple-element.185), channel_id=1, source_target_pairs={{0,6},{1,7},{2,4},{3,5},{4,2},{5,3},{6,0},{7,1},{8,14},{9,15},{10,... | collective-permute-start | bytes 2359304 | tf_op jit(solution)/shard_map/cond/branch_1_fun/ppermute | solution.py:70
  302.4 146.4 %reduce-scatter.9.cloned.1.call-start = ((), (), s32[]{:S(2)}) async-start(), calls=%async_computation.6 | async-start | bytes 3932160 | tf_op jit(solution)/shard_map/reduce_scatter | solution.py:688
  326.8 32.9 %collective-permute-start.20 = (bf16[4,48,1664]{2,1,0:T(8,128)(2,1)}, bf16[4,48,1664]{2,1,0:T(8,128)(2,1)}, u32[]{:S(2)}, u32[]{:S(2)}) collective-permute-start(bf16[4,48,1664]{2,1,0:T(8,128)(2,1)} %bitcast.5), channel_id=1, source_target_pairs={{0,2},{1,3},{2,0},{3,1},{4,6},{5,7},{6,4},{7,5},{8,10},{9,11},{10,... | collective-permute-start | bytes 1916936 | tf_op jit(solution)/shard_map/cond/branch_1_fun/ppermute | solution.py:70
  327.4 32.3 %collective-permute-start.21 = (bf16[4,48,1664]{2,1,0:T(8,128)(2,1)}, bf16[4,48,1664]{2,1,0:T(8,128)(2,1)}, u32[]{:S(2)}, u32[]{:S(2)}) collective-permute-start(bf16[4,48,1664]{2,1,0:T(8,128)(2,1)} %bitcast.6), channel_id=1, source_target_pairs={{0,4},{1,5},{2,6},{3,7},{4,0},{5,1},{6,2},{7,3},{8,12},{9,13},{10,... | collective-permute-start | bytes 1916936 | tf_op jit(solution)/shard_map/cond/branch_1_fun/ppermute | solution.py:70
  328.8 30.9 %collective-permute-start.22 = (bf16[4,48,1664]{2,1,0:T(8,128)(2,1)}, bf16[4,48,1664]{2,1,0:T(8,128)(2,1)}, u32[]{:S(2)}, u32[]{:S(2)}) collective-permute-start(bf16[4,48,1664]{2,1,0:T(8,128)(2,1)} %bitcast.7), channel_id=1, source_target_pairs={{0,6},{1,7},{2,4},{3,5},{4,2},{5,3},{6,0},{7,1},{8,14},{9,15},{10,... | collective-permute-start | bytes 1916936 | tf_op jit(solution)/shard_map/cond/branch_1_fun/ppermute | solution.py:70
  376.0 118.4 %reduce-scatter.11.cloned.1.call-start = ((), (), s32[]{:S(2)}) async-start(), calls=%async_computation.7 | async-start | bytes 2273280 | tf_op jit(solution)/shard_map/reduce_scatter | solution.py:688
  388.6 28.9 %collective-permute-start.48 = (bf16[4,48,3072]{2,1,0:T(8,128)(2,1)S(1)}, bf16[4,48,3072]{2,1,0:T(8,128)(2,1)S(1)}, u32[]{:S(2)}, u32[]{:S(2)}) collective-permute-start(bf16[4,48,3072]{2,1,0:T(8,128)(2,1)S(1)} %get-tuple-element.374), channel_id=1, source_target_pairs={{0,2},{1,3},{2,0},{3,1},{4,6},{5,7},{6,4},{7,5},{8,10},{9,11},{10,... | collective-permute-start | bytes 3538952 | tf_op jit(solution)/shard_map/ppermute | solution.py:70
  389.4 52.9 %collective-permute-start.50 = (bf16[4,48,3072]{2,1,0:T(8,128)(2,1)S(1)}, bf16[4,48,3072]{2,1,0:T(8,128)(2,1)S(1)}, u32[]{:S(2)}, u32[]{:S(2)}) collective-permute-start(bf16[4,48,3072]{2,1,0:T(8,128)(2,1)S(1)} %get-tuple-element.375), channel_id=1, source_target_pairs={{0,6},{1,7},{2,4},{3,5},{4,2},{5,3},{6,0},{7,1},{8,14},{9,15},{10,... | collective-permute-start | bytes 3538952 | tf_op jit(solution)/shard_map/ppermute | solution.py:70
  390.9 52.7 %collective-permute-start.49 = (bf16[4,48,3072]{2,1,0:T(8,128)(2,1)S(1)}, bf16[4,48,3072]{2,1,0:T(8,128)(2,1)S(1)}, u32[]{:S(2)}, u32[]{:S(2)}) collective-permute-start(bf16[4,48,3072]{2,1,0:T(8,128)(2,1)S(1)} %get-tuple-element.376), channel_id=1, source_target_pairs={{0,4},{1,5},{2,6},{3,7},{4,0},{5,1},{6,2},{7,3},{8,12},{9,13},{10,... | collective-permute-start | bytes 3538952 | tf_op jit(solution)/shard_map/ppermute | solution.py:70
  451.1 20.5 %collective-permute-start.51 = (bf16[256,1536]{1,0:T(8,128)(2,1)S(1)}, bf16[256,1536]{1,0:T(8,128)(2,1)S(1)}, u32[]{:S(2)}, u32[]{:S(2)}) collective-permute-start(bf16[256,1536]{1,0:T(8,128)(2,1)S(1)} %get-tuple-element.377), channel_id=1, source_target_pairs={{0,2},{1,3},{2,0},{3,1},{4,6},{5,7},{6,4},{7,5},{8,10},{9,11},{10,... | collective-permute-start | bytes 2359304 | tf_op jit(solution)/shard_map/ppermute | solution.py:70
  452.5 33.7 %collective-permute-start.53 = (bf16[256,1536]{1,0:T(8,128)(2,1)S(1)}, bf16[256,1536]{1,0:T(8,128)(2,1)S(1)}, u32[]{:S(2)}, u32[]{:S(2)}) collective-permute-start(bf16[256,1536]{1,0:T(8,128)(2,1)S(1)} %get-tuple-element.378), channel_id=1, source_target_pairs={{0,6},{1,7},{2,4},{3,5},{4,2},{5,3},{6,0},{7,1},{8,14},{9,15},{10,... | collective-permute-start | bytes 2359304 | tf_op jit(solution)/shard_map/ppermute | solution.py:70
  453.9 33.7 %collective-permute-start.52 = (bf16[256,1536]{1,0:T(8,128)(2,1)S(1)}, bf16[256,1536]{1,0:T(8,128)(2,1)S(1)}, u32[]{:S(2)}, u32[]{:S(2)}) collective-permute-start(bf16[256,1536]{1,0:T(8,128)(2,1)S(1)} %get-tuple-element.379), channel_id=1, source_target_pairs={{0,4},{1,5},{2,6},{3,7},{4,0},{5,1},{6,2},{7,3},{8,12},{9,13},{10,... | collective-permute-start | bytes 2359304 | tf_op jit(solution)/shard_map/ppermute | solution.py:70
  (63 other events, 762.5 us)
Sparse Core Ops, SparseCore 0:
  10.6 88.2 all-gather.4
  100.4 90.8 all-gather.6
  252.3 32.8 reduce-scatter.4
  302.5 57.3 reduce-scatter.6
  376.1 57.9 reduce-scatter.8
  448.9 36.9 reduce-scatter.10

commit v5 on v4

--- a/solution.py
+++ b/solution.py
@@ -184,21 +184,22 @@
     pieces, refs = refs[:count], refs[count:]
     (
         query_t, pair_t, normed_t, gains,
-        pair_v, query_v, normed, own, pair_sems, query_sems,
+        pair_v, query_v, gains_v, normed, own, pair_sems, query_sems, gain_sems,
     ) = refs
     place = meta[0]
     rows = own.shape[0] // seqs
     pair_width = KV_HEADS * HEAD
-    pair_copies = load_rows(meta, places, lines, pieces, pair_v, pair_sems, pl.ds(0, PAIR + 128))
+    gain_copies = load_rows(meta, places, lines, pieces, gains_v, gain_sems, pl.ds(PAIR, 128))
+    pair_copies = load_rows(meta, places, lines, pieces, pair_v, pair_sems, pl.ds(0, PAIR))
     query_copies = load_rows(meta, places, lines, pieces, query_v, query_sems, pl.ds(PAIR + 128, QUERY))
-    for copy in pair_copies:
+    for copy in gain_copies:
         copy.wait()
-    gains[...] = pair_v[:, PAIR:].astype(F32).T[:8]
+    gains[...] = gains_v[...].astype(F32).T[:8]
     gain = gains[0:1]
     for s in range(seqs):
         for z in range(wide // rows):
             cut = slice(s * wide + z * rows, s * wide + (z + 1) * rows)
-            values = tokens[z, s, :, : normed.shape[1]].astype(F32)
+            values = tokens[z, s].astype(F32)
             block = (values * inverse_rms(values) * gain).astype(BF)
             normed[cut, :] = block
             normed_t[:, cut] = flip(block)
@@ -206,13 +207,16 @@
         own[s * rows : (s + 1) * rows, :] = normed[
             pl.ds(pl.multiple_of(s * wide + place * rows, 128), rows), :
         ]
-    width = 4 * HEAD
+    for copy in pair_copies:
+        copy.wait()
+    heads = 8
+    width = heads * HEAD
     for n in range(2 * pair_width // width):
         for s in range(seqs):
             lanes = slice(s * wide, (s + 1) * wide)
             block = mm(normed[lanes, :], pair_v[:, n * width : (n + 1) * width]).T
             if (n + 1) * width <= pair_width:
-                for h in range(4):
+                for h in range(heads):
                     turned_store(
                         pair_t, n * width + h * HEAD, lanes, block[h * HEAD : (h + 1) * HEAD],
                         cosine[:, lanes], sine[:, lanes],
@@ -226,7 +230,7 @@
         for s in range(seqs):
             lanes = slice(s * rows, (s + 1) * rows)
             here = pl.ds(pl.multiple_of(s * wide + place * rows, 128), rows)
-            for h in range(4):
+            for h in range(heads):
                 turned_store(
                     query_t, n * width + h * HEAD, lanes, block[h * HEAD : (h + 1) * HEAD, lanes],
                     cosine[:, here], sine[:, here],
@@ -272,8 +276,9 @@
         [SMEM, VMEM, VMEM, VMEM] + [ANY] * len(pieces),
         (VMEM,) * 4,
         [
-            pltpu.VMEM((width, PAIR + 128), BF), pltpu.VMEM((width, QUERY), BF),
-            pltpu.VMEM((count, width), BF), pltpu.VMEM((own, width), BF), copies_of(pieces), copies_of(pieces),
+            pltpu.VMEM((width, PAIR), BF), pltpu.VMEM((width, QUERY), BF), pltpu.VMEM((width, 128), BF),
+            pltpu.VMEM((count, width), BF), pltpu.VMEM((own, width), BF),
+            copies_of(pieces), copies_of(pieces), copies_of(pieces),
         ],
         2 * count * width * PAIR + 2 * own * width * QUERY,
         20 << 20,
@@ -301,7 +306,7 @@
 
 
 def attend_backward_body(
-    seqs, wide, meta, query_t, pair_t, grad_t, logs, cosine, sine, query_back, pair_back
+    seqs, wide, meta, query_t, pair_t, grad_t, logs, cosine, sine, query_back, pair_back, pair_blocks
 ):
     place = meta[0]
     rows = query_t.shape[1] // seqs
@@ -334,6 +339,10 @@
             pair_back[pl.ds(row + pair_width, HEAD), lanes] = mm_t(
                 grads, probs.astype(BF)
             ).astype(BF)
+            for z in range(wide // rows):
+                from_z = slice(s * wide + z * rows, s * wide + (z + 1) * rows)
+                for first in (row, row + pair_width):
+                    pair_blocks[z, pl.ds(first, HEAD), mine] = pair_back[pl.ds(first, HEAD), from_z]
         return 0
 
     lax.fori_loop(0, KV_HEADS, one, 0)
@@ -343,9 +352,13 @@
     wide = pair_t.shape[1] // seqs
     return kernel_call(
         functools.partial(attend_backward_body, seqs, wide),
-        (jax.ShapeDtypeStruct(query_t.shape, BF), jax.ShapeDtypeStruct(pair_t.shape, BF)),
+        (
+            jax.ShapeDtypeStruct(query_t.shape, BF),
+            jax.ShapeDtypeStruct(pair_t.shape, BF),
+            jax.ShapeDtypeStruct((pair_t.shape[1] // query_t.shape[1], PAIR, query_t.shape[1]), BF),
+        ),
         [SMEM] + [VMEM] * 6,
-        (VMEM, VMEM),
+        (VMEM,) * 3,
         [],
         10**12,
         12 << 20,
@@ -425,61 +438,88 @@
 
 def ffn_body(count, *refs):
     second, grads, shards = refs[:count], refs[count : 2 * count], refs[2 * count]
-    out_a, out_b, back_a, back_b, hidden_t, gate_t, up_t = refs[2 * count + 1 : 2 * count + 8]
-    second_v, grads_v, weights, hidden, gate_g, up_g, sems = refs[2 * count + 8 :]
+    out_a, out_b, back_a, back_b, sums = refs[2 * count + 1 : 2 * count + 6]
+    (
+        second_v, grads_v, weights, hidden, gate_g, up_g, hidden_t, gate_t, up_t, sums_v, sems, row_sems, sum_sem,
+    ) = refs[2 * count + 6 :]
     rows = second[0].shape[0]
     blocks, units = shards.shape[0], shards.shape[1] // 3
-    copies = [
+    weight_copies = [
         pltpu.make_async_copy(
             shards.at[b, pl.ds(p * units, units)], weights.at[p, pl.ds(b * units, units)], sems.at[p, b]
         )
+        for p in range(3)
         for b in range(blocks)
-        for p in range(3)
     ]
+    for copy in weight_copies:
+        copy.start()
     for i in range(count):
         cut = pl.ds(i * rows, rows)
-        copies.append(pltpu.make_async_copy(second[i], second_v.at[cut], sems.at[3, i]))
-        copies.append(pltpu.make_async_copy(grads[i], grads_v.at[cut], sems.at[4, i]))
-    for copy in copies:
-        copy.start()
+        pltpu.make_async_copy(second[i], second_v.at[cut], sems.at[3, i]).start()
+        pltpu.make_async_copy(grads[i], grads_v.at[cut], sems.at[4, i]).start()
+    for copy in weight_copies:
+        copy.wait()
+    per = 2
+    step = per * rows
+
+    def one(m, _):
+        here = pl.ds(pl.multiple_of(m * step, step), step)
+        for i in range(per):
+            cut = pl.ds(pl.multiple_of((m * per + i) * rows, rows), rows)
+            pltpu.make_async_copy(second_v.at[cut], second_v.at[cut], sems.at[3, m * per + i]).wait()
+            pltpu.make_async_copy(grads_v.at[cut], grads_v.at[cut], sems.at[4, m * per + i]).wait()
+        gate = mm_t(second_v[here, :], weights[0])
+        up = mm_t(second_v[here, :], weights[1])
+        hidden_grad = mm_t(grads_v[here, :], weights[2])
+        sigma = jax.nn.sigmoid(gate)
+        silu = gate * sigma
+        mixed = silu * up
+        hidden[here, :] = mixed.astype(BF)
+        hidden_t[:, here] = mixed.T.astype(BF)
+        gate_grad = hidden_grad * up * (sigma + silu * (1.0 - sigma))
+        gate_g[here, :] = gate_grad.astype(BF)
+        gate_t[:, here] = gate_grad.T.astype(BF)
+        up_grad = hidden_grad * silu
+        up_g[here, :] = up_grad.astype(BF)
+        up_t[:, here] = up_grad.T.astype(BF)
+        return 0
+
+    lax.fori_loop(0, count // per, one, 0)
+
+    width = second_v.shape[1]
+    for n, (left, right) in enumerate(((gate_t, second_v), (up_t, second_v), (hidden_t, grads_v))):
+        for c in range(width // step):
+            cut = slice(c * step, (c + 1) * step)
+            part = mm(left[...], right[:, cut]).astype(BF)
+            for b in range(blocks):
+                sums_v[b, n * units : (n + 1) * units, cut] = part[b * units : (b + 1) * units]
+    sum_copy = pltpu.make_async_copy(sums_v, sums, sum_sem)
+    sum_copy.start()
+
+    half = count * rows // 2
+    copies = []
+    for n, (kind, first, target) in enumerate(
+        (("b", half, back_b), ("b", 0, back_a), ("o", half, out_b), ("o", 0, out_a))
+    ):
+        place = second_v if kind == "b" else grads_v
+        for k in range(half // step):
+            here = slice(first + k * step, first + (k + 1) * step)
+            if kind == "b":
+                value = mm(gate_g[here, :], weights[0]) + mm(up_g[here, :], weights[1])
+            else:
+                value = mm(hidden[here, :], weights[2])
+            place[here, :] = value.astype(BF)
+            copies.append(
+                pltpu.make_async_copy(
+                    place.at[pl.ds(first + k * step, step)],
+                    target.at[pl.ds(k * step, step)],
+                    row_sems.at[n, k],
+                )
+            )
+            copies[-1].start()
+    sum_copy.wait()
     for copy in copies:
         copy.wait()
-    step = 256
-    total = blocks * units
-    for n in range(total // step):
-        cut = slice(n * step, (n + 1) * step)
-        gate_w, up_w, down_w = weights[0, cut], weights[1, cut], weights[2, cut]
-
-        def one(m, _):
-            here = pl.ds(pl.multiple_of(m * step, step), step)
-            gate = mm_t(second_v[here, :], gate_w)
-            up = mm_t(second_v[here, :], up_w)
-            hidden_grad = mm_t(grads_v[here, :], down_w)
-            sigma = jax.nn.sigmoid(gate)
-            mixed = gate * sigma * up
-            hidden[here, cut] = mixed.astype(BF)
-            hidden_t[cut, here] = mixed.T.astype(BF)
-            gate_grad = hidden_grad * up * sigma * (1.0 + gate * (1.0 - sigma))
-            gate_g[here, cut] = gate_grad.astype(BF)
-            gate_t[cut, here] = gate_grad.T.astype(BF)
-            up_grad = hidden_grad * (gate * sigma)
-            up_g[here, cut] = up_grad.astype(BF)
-            up_t[cut, here] = up_grad.T.astype(BF)
-            return 0
-
-        lax.fori_loop(0, count * rows // step, one, 0)
-
-    half = count * rows // 2
-    for first, out, back in ((0, out_a, back_a), (half, out_b, back_b)):
-
-        def two(m, _):
-            to = pl.ds(pl.multiple_of(m * step, step), step)
-            here = pl.ds(pl.multiple_of(first + m * step, step), step)
-            back[to, :] = (mm(gate_g[here, :], weights[0]) + mm(up_g[here, :], weights[1])).astype(back.dtype)
-            out[to, :] = mm(hidden[here, :], weights[2]).astype(out.dtype)
-            return 0
-
-        lax.fori_loop(0, half // step, two, 0)
 
 
 def ffn(tokens_of, weights):
@@ -489,56 +529,22 @@
     sds = jax.ShapeDtypeStruct
     return kernel_call(
         functools.partial(ffn_body, pieces),
-        (sds((count // 2, width), BF),) * 4 + (sds((total, count), BF),) * 3,
+        (sds((count // 2, width), BF),) * 4 + (sds(weights.shape, BF),),
         [ANY] * (2 * pieces + 1),
-        (VMEM,) * 7,
+        (ANY,) * 5,
         [
             pltpu.VMEM((count, width), BF), pltpu.VMEM((count, width), BF),
             pltpu.VMEM((3, total, width), BF),
             pltpu.VMEM((count, total), BF), pltpu.VMEM((count, total), BF), pltpu.VMEM((count, total), BF),
+            pltpu.VMEM((total, count), BF), pltpu.VMEM((total, count), BF), pltpu.VMEM((total, count), BF),
+            pltpu.VMEM(weights.shape, BF),
             pltpu.SemaphoreType.DMA((5, max(weights.shape[0], pieces))),
+            pltpu.SemaphoreType.DMA((4, max(count // 2 // (2 * rows), 1))),
+            pltpu.SemaphoreType.DMA,
         ],
-        12 * count * total * width,
+        18 * count * total * width,
         34 << 20,
         (*tokens_of, weights),
-    )
-
-
-def ffn_sums_body(count, units, parts, *refs):
-    tokens_of, lefts = refs[:count], refs[count : count + len(parts)]
-    out, tokens_v, sems = refs[count + len(parts) :]
-    rows = tokens_of[0].shape[0]
-    copies = [
-        pltpu.make_async_copy(tokens_of[i], tokens_v.at[pl.ds(i * rows, rows)], sems.at[i])
-        for i in range(count)
-    ]
-    for copy in copies:
-        copy.start()
-    for copy in copies:
-        copy.wait()
-    for n, left in enumerate(lefts):
-
-        def one(b, _):
-            here = pl.ds(pl.multiple_of(b * units, units), units)
-            out[b, n * units : (n + 1) * units, :] = mm(left[here, :], tokens_v[...]).astype(BF)
-            return 0
-
-        lax.fori_loop(0, out.shape[0], one, 0)
-
-
-def ffn_sums(parts, hidden_t, gate_t, up_t, tokens_of, units, cost):
-    pieces = len(tokens_of) // 2
-    rows, width = tokens_of[0].shape
-    total = hidden_t.shape[0]
-    return kernel_call(
-        functools.partial(ffn_sums_body, pieces, units, parts),
-        jax.ShapeDtypeStruct((total // units, len(parts) * units, width), BF),
-        [ANY] * pieces + [VMEM] * len(parts),
-        VMEM,
-        [pltpu.VMEM((pieces * rows, width), BF), pltpu.SemaphoreType.DMA((pieces,))],
-        cost,
-        16 << 20,
-        (*tokens_of[pieces if parts == (2,) else 0 :][:pieces], *[(gate_t, up_t, hidden_t)[p] for p in parts]),
     )
 
 
@@ -569,56 +575,22 @@
         [SMEM, VMEM, VMEM, VMEM],
         (VMEM,) * 2,
         [],
-        2 * width * (query_back.size + pair_back.size),
+        1,
         26 << 20,
         (meta, normed_t, query_back, pair_back),
     )
 
 
-def project_back_body(seqs, places, lines, meta, query_back, pair_back, *refs):
-    count = len(places)
-    pieces, refs = refs[:count], refs[count:]
-    query_grad, pair_grad, pair_v, query_v, pair_sems, query_sems = refs
+def input_grad_body(places, lines, meta, tokens, gain, first_grad, query_back, pair_back, *refs):
+    pieces, (out, pair_v, query_v, pair_sems, query_sems) = refs[: len(places)], refs[len(places) :]
+    query_copies = load_rows(meta, places, lines, pieces, query_v, query_sems, pl.ds(PAIR + 128, QUERY))
     pair_copies = load_rows(meta, places, lines, pieces, pair_v, pair_sems, pl.ds(0, PAIR))
-    query_copies = load_rows(meta, places, lines, pieces, query_v, query_sems, pl.ds(PAIR + 128, QUERY))
-    blocks, _, own = pair_grad.shape
-    rows = own // seqs
-    wide = pair_back.shape[1] // seqs
-    step = 512
+    for copy in query_copies:
+        copy.wait()
+    back = mm(query_v[...], query_back[...])
     for copy in pair_copies:
         copy.wait()
-    for n in range(pair_v.shape[0] // step):
-        cut = slice(n * step, (n + 1) * step)
-        for s in range(seqs):
-            part = mm(pair_v[cut, :], pair_back[:, s * wide : (s + 1) * wide])
-            for z in range(blocks):
-                pair_grad[z, cut, s * rows : (s + 1) * rows] = part[:, z * rows : (z + 1) * rows].astype(BF)
-    for copy in query_copies:
-        copy.wait()
-    for n in range(query_v.shape[0] // step):
-        cut = slice(n * step, (n + 1) * step)
-        query_grad[cut, :] = mm(query_v[cut, :], query_back[...])
-
-
-def project_back(meta, query_back, pair_back, pieces, lines, width, seqs, blocks):
-    own = query_back.shape[1]
-    return kernel_call(
-        functools.partial(project_back_body, seqs, places_of(pieces), lines),
-        (
-            jax.ShapeDtypeStruct((width, own), F32),
-            jax.ShapeDtypeStruct((blocks, width, own), BF),
-        ),
-        [SMEM, VMEM, VMEM] + [ANY] * len(pieces),
-        (VMEM, VMEM),
-        [pltpu.VMEM((width, PAIR), BF), pltpu.VMEM((width, QUERY), BF), copies_of(pieces), copies_of(pieces)],
-        1,
-        20 << 20,
-        (meta, query_back, pair_back, *arrays_of(pieces)),
-    )
-
-
-def input_grad_body(tokens, gain, first_grad, query_grad, pair_grad, out):
-    back = (query_grad[...] + pair_grad[...].astype(F32)).T
+    back = (back + mm(pair_v[...], pair_back[...])).T
     value = tokens[...].astype(F32)
     inverse = inverse_rms(value)
     scaled = back * gain[0:1]
@@ -629,16 +601,19 @@
     ).astype(BF)
 
 
-def input_grad(tokens, gain, first_grad, query_grad, pair_grad):
+def input_grad(meta, tokens, gain, first_grad, query_back, pair_back, pieces, lines):
+    width = tokens.shape[1]
     return kernel_call(
-        input_grad_body,
+        functools.partial(input_grad_body, places_of(pieces), lines),
         jax.ShapeDtypeStruct(tokens.shape, BF),
-        [VMEM] * 5,
+        [SMEM] + [VMEM] * 5 + [ANY] * len(pieces),
         VMEM,
-        [],
-        tokens.size * 20,
-        8 << 20,
-        (tokens, gain, first_grad, query_grad, pair_grad),
+        [
+            pltpu.VMEM((width, PAIR), BF), pltpu.VMEM((width, QUERY), BF), copies_of(pieces), copies_of(pieces),
+        ],
+        2 * width * (query_back.size + pair_back.size),
+        14 << 20,
+        (meta, tokens, gain, first_grad, query_back, pair_back, *arrays_of(pieces)),
     )
 
 
@@ -687,10 +662,13 @@
     def sum_z(value):
         return lax.psum_scatter(value, "seq", scatter_dimension=0, tiled=False)
 
-    gains_in = jnp.pad(jnp.stack([gain_attn, gain_ffn], axis=1), ((0, 0), (0, 126)))
+    columns = -(-own_rows // share)
+    spots = jnp.pad(positions.reshape(own_rows), (0, columns * share - own_rows)).reshape(share, columns)
+    gains_in = jnp.concatenate(
+        [gain_attn[:, None], gain_ffn[:, None], (spots // 256).astype(BF), (spots % 256).astype(BF)], axis=1
+    )
+    gains_in = jnp.pad(gains_in, ((0, 0), (0, 126 - 2 * columns)))
     pack0 = jnp.concatenate([w_key, w_value, gains_in, w_query], axis=1)
-    places = jnp.stack([positions // 256, positions % 256], axis=-1).astype(BF)
-    carried = jnp.concatenate([tokens, jnp.pad(places, ((0, 0), (0, 0), (0, 126)))], axis=-1)
     ffn_in = jnp.concatenate([w_gate, w_up, w_down], axis=0)
     half = len(near)
 
@@ -700,9 +678,11 @@
     def cores(pieces):
         return tuple(pieces) + tuple(step("c", piece) for piece in pieces)
 
-    def added(own, other):
-        sums = [in_f32(own[n]) + in_f32(other[n]) for n in range(len(near))]
-        return sums[0], [part.astype(BF) for part in sums[1:]]
+    def to_send(own, other):
+        return [(in_f32(own[n]) + in_f32(other[n])).astype(BF) for n in range(1, half)]
+
+    def halves(parts):
+        return [part.reshape(half, own_rows, width) for part in parts]
 
     def blocks_to(blocks, *held):
         return [after(step((-j % Q, i), block), *held) for block, (j, i) in zip(blocks, near[1:])]
@@ -729,13 +709,25 @@
                 whole = lax.dynamic_update_slice(whole, array[k][None, None, None, None], at)
         return [(whole.reshape(-1, rows.shape[-1]), 0, 0, 0, 0)]
 
-    tokens_all = over_z(carried)
     if rounds:
-        up, down = move.around(1, pack0), move.around(-1, pack0)
-        grad_spread = spread(grad_out)
-        ffn_w = over_z(after(ffn_in, up))
-        pack = jnp.stack([pack0, up, move.around(1, up), down])
-        pack, *grad_spread = lax.optimization_barrier((pack, *grad_spread))
+        def round0(pack0, grad_out):
+            return (
+                move.around(1, pack0), move.around(-1, pack0), step((0, 1), grad_out), step((1, 0), grad_out)
+            )
+
+        up, down, grad_x, grad_q = window(round0, pack0, grad_out)
+        carried, ffn_in, up, down = lax.optimization_barrier((tokens, ffn_in, up, down))
+        tokens_all = over_z(carried)
+        ffn_w = over_z(ffn_in)
+
+        def round1(pack0, up, down, grad_x, grad_q):
+            middle = own_rows // 2
+            far = move.around(1, up)
+            corner = step((0, 1), grad_q[:middle]), step((1, 0), grad_x[middle:])
+            return jnp.stack([pack0, up, far, down]), jnp.concatenate(corner)
+
+        pack, grad_xq = window(round1, pack0, up, down, grad_x, grad_q)
+        grad_spread = (grad_out, grad_x, grad_q, grad_xq)
 
         def round2(pack, output0):
             return (
@@ -761,14 +753,21 @@
             (corner_b, 1, 1, 0, 2), (step("c", corner_b), 1, 1, 1, 2),
         ]
     else:
+        tokens_all = over_z(tokens)
         pack = over_z(pack0)
         grad_spread = spread(grad_out)
         ffn_w = over_z(ffn_in)
         out_pack = over_z(w_output)
         pieces = everywhere(chips_of(pack))
 
-    placed = in_f32(tokens_all[..., width]) * 256 + in_f32(tokens_all[..., width + 1])
-    cosine, sine = angle_tables(placed.transpose(1, 0, 2).reshape(seqs * wide))
+    spots = in_f32(pack[:, :, 2 * pair_width + 2 : 2 * pair_width + 2 + 2 * columns])
+    spots = (spots[..., :columns] * 256 + spots[..., columns:]).reshape(Z, -1)[:, :own_rows]
+    if rounds:
+        order = (move.zi - jnp.arange(Z)) % Z
+        spots = jnp.sum(jnp.where((order[:, None] == jnp.arange(Z)[None])[..., None], spots[None], 0), axis=1)
+    cosine, sine = angle_tables(
+        spots.reshape(Z, seqs, rows).transpose(1, 0, 2).reshape(seqs * wide)
+    )
 
     if rounds:
 
@@ -807,44 +806,23 @@
     grad_spread = cores(tuple(after(piece, mixed) for piece in grad_spread))
 
     second_spread = cores(spread(second))
-    chunks, outs, backs = [], [], []
+    outs, backs, ffn_sum = [], [], None
     for n in range(0, 2 * half, 8):
-        tokens_of = second_spread[n : n + 8] + grad_spread[n : n + 8]
-        *parts, hidden_t, gate_t, up_t = ffn(tokens_of, ffn_w)
-        chunks.append((tokens_of, (hidden_t, gate_t, up_t)))
+        *parts, sums = ffn(second_spread[n : n + 8] + grad_spread[n : n + 8], ffn_w)
         outs += parts[:2]
         backs += parts[2:]
+        ffn_sum = sums if ffn_sum is None else in_f32(ffn_sum) + in_f32(sums)
     if len(outs) > 2:
         outs = (jnp.concatenate(outs[: len(outs) // 2]), jnp.concatenate(outs[len(outs) // 2 :]))
         backs = (jnp.concatenate(backs[: len(backs) // 2]), jnp.concatenate(backs[len(backs) // 2 :]))
-
-    def joined(parts, other):
-        shape = (half, own_rows, width)
-        return added(parts[0].reshape(shape), other.reshape(shape))
-
-    def sums_over(parts, tied, cost):
-        found = None
-        for tokens_of, made in chunks:
-            part = ffn_sums(parts, after(made[0], *tied), made[1], made[2], tokens_of, units, cost)
-            found = part if found is None else in_f32(found) + in_f32(part)
-        return found.astype(BF)
-
-    down_sum = sums_over((2,), (), 10**12)
-    second_grad, blocks = joined(backs, after(step("c", backs[1]), down_sum))
-
-    def sums_beside(second_grad, blocks, made):
-        moved = blocks_to(blocks)
-        gate_sum = None
-        for (tokens_of, _), part in zip(chunks, made):
-            part = ffn_sums((0, 1), *part, tokens_of, units, 10**12)
-            gate_sum = part if gate_sum is None else in_f32(gate_sum) + in_f32(part)
-        gate_sum, moved = lax.optimization_barrier((gate_sum.astype(BF), moved))
-        return gate_sum, total(second_grad, moved)
-
-    gate_sum, second_grad = window(sums_beside, second_grad, blocks, [made for _, made in chunks])
-    grad_down = sum_z(down_sum)
-    gate_sum, grad_down = lax.optimization_barrier((gate_sum, grad_down))
-    grad_ffn = sum_z(gate_sum)
+    grad_ffn = sum_z(ffn_sum.astype(BF))
+    back, other = halves((backs[0], step("c", backs[1])))
+
+    def second_round(first, second, blocks, out):
+        moved, out = lax.optimization_barrier((blocks_to(blocks), step("c", out)))
+        return total(in_f32(first) + in_f32(second), moved), out
+
+    second_grad, out_other = window(second_round, back[0], other[0], to_send(back, other), outs[1])
 
     def pieces_for(send, keep):
         if split:
@@ -869,38 +847,37 @@
         meta, grad_out, first_sum, second_grad, gains, mixed_t, out_pieces, (Z, Q), split
     )
     out_send, out_keep = pieces_for(out_send, out_keep)
-    out_send, out_other = lax.optimization_barrier(
-        (step("c", out_send), step("c", after(outs[1], out_keep)))
-    )
-    out_rows, blocks = added(out_keep, out_send)
-
-    def attention_beside(out_rows, blocks, meta, query_t, pair_t, mixed_grad_t, logs, cosine, sine, arrays):
+    out_send = step("c", out_send)
+    blocks = to_send(out_keep, out_send)
+
+    def attention_beside(first, second, blocks, meta, query_t, pair_t, mixed_grad_t, logs, cosine, sine, normed_t):
         moved = blocks_to(blocks)
-        query_back, pair_back = attend_backward(
+        query_back, pair_back, pair_blocks = attend_backward(
             meta, query_t, pair_t, mixed_grad_t, logs, cosine, sine, seqs
         )
-        found = [(array,) + piece[1:] for array, piece in zip(arrays, pieces)]
-        query_grad, pair_grad = project_back(meta, query_back, pair_back, found, Q, width, seqs, Z)
-        query_grad, moved = lax.optimization_barrier((query_grad, moved))
-        return total(out_rows, moved).astype(BF), query_back, pair_back, query_grad, pair_grad
-
-    out_rows, query_back, pair_back, query_grad, pair_grad = window(
-        attention_beside, out_rows, blocks, meta, query_t, pair_t, mixed_grad_t, logs, cosine, sine,
-        arrays_of(pieces),
-    )
-    send, keep = project_sums(meta, normed_t, query_back, pair_back, seqs, (Z, Q), split)
+        send, keep = project_sums(meta, normed_t, query_back, pair_back, seqs, (Z, Q), split)
+        keep, moved = lax.optimization_barrier((keep, moved))
+        out_rows = total(in_f32(first) + in_f32(second), moved).astype(BF)
+        return out_rows, query_back, pair_blocks, send, keep
+
+    out_rows, query_back, pair_blocks, send, keep = window(
+        attention_beside, out_keep[0], out_send[0], blocks, meta, query_t, pair_t, mixed_grad_t, logs,
+        cosine, sine, normed_t,
+    )
+    grad_ffn, pair_blocks = lax.optimization_barrier((grad_ffn, pair_blocks))
+    pair_own = sum_z(pair_blocks)
     send, keep = pieces_for(send, keep)
-    grad_ffn, pair_grad = lax.optimization_barrier((grad_ffn, pair_grad))
-    pair_grad = sum_z(pair_grad)
-    rows_of, blocks = added(keep, step("c", send))
-    rows_of = total(rows_of, blocks_to(blocks)).astype(BF)
-    layer, blocks = joined((outs[0], None), after(out_other, rows_of))
-    layer = total(first_sum + layer, blocks_to(blocks))
-    sums = in_f32(sum_z(after(jnp.concatenate([rows_of, out_rows], axis=-1), pair_grad)))
+    send = step("c", send)
+    rows_of = total(in_f32(keep[0]) + in_f32(send[0]), blocks_to(to_send(keep, send))).astype(BF)
+    out, out_other = halves((outs[0], out_other))
+    blocks = [after(block, rows_of) for block in to_send(out, out_other)]
+    rows_of, pair_own = lax.optimization_barrier((jnp.concatenate([rows_of, out_rows], axis=-1), pair_own))
+    sums = in_f32(sum_z(rows_of))
+    in_grad = input_grad(meta, inputs, gains, first_grad, query_back, pair_own, pieces, Q)
+    layer = total(first_sum + in_f32(out[0]) + in_f32(out_other[0]), blocks_to(blocks, in_grad))
     layer_out = layer.astype(BF)
-    in_grad = input_grad(inputs, gains, first_grad, query_grad, pair_grad)
-    grad_ffn, grad_down = in_f32(grad_ffn), in_f32(grad_down)
-    grad_gate, grad_up = grad_ffn[:units], grad_ffn[units:]
+    grad_ffn = in_f32(grad_ffn)
+    grad_gate, grad_up, grad_down = grad_ffn[:units], grad_ffn[units : 2 * units], grad_ffn[2 * units :]
 
     grad_key, grad_value = sums[:, :pair_width], sums[:, pair_width : 2 * pair_width]
     grad_query = sums[:, 2 * pair_width : 2 * pair_width + QUERY]

time: 509 us -> 476 us (0.935); the launches traced: 506 us -> 467 us
  Pallas kernels: 154 us -> 125 us
  waiting for transfers between devices: 236 us -> 226 us
    pallas_call x11 -> x8, Pallas kernels: 154 us -> 125 us  [kernel_call(): pl.pallas_call(body, out_shape=out_shape, in_specs=in_specs, out_specs=ou...]
    ppermute x6, waiting for transfers between devices: 52.9 us -> 43.2 us  [around(): lax.ppermute(value, 'seq', [(n, (n + hop) % self.Z) for n in range(self.Z)])]
    ppermute x26 -> x27, waiting for transfers between devices: 161 us -> 152 us  [step(): lax.ppermute(value, 'dp', [(n, n % 4 ^ 2 * i | 4 * ((n // 4 + j) % self.Q...]
    convert_element_type x4 -> x2, other arithmetic: 7.3 us -> 1.2 us  [in_f32(): return value.astype(F32)]
    all_gather x2, waiting for transfers between devices: 0.01 us -> 5.89 us  [over_z(): return lax.all_gather(value, 'seq', axis=0, tiled=False)]
    ppermute x26 -> x27, starting transfers between devices: 29.9 us -> 33.1 us  [step(): lax.ppermute(value, 'dp', [(n, n % 4 ^ 2 * i | 4 * ((n // 4 + j) % self.Q...]
    convert_element_type x6 -> x8, other arithmetic: 19.4 us -> 19.8 us  [the longest x4 14.1 us: to_send(): (in_f32(own[n]) + in_f32(other[n])).astype(BF)]
  transfers between devices with their start and end apart: 60 -> 60, of which waited for: 28 -> 31; matrix products, arithmetic and copies ran while one was open for 9% -> 9% of each run, Pallas kernels for 23% -> 19%
where the time goes in v5:
time: 476 us; the launch traced here: 467 us
  waiting for transfers between devices  226 us (47%)
  Pallas kernels  125 us (26%)
  starting transfers between devices  46.6 us (10%)
  other arithmetic  41.1 us (9%)
  between operations  14.4 us (3%)
  local copies, waits for them, and re-layouts  13.5 us (3%)
    ppermute x27, waiting for transfers between devices, step(): lax.ppermute(value, 'dp', [(n, n % 4 ^ 2 * i | 4 * ((n // 4 + j) % self.Q...  152 us
    pallas_call x8, Pallas kernels, kernel_call(): pl.pallas_call(body, out_shape=out_shape, in_specs=in_specs, out_specs=ou...  125 us
    ppermute x6, waiting for transfers between devices, around(): lax.ppermute(value, 'seq', [(n, (n + hop) % self.Z) for n in range(self.Z)])  43.2 us
    ppermute x27, starting transfers between devices, step(): lax.ppermute(value, 'dp', [(n, n % 4 ^ 2 * i | 4 * ((n // 4 + j) % self.Q...  33.1 us
    ppermute x22, waiting for transfers between devices, step(): return lax.ppermute(value, 'dp', [(n, n ^ 1) for n in range(self.DP)])  24.2 us
    convert_element_type x4, other arithmetic, to_send(): (in_f32(own[n]) + in_f32(other[n])).astype(BF)  14.1 us
  transfers between devices with their start and end apart: 60, of which 31 were waited for; matrix products, arithmetic and copies ran while one was open for 9% of the time, Pallas kernels for 19%

profile of v5, /device:TPU:0, one launch (start us, length us, event | category | flops | bytes accessed | tf_op | source)
XLA Modules:
  0.0 467.0 jit_solution(7741333648365499093)
XLA Ops:
  10.1 2.4 pad_maximum_fusion.4
  12.5 22.1 %conditional.8 = (bf16[48,3200]{1,0:T(8,128)(2,1)}, bf16[48,3200]{1,0:T(8,128)(2,1)}, bf16[256,1536]{1,0:T(8,128)(2,1)}, bf16[256,1536]{1,0:T(8,128)(2,1)}) conditional(s32[]{:T(128)} %convert_element_type.255, () %tuple.92, (bf16[48,3200]{1,0:T(8,128)(2,1)S(1)}, bf16[256,1536]{1,0:T(8,128)(2,1)S(1)}) %tuple.162), branch_computations={%region_0.1_spmd, %region_1.2_spmd} | conditional | bytes 8749248 | solution.py:652
  12.5 3.0 collective-permute-start.3
  16.9 3.6 collective-permute-start.1
  20.5 7.7 %collective-permute-done.1 = bf16[48,3200]{1,0:T(8,128)(2,1)} collective-permute-done((bf16[48,3200]{1,0:T(8,128)(2,1)S(1)}, bf16[48,3200]{1,0:T(8,128)(2,1)}, u32[]{:S(2)}, u32[]{:S(2)}) %collective-permute-start.1) | collective-permute-done | bytes 307232 | tf_op jit(solution)/shard_map/cond/branch_1_fun/ppermute | solution.py:64
  28.2 5.8 %collective-permute-done = bf16[48,3200]{1,0:T(8,128)(2,1)} collective-permute-done((bf16[48,3200]{1,0:T(8,128)(2,1)S(1)}, bf16[48,3200]{1,0:T(8,128)(2,1)}, u32[]{:S(2)}, u32[]{:S(2)}) %collective-permute-start) | collective-permute-done | bytes 307232 | tf_op jit(solution)/shard_map/cond/branch_1_fun/ppermute | solution.py:64
  35.4 13.6 %conditional.9 = (bf16[4,48,3200]{2,1,0:T(8,128)(2,1)S(1)}, bf16[256,1536]{1,0:T(8,128)(2,1)S(1)}) conditional(s32[]{:T(128)} %convert_element_type.255, () %tuple.91, (bf16[48,3200]{1,0:T(8,128)(2,1)S(1)}, bf16[48,3200]{1,0:T(8,128)(2,1)}, bf16[48,3200]{1,0:T(8,128)(2,1)}, bf16[256,1536]{1,0:T(8,128)(2,1)}, bf16[256,1536]{1,0:T(8,128)(2,1)}) %tuple.95), branch_computations={%region_2.3_spmd, %region_3.4_spmd} | conditional | flops 3416064 | bytes 9977992 | solution.py:652
  41.2 4.1 collective-permute-done.16
  49.8 30.7 %conditional.10 = (bf16[4,48,3200]{2,1,0:T(8,128)(2,1)}, bf16[4,48,3200]{2,1,0:T(8,128)(2,1)}, bf16[4,48,3200]{2,1,0:T(8,128)(2,1)}, bf16[48,1536]{1,0:T(8,128)(2,1)}, bf16[48,1536]{1,0:T(8,128)(2,1)}) conditional(s32[]{:T(128)} %convert_element_type.255, () %tuple.90, (bf16[4,48,3200]{2,1,0:T(8,128)(2,1)S(1)}, bf16[48,1536]{1,0:T(8,128)(2,1)S(1)}) %tuple.165), branch_computations={%region_4.5_spmd, %region_5.6_spmd} | conditional | bytes 15925488 | solution.py:652
  55.1 11.4 %collective-permute-done.8 = bf16[48,1536]{1,0:T(8,128)(2,1)} collective-permute-done((bf16[48,1536]{1,0:T(8,128)(2,1)S(1)}, bf16[48,1536]{1,0:T(8,128)(2,1)}, u32[]{:S(2)}, u32[]{:S(2)}) %collective-permute-start.8) | collective-permute-done | bytes 147488 | tf_op jit(solution)/shard_map/cond/branch_1_fun/ppermute | solution.py:64
  66.5 4.2 collective-permute-done.7
  70.8 8.6 %collective-permute-done.5 = bf16[4,48,3200]{2,1,0:T(8,128)(2,1)} collective-permute-done((bf16[4,48,3200]{2,1,0:T(8,128)(2,1)S(1)}, bf16[4,48,3200]{2,1,0:T(8,128)(2,1)}, u32[]{:S(2)}, u32[]{:S(2)}) %collective-permute-start.5) | collective-permute-done | bytes 1228832 | tf_op jit(solution)/shard_map/cond/branch_1_fun/ppermute | solution.py:70
  80.5 19.1 %conditional.11 = (bf16[2,48,3200]{2,1,0:T(8,128)(2,1)}, bf16[2,48,3200]{2,1,0:T(8,128)(2,1)}, bf16[4,48,3200]{2,1,0:T(8,128)(2,1)}, bf16[4,48,3200]{2,1,0:T(8,128)(2,1)}, bf16[4,48,1536]{2,1,0:T(8,128)(2,1)}) conditional(s32[]{:T(128)} %convert_element_type.255, () %tuple.89, (bf16[4,48,3200]{2,1,0:T(8,128)(2,1)}, bf16[4,48,3200]{2,1,0:T(8,128)(2,1)}, ...), branch_computations={%region_6.7_spmd, %region_7.8_spmd} | conditional | flops 884736 | bytes 18972912 | solution.py:652
  87.1 9.8 %collective-permute-done.23 = bf16[48,1536]{1,0:T(8,128)(2,1)S(1)} collective-permute-done((bf16[48,1536]{1,0:T(8,128)(2,1)}, bf16[48,1536]{1,0:T(8,128)(2,1)S(1)}, u32[]{:S(2)}, u32[]{:S(2)}) %collective-permute-start.23) | collective-permute-done | bytes 147488 | tf_op jit(solution)/shard_map/cond/branch_1_fun/ppermute | solution.py:64
  102.7 5.1 %all-gather.5.cloned.1.call-done = bf16[8,128,1536]{2,1,0:T(8,128)(2,1)} async-done(((bf16[2,128,1536]{2,1,0:T(8,128)(2,1)}), bf16[8,128,1536]{2,1,0:T(8,128)(2,1)}) %all-gather.5.cloned.1.call-update) | async-done | bytes 3145744 | tf_op jit(solution)/shard_map/all_gather | solution.py:660
  107.8 20.1 %conditional.12 = (bf16[4,48,1536]{2,1,0:T(8,128)(2,1)}, bf16[4,48,1536]{2,1,0:T(8,128)(2,1)}, bf16[1536,256]{1,0:T(8,128)(2,1)}, bf16[1536,1024]{1,0:T(8,128)(2...) conditional(s32[]{:T(128)} %convert_element_type.255, () %tuple.88, ...), branch_computations={%region_9.10_spmd, %region_10.11_spmd} | conditional | flops 6039797760 | bytes 35520724 | solution.py:652
  110.9 17.0 %branch_1_fun.4 = (bf16[1536,256]{1,0:T(8,128)(2,1)}, bf16[1536,1024]{1,0:T(8,128)(2,1)S(1)}, bf16[1536,1024]{1,0:T(8,128)(2,1)}, f32[8,1536]{1,0:T(8,128)S(1)}) custom-call(s32[4]{0:T(128)S(1)} %get-tuple-element.129.meta, bf16[4,2,128,1536]{3,2,1,0:T(8,128)(2,1)} %bitcast.75, f32[48,1024]{1,0:T(8,128)} %get-tuple-element.131.cosine, ...), custom_call_target="tpu_custom_call" | custom-call | flops 6039797760 | bytes 20971520 | tf_op jit(solution)/shard_map/cond/branch_1_fun/pallas_call | solution.py:85
  127.9 15.6 %conditional.13 = (bf16[2,48,1536]{2,1,0:T(8,128)(2,1)}, bf16[2,48,1536]{2,1,0:T(8,128)(2,1)}, bf16[4,48,1536]{2,1,0:T(8,128)(2,1)}, bf16[4,48,1536]{2,1,0:T(8,1...) conditional(s32[]{:T(128)} %convert_element_type.255, () %tuple.87, ...), branch_computations={%region_11.12_spmd, %region_12.13_spmd} | conditional | flops 805306368 | bytes 16908552 | solution.py:652
  131.3 12.2 %branch_1_fun.5 = (bf16[256,1536]{1,0:T(8,128)(2,1)}, bf16[1536,256]{1,0:T(8,128)(2,1)}, f32[8,2,1,256]{3,2,1,0:T(1,128)}) custom-call(s32[4]{0:T(128)S(1)} %get-tuple-element.150.meta, bf16[1536,256]{1,0:T(8,128)(2,1)} %get-tuple-element.151.query_t, bf16[1536,1024]{1,0:T(8,128)(2,1)S(1)} %get-tuple-element.152.pair_t), custom_call_target="tpu_custom_call" | custom-call | flops 805306368 | bytes 6291456 | tf_op jit(solution)/shard_map/cond/branch_1_fun/pallas_call | solution.py:85
  148.2 6.9 %shard_map.203 = (f32[256,1536]{1,0:T(8,128)}, bf16[256,1536]{1,0:T(8,128)(2,1)}) custom-call(s32[4]{0:T(128)S(1)} %pad_add_fusion.meta, bf16[256,1536]{1,0:T(8,128)(2,1)} %bitcast.56, bf16[256,1536]{1,0:T(8,128)(2,1)} %get-tuple-element.287.mixed, f32[8,1536]{1,0:T(8,128)S(1)} %get-tuple-element.288.gain, bf16[4,48,1536]{2,1,0:T(8,128)(2,1)} %get-tuple-element.276.refs_0_, ...), custom_call_target="tpu_custom_call" | custom-call | flops 1207959552 | bytes 10485760 | tf_op jit(solution)/shard_map/pallas_call | solution.py:85
  155.2 2.9 collective-permute-start.37
  159.2 17.5 %collective-permute-done.37.refs_3_ = bf16[256,1536]{1,0:T(8,128)(2,1)S(1)} collective-permute-done((bf16[256,1536]{1,0:T(8,128)(2,1)}, bf16[256,1536]{1,0:T(8,128)(2,1)S(1)}, u32[]{:S(2)}, u32[]{:S(2)}) %collective-permute-start.37) | collective-permute-done | bytes 786464 | tf_op jit(solution)/shard_map/ppermute | solution.py:70
  177.6 15.6 %collective-permute-done.36.refs_2_ = bf16[256,1536]{1,0:T(8,128)(2,1)S(1)} collective-permute-done((bf16[256,1536]{1,0:T(8,128)(2,1)}, bf16[256,1536]{1,0:T(8,128)(2,1)S(1)}, u32[]{:S(2)}, u32[]{:S(2)}) %collective-permute-start.36) | collective-permute-done | bytes 786464 | tf_op jit(solution)/shard_map/ppermute | solution.py:70
  197.5 38.3 %shard_map.204 = (bf16[1024,1536]{1,0:T(8,128)(2,1)}, bf16[1024,1536]{1,0:T(8,128)(2,1)}, bf16[1024,1536]{1,0:T(8,128)(2,1)}, bf16[1024,1536]{1,0:T(8,128)(2,1)}, bf16[4,384,1536]{2,1,0:T(8,128)(2,1)}) custom-call(bf16[256,1536]{1,0:T(8,128)(2,1)} %get-tuple-element.295.refs_0_, bf16[256,1536]{1,0:T(8,128)(2,1)} %copy-done.29, bf16[256,1536]{1,0:T(8,128)(2,1)} %copy-done.28, ...), custom_call_target="tpu_custom_call" | custom-call | flops 28991029248 | bytes 35651584 | tf_op jit(solution)/shard_map/pallas_call | solution.py:85
  236.0 5.9 %collective-permute-done.46 = bf16[1024,1536]{1,0:T(8,128)(2,1)S(1)} collective-permute-done((bf16[1024,1536]{1,0:T(8,128)(2,1)}, bf16[1024,1536]{1,0:T(8,128)(2,1)S(1)}, u32[]{:S(2)}, u32[]{:S(2)}) %collective-permute-start.46) | collective-permute-done | bytes 3145760 | tf_op jit(solution)/shard_map/ppermute | solution.py:68
  241.8 2.4 add_convert_fusion.7
  244.4 40.9 %conditional.14 = (f32[256,1536]{1,0:T(8,128)}, bf16[1024,1536]{1,0:T(8,128)(2,1)}) conditional(s32[]{:T(128)} %convert_element_type.255, () %tuple.104, (bf16[1024,1536]{1,0:T(8,128)(2,1)}, bf16[1024,1536]{1,0:T(8,128)(2,1)S(1)}, bf16[256,1536]{1,0:T(8,128)(2,1)S(1)}, bf16[256,1536]{1,0:T(8,128)(2,1)S(1)}, bf16[256,1536]{1,0:T(8,128)(2,1)S(1)}, ...), branch_computations={%region_13.14_spmd, %region_14.15_spmd} | conditional | flops 3538944 | bytes 27525296 | solution.py:652
  248.1 16.9 %collective-permute-done.24 = bf16[256,1536]{1,0:T(8,128)(2,1)S(1)} collective-permute-done((bf16[256,1536]{1,0:T(8,128)(2,1)S(1)}, bf16[256,1536]{1,0:T(8,128)(2,1)S(1)}, u32[]{:S(2)}, u32[]{:S(2)}) %collective-permute-start.24) | collective-permute-done | bytes 786464 | tf_op jit(solution)/shard_map/cond/branch_1_fun/ppermute | solution.py:70
  264.9 17.5 %collective-permute-done.25 = bf16[256,1536]{1,0:T(8,128)(2,1)S(1)} collective-permute-done((bf16[256,1536]{1,0:T(8,128)(2,1)S(1)}, bf16[256,1536]{1,0:T(8,128)(2,1)S(1)}, u32[]{:S(2)}, u32[]{:S(2)}) %collective-permute-start.25) | collective-permute-done | bytes 786464 | tf_op jit(solution)/shard_map/cond/branch_1_fun/ppermute | solution.py:70
  282.5 2.8 convert_add_fusion
  285.3 10.3 %shard_map.205 = (f32[256,1536]{1,0:T(8,128)}, bf16[1536,256]{1,0:T(8,128)(2,1)}, bf16[4,4,48,1664]{3,2,1,0:T(8,128)(2,1)}, bf16[4,4,48,1664]{3,2,1,0:T(8,128)(2,1)}) custom-call(s32[4]{0:T(128)S(1)} %pad_add_fusion.meta, bf16[256,1536]{1,0:T(8,128)(2,1)} %bitcast.64, f32[256,1536]{1,0:T(8,128)} %get-tuple-element.294.total, ...), custom_call_target="tpu_custom_call" | custom-call | flops 2415919104 | bytes 23068672 | tf_op jit(solution)/shard_map/pallas_call | solution.py:85
  295.7 5.0 %collective-permute-done.47 = bf16[4,4,48,1664]{3,2,1,0:T(8,128)(2,1)S(1)} collective-permute-done((bf16[4,4,48,1664]{3,2,1,0:T(8,128)(2,1)}, bf16[4,4,48,1664]{3,2,1,0:T(8,128)(2,1)S(1)}, u32[]{:S(2)}, u32[]{:S(2)}) %collective-permute-start.47) | collective-permute-done | bytes 2555936 | tf_op jit(solution)/shard_map/ppermute | solution.py:68
  300.7 3.9 add_convert_fusion.10
  304.7 35.7 %conditional.15 = (bf16[4,48,1664]{2,1,0:T(8,128)(2,1)}, bf16[1536,256]{1,0:T(8,128)(2,1)}, bf16[4,1536,256]{2,1,0:T(8,128)(2,1)}, bf16[4,4,48,3072]{3,2,1,0:T(8,128)(2,1)}, bf16[4,4,48,3072]{3,2,1,0:T(8,128)(2,1)}) conditional(s32[]{:T(128)} %convert_element_type.255, () %tuple.106, (bf16[4,4,48,1664]{3,2,1,0:T(8,128)(2,1)}, ...), branch_computations={%region_15.16_spmd, %region_16.17_spmd} | conditional | flops 1000003207168 | bytes 51347616 | solution.py:652
  308.2 15.9 %branch_1_fun.6 = (bf16[1536,256]{1,0:T(8,128)(2,1)}, bf16[1536,1024]{1,0:T(8,128)(2,1)}, bf16[4,1536,256]{2,1,0:T(8,128)(2,1)}) custom-call(s32[4]{0:T(128)S(1)} %get-tuple-element.168.meta, bf16[1536,256]{1,0:T(8,128)(2,1)} %get-tuple-element.170.query_t, bf16[1536,1024]{1,0:T(8,128)(2,1)S(1)} %get-tuple-element.171.pair_t, ...), custom_call_target="tpu_custom_call" | custom-call | flops 999999995904 | bytes 12582912 | tf_op jit(solution)/shard_map/cond/branch_1_fun/pallas_call | solution.py:85
  324.1 13.1 %branch_1_fun.7 = (bf16[4,4,48,3072]{3,2,1,0:T(8,128)(2,1)}, bf16[4,4,48,3072]{3,2,1,0:T(8,128)(2,1)}) custom-call(s32[4]{0:T(128)S(1)} %get-tuple-element.168.meta, bf16[1536,1024]{1,0:T(8,128)(2,1)} %get-tuple-element.169.normed_t, bf16[1536,256]{1,0:T(8,128)(2,1)} %get-tuple-element.433.query_back, bf16[1536,1024]{1,0:T(8,128)(2,1)} %get-tuple-element.177.pair_back), custom_call_target="tpu_custom_call" | custom-call | flops 1 | bytes 27262976 | tf_op jit(solution)/shard_map/cond/branch_1_fun/pallas_call | solution.py:85
  337.2 3.1 fusion.2
  340.4 8.2 %collective-permute-done.48 = bf16[4,4,48,3072]{3,2,1,0:T(8,128)(2,1)} collective-permute-done((bf16[4,4,48,3072]{3,2,1,0:T(8,128)(2,1)}, bf16[4,4,48,3072]{3,2,1,0:T(8,128)(2,1)}, u32[]{:S(2)}, u32[]{:S(2)}) %collective-permute-start.48) | collective-permute-done | bytes 4718624 | tf_op jit(solution)/shard_map/ppermute | solution.py:68
  348.6 4.4 fusion.6
  356.5 25.3 %collective-permute-done.49 = bf16[4,48,3072]{2,1,0:T(8,128)(2,1)S(1)} collective-permute-done((bf16[4,48,3072]{2,1,0:T(8,128)(2,1)S(1)}, bf16[4,48,3072]{2,1,0:T(8,128)(2,1)S(1)}, u32[]{:S(2)}, u32[]{:S(2)}) %collective-permute-start.49) | collective-permute-done | bytes 1179680 | tf_op jit(solution)/shard_map/ppermute | solution.py:70
  381.8 25.5 %collective-permute-done.51 = bf16[4,48,3072]{2,1,0:T(8,128)(2,1)S(1)} collective-permute-done((bf16[4,48,3072]{2,1,0:T(8,128)(2,1)S(1)}, bf16[4,48,3072]{2,1,0:T(8,128)(2,1)S(1)}, u32[]{:S(2)}, u32[]{:S(2)}) %collective-permute-start.51) | collective-permute-done | bytes 1179680 | tf_op jit(solution)/shard_map/ppermute | solution.py:70
  408.7 2.6 fusion.5
  411.3 2.6 pad_maximum_fusion.3
  413.9 3.4 add_convert_fusion.6
  422.3 11.0 %shard_map.206 = bf16[256,1536]{1,0:T(8,128)(2,1)} custom-call(s32[4]{0:T(128)S(1)} %pad_add_fusion.meta, bf16[256,1536]{1,0:T(8,128)(2,1)} %bitcast.57, f32[8,1536]{1,0:T(8,128)S(1)} %copy-done.10, f32[256,1536]{1,0:T(8,128)} %get-tuple-element.317.first_grad, bf16[1536,256]{1,0:T(8,128)(2,1)} %get-tuple-element.318.query_back, bf16[1536,256]{1,0:T(8,128)(2,1)} %bitcast.60, ...), custom_call_target="tpu_custom_call" | custom-call | flops 2415919104 | bytes 14680064 | tf_op jit(solution)/shard_map/pallas_call | solution.py:85
  433.3 5.6 %collective-permute-done.54 = bf16[256,1536]{1,0:T(8,128)(2,1)S(1)} collective-permute-done((bf16[256,1536]{1,0:T(8,128)(2,1)}, bf16[256,1536]{1,0:T(8,128)(2,1)S(1)}, u32[]{:S(2)}, u32[]{:S(2)}) %collective-permute-start.54) | collective-permute-done | bytes 786464 | tf_op jit(solution)/shard_map/ppermute | solution.py:70
  438.9 13.8 %collective-permute-done.53 = bf16[256,1536]{1,0:T(8,128)(2,1)} collective-permute-done((bf16[256,1536]{1,0:T(8,128)(2,1)}, bf16[256,1536]{1,0:T(8,128)(2,1)}, u32[]{:S(2)}, u32[]{:S(2)}) %collective-permute-start.53) | collective-permute-done | bytes 786464 | tf_op jit(solution)/shard_map/ppermute | solution.py:70
  452.8 3.3 add_convert_fusion.3
  (206 shorter events, 73.8 us)
Async XLA Ops:
  7.2 100.6 %all-gather.5.cloned.1.call-start = ((), (), s32[]{:S(2)}) async-start(), calls=%async_computation.6 | async-start | bytes 3932160 | tf_op jit(solution)/shard_map/all_gather | solution.py:660
  12.5 21.6 %collective-permute-start.3 = (bf16[256,1536]{1,0:T(8,128)(2,1)S(1)}, bf16[256,1536]{1,0:T(8,128)(2,1)}, u32[]{:S(2)}, u32[]{:S(2)}) collective-permute-start(bf16[256,1536]{1,0:T(8,128)(2,1)S(1)} %get-tuple-element.115), channel_id=1, source_target_pairs={{0,4},{1,5},{2,6},{3,7},{4,0},{5,1},{6,2},{7,3},{8,12},{9,13},{10,... | collective-permute-start | bytes 2359304 | tf_op jit(solution)/shard_map/cond/branch_1_fun/ppermute | solution.py:70
  15.4 19.1 %collective-permute-start.2 = (bf16[256,1536]{1,0:T(8,128)(2,1)S(1)}, bf16[256,1536]{1,0:T(8,128)(2,1)}, u32[]{:S(2)}, u32[]{:S(2)}) collective-permute-start(bf16[256,1536]{1,0:T(8,128)(2,1)S(1)} %get-tuple-element.115), channel_id=1, source_target_pairs={{0,2},{1,3},{2,0},{3,1},{4,6},{5,7},{6,4},{7,5},{8,10},{9,11},{10,... | collective-permute-start | bytes 2359304 | tf_op jit(solution)/shard_map/cond/branch_1_fun/ppermute | solution.py:70
  16.9 11.3 %collective-permute-start.1 = (bf16[48,3200]{1,0:T(8,128)(2,1)S(1)}, bf16[48,3200]{1,0:T(8,128)(2,1)}, u32[]{:S(2)}, u32[]{:S(2)}) collective-permute-start(bf16[48,3200]{1,0:T(8,128)(2,1)S(1)} %get-tuple-element.114), channel_id=1, source_target_pairs={{0,24},{8,0},{16,8},{24,16},{1,25},{9,1},{17,9},{25,17},{2,26},{10... | collective-permute-start | bytes 921608 | tf_op jit(solution)/shard_map/cond/branch_1_fun/ppermute | solution.py:64
  20.5 13.6 %collective-permute-start = (bf16[48,3200]{1,0:T(8,128)(2,1)S(1)}, bf16[48,3200]{1,0:T(8,128)(2,1)}, u32[]{:S(2)}, u32[]{:S(2)}) collective-permute-start(bf16[48,3200]{1,0:T(8,128)(2,1)S(1)} %get-tuple-element.114), channel_id=1, source_target_pairs={{0,8},{8,16},{16,24},{24,0},{1,9},{9,17},{17,25},{25,1},{2,10},{10... | collective-permute-start | bytes 921608 | tf_op jit(solution)/shard_map/cond/branch_1_fun/ppermute | solution.py:64
  34.6 163.0 %all-gather.7.cloned.1.call-start = ((), (), s32[]{:S(2)}) async-start(), calls=%async_computation.7 | async-start | bytes 5898240 | tf_op jit(solution)/shard_map/all_gather | solution.py:660
  35.3 305.0 %reduce-scatter.4.cloned.1.call-start = ((), (), s32[]{:S(2)}) async-start(), calls=%async_computation.3 | async-start | bytes 5898240 | tf_op jit(solution)/shard_map/reduce_scatter | solution.py:663
  49.8 20.9 %collective-permute-start.6 = (bf16[4,48,3200]{2,1,0:T(8,128)(2,1)S(1)}, bf16[4,48,3200]{2,1,0:T(8,128)(2,1)}, u32[]{:S(2)}, u32[]{:S(2)}) collective-permute-start(bf16[4,48,3200]{2,1,0:T(8,128)(2,1)S(1)} %get-tuple-element.121), channel_id=1, source_target_pairs={{0,1},{1,0},{2,3},{3,2},{4,5},{5,4},{6,7},{7,6},{8,9},{9,8},{10,11... | collective-permute-start | bytes 3686408 | tf_op jit(solution)/shard_map/cond/branch_1_fun/ppermute | solution.py:68
  49.8 29.5 %collective-permute-start.5 = (bf16[4,48,3200]{2,1,0:T(8,128)(2,1)S(1)}, bf16[4,48,3200]{2,1,0:T(8,128)(2,1)}, u32[]{:S(2)}, u32[]{:S(2)}) collective-permute-start(bf16[4,48,3200]{2,1,0:T(8,128)(2,1)S(1)} %get-tuple-element.121), channel_id=1, source_target_pairs={{0,4},{1,5},{2,6},{3,7},{4,0},{5,1},{6,2},{7,3},{8,12},{9,13},{10,... | collective-permute-start | bytes 3686408 | tf_op jit(solution)/shard_map/cond/branch_1_fun/ppermute | solution.py:70
  51.3 29.3 %collective-permute-start.4 = (bf16[4,48,3200]{2,1,0:T(8,128)(2,1)S(1)}, bf16[4,48,3200]{2,1,0:T(8,128)(2,1)}, u32[]{:S(2)}, u32[]{:S(2)}) collective-permute-start(bf16[4,48,3200]{2,1,0:T(8,128)(2,1)S(1)} %get-tuple-element.121), channel_id=1, source_target_pairs={{0,2},{1,3},{2,0},{3,1},{4,6},{5,7},{6,4},{7,5},{8,10},{9,11},{10,... | collective-permute-start | bytes 3686408 | tf_op jit(solution)/shard_map/cond/branch_1_fun/ppermute | solution.py:70
  52.7 13.8 %collective-permute-start.8 = (bf16[48,1536]{1,0:T(8,128)(2,1)S(1)}, bf16[48,1536]{1,0:T(8,128)(2,1)}, u32[]{:S(2)}, u32[]{:S(2)}) collective-permute-start(bf16[48,1536]{1,0:T(8,128)(2,1)S(1)} %get-tuple-element.122), channel_id=1, source_target_pairs={{0,24},{8,0},{16,8},{24,16},{1,25},{9,1},{17,9},{25,17},{2,26},{10... | collective-permute-start | bytes 442376 | tf_op jit(solution)/shard_map/cond/branch_1_fun/ppermute | solution.py:64
  55.1 15.7 %collective-permute-start.7 = (bf16[48,1536]{1,0:T(8,128)(2,1)S(1)}, bf16[48,1536]{1,0:T(8,128)(2,1)}, u32[]{:S(2)}, u32[]{:S(2)}) collective-permute-start(bf16[48,1536]{1,0:T(8,128)(2,1)S(1)} %get-tuple-element.122), channel_id=1, source_target_pairs={{0,8},{8,16},{16,24},{24,0},{1,9},{9,17},{17,25},{25,1},{2,10},{10... | collective-permute-start | bytes 442376 | tf_op jit(solution)/shard_map/cond/branch_1_fun/ppermute | solution.py:64
  80.5 19.1 %collective-permute-start.22 = (bf16[4,48,3200]{2,1,0:T(8,128)(2,1)}, bf16[4,48,3200]{2,1,0:T(8,128)(2,1)}, u32[]{:S(2)}, u32[]{:S(2)}) collective-permute-start(bf16[4,48,3200]{2,1,0:T(8,128)(2,1)} %get-tuple-element.123), channel_id=1, source_target_pairs={{0,1},{1,0},{2,3},{3,2},{4,5},{5,4},{6,7},{7,6},{8,9},{9,8},{10,11... | collective-permute-start | bytes 3686408 | tf_op jit(solution)/shard_map/cond/branch_1_fun/ppermute | solution.py:68
  80.5 19.1 %collective-permute-start.21 = (bf16[4,48,3200]{2,1,0:T(8,128)(2,1)}, bf16[4,48,3200]{2,1,0:T(8,128)(2,1)}, u32[]{:S(2)}, u32[]{:S(2)}) collective-permute-start(bf16[4,48,3200]{2,1,0:T(8,128)(2,1)} %get-tuple-element.124), channel_id=1, source_target_pairs={{0,1},{1,0},{2,3},{3,2},{4,5},{5,4},{6,7},{7,6},{8,9},{9,8},{10,11... | collective-permute-start | bytes 3686408 | tf_op jit(solution)/shard_map/cond/branch_1_fun/ppermute | solution.py:68
  82.1 16.6 %collective-permute-start.20 = (bf16[2,48,3200]{2,1,0:T(8,128)(2,1)S(1)}, bf16[2,48,3200]{2,1,0:T(8,128)(2,1)}, u32[]{:S(2)}, u32[]{:S(2)}) collective-permute-start(bf16[2,48,3200]{2,1,0:T(8,128)(2,1)S(1)} %slice.126), channel_id=1, source_target_pairs={{0,4},{1,5},{2,6},{3,7},{4,0},{5,1},{6,2},{7,3},{8,12},{9,13},{10,... | collective-permute-start | bytes 1843208 | tf_op jit(solution)/shard_map/cond/branch_1_fun/ppermute | solution.py:70
  83.9 15.7 %collective-permute-start.19 = (bf16[2,48,3200]{2,1,0:T(8,128)(2,1)S(1)}, bf16[2,48,3200]{2,1,0:T(8,128)(2,1)}, u32[]{:S(2)}, u32[]{:S(2)}) collective-permute-start(bf16[2,48,3200]{2,1,0:T(8,128)(2,1)S(1)} %slice.125), channel_id=1, source_target_pairs={{0,2},{1,3},{2,0},{3,1},{4,6},{5,7},{6,4},{7,5},{8,10},{9,11},{10,... | collective-permute-start | bytes 1843208 | tf_op jit(solution)/shard_map/cond/branch_1_fun/ppermute | solution.py:70
  85.5 11.3 %collective-permute-start.23 = (bf16[48,1536]{1,0:T(8,128)(2,1)}, bf16[48,1536]{1,0:T(8,128)(2,1)S(1)}, u32[]{:S(2)}, u32[]{:S(2)}) collective-permute-start(bf16[48,1536]{1,0:T(8,128)(2,1)} %get-tuple-element.126), channel_id=1, source_target_pairs={{0,8},{8,16},{16,24},{24,0},{1,9},{9,17},{17,25},{25,1},{2,10},{10... | collective-permute-start | bytes 442376 | tf_op jit(solution)/shard_map/cond/branch_1_fun/ppermute | solution.py:64
  107.9 20.0 %collective-permute-start.10 = (bf16[4,48,1536]{2,1,0:T(8,128)(2,1)}, bf16[4,48,1536]{2,1,0:T(8,128)(2,1)}, u32[]{:S(2)}, u32[]{:S(2)}) collective-permute-start(bf16[4,48,1536]{2,1,0:T(8,128)(2,1)} %get-tuple-element.128), channel_id=1, source_target_pairs={{0,4},{1,5},{2,6},{3,7},{4,0},{5,1},{6,2},{7,3},{8,12},{9,13},{10,... | collective-permute-start | bytes 1769480 | tf_op jit(solution)/shard_map/cond/branch_1_fun/ppermute | solution.py:70
  109.4 18.5 %collective-permute-start.9 = (bf16[4,48,1536]{2,1,0:T(8,128)(2,1)}, bf16[4,48,1536]{2,1,0:T(8,128)(2,1)}, u32[]{:S(2)}, u32[]{:S(2)}) collective-permute-start(bf16[4,48,1536]{2,1,0:T(8,128)(2,1)} %get-tuple-element.128), channel_id=1, source_target_pairs={{0,2},{1,3},{2,0},{3,1},{4,6},{5,7},{6,4},{7,5},{8,10},{9,11},{10,... | collective-permute-start | bytes 1769480 | tf_op jit(solution)/shard_map/cond/branch_1_fun/ppermute | solution.py:70
  127.9 15.6 %collective-permute-start.13 = (bf16[4,48,1536]{2,1,0:T(8,128)(2,1)}, bf16[4,48,1536]{2,1,0:T(8,128)(2,1)}, u32[]{:S(2)}, u32[]{:S(2)}) collective-permute-start(bf16[4,48,1536]{2,1,0:T(8,128)(2,1)} %get-tuple-element.149), channel_id=1, source_target_pairs={{0,1},{1,0},{2,3},{3,2},{4,5},{5,4},{6,7},{7,6},{8,9},{9,8},{10,11... | collective-permute-start | bytes 1769480 | tf_op jit(solution)/shard_map/cond/branch_1_fun/ppermute | solution.py:68
  128.0 15.5 %collective-permute-start.15 = (bf16[4,48,1536]{2,1,0:T(8,128)(2,1)}, bf16[4,48,1536]{2,1,0:T(8,128)(2,1)}, u32[]{:S(2)}, u32[]{:S(2)}) collective-permute-start(bf16[4,48,1536]{2,1,0:T(8,128)(2,1)} %get-tuple-element.147), channel_id=1, source_target_pairs={{0,1},{1,0},{2,3},{3,2},{4,5},{5,4},{6,7},{7,6},{8,9},{9,8},{10,11... | collective-permute-start | bytes 1769480 | tf_op jit(solution)/shard_map/cond/branch_1_fun/ppermute | solution.py:68
  128.5 15.0 %collective-permute-start.14 = (bf16[4,48,1536]{2,1,0:T(8,128)(2,1)}, bf16[4,48,1536]{2,1,0:T(8,128)(2,1)}, u32[]{:S(2)}, u32[]{:S(2)}) collective-permute-start(bf16[4,48,1536]{2,1,0:T(8,128)(2,1)} %get-tuple-element.148), channel_id=1, source_target_pairs={{0,1},{1,0},{2,3},{3,2},{4,5},{5,4},{6,7},{7,6},{8,9},{9,8},{10,11... | collective-permute-start | bytes 1769480 | tf_op jit(solution)/shard_map/cond/branch_1_fun/ppermute | solution.py:68
  129.6 13.9 %collective-permute-start.12 = (bf16[2,48,1536]{2,1,0:T(8,128)(2,1)S(1)}, bf16[2,48,1536]{2,1,0:T(8,128)(2,1)}, u32[]{:S(2)}, u32[]{:S(2)}) collective-permute-start(bf16[2,48,1536]{2,1,0:T(8,128)(2,1)S(1)} %slice.128), channel_id=1, source_target_pairs={{0,4},{1,5},{2,6},{3,7},{4,0},{5,1},{6,2},{7,3},{8,12},{9,13},{10,... | collective-permute-start | bytes 884744 | tf_op jit(solution)/shard_map/cond/branch_1_fun/ppermute | solution.py:70
  130.8 12.7 %collective-permute-start.11 = (bf16[2,48,1536]{2,1,0:T(8,128)(2,1)S(1)}, bf16[2,48,1536]{2,1,0:T(8,128)(2,1)}, u32[]{:S(2)}, u32[]{:S(2)}) collective-permute-start(bf16[2,48,1536]{2,1,0:T(8,128)(2,1)S(1)} %slice.127), channel_id=1, source_target_pairs={{0,2},{1,3},{2,0},{3,1},{4,6},{5,7},{6,4},{7,5},{8,10},{9,11},{10,... | collective-permute-start | bytes 884744 | tf_op jit(solution)/shard_map/cond/branch_1_fun/ppermute | solution.py:70
  143.6 14.7 %collective-permute-start.42 = (bf16[256,1536]{1,0:T(8,128)(2,1)}, bf16[256,1536]{1,0:T(8,128)(2,1)}, u32[]{:S(2)}, u32[]{:S(2)}) collective-permute-start(bf16[256,1536]{1,0:T(8,128)(2,1)} %bitcast.62), channel_id=1, source_target_pairs={{0,1},{1,0},{2,3},{3,2},{4,5},{5,4},{6,7},{7,6},{8,9},{9,8},{10,11... | collective-permute-start | bytes 2359304 | tf_op jit(solution)/shard_map/ppermute | solution.py:68
  144.2 14.5 %collective-permute-start.43 = (bf16[256,1536]{1,0:T(8,128)(2,1)}, bf16[256,1536]{1,0:T(8,128)(2,1)}, u32[]{:S(2)}, u32[]{:S(2)}) collective-permute-start(bf16[256,1536]{1,0:T(8,128)(2,1)} %get-tuple-element.297.refs_9_), channel_id=1, source_target_pairs={{0,1},{1,0},{2,3},{3,2},{4,5},{5,4},{6,7},{7,6},{8,9},{9,8},{10,11... | collective-permute-start | bytes 2359304 | tf_op jit(solution)/shard_map/ppermute | solution.py:68
  144.7 14.1 %collective-permute-start.44 = (bf16[256,1536]{1,0:T(8,128)(2,1)}, bf16[256,1536]{1,0:T(8,128)(2,1)}, u32[]{:S(2)}, u32[]{:S(2)}) collective-permute-start(bf16[256,1536]{1,0:T(8,128)(2,1)} %get-tuple-element.298.refs_10_), channel_id=1, source_target_pairs={{0,1},{1,0},{2,3},{3,2},{4,5},{5,4},{6,7},{7,6},{8,9},{9,8},{10,11... | collective-permute-start | bytes 2359304 | tf_op jit(solution)/shard_map/ppermute | solution.py:68
  155.2 21.6 %collective-permute-start.37 = (bf16[256,1536]{1,0:T(8,128)(2,1)}, bf16[256,1536]{1,0:T(8,128)(2,1)S(1)}, u32[]{:S(2)}, u32[]{:S(2)}) collective-permute-start(bf16[256,1536]{1,0:T(8,128)(2,1)} %get-tuple-element.295.refs_0_), channel_id=1, source_target_pairs={{0,6},{1,7},{2,4},{3,5},{4,2},{5,3},{6,0},{7,1},{8,14},{9,15},{10,... | collective-permute-start | bytes 2359304 | tf_op jit(solution)/shard_map/ppermute | solution.py:70
  158.1 35.1 %collective-permute-start.36 = (bf16[256,1536]{1,0:T(8,128)(2,1)}, bf16[256,1536]{1,0:T(8,128)(2,1)S(1)}, u32[]{:S(2)}, u32[]{:S(2)}) collective-permute-start(bf16[256,1536]{1,0:T(8,128)(2,1)} %get-tuple-element.295.refs_0_), channel_id=1, source_target_pairs={{0,4},{1,5},{2,6},{3,7},{4,0},{5,1},{6,2},{7,3},{8,12},{9,13},{10,... | collective-permute-start | bytes 2359304 | tf_op jit(solution)/shard_map/ppermute | solution.py:70
  158.2 35.0 %collective-permute-start.35 = (bf16[256,1536]{1,0:T(8,128)(2,1)}, bf16[256,1536]{1,0:T(8,128)(2,1)S(1)}, u32[]{:S(2)}, u32[]{:S(2)}) collective-permute-start(bf16[256,1536]{1,0:T(8,128)(2,1)} %get-tuple-element.295.refs_0_), channel_id=1, source_target_pairs={{0,2},{1,3},{2,0},{3,1},{4,6},{5,7},{6,4},{7,5},{8,10},{9,11},{10,... | collective-permute-start | bytes 2359304 | tf_op jit(solution)/shard_map/ppermute | solution.py:70
  158.7 35.0 %collective-permute-start.45 = (bf16[256,1536]{1,0:T(8,128)(2,1)}, bf16[256,1536]{1,0:T(8,128)(2,1)S(1)}, u32[]{:S(2)}, u32[]{:S(2)}) collective-permute-start(bf16[256,1536]{1,0:T(8,128)(2,1)} %copy-done.12), channel_id=1, source_target_pairs={{0,1},{1,0},{2,3},{3,2},{4,5},{5,4},{6,7},{7,6},{8,9},{9,8},{10,11... | collective-permute-start | bytes 2359304 | tf_op jit(solution)/shard_map/ppermute | solution.py:68
  158.7 35.0 %collective-permute-start.38 = (bf16[256,1536]{1,0:T(8,128)(2,1)}, bf16[256,1536]{1,0:T(8,128)(2,1)S(1)}, u32[]{:S(2)}, u32[]{:S(2)}) collective-permute-start(bf16[256,1536]{1,0:T(8,128)(2,1)} %get-tuple-element.295.refs_0_), channel_id=1, source_target_pairs={{0,1},{1,0},{2,3},{3,2},{4,5},{5,4},{6,7},{7,6},{8,9},{9,8},{10,11... | collective-permute-start | bytes 2359304 | tf_op jit(solution)/shard_map/ppermute | solution.py:68
  177.6 16.1 %collective-permute-start.41 = (bf16[256,1536]{1,0:T(8,128)(2,1)S(1)}, bf16[256,1536]{1,0:T(8,128)(2,1)S(1)}, u32[]{:S(2)}, u32[]{:S(2)}) collective-permute-start(bf16[256,1536]{1,0:T(8,128)(2,1)S(1)} %collective-permute-done.37.refs_3_), channel_id=1, source_target_pairs={{0,1},{1,0},{2,3},{3,2},{4,5},{5,4},{6,7},{7,6},{8,9},{9,8},{10,11... | collective-permute-start | bytes 2359304 | tf_op jit(solution)/shard_map/ppermute | solution.py:68
  235.8 178.0 %reduce-scatter.6.cloned.1.call-start = ((), (), s32[]{:S(2)}) async-start(), calls=%async_computation.4 | async-start | bytes 3932160 | tf_op jit(solution)/shard_map/reduce_scatter | solution.py:663
  244.4 38.1 %collective-permute-start.27 = (bf16[1024,1536]{1,0:T(8,128)(2,1)S(1)}, bf16[1024,1536]{1,0:T(8,128)(2,1)}, u32[]{:S(2)}, u32[]{:S(2)}) collective-permute-start(bf16[1024,1536]{1,0:T(8,128)(2,1)S(1)} %get-tuple-element.161), channel_id=1, source_target_pairs={{0,1},{1,0},{2,3},{3,2},{4,5},{5,4},{6,7},{7,6},{8,9},{9,8},{10,11... | collective-permute-start | bytes 9437192 | tf_op jit(solution)/shard_map/cond/branch_1_fun/ppermute | solution.py:68
  244.6 20.4 %collective-permute-start.24 = (bf16[256,1536]{1,0:T(8,128)(2,1)S(1)}, bf16[256,1536]{1,0:T(8,128)(2,1)S(1)}, u32[]{:S(2)}, u32[]{:S(2)}) collective-permute-start(bf16[256,1536]{1,0:T(8,128)(2,1)S(1)} %get-tuple-element.158), channel_id=1, source_target_pairs={{0,2},{1,3},{2,0},{3,1},{4,6},{5,7},{6,4},{7,5},{8,10},{9,11},{10,... | collective-permute-start | bytes 2359304 | tf_op jit(solution)/shard_map/cond/branch_1_fun/ppermute | solution.py:70
  246.1 36.4 %collective-permute-start.25 = (bf16[256,1536]{1,0:T(8,128)(2,1)S(1)}, bf16[256,1536]{1,0:T(8,128)(2,1)S(1)}, u32[]{:S(2)}, u32[]{:S(2)}) collective-permute-start(bf16[256,1536]{1,0:T(8,128)(2,1)S(1)} %get-tuple-element.159), channel_id=1, source_target_pairs={{0,4},{1,5},{2,6},{3,7},{4,0},{5,1},{6,2},{7,3},{8,12},{9,13},{10,... | collective-permute-start | bytes 2359304 | tf_op jit(solution)/shard_map/cond/branch_1_fun/ppermute | solution.py:70
  247.6 34.9 %collective-permute-start.26 = (bf16[256,1536]{1,0:T(8,128)(2,1)S(1)}, bf16[256,1536]{1,0:T(8,128)(2,1)S(1)}, u32[]{:S(2)}, u32[]{:S(2)}) collective-permute-start(bf16[256,1536]{1,0:T(8,128)(2,1)S(1)} %get-tuple-element.160), channel_id=1, source_target_pairs={{0,6},{1,7},{2,4},{3,5},{4,2},{5,3},{6,0},{7,1},{8,14},{9,15},{10,... | collective-permute-start | bytes 2359304 | tf_op jit(solution)/shard_map/cond/branch_1_fun/ppermute | solution.py:70
  304.7 32.5 %collective-permute-start.28 = (bf16[4,48,1664]{2,1,0:T(8,128)(2,1)}, bf16[4,48,1664]{2,1,0:T(8,128)(2,1)}, u32[]{:S(2)}, u32[]{:S(2)}) collective-permute-start(bf16[4,48,1664]{2,1,0:T(8,128)(2,1)} %bitcast.10), channel_id=1, source_target_pairs={{0,2},{1,3},{2,0},{3,1},{4,6},{5,7},{6,4},{7,5},{8,10},{9,11},{10,... | collective-permute-start | bytes 1916936 | tf_op jit(solution)/shard_map/cond/branch_1_fun/ppermute | solution.py:70
  306.0 31.2 %collective-permute-start.29 = (bf16[4,48,1664]{2,1,0:T(8,128)(2,1)}, bf16[4,48,1664]{2,1,0:T(8,128)(2,1)}, u32[]{:S(2)}, u32[]{:S(2)}) collective-permute-start(bf16[4,48,1664]{2,1,0:T(8,128)(2,1)} %bitcast.11), channel_id=1, source_target_pairs={{0,4},{1,5},{2,6},{3,7},{4,0},{5,1},{6,2},{7,3},{8,12},{9,13},{10,... | collective-permute-start | bytes 1916936 | tf_op jit(solution)/shard_map/cond/branch_1_fun/ppermute | solution.py:70
  306.8 30.4 %collective-permute-start.30 = (bf16[4,48,1664]{2,1,0:T(8,128)(2,1)}, bf16[4,48,1664]{2,1,0:T(8,128)(2,1)}, u32[]{:S(2)}, u32[]{:S(2)}) collective-permute-start(bf16[4,48,1664]{2,1,0:T(8,128)(2,1)} %bitcast.12), channel_id=1, source_target_pairs={{0,6},{1,7},{2,4},{3,5},{4,2},{5,3},{6,0},{7,1},{8,14},{9,15},{10,... | collective-permute-start | bytes 1916936 | tf_op jit(solution)/shard_map/cond/branch_1_fun/ppermute | solution.py:70
  340.3 115.7 %reduce-scatter.8.cloned.1.call-start = ((), (), s32[]{:S(2)}) async-start(), calls=%async_computation.5 | async-start | bytes 2273280 | tf_op jit(solution)/shard_map/reduce_scatter | solution.py:663
  352.9 28.9 %collective-permute-start.49 = (bf16[4,48,3072]{2,1,0:T(8,128)(2,1)S(1)}, bf16[4,48,3072]{2,1,0:T(8,128)(2,1)S(1)}, u32[]{:S(2)}, u32[]{:S(2)}) collective-permute-start(bf16[4,48,3072]{2,1,0:T(8,128)(2,1)S(1)} %get-tuple-element.341), channel_id=1, source_target_pairs={{0,2},{1,3},{2,0},{3,1},{4,6},{5,7},{6,4},{7,5},{8,10},{9,11},{10,... | collective-permute-start | bytes 3538952 | tf_op jit(solution)/shard_map/ppermute | solution.py:70
  354.2 53.1 %collective-permute-start.51 = (bf16[4,48,3072]{2,1,0:T(8,128)(2,1)S(1)}, bf16[4,48,3072]{2,1,0:T(8,128)(2,1)S(1)}, u32[]{:S(2)}, u32[]{:S(2)}) collective-permute-start(bf16[4,48,3072]{2,1,0:T(8,128)(2,1)S(1)} %get-tuple-element.342), channel_id=1, source_target_pairs={{0,6},{1,7},{2,4},{3,5},{4,2},{5,3},{6,0},{7,1},{8,14},{9,15},{10,... | collective-permute-start | bytes 3538952 | tf_op jit(solution)/shard_map/ppermute | solution.py:70
  356.0 52.7 %collective-permute-start.50 = (bf16[4,48,3072]{2,1,0:T(8,128)(2,1)S(1)}, bf16[4,48,3072]{2,1,0:T(8,128)(2,1)S(1)}, u32[]{:S(2)}, u32[]{:S(2)}) collective-permute-start(bf16[4,48,3072]{2,1,0:T(8,128)(2,1)S(1)} %get-tuple-element.343), channel_id=1, source_target_pairs={{0,4},{1,5},{2,6},{3,7},{4,0},{5,1},{6,2},{7,3},{8,12},{9,13},{10,... | collective-permute-start | bytes 3538952 | tf_op jit(solution)/shard_map/ppermute | solution.py:70
  417.3 21.6 %collective-permute-start.54 = (bf16[256,1536]{1,0:T(8,128)(2,1)}, bf16[256,1536]{1,0:T(8,128)(2,1)S(1)}, u32[]{:S(2)}, u32[]{:S(2)}) collective-permute-start(bf16[256,1536]{1,0:T(8,128)(2,1)} %get-tuple-element.327), channel_id=1, source_target_pairs={{0,6},{1,7},{2,4},{3,5},{4,2},{5,3},{6,0},{7,1},{8,14},{9,15},{10,... | collective-permute-start | bytes 2359304 | tf_op jit(solution)/shard_map/ppermute | solution.py:70
  418.5 34.2 %collective-permute-start.53 = (bf16[256,1536]{1,0:T(8,128)(2,1)}, bf16[256,1536]{1,0:T(8,128)(2,1)}, u32[]{:S(2)}, u32[]{:S(2)}) collective-permute-start(bf16[256,1536]{1,0:T(8,128)(2,1)} %get-tuple-element.325), channel_id=1, source_target_pairs={{0,4},{1,5},{2,6},{3,7},{4,0},{5,1},{6,2},{7,3},{8,12},{9,13},{10,... | collective-permute-start | bytes 2359304 | tf_op jit(solution)/shard_map/ppermute | solution.py:70
  419.3 33.4 %collective-permute-start.52 = (bf16[256,1536]{1,0:T(8,128)(2,1)}, bf16[256,1536]{1,0:T(8,128)(2,1)}, u32[]{:S(2)}, u32[]{:S(2)}) collective-permute-start(bf16[256,1536]{1,0:T(8,128)(2,1)} %get-tuple-element.316), channel_id=1, source_target_pairs={{0,2},{1,3},{2,0},{3,1},{4,6},{5,7},{6,4},{7,5},{8,10},{9,11},{10,... | collective-permute-start | bytes 2359304 | tf_op jit(solution)/shard_map/ppermute | solution.py:70
  (46 other events, 458.9 us)
Sparse Core Ops, SparseCore 0:
  34.7 73.0 all-gather.4
  109.4 88.0 all-gather.6
  236.0 83.6 reduce-scatter.3
  340.5 58.7 reduce-scatter.5
  414.0 37.2 reduce-scatter.7

commit v6 on v5

--- a/solution.py
+++ b/solution.py
@@ -388,9 +388,7 @@
     )
 
 
-def output_back_body(places, lines, split, meta, grad, total, second_grad, gain, mixed_t, *refs):
-    pieces, (first_grad, mixed_grad_t, send, keep, weights_v, da, sems) = refs[:-7], refs[-7:]
-    copies = load_rows(meta, places, lines, pieces, weights_v, sems, pl.ds(0, weights_v.shape[1]))
+def output_back_body(split, grad, total, second_grad, gain, mixed_t, meta, first_grad, da, send, keep):
     value = total[...]
     inverse = inverse_rms(value)
     back = second_grad[...]
@@ -411,28 +409,47 @@
     for n in range(width // step):
         cut = slice(n * step, (n + 1) * step)
         store_rows(meta, split, mm(mixed_t[cut, :], da[...]), n * step, send, keep, pl.ds(0, width))
-    for copy in copies:
+
+
+def output_backward(grad, total, second_grad, gain, mixed_t, meta, parts, split):
+    own, width = grad.shape
+    return kernel_call(
+        functools.partial(output_back_body, split),
+        (
+            jax.ShapeDtypeStruct((own, width), F32),
+            jax.ShapeDtypeStruct((own, width), BF),
+            *sums_shapes(split, parts, QUERY, width + 128),
+        ),
+        [VMEM] * 5 + [SMEM],
+        (VMEM,) * 4,
+        [],
+        2 * own * width * QUERY,
+        14 << 20,
+        (grad, total, second_grad, gain, mixed_t, meta),
+    )
+
+
+def mixed_back_body(places, lines, meta, da, *refs):
+    pieces, (mixed_grad_t, weights_v, sems) = refs[:-3], refs[-3:]
+    for copy in load_rows(meta, places, lines, pieces, weights_v, sems, pl.ds(0, weights_v.shape[1])):
         copy.wait()
-    for n in range(width // step):
+    step = 384
+    for n in range(weights_v.shape[0] // step):
         cut = slice(n * step, (n + 1) * step)
         mixed_grad_t[cut, :] = mm_t(weights_v[cut, :], da[...]).astype(BF)
 
 
-def output_backward(meta, grad, total, second_grad, gain, mixed_t, pieces, parts, split):
-    own, width = grad.shape
+def mixed_backward(meta, da, pieces, lines):
+    own, width = da.shape
     return kernel_call(
-        functools.partial(output_back_body, places_of(pieces), parts[1], split),
-        (
-            jax.ShapeDtypeStruct((own, width), F32),
-            jax.ShapeDtypeStruct(mixed_t.shape, BF),
-            *sums_shapes(split, parts, QUERY, width + 128),
-        ),
-        [SMEM] + [VMEM] * 5 + [ANY] * len(pieces),
-        (VMEM,) * 4,
-        [pltpu.VMEM((QUERY, width), BF), pltpu.VMEM((own, width), BF), copies_of(pieces)],
-        4 * own * width * QUERY,
-        22 << 20,
-        (meta, grad, total, second_grad, gain, mixed_t, *arrays_of(pieces)),
+        functools.partial(mixed_back_body, places_of(pieces), lines),
+        jax.ShapeDtypeStruct((QUERY, own), BF),
+        [SMEM, VMEM] + [ANY] * len(pieces),
+        VMEM,
+        [pltpu.VMEM((QUERY, width), BF), copies_of(pieces)],
+        10**12,
+        8 << 20,
+        (meta, da, *arrays_of(pieces)),
     )
 
 
@@ -843,11 +860,13 @@
 
         return cut(1 - move.ci), cut(move.ci)
 
-    first_grad, mixed_grad_t, out_send, out_keep = output_backward(
-        meta, grad_out, first_sum, second_grad, gains, mixed_t, out_pieces, (Z, Q), split
+    first_grad, rounded, out_send, out_keep = output_backward(
+        grad_out, first_sum, second_grad, gains, mixed_t, meta, (Z, Q), split
     )
     out_send, out_keep = pieces_for(out_send, out_keep)
-    out_send = step("c", out_send)
+    moving = step("c", out_send)
+    mixed_grad_t = mixed_backward(meta, rounded, out_pieces, Q)
+    out_send, mixed_grad_t = lax.optimization_barrier((moving, mixed_grad_t))
     blocks = to_send(out_keep, out_send)
 
     def attention_beside(first, second, blocks, meta, query_t, pair_t, mixed_grad_t, logs, cosine, sine, normed_t):

time: 476 us -> 472 us (level)
  waiting for transfers between devices: 226 us -> 220 us
    ppermute x22, waiting for transfers between devices: 24.2 us -> 18.5 us  [step(): return lax.ppermute(value, 'dp', [(n, n ^ 1) for n in range(self.DP)])]
    pallas_call x8 -> x9, Pallas kernels: 125 us -> 127 us  [kernel_call(): pl.pallas_call(body, out_shape=out_shape, in_specs=in_specs, out_specs=ou...]
  transfers between devices with their start and end apart: 60 -> 60, of which waited for: 31 -> 29; matrix products, arithmetic and copies ran while one was open for 9% -> 9% of each run, Pallas kernels for 19% -> 19%
where the time goes in v6:
time: 472 us; the launch traced here: 463 us
  waiting for transfers between devices  220 us (47%)
  Pallas kernels  127 us (27%)
  starting transfers between devices  46.6 us (10%)
  other arithmetic  39.9 us (8%)
  local copies, waits for them, and re-layouts  14.5 us (3%)
  between operations  14.5 us (3%)
    ppermute x27, waiting for transfers between devices, step(): lax.ppermute(value, 'dp', [(n, n % 4 ^ 2 * i | 4 * ((n // 4 + j) % self.Q...  153 us
    pallas_call x9, Pallas kernels, kernel_call(): pl.pallas_call(body, out_shape=out_shape, in_specs=in_specs, out_specs=ou...  127 us
    ppermute x6, waiting for transfers between devices, around(): lax.ppermute(value, 'seq', [(n, (n + hop) % self.Z) for n in range(self.Z)])  43.1 us
    ppermute x27, starting transfers between devices, step(): lax.ppermute(value, 'dp', [(n, n % 4 ^ 2 * i | 4 * ((n // 4 + j) % self.Q...  33.2 us
    ppermute x22, waiting for transfers between devices, step(): return lax.ppermute(value, 'dp', [(n, n ^ 1) for n in range(self.DP)])  18.5 us
    convert_element_type x4, other arithmetic, to_send(): (in_f32(own[n]) + in_f32(other[n])).astype(BF)  13.8 us
  transfers between devices with their start and end apart: 60, of which 29 were waited for; matrix products, arithmetic and copies ran while one was open for 9% of the time, Pallas kernels for 19%

profile of v6, /device:TPU:0, one launch (start us, length us, event | category | flops | bytes accessed | tf_op | source)
XLA Modules:
  0.0 462.8 jit_solution(4260348786009539417)
XLA Ops:
  10.1 2.4 pad_maximum_fusion.4
  12.5 22.1 %conditional.8 = (bf16[48,3200]{1,0:T(8,128)(2,1)}, bf16[48,3200]{1,0:T(8,128)(2,1)}, bf16[256,1536]{1,0:T(8,128)(2,1)}, bf16[256,1536]{1,0:T(8,128)(2,1)}) conditional(s32[]{:T(128)} %convert_element_type.255, () %tuple.93, (bf16[48,3200]{1,0:T(8,128)(2,1)S(1)}, bf16[256,1536]{1,0:T(8,128)(2,1)S(1)}) %tuple.164), branch_computations={%region_0.1_spmd, %region_1.2_spmd} | conditional | bytes 8749248 | solution.py:669
  12.5 3.0 collective-permute-start.3
  16.9 3.6 collective-permute-start.1
  20.5 7.7 %collective-permute-done.1 = bf16[48,3200]{1,0:T(8,128)(2,1)} collective-permute-done((bf16[48,3200]{1,0:T(8,128)(2,1)S(1)}, bf16[48,3200]{1,0:T(8,128)(2,1)}, u32[]{:S(2)}, u32[]{:S(2)}) %collective-permute-start.1) | collective-permute-done | bytes 307232 | tf_op jit(solution)/shard_map/cond/branch_1_fun/ppermute | solution.py:64
  28.2 5.8 %collective-permute-done = bf16[48,3200]{1,0:T(8,128)(2,1)} collective-permute-done((bf16[48,3200]{1,0:T(8,128)(2,1)S(1)}, bf16[48,3200]{1,0:T(8,128)(2,1)}, u32[]{:S(2)}, u32[]{:S(2)}) %collective-permute-start) | collective-permute-done | bytes 307232 | tf_op jit(solution)/shard_map/cond/branch_1_fun/ppermute | solution.py:64
  35.4 13.6 %conditional.9 = (bf16[4,48,3200]{2,1,0:T(8,128)(2,1)S(1)}, bf16[256,1536]{1,0:T(8,128)(2,1)S(1)}) conditional(s32[]{:T(128)} %convert_element_type.255, () %tuple.92, (bf16[48,3200]{1,0:T(8,128)(2,1)S(1)}, bf16[48,3200]{1,0:T(8,128)(2,1)}, bf16[48,3200]{1,0:T(8,128)(2,1)}, bf16[256,1536]{1,0:T(8,128)(2,1)}, bf16[256,1536]{1,0:T(8,128)(2,1)}) %tuple.96), branch_computations={%region_2.3_spmd, %region_3.4_spmd} | conditional | flops 3416064 | bytes 9977992 | solution.py:669
  41.2 4.1 collective-permute-done.16
  49.9 30.7 %conditional.10 = (bf16[4,48,3200]{2,1,0:T(8,128)(2,1)}, bf16[4,48,3200]{2,1,0:T(8,128)(2,1)}, bf16[4,48,3200]{2,1,0:T(8,128)(2,1)}, bf16[48,1536]{1,0:T(8,128)(2,1)}, bf16[48,1536]{1,0:T(8,128)(2,1)}) conditional(s32[]{:T(128)} %convert_element_type.255, () %tuple.91, (bf16[4,48,3200]{2,1,0:T(8,128)(2,1)S(1)}, bf16[48,1536]{1,0:T(8,128)(2,1)S(1)}) %tuple.167), branch_computations={%region_4.5_spmd, %region_5.6_spmd} | conditional | bytes 15925488 | solution.py:669
  52.8 2.3 collective-permute-start.8
  55.1 11.4 %collective-permute-done.8 = bf16[48,1536]{1,0:T(8,128)(2,1)} collective-permute-done((bf16[48,1536]{1,0:T(8,128)(2,1)S(1)}, bf16[48,1536]{1,0:T(8,128)(2,1)}, u32[]{:S(2)}, u32[]{:S(2)}) %collective-permute-start.8) | collective-permute-done | bytes 147488 | tf_op jit(solution)/shard_map/cond/branch_1_fun/ppermute | solution.py:64
  66.5 4.3 collective-permute-done.7
  70.8 8.6 %collective-permute-done.5 = bf16[4,48,3200]{2,1,0:T(8,128)(2,1)} collective-permute-done((bf16[4,48,3200]{2,1,0:T(8,128)(2,1)S(1)}, bf16[4,48,3200]{2,1,0:T(8,128)(2,1)}, u32[]{:S(2)}, u32[]{:S(2)}) %collective-permute-start.5) | collective-permute-done | bytes 1228832 | tf_op jit(solution)/shard_map/cond/branch_1_fun/ppermute | solution.py:70
  80.6 19.1 %conditional.11 = (bf16[2,48,3200]{2,1,0:T(8,128)(2,1)}, bf16[2,48,3200]{2,1,0:T(8,128)(2,1)}, bf16[4,48,3200]{2,1,0:T(8,128)(2,1)}, bf16[4,48,3200]{2,1,0:T(8,128)(2,1)}, bf16[4,48,1536]{2,1,0:T(8,128)(2,1)}) conditional(s32[]{:T(128)} %convert_element_type.255, () %tuple.90, (bf16[4,48,3200]{2,1,0:T(8,128)(2,1)}, bf16[4,48,3200]{2,1,0:T(8,128)(2,1)}, ...), branch_computations={%region_6.7_spmd, %region_7.8_spmd} | conditional | flops 884736 | bytes 18972912 | solution.py:669
  87.1 9.8 %collective-permute-done.23 = bf16[48,1536]{1,0:T(8,128)(2,1)S(1)} collective-permute-done((bf16[48,1536]{1,0:T(8,128)(2,1)}, bf16[48,1536]{1,0:T(8,128)(2,1)S(1)}, u32[]{:S(2)}, u32[]{:S(2)}) %collective-permute-start.23) | collective-permute-done | bytes 147488 | tf_op jit(solution)/shard_map/cond/branch_1_fun/ppermute | solution.py:64
  102.8 5.0 %all-gather.5.cloned.1.call-done = bf16[8,128,1536]{2,1,0:T(8,128)(2,1)} async-done(((bf16[2,128,1536]{2,1,0:T(8,128)(2,1)}), bf16[8,128,1536]{2,1,0:T(8,128)(2,1)}) %all-gather.5.cloned.1.call-update) | async-done | bytes 3145744 | tf_op jit(solution)/shard_map/all_gather | solution.py:677
  107.8 20.1 %conditional.12 = (bf16[4,48,1536]{2,1,0:T(8,128)(2,1)}, bf16[4,48,1536]{2,1,0:T(8,128)(2,1)}, bf16[1536,256]{1,0:T(8,128)(2,1)}, bf16[1536,1024]{1,0:T(8,128)(2...) conditional(s32[]{:T(128)} %convert_element_type.255, () %tuple.89, ...), branch_computations={%region_9.10_spmd, %region_10.11_spmd} | conditional | flops 6039797760 | bytes 35520724 | solution.py:669
  110.9 17.0 %branch_1_fun.4 = (bf16[1536,256]{1,0:T(8,128)(2,1)}, bf16[1536,1024]{1,0:T(8,128)(2,1)S(1)}, bf16[1536,1024]{1,0:T(8,128)(2,1)}, f32[8,1536]{1,0:T(8,128)S(1)}) custom-call(s32[4]{0:T(128)S(1)} %get-tuple-element.129.meta, bf16[4,2,128,1536]{3,2,1,0:T(8,128)(2,1)} %bitcast.75, f32[48,1024]{1,0:T(8,128)} %get-tuple-element.131.cosine, ...), custom_call_target="tpu_custom_call" | custom-call | flops 6039797760 | bytes 20971520 | tf_op jit(solution)/shard_map/cond/branch_1_fun/pallas_call | solution.py:85
  129.7 15.5 %conditional.13 = (bf16[2,48,1536]{2,1,0:T(8,128)(2,1)}, bf16[2,48,1536]{2,1,0:T(8,128)(2,1)}, bf16[4,48,1536]{2,1,0:T(8,128)(2,1)}, bf16[4,48,1536]{2,1,0:T(8,1...) conditional(s32[]{:T(128)} %convert_element_type.255, () %tuple.88, ...), branch_computations={%region_11.12_spmd, %region_12.13_spmd} | conditional | flops 805306368 | bytes 16908552 | solution.py:669
  132.9 12.2 %branch_1_fun.5 = (bf16[256,1536]{1,0:T(8,128)(2,1)}, bf16[1536,256]{1,0:T(8,128)(2,1)}, f32[8,2,1,256]{3,2,1,0:T(1,128)}) custom-call(s32[4]{0:T(128)S(1)} %get-tuple-element.150.meta, bf16[1536,256]{1,0:T(8,128)(2,1)} %get-tuple-element.151.query_t, bf16[1536,1024]{1,0:T(8,128)(2,1)S(1)} %get-tuple-element.152.pair_t), custom_call_target="tpu_custom_call" | custom-call | flops 805306368 | bytes 6291456 | tf_op jit(solution)/shard_map/cond/branch_1_fun/pallas_call | solution.py:85
  149.3 7.0 %shard_map.203 = (f32[256,1536]{1,0:T(8,128)}, bf16[256,1536]{1,0:T(8,128)(2,1)}) custom-call(s32[4]{0:T(128)S(1)} %pad_add_fusion.meta, bf16[256,1536]{1,0:T(8,128)(2,1)} %bitcast.56, bf16[256,1536]{1,0:T(8,128)(2,1)} %get-tuple-element.289.mixed, f32[8,1536]{1,0:T(8,128)S(1)} %get-tuple-element.290.gain, bf16[4,48,1536]{2,1,0:T(8,128)(2,1)} %get-tuple-element.278.refs_0_, ...), custom_call_target="tpu_custom_call" | custom-call | flops 1207959552 | bytes 10485760 | tf_op jit(solution)/shard_map/pallas_call | solution.py:85
  156.3 2.9 collective-permute-start.37
  160.4 17.4 %collective-permute-done.37.refs_3_ = bf16[256,1536]{1,0:T(8,128)(2,1)S(1)} collective-permute-done((bf16[256,1536]{1,0:T(8,128)(2,1)}, bf16[256,1536]{1,0:T(8,128)(2,1)S(1)}, u32[]{:S(2)}, u32[]{:S(2)}) %collective-permute-start.37) | collective-permute-done | bytes 786464 | tf_op jit(solution)/shard_map/ppermute | solution.py:70
  177.8 16.2 %collective-permute-done.36.refs_2_ = bf16[256,1536]{1,0:T(8,128)(2,1)S(1)} collective-permute-done((bf16[256,1536]{1,0:T(8,128)(2,1)}, bf16[256,1536]{1,0:T(8,128)(2,1)S(1)}, u32[]{:S(2)}, u32[]{:S(2)}) %collective-permute-start.36) | collective-permute-done | bytes 786464 | tf_op jit(solution)/shard_map/ppermute | solution.py:70
  197.6 37.7 %shard_map.204 = (bf16[1024,1536]{1,0:T(8,128)(2,1)}, bf16[1024,1536]{1,0:T(8,128)(2,1)}, bf16[1024,1536]{1,0:T(8,128)(2,1)S(1)}, bf16[1024,1536]{1,0:T(8,128)(2,1)}, bf16[4,384,1536]{2,1,0:T(8,128)(2,1)}) custom-call(bf16[256,1536]{1,0:T(8,128)(2,1)} %get-tuple-element.297.refs_0_, bf16[256,1536]{1,0:T(8,128)(2,1)} %copy-done.35, ...), custom_call_target="tpu_custom_call" | custom-call | flops 28991029248 | bytes 35651584 | tf_op jit(solution)/shard_map/pallas_call | solution.py:85
  235.6 5.8 %collective-permute-done.46 = bf16[1024,1536]{1,0:T(8,128)(2,1)} collective-permute-done((bf16[1024,1536]{1,0:T(8,128)(2,1)}, bf16[1024,1536]{1,0:T(8,128)(2,1)}, u32[]{:S(2)}, u32[]{:S(2)}) %collective-permute-start.46) | collective-permute-done | bytes 3145760 | tf_op jit(solution)/shard_map/ppermute | solution.py:68
  241.4 2.4 add_convert_fusion.7
  244.0 39.8 %conditional.14 = (f32[256,1536]{1,0:T(8,128)S(1)}, bf16[1024,1536]{1,0:T(8,128)(2,1)}) conditional(s32[]{:T(128)} %convert_element_type.255, () %tuple.105, (bf16[1024,1536]{1,0:T(8,128)(2,1)S(1)}, bf16[1024,1536]{1,0:T(8,128)(2,1)}, bf16[256,1536]{1,0:T(8,128)(2,1)S(1)}, bf16[256,1536]{1,0:T(8,128)(2,1)S(1)}, bf16[256,1536]{1,0:T(8,128)(2,1)S(1)}, ...), branch_computations={%region_13.14_spmd, %region_14.15_spmd} | conditional | flops 3538944 | bytes 40108236 | solution.py:669
  247.7 16.9 %collective-permute-done.24 = bf16[256,1536]{1,0:T(8,128)(2,1)S(1)} collective-permute-done((bf16[256,1536]{1,0:T(8,128)(2,1)S(1)}, bf16[256,1536]{1,0:T(8,128)(2,1)S(1)}, u32[]{:S(2)}, u32[]{:S(2)}) %collective-permute-start.24) | collective-permute-done | bytes 786464 | tf_op jit(solution)/shard_map/cond/branch_1_fun/ppermute | solution.py:70
  264.5 17.4 %collective-permute-done.25 = bf16[256,1536]{1,0:T(8,128)(2,1)S(1)} collective-permute-done((bf16[256,1536]{1,0:T(8,128)(2,1)S(1)}, bf16[256,1536]{1,0:T(8,128)(2,1)S(1)}, u32[]{:S(2)}, u32[]{:S(2)}) %collective-permute-start.25) | collective-permute-done | bytes 786464 | tf_op jit(solution)/shard_map/cond/branch_1_fun/ppermute | solution.py:70
  283.8 6.7 %shard_map.205 = (f32[256,1536]{1,0:T(8,128)}, bf16[256,1536]{1,0:T(8,128)(2,1)}, bf16[4,4,48,1664]{3,2,1,0:T(8,128)(2,1)}, bf16[4,4,48,1664]{3,2,1,0:T(8,128)(2,1)}) custom-call(bf16[256,1536]{1,0:T(8,128)(2,1)} %bitcast.64, f32[256,1536]{1,0:T(8,128)} %get-tuple-element.296.total, f32[256,1536]{1,0:T(8,128)S(1)} %get-tuple-element.309.second_grad, ...), custom_call_target="tpu_custom_call" | custom-call | flops 1207959552 | bytes 14680064 | tf_op jit(solution)/shard_map/pallas_call | solution.py:85
  290.5 6.2 %shard_map.206 = bf16[1536,256]{1,0:T(8,128)(2,1)} custom-call(s32[4]{0:T(128)S(1)} %pad_add_fusion.meta, bf16[256,1536]{1,0:T(8,128)(2,1)} %get-tuple-element.313.da, bf16[4,48,1536]{2,1,0:T(8,128)(2,1)} %get-tuple-element.278.refs_0_, bf16[4,48,1536]{2,1,0:T(8,128)(2,1)} %get-tuple-element.291.refs_1_, bf16[4,48,1536]{2,1,0:T(8,128)(2,1)} %get-tuple-element.286.refs_2_, ...), custom_call_target="tpu_custom_call" | custom-call | flops 999999995904 | bytes 8388608 | tf_op jit(solution)/shard_map/pallas_call | solution.py:85
  296.8 3.7 add_convert_fusion.10
  300.5 35.8 %conditional.15 = (bf16[4,48,1664]{2,1,0:T(8,128)(2,1)}, bf16[1536,256]{1,0:T(8,128)(2,1)}, bf16[4,1536,256]{2,1,0:T(8,128)(2,1)}, bf16[4,4,48,3072]{3,2,1,0:T(8,128)(2,1)}, bf16[4,4,48,3072]{3,2,1,0:T(8,128)(2,1)}) conditional(s32[]{:T(128)} %convert_element_type.255, () %tuple.107, (bf16[4,4,48,1664]{3,2,1,0:T(8,128)(2,1)}, ...), branch_computations={%region_15.16_spmd, %region_16.17_spmd} | conditional | flops 1000003207168 | bytes 51347616 | solution.py:669
  304.0 16.0 %branch_1_fun.6 = (bf16[1536,256]{1,0:T(8,128)(2,1)}, bf16[1536,1024]{1,0:T(8,128)(2,1)}, bf16[4,1536,256]{2,1,0:T(8,128)(2,1)}) custom-call(s32[4]{0:T(128)S(1)} %get-tuple-element.168.meta, bf16[1536,256]{1,0:T(8,128)(2,1)} %get-tuple-element.170.query_t, bf16[1536,1024]{1,0:T(8,128)(2,1)S(1)} %get-tuple-element.171.pair_t, ...), custom_call_target="tpu_custom_call" | custom-call | flops 999999995904 | bytes 12582912 | tf_op jit(solution)/shard_map/cond/branch_1_fun/pallas_call | solution.py:85
  320.0 13.1 %branch_1_fun.7 = (bf16[4,4,48,3072]{3,2,1,0:T(8,128)(2,1)}, bf16[4,4,48,3072]{3,2,1,0:T(8,128)(2,1)}) custom-call(s32[4]{0:T(128)S(1)} %get-tuple-element.168.meta, bf16[1536,1024]{1,0:T(8,128)(2,1)} %get-tuple-element.169.normed_t, bf16[1536,256]{1,0:T(8,128)(2,1)} %get-tuple-element.437.query_back, bf16[1536,1024]{1,0:T(8,128)(2,1)} %get-tuple-element.177.pair_back), custom_call_target="tpu_custom_call" | custom-call | flops 1 | bytes 27262976 | tf_op jit(solution)/shard_map/cond/branch_1_fun/pallas_call | solution.py:85
  333.1 3.1 fusion.2
  336.3 8.2 %collective-permute-done.48 = bf16[4,4,48,3072]{3,2,1,0:T(8,128)(2,1)} collective-permute-done((bf16[4,4,48,3072]{3,2,1,0:T(8,128)(2,1)}, bf16[4,4,48,3072]{3,2,1,0:T(8,128)(2,1)}, u32[]{:S(2)}, u32[]{:S(2)}) %collective-permute-start.48) | collective-permute-done | bytes 4718624 | tf_op jit(solution)/shard_map/ppermute | solution.py:68
  344.5 4.4 fusion.6
  352.4 25.3 %collective-permute-done.49 = bf16[4,48,3072]{2,1,0:T(8,128)(2,1)S(1)} collective-permute-done((bf16[4,48,3072]{2,1,0:T(8,128)(2,1)S(1)}, bf16[4,48,3072]{2,1,0:T(8,128)(2,1)S(1)}, u32[]{:S(2)}, u32[]{:S(2)}) %collective-permute-start.49) | collective-permute-done | bytes 1179680 | tf_op jit(solution)/shard_map/ppermute | solution.py:70
  377.7 25.5 %collective-permute-done.51 = bf16[4,48,3072]{2,1,0:T(8,128)(2,1)S(1)} collective-permute-done((bf16[4,48,3072]{2,1,0:T(8,128)(2,1)S(1)}, bf16[4,48,3072]{2,1,0:T(8,128)(2,1)S(1)}, u32[]{:S(2)}, u32[]{:S(2)}) %collective-permute-start.51) | collective-permute-done | bytes 1179680 | tf_op jit(solution)/shard_map/ppermute | solution.py:70
  404.6 2.6 fusion.5
  407.2 2.6 pad_maximum_fusion.3
  409.8 3.4 add_convert_fusion.6
  418.2 11.0 %shard_map.207 = bf16[256,1536]{1,0:T(8,128)(2,1)} custom-call(s32[4]{0:T(128)S(1)} %pad_add_fusion.meta, bf16[256,1536]{1,0:T(8,128)(2,1)} %bitcast.57, f32[8,1536]{1,0:T(8,128)S(1)} %copy-done.10, f32[256,1536]{1,0:T(8,128)} %get-tuple-element.321.first_grad, bf16[1536,256]{1,0:T(8,128)(2,1)} %get-tuple-element.322.query_back, bf16[1536,256]{1,0:T(8,128)(2,1)} %bitcast.60, ...), custom_call_target="tpu_custom_call" | custom-call | flops 2415919104 | bytes 14680064 | tf_op jit(solution)/shard_map/pallas_call | solution.py:85
  429.2 5.6 %collective-permute-done.54 = bf16[256,1536]{1,0:T(8,128)(2,1)S(1)} collective-permute-done((bf16[256,1536]{1,0:T(8,128)(2,1)}, bf16[256,1536]{1,0:T(8,128)(2,1)S(1)}, u32[]{:S(2)}, u32[]{:S(2)}) %collective-permute-start.54) | collective-permute-done | bytes 786464 | tf_op jit(solution)/shard_map/ppermute | solution.py:70
  434.8 13.8 %collective-permute-done.53 = bf16[256,1536]{1,0:T(8,128)(2,1)} collective-permute-done((bf16[256,1536]{1,0:T(8,128)(2,1)}, bf16[256,1536]{1,0:T(8,128)(2,1)}, u32[]{:S(2)}, u32[]{:S(2)}) %collective-permute-start.53) | collective-permute-done | bytes 786464 | tf_op jit(solution)/shard_map/ppermute | solution.py:70
  448.6 3.3 add_convert_fusion.3
  (219 shorter events, 72.9 us)
Async XLA Ops:
  7.2 100.6 %all-gather.5.cloned.1.call-start = ((), (), s32[]{:S(2)}) async-start(), calls=%async_computation.6 | async-start | bytes 3932160 | tf_op jit(solution)/shard_map/all_gather | solution.py:677
  12.5 21.6 %collective-permute-start.3 = (bf16[256,1536]{1,0:T(8,128)(2,1)S(1)}, bf16[256,1536]{1,0:T(8,128)(2,1)}, u32[]{:S(2)}, u32[]{:S(2)}) collective-permute-start(bf16[256,1536]{1,0:T(8,128)(2,1)S(1)} %get-tuple-element.115), channel_id=1, source_target_pairs={{0,4},{1,5},{2,6},{3,7},{4,0},{5,1},{6,2},{7,3},{8,12},{9,13},{10,... | collective-permute-start | bytes 2359304 | tf_op jit(solution)/shard_map/cond/branch_1_fun/ppermute | solution.py:70
  15.4 19.1 %collective-permute-start.2 = (bf16[256,1536]{1,0:T(8,128)(2,1)S(1)}, bf16[256,1536]{1,0:T(8,128)(2,1)}, u32[]{:S(2)}, u32[]{:S(2)}) collective-permute-start(bf16[256,1536]{1,0:T(8,128)(2,1)S(1)} %get-tuple-element.115), channel_id=1, source_target_pairs={{0,2},{1,3},{2,0},{3,1},{4,6},{5,7},{6,4},{7,5},{8,10},{9,11},{10,... | collective-permute-start | bytes 2359304 | tf_op jit(solution)/shard_map/cond/branch_1_fun/ppermute | solution.py:70
  16.9 11.3 %collective-permute-start.1 = (bf16[48,3200]{1,0:T(8,128)(2,1)S(1)}, bf16[48,3200]{1,0:T(8,128)(2,1)}, u32[]{:S(2)}, u32[]{:S(2)}) collective-permute-start(bf16[48,3200]{1,0:T(8,128)(2,1)S(1)} %get-tuple-element.114), channel_id=1, source_target_pairs={{0,24},{8,0},{16,8},{24,16},{1,25},{9,1},{17,9},{25,17},{2,26},{10... | collective-permute-start | bytes 921608 | tf_op jit(solution)/shard_map/cond/branch_1_fun/ppermute | solution.py:64
  20.5 13.6 %collective-permute-start = (bf16[48,3200]{1,0:T(8,128)(2,1)S(1)}, bf16[48,3200]{1,0:T(8,128)(2,1)}, u32[]{:S(2)}, u32[]{:S(2)}) collective-permute-start(bf16[48,3200]{1,0:T(8,128)(2,1)S(1)} %get-tuple-element.114), channel_id=1, source_target_pairs={{0,8},{8,16},{16,24},{24,0},{1,9},{9,17},{17,25},{25,1},{2,10},{10... | collective-permute-start | bytes 921608 | tf_op jit(solution)/shard_map/cond/branch_1_fun/ppermute | solution.py:64
  34.6 163.1 %all-gather.7.cloned.1.call-start = ((), (), s32[]{:S(2)}) async-start(), calls=%async_computation.7 | async-start | bytes 5898240 | tf_op jit(solution)/shard_map/all_gather | solution.py:677
  35.3 300.9 %reduce-scatter.4.cloned.1.call-start = ((), (), s32[]{:S(2)}) async-start(), calls=%async_computation.3 | async-start | bytes 5898240 | tf_op jit(solution)/shard_map/reduce_scatter | solution.py:680
  49.9 20.9 %collective-permute-start.6 = (bf16[4,48,3200]{2,1,0:T(8,128)(2,1)S(1)}, bf16[4,48,3200]{2,1,0:T(8,128)(2,1)}, u32[]{:S(2)}, u32[]{:S(2)}) collective-permute-start(bf16[4,48,3200]{2,1,0:T(8,128)(2,1)S(1)} %get-tuple-element.121), channel_id=1, source_target_pairs={{0,1},{1,0},{2,3},{3,2},{4,5},{5,4},{6,7},{7,6},{8,9},{9,8},{10,11... | collective-permute-start | bytes 3686408 | tf_op jit(solution)/shard_map/cond/branch_1_fun/ppermute | solution.py:68
  49.9 29.5 %collective-permute-start.5 = (bf16[4,48,3200]{2,1,0:T(8,128)(2,1)S(1)}, bf16[4,48,3200]{2,1,0:T(8,128)(2,1)}, u32[]{:S(2)}, u32[]{:S(2)}) collective-permute-start(bf16[4,48,3200]{2,1,0:T(8,128)(2,1)S(1)} %get-tuple-element.121), channel_id=1, source_target_pairs={{0,4},{1,5},{2,6},{3,7},{4,0},{5,1},{6,2},{7,3},{8,12},{9,13},{10,... | collective-permute-start | bytes 3686408 | tf_op jit(solution)/shard_map/cond/branch_1_fun/ppermute | solution.py:70
  51.3 29.3 %collective-permute-start.4 = (bf16[4,48,3200]{2,1,0:T(8,128)(2,1)S(1)}, bf16[4,48,3200]{2,1,0:T(8,128)(2,1)}, u32[]{:S(2)}, u32[]{:S(2)}) collective-permute-start(bf16[4,48,3200]{2,1,0:T(8,128)(2,1)S(1)} %get-tuple-element.121), channel_id=1, source_target_pairs={{0,2},{1,3},{2,0},{3,1},{4,6},{5,7},{6,4},{7,5},{8,10},{9,11},{10,... | collective-permute-start | bytes 3686408 | tf_op jit(solution)/shard_map/cond/branch_1_fun/ppermute | solution.py:70
  52.8 13.7 %collective-permute-start.8 = (bf16[48,1536]{1,0:T(8,128)(2,1)S(1)}, bf16[48,1536]{1,0:T(8,128)(2,1)}, u32[]{:S(2)}, u32[]{:S(2)}) collective-permute-start(bf16[48,1536]{1,0:T(8,128)(2,1)S(1)} %get-tuple-element.122), channel_id=1, source_target_pairs={{0,24},{8,0},{16,8},{24,16},{1,25},{9,1},{17,9},{25,17},{2,26},{10... | collective-permute-start | bytes 442376 | tf_op jit(solution)/shard_map/cond/branch_1_fun/ppermute | solution.py:64
  55.1 15.7 %collective-permute-start.7 = (bf16[48,1536]{1,0:T(8,128)(2,1)S(1)}, bf16[48,1536]{1,0:T(8,128)(2,1)}, u32[]{:S(2)}, u32[]{:S(2)}) collective-permute-start(bf16[48,1536]{1,0:T(8,128)(2,1)S(1)} %get-tuple-element.122), channel_id=1, source_target_pairs={{0,8},{8,16},{16,24},{24,0},{1,9},{9,17},{17,25},{25,1},{2,10},{10... | collective-permute-start | bytes 442376 | tf_op jit(solution)/shard_map/cond/branch_1_fun/ppermute | solution.py:64
  80.6 19.1 %collective-permute-start.22 = (bf16[4,48,3200]{2,1,0:T(8,128)(2,1)}, bf16[4,48,3200]{2,1,0:T(8,128)(2,1)}, u32[]{:S(2)}, u32[]{:S(2)}) collective-permute-start(bf16[4,48,3200]{2,1,0:T(8,128)(2,1)} %get-tuple-element.123), channel_id=1, source_target_pairs={{0,1},{1,0},{2,3},{3,2},{4,5},{5,4},{6,7},{7,6},{8,9},{9,8},{10,11... | collective-permute-start | bytes 3686408 | tf_op jit(solution)/shard_map/cond/branch_1_fun/ppermute | solution.py:68
  80.6 19.1 %collective-permute-start.21 = (bf16[4,48,3200]{2,1,0:T(8,128)(2,1)}, bf16[4,48,3200]{2,1,0:T(8,128)(2,1)}, u32[]{:S(2)}, u32[]{:S(2)}) collective-permute-start(bf16[4,48,3200]{2,1,0:T(8,128)(2,1)} %get-tuple-element.124), channel_id=1, source_target_pairs={{0,1},{1,0},{2,3},{3,2},{4,5},{5,4},{6,7},{7,6},{8,9},{9,8},{10,11... | collective-permute-start | bytes 3686408 | tf_op jit(solution)/shard_map/cond/branch_1_fun/ppermute | solution.py:68
  82.2 16.6 %collective-permute-start.20 = (bf16[2,48,3200]{2,1,0:T(8,128)(2,1)S(1)}, bf16[2,48,3200]{2,1,0:T(8,128)(2,1)}, u32[]{:S(2)}, u32[]{:S(2)}) collective-permute-start(bf16[2,48,3200]{2,1,0:T(8,128)(2,1)S(1)} %slice.126), channel_id=1, source_target_pairs={{0,4},{1,5},{2,6},{3,7},{4,0},{5,1},{6,2},{7,3},{8,12},{9,13},{10,... | collective-permute-start | bytes 1843208 | tf_op jit(solution)/shard_map/cond/branch_1_fun/ppermute | solution.py:70
  84.0 15.7 %collective-permute-start.19 = (bf16[2,48,3200]{2,1,0:T(8,128)(2,1)S(1)}, bf16[2,48,3200]{2,1,0:T(8,128)(2,1)}, u32[]{:S(2)}, u32[]{:S(2)}) collective-permute-start(bf16[2,48,3200]{2,1,0:T(8,128)(2,1)S(1)} %slice.125), channel_id=1, source_target_pairs={{0,2},{1,3},{2,0},{3,1},{4,6},{5,7},{6,4},{7,5},{8,10},{9,11},{10,... | collective-permute-start | bytes 1843208 | tf_op jit(solution)/shard_map/cond/branch_1_fun/ppermute | solution.py:70
  85.5 11.3 %collective-permute-start.23 = (bf16[48,1536]{1,0:T(8,128)(2,1)}, bf16[48,1536]{1,0:T(8,128)(2,1)S(1)}, u32[]{:S(2)}, u32[]{:S(2)}) collective-permute-start(bf16[48,1536]{1,0:T(8,128)(2,1)} %get-tuple-element.126), channel_id=1, source_target_pairs={{0,8},{8,16},{16,24},{24,0},{1,9},{9,17},{17,25},{25,1},{2,10},{10... | collective-permute-start | bytes 442376 | tf_op jit(solution)/shard_map/cond/branch_1_fun/ppermute | solution.py:64
  107.9 20.0 %collective-permute-start.10 = (bf16[4,48,1536]{2,1,0:T(8,128)(2,1)}, bf16[4,48,1536]{2,1,0:T(8,128)(2,1)}, u32[]{:S(2)}, u32[]{:S(2)}) collective-permute-start(bf16[4,48,1536]{2,1,0:T(8,128)(2,1)} %get-tuple-element.128), channel_id=1, source_target_pairs={{0,4},{1,5},{2,6},{3,7},{4,0},{5,1},{6,2},{7,3},{8,12},{9,13},{10,... | collective-permute-start | bytes 1769480 | tf_op jit(solution)/shard_map/cond/branch_1_fun/ppermute | solution.py:70
  109.4 18.5 %collective-permute-start.9 = (bf16[4,48,1536]{2,1,0:T(8,128)(2,1)}, bf16[4,48,1536]{2,1,0:T(8,128)(2,1)}, u32[]{:S(2)}, u32[]{:S(2)}) collective-permute-start(bf16[4,48,1536]{2,1,0:T(8,128)(2,1)} %get-tuple-element.128), channel_id=1, source_target_pairs={{0,2},{1,3},{2,0},{3,1},{4,6},{5,7},{6,4},{7,5},{8,10},{9,11},{10,... | collective-permute-start | bytes 1769480 | tf_op jit(solution)/shard_map/cond/branch_1_fun/ppermute | solution.py:70
  129.7 15.5 %collective-permute-start.13 = (bf16[4,48,1536]{2,1,0:T(8,128)(2,1)}, bf16[4,48,1536]{2,1,0:T(8,128)(2,1)}, u32[]{:S(2)}, u32[]{:S(2)}) collective-permute-start(bf16[4,48,1536]{2,1,0:T(8,128)(2,1)} %get-tuple-element.149), channel_id=1, source_target_pairs={{0,1},{1,0},{2,3},{3,2},{4,5},{5,4},{6,7},{7,6},{8,9},{9,8},{10,11... | collective-permute-start | bytes 1769480 | tf_op jit(solution)/shard_map/cond/branch_1_fun/ppermute | solution.py:68
  129.7 15.5 %collective-permute-start.15 = (bf16[4,48,1536]{2,1,0:T(8,128)(2,1)}, bf16[4,48,1536]{2,1,0:T(8,128)(2,1)}, u32[]{:S(2)}, u32[]{:S(2)}) collective-permute-start(bf16[4,48,1536]{2,1,0:T(8,128)(2,1)} %get-tuple-element.147), channel_id=1, source_target_pairs={{0,1},{1,0},{2,3},{3,2},{4,5},{5,4},{6,7},{7,6},{8,9},{9,8},{10,11... | collective-permute-start | bytes 1769480 | tf_op jit(solution)/shard_map/cond/branch_1_fun/ppermute | solution.py:68
  130.2 15.0 %collective-permute-start.14 = (bf16[4,48,1536]{2,1,0:T(8,128)(2,1)}, bf16[4,48,1536]{2,1,0:T(8,128)(2,1)}, u32[]{:S(2)}, u32[]{:S(2)}) collective-permute-start(bf16[4,48,1536]{2,1,0:T(8,128)(2,1)} %get-tuple-element.148), channel_id=1, source_target_pairs={{0,1},{1,0},{2,3},{3,2},{4,5},{5,4},{6,7},{7,6},{8,9},{9,8},{10,11... | collective-permute-start | bytes 1769480 | tf_op jit(solution)/shard_map/cond/branch_1_fun/ppermute | solution.py:68
  131.2 13.9 %collective-permute-start.12 = (bf16[2,48,1536]{2,1,0:T(8,128)(2,1)S(1)}, bf16[2,48,1536]{2,1,0:T(8,128)(2,1)}, u32[]{:S(2)}, u32[]{:S(2)}) collective-permute-start(bf16[2,48,1536]{2,1,0:T(8,128)(2,1)S(1)} %slice.128), channel_id=1, source_target_pairs={{0,4},{1,5},{2,6},{3,7},{4,0},{5,1},{6,2},{7,3},{8,12},{9,13},{10,... | collective-permute-start | bytes 884744 | tf_op jit(solution)/shard_map/cond/branch_1_fun/ppermute | solution.py:70
  132.4 12.7 %collective-permute-start.11 = (bf16[2,48,1536]{2,1,0:T(8,128)(2,1)S(1)}, bf16[2,48,1536]{2,1,0:T(8,128)(2,1)}, u32[]{:S(2)}, u32[]{:S(2)}) collective-permute-start(bf16[2,48,1536]{2,1,0:T(8,128)(2,1)S(1)} %slice.127), channel_id=1, source_target_pairs={{0,2},{1,3},{2,0},{3,1},{4,6},{5,7},{6,4},{7,5},{8,10},{9,11},{10,... | collective-permute-start | bytes 884744 | tf_op jit(solution)/shard_map/cond/branch_1_fun/ppermute | solution.py:70
  145.2 14.2 %collective-permute-start.42 = (bf16[256,1536]{1,0:T(8,128)(2,1)}, bf16[256,1536]{1,0:T(8,128)(2,1)S(1)}, u32[]{:S(2)}, u32[]{:S(2)}) collective-permute-start(bf16[256,1536]{1,0:T(8,128)(2,1)} %bitcast.62), channel_id=1, source_target_pairs={{0,1},{1,0},{2,3},{3,2},{4,5},{5,4},{6,7},{7,6},{8,9},{9,8},{10,11... | collective-permute-start | bytes 2359304 | tf_op jit(solution)/shard_map/ppermute | solution.py:68
  145.8 14.0 %collective-permute-start.43 = (bf16[256,1536]{1,0:T(8,128)(2,1)}, bf16[256,1536]{1,0:T(8,128)(2,1)S(1)}, u32[]{:S(2)}, u32[]{:S(2)}) collective-permute-start(bf16[256,1536]{1,0:T(8,128)(2,1)} %get-tuple-element.299.refs_9_), channel_id=1, source_target_pairs={{0,1},{1,0},{2,3},{3,2},{4,5},{5,4},{6,7},{7,6},{8,9},{9,8},{10,11... | collective-permute-start | bytes 2359304 | tf_op jit(solution)/shard_map/ppermute | solution.py:68
  146.2 13.7 %collective-permute-start.44 = (bf16[256,1536]{1,0:T(8,128)(2,1)}, bf16[256,1536]{1,0:T(8,128)(2,1)S(1)}, u32[]{:S(2)}, u32[]{:S(2)}) collective-permute-start(bf16[256,1536]{1,0:T(8,128)(2,1)} %get-tuple-element.300.refs_10_), channel_id=1, source_target_pairs={{0,1},{1,0},{2,3},{3,2},{4,5},{5,4},{6,7},{7,6},{8,9},{9,8},{10,11... | collective-permute-start | bytes 2359304 | tf_op jit(solution)/shard_map/ppermute | solution.py:68
  156.3 21.6 %collective-permute-start.37 = (bf16[256,1536]{1,0:T(8,128)(2,1)}, bf16[256,1536]{1,0:T(8,128)(2,1)S(1)}, u32[]{:S(2)}, u32[]{:S(2)}) collective-permute-start(bf16[256,1536]{1,0:T(8,128)(2,1)} %get-tuple-element.297.refs_0_), channel_id=1, source_target_pairs={{0,6},{1,7},{2,4},{3,5},{4,2},{5,3},{6,0},{7,1},{8,14},{9,15},{10,... | collective-permute-start | bytes 2359304 | tf_op jit(solution)/shard_map/ppermute | solution.py:70
  159.2 34.9 %collective-permute-start.36 = (bf16[256,1536]{1,0:T(8,128)(2,1)}, bf16[256,1536]{1,0:T(8,128)(2,1)S(1)}, u32[]{:S(2)}, u32[]{:S(2)}) collective-permute-start(bf16[256,1536]{1,0:T(8,128)(2,1)} %get-tuple-element.297.refs_0_), channel_id=1, source_target_pairs={{0,4},{1,5},{2,6},{3,7},{4,0},{5,1},{6,2},{7,3},{8,12},{9,13},{10,... | collective-permute-start | bytes 2359304 | tf_op jit(solution)/shard_map/ppermute | solution.py:70
  159.4 34.8 %collective-permute-start.35 = (bf16[256,1536]{1,0:T(8,128)(2,1)}, bf16[256,1536]{1,0:T(8,128)(2,1)S(1)}, u32[]{:S(2)}, u32[]{:S(2)}) collective-permute-start(bf16[256,1536]{1,0:T(8,128)(2,1)} %get-tuple-element.297.refs_0_), channel_id=1, source_target_pairs={{0,2},{1,3},{2,0},{3,1},{4,6},{5,7},{6,4},{7,5},{8,10},{9,11},{10,... | collective-permute-start | bytes 2359304 | tf_op jit(solution)/shard_map/ppermute | solution.py:70
  159.8 34.8 %collective-permute-start.45 = (bf16[256,1536]{1,0:T(8,128)(2,1)S(1)}, bf16[256,1536]{1,0:T(8,128)(2,1)S(1)}, u32[]{:S(2)}, u32[]{:S(2)}) collective-permute-start(bf16[256,1536]{1,0:T(8,128)(2,1)S(1)} %copy-done.13), channel_id=1, source_target_pairs={{0,1},{1,0},{2,3},{3,2},{4,5},{5,4},{6,7},{7,6},{8,9},{9,8},{10,11... | collective-permute-start | bytes 2359304 | tf_op jit(solution)/shard_map/ppermute | solution.py:68
  159.9 34.7 %collective-permute-start.38 = (bf16[256,1536]{1,0:T(8,128)(2,1)}, bf16[256,1536]{1,0:T(8,128)(2,1)S(1)}, u32[]{:S(2)}, u32[]{:S(2)}) collective-permute-start(bf16[256,1536]{1,0:T(8,128)(2,1)} %get-tuple-element.297.refs_0_), channel_id=1, source_target_pairs={{0,1},{1,0},{2,3},{3,2},{4,5},{5,4},{6,7},{7,6},{8,9},{9,8},{10,11... | collective-permute-start | bytes 2359304 | tf_op jit(solution)/shard_map/ppermute | solution.py:68
  177.8 16.8 %collective-permute-start.41 = (bf16[256,1536]{1,0:T(8,128)(2,1)S(1)}, bf16[256,1536]{1,0:T(8,128)(2,1)S(1)}, u32[]{:S(2)}, u32[]{:S(2)}) collective-permute-start(bf16[256,1536]{1,0:T(8,128)(2,1)S(1)} %collective-permute-done.37.refs_3_), channel_id=1, source_target_pairs={{0,1},{1,0},{2,3},{3,2},{4,5},{5,4},{6,7},{7,6},{8,9},{9,8},{10,11... | collective-permute-start | bytes 2359304 | tf_op jit(solution)/shard_map/ppermute | solution.py:68
  235.6 174.2 %reduce-scatter.6.cloned.1.call-start = ((), (), s32[]{:S(2)}) async-start(), calls=%async_computation.4 | async-start | bytes 3932160 | tf_op jit(solution)/shard_map/reduce_scatter | solution.py:680
  244.0 37.9 %collective-permute-start.27 = (bf16[1024,1536]{1,0:T(8,128)(2,1)S(1)}, bf16[1024,1536]{1,0:T(8,128)(2,1)}, u32[]{:S(2)}, u32[]{:S(2)}) collective-permute-start(bf16[1024,1536]{1,0:T(8,128)(2,1)S(1)} %get-tuple-element.161), channel_id=1, source_target_pairs={{0,1},{1,0},{2,3},{3,2},{4,5},{5,4},{6,7},{7,6},{8,9},{9,8},{10,11... | collective-permute-start | bytes 9437192 | tf_op jit(solution)/shard_map/cond/branch_1_fun/ppermute | solution.py:68
  244.2 20.4 %collective-permute-start.24 = (bf16[256,1536]{1,0:T(8,128)(2,1)S(1)}, bf16[256,1536]{1,0:T(8,128)(2,1)S(1)}, u32[]{:S(2)}, u32[]{:S(2)}) collective-permute-start(bf16[256,1536]{1,0:T(8,128)(2,1)S(1)} %get-tuple-element.158), channel_id=1, source_target_pairs={{0,2},{1,3},{2,0},{3,1},{4,6},{5,7},{6,4},{7,5},{8,10},{9,11},{10,... | collective-permute-start | bytes 2359304 | tf_op jit(solution)/shard_map/cond/branch_1_fun/ppermute | solution.py:70
  245.6 36.4 %collective-permute-start.25 = (bf16[256,1536]{1,0:T(8,128)(2,1)S(1)}, bf16[256,1536]{1,0:T(8,128)(2,1)S(1)}, u32[]{:S(2)}, u32[]{:S(2)}) collective-permute-start(bf16[256,1536]{1,0:T(8,128)(2,1)S(1)} %get-tuple-element.159), channel_id=1, source_target_pairs={{0,4},{1,5},{2,6},{3,7},{4,0},{5,1},{6,2},{7,3},{8,12},{9,13},{10,... | collective-permute-start | bytes 2359304 | tf_op jit(solution)/shard_map/cond/branch_1_fun/ppermute | solution.py:70
  247.0 34.9 %collective-permute-start.26 = (bf16[256,1536]{1,0:T(8,128)(2,1)S(1)}, bf16[256,1536]{1,0:T(8,128)(2,1)S(1)}, u32[]{:S(2)}, u32[]{:S(2)}) collective-permute-start(bf16[256,1536]{1,0:T(8,128)(2,1)S(1)} %get-tuple-element.160), channel_id=1, source_target_pairs={{0,6},{1,7},{2,4},{3,5},{4,2},{5,3},{6,0},{7,1},{8,14},{9,15},{10,... | collective-permute-start | bytes 2359304 | tf_op jit(solution)/shard_map/cond/branch_1_fun/ppermute | solution.py:70
  300.5 32.6 %collective-permute-start.28 = (bf16[4,48,1664]{2,1,0:T(8,128)(2,1)}, bf16[4,48,1664]{2,1,0:T(8,128)(2,1)}, u32[]{:S(2)}, u32[]{:S(2)}) collective-permute-start(bf16[4,48,1664]{2,1,0:T(8,128)(2,1)} %bitcast.10), channel_id=1, source_target_pairs={{0,2},{1,3},{2,0},{3,1},{4,6},{5,7},{6,4},{7,5},{8,10},{9,11},{10,... | collective-permute-start | bytes 1916936 | tf_op jit(solution)/shard_map/cond/branch_1_fun/ppermute | solution.py:70
  301.8 31.3 %collective-permute-start.29 = (bf16[4,48,1664]{2,1,0:T(8,128)(2,1)}, bf16[4,48,1664]{2,1,0:T(8,128)(2,1)}, u32[]{:S(2)}, u32[]{:S(2)}) collective-permute-start(bf16[4,48,1664]{2,1,0:T(8,128)(2,1)} %bitcast.11), channel_id=1, source_target_pairs={{0,4},{1,5},{2,6},{3,7},{4,0},{5,1},{6,2},{7,3},{8,12},{9,13},{10,... | collective-permute-start | bytes 1916936 | tf_op jit(solution)/shard_map/cond/branch_1_fun/ppermute | solution.py:70
  302.6 30.5 %collective-permute-start.30 = (bf16[4,48,1664]{2,1,0:T(8,128)(2,1)}, bf16[4,48,1664]{2,1,0:T(8,128)(2,1)}, u32[]{:S(2)}, u32[]{:S(2)}) collective-permute-start(bf16[4,48,1664]{2,1,0:T(8,128)(2,1)} %bitcast.12), channel_id=1, source_target_pairs={{0,6},{1,7},{2,4},{3,5},{4,2},{5,3},{6,0},{7,1},{8,14},{9,15},{10,... | collective-permute-start | bytes 1916936 | tf_op jit(solution)/shard_map/cond/branch_1_fun/ppermute | solution.py:70
  336.2 115.7 %reduce-scatter.8.cloned.1.call-start = ((), (), s32[]{:S(2)}) async-start(), calls=%async_computation.5 | async-start | bytes 2273280 | tf_op jit(solution)/shard_map/reduce_scatter | solution.py:680
  348.8 28.9 %collective-permute-start.49 = (bf16[4,48,3072]{2,1,0:T(8,128)(2,1)S(1)}, bf16[4,48,3072]{2,1,0:T(8,128)(2,1)S(1)}, u32[]{:S(2)}, u32[]{:S(2)}) collective-permute-start(bf16[4,48,3072]{2,1,0:T(8,128)(2,1)S(1)} %get-tuple-element.345), channel_id=1, source_target_pairs={{0,2},{1,3},{2,0},{3,1},{4,6},{5,7},{6,4},{7,5},{8,10},{9,11},{10,... | collective-permute-start | bytes 3538952 | tf_op jit(solution)/shard_map/ppermute | solution.py:70
  350.1 53.1 %collective-permute-start.51 = (bf16[4,48,3072]{2,1,0:T(8,128)(2,1)S(1)}, bf16[4,48,3072]{2,1,0:T(8,128)(2,1)S(1)}, u32[]{:S(2)}, u32[]{:S(2)}) collective-permute-start(bf16[4,48,3072]{2,1,0:T(8,128)(2,1)S(1)} %get-tuple-element.346), channel_id=1, source_target_pairs={{0,6},{1,7},{2,4},{3,5},{4,2},{5,3},{6,0},{7,1},{8,14},{9,15},{10,... | collective-permute-start | bytes 3538952 | tf_op jit(solution)/shard_map/ppermute | solution.py:70
  351.8 52.7 %collective-permute-start.50 = (bf16[4,48,3072]{2,1,0:T(8,128)(2,1)S(1)}, bf16[4,48,3072]{2,1,0:T(8,128)(2,1)S(1)}, u32[]{:S(2)}, u32[]{:S(2)}) collective-permute-start(bf16[4,48,3072]{2,1,0:T(8,128)(2,1)S(1)} %get-tuple-element.347), channel_id=1, source_target_pairs={{0,4},{1,5},{2,6},{3,7},{4,0},{5,1},{6,2},{7,3},{8,12},{9,13},{10,... | collective-permute-start | bytes 3538952 | tf_op jit(solution)/shard_map/ppermute | solution.py:70
  413.2 21.6 %collective-permute-start.54 = (bf16[256,1536]{1,0:T(8,128)(2,1)}, bf16[256,1536]{1,0:T(8,128)(2,1)S(1)}, u32[]{:S(2)}, u32[]{:S(2)}) collective-permute-start(bf16[256,1536]{1,0:T(8,128)(2,1)} %get-tuple-element.331), channel_id=1, source_target_pairs={{0,6},{1,7},{2,4},{3,5},{4,2},{5,3},{6,0},{7,1},{8,14},{9,15},{10,... | collective-permute-start | bytes 2359304 | tf_op jit(solution)/shard_map/ppermute | solution.py:70
  414.4 34.2 %collective-permute-start.53 = (bf16[256,1536]{1,0:T(8,128)(2,1)}, bf16[256,1536]{1,0:T(8,128)(2,1)}, u32[]{:S(2)}, u32[]{:S(2)}) collective-permute-start(bf16[256,1536]{1,0:T(8,128)(2,1)} %get-tuple-element.329), channel_id=1, source_target_pairs={{0,4},{1,5},{2,6},{3,7},{4,0},{5,1},{6,2},{7,3},{8,12},{9,13},{10,... | collective-permute-start | bytes 2359304 | tf_op jit(solution)/shard_map/ppermute | solution.py:70
  415.2 33.4 %collective-permute-start.52 = (bf16[256,1536]{1,0:T(8,128)(2,1)}, bf16[256,1536]{1,0:T(8,128)(2,1)}, u32[]{:S(2)}, u32[]{:S(2)}) collective-permute-start(bf16[256,1536]{1,0:T(8,128)(2,1)} %get-tuple-element.320), channel_id=1, source_target_pairs={{0,2},{1,3},{2,0},{3,1},{4,6},{5,7},{6,4},{7,5},{8,10},{9,11},{10,... | collective-permute-start | bytes 2359304 | tf_op jit(solution)/shard_map/ppermute | solution.py:70
  (52 other events, 636.7 us)
Sparse Core Ops, SparseCore 0:
  34.7 73.0 all-gather.4
  109.4 88.0 all-gather.6
  235.7 83.6 reduce-scatter.3
  336.4 58.6 reduce-scatter.5
  409.9 37.2 reduce-scatter.7

commit v7 on v6

--- a/solution.py
+++ b/solution.py
@@ -455,10 +455,10 @@
 
 def ffn_body(count, *refs):
     second, grads, shards = refs[:count], refs[count : 2 * count], refs[2 * count]
-    out_a, out_b, back_a, back_b, sums = refs[2 * count + 1 : 2 * count + 6]
+    out_a, out_b, *backs, sums = refs[2 * count + 1 : 3 * count + 4]
     (
         second_v, grads_v, weights, hidden, gate_g, up_g, hidden_t, gate_t, up_t, sums_v, sems, row_sems, sum_sem,
-    ) = refs[2 * count + 6 :]
+    ) = refs[3 * count + 4 :]
     rows = second[0].shape[0]
     blocks, units = shards.shape[0], shards.shape[1] // 3
     weight_copies = [
@@ -515,9 +515,7 @@
 
     half = count * rows // 2
     copies = []
-    for n, (kind, first, target) in enumerate(
-        (("b", half, back_b), ("b", 0, back_a), ("o", half, out_b), ("o", 0, out_a))
-    ):
+    for n, (kind, first) in enumerate((("b", half), ("b", 0), ("o", half), ("o", 0))):
         place = second_v if kind == "b" else grads_v
         for k in range(half // step):
             here = slice(first + k * step, first + (k + 1) * step)
@@ -526,14 +524,18 @@
             else:
                 value = mm(hidden[here, :], weights[2])
             place[here, :] = value.astype(BF)
-            copies.append(
-                pltpu.make_async_copy(
-                    place.at[pl.ds(first + k * step, step)],
-                    target.at[pl.ds(k * step, step)],
-                    row_sems.at[n, k],
+            for i in range(per):
+                row = first + k * step + i * rows
+                if kind == "b":
+                    target = backs[row // rows]
+                else:
+                    target = (out_b if first else out_a).at[pl.ds(row - first, rows)]
+                copies.append(
+                    pltpu.make_async_copy(
+                        place.at[pl.ds(row, rows)], target, row_sems.at[n, k * per + i]
+                    )
                 )
-            )
-            copies[-1].start()
+                copies[-1].start()
     sum_copy.wait()
     for copy in copies:
         copy.wait()
@@ -546,9 +548,9 @@
     sds = jax.ShapeDtypeStruct
     return kernel_call(
         functools.partial(ffn_body, pieces),
-        (sds((count // 2, width), BF),) * 4 + (sds(weights.shape, BF),),
+        (sds((count // 2, width), BF),) * 2 + (sds((rows, width), BF),) * pieces + (sds(weights.shape, BF),),
         [ANY] * (2 * pieces + 1),
-        (ANY,) * 5,
+        (ANY,) * (pieces + 3),
         [
             pltpu.VMEM((count, width), BF), pltpu.VMEM((count, width), BF),
             pltpu.VMEM((3, total, width), BF),
@@ -556,7 +558,7 @@
             pltpu.VMEM((total, count), BF), pltpu.VMEM((total, count), BF), pltpu.VMEM((total, count), BF),
             pltpu.VMEM(weights.shape, BF),
             pltpu.SemaphoreType.DMA((5, max(weights.shape[0], pieces))),
-            pltpu.SemaphoreType.DMA((4, max(count // 2 // (2 * rows), 1))),
+            pltpu.SemaphoreType.DMA((4, pieces // 2)),
             pltpu.SemaphoreType.DMA,
         ],
         18 * count * total * width,
@@ -565,7 +567,9 @@
     )
 
 
-def project_sums_body(seqs, split, meta, normed_t, query_back, pair_back, send, keep):
+def project_sums_body(
+    seqs, split, meta, normed_t, query_back, pair_back, pair_send, pair_keep, query_send, query_keep
+):
     place = meta[0]
     wide = normed_t.shape[1] // seqs
     rows = query_back.shape[1] // seqs
@@ -577,10 +581,10 @@
             axis=1,
         )
         store_rows(
-            meta, split, mm_t(own, query_back[...]), n * step, send, keep, pl.ds(PAIR, QUERY)
+            meta, split, mm_t(own, query_back[...]), n * step, query_send, query_keep, pl.ds(0, QUERY)
         )
         store_rows(
-            meta, split, mm_t(normed_t[cut, :], pair_back[...]), n * step, send, keep, pl.ds(0, PAIR)
+            meta, split, mm_t(normed_t[cut, :], pair_back[...]), n * step, pair_send, pair_keep, pl.ds(0, PAIR)
         )
 
 
@@ -588,9 +592,9 @@
     width = normed_t.shape[0]
     return kernel_call(
         functools.partial(project_sums_body, seqs, split),
-        sums_shapes(split, parts, width, PAIR + QUERY),
+        (*sums_shapes(split, parts, width, PAIR), *sums_shapes(split, parts, width, QUERY)),
         [SMEM, VMEM, VMEM, VMEM],
-        (VMEM,) * 2,
+        (VMEM,) * 4,
         [],
         1,
         26 << 20,
@@ -825,21 +829,15 @@
     second_spread = cores(spread(second))
     outs, backs, ffn_sum = [], [], None
     for n in range(0, 2 * half, 8):
-        *parts, sums = ffn(second_spread[n : n + 8] + grad_spread[n : n + 8], ffn_w)
-        outs += parts[:2]
-        backs += parts[2:]
+        out_a, out_b, *parts, sums = ffn(second_spread[n : n + 8] + grad_spread[n : n + 8], ffn_w)
+        outs += [out_a, out_b]
+        backs += parts
         ffn_sum = sums if ffn_sum is None else in_f32(ffn_sum) + in_f32(sums)
     if len(outs) > 2:
         outs = (jnp.concatenate(outs[: len(outs) // 2]), jnp.concatenate(outs[len(outs) // 2 :]))
-        backs = (jnp.concatenate(backs[: len(backs) // 2]), jnp.concatenate(backs[len(backs) // 2 :]))
     grad_ffn = sum_z(ffn_sum.astype(BF))
-    back, other = halves((backs[0], step("c", backs[1])))
-
-    def second_round(first, second, blocks, out):
-        moved, out = lax.optimization_barrier((blocks_to(blocks), step("c", out)))
-        return total(in_f32(first) + in_f32(second), moved), out
-
-    second_grad, out_other = window(second_round, back[0], other[0], to_send(back, other), outs[1])
+    back, other = backs[:half], [step("c", part) for part in backs[half:]]
+    second_grad = total(in_f32(back[0]) + in_f32(other[0]), blocks_to(to_send(back, other)))
 
     def pieces_for(send, keep):
         if split:
@@ -869,25 +867,30 @@
     out_send, mixed_grad_t = lax.optimization_barrier((moving, mixed_grad_t))
     blocks = to_send(out_keep, out_send)
 
-    def attention_beside(first, second, blocks, meta, query_t, pair_t, mixed_grad_t, logs, cosine, sine, normed_t):
-        moved = blocks_to(blocks)
+    def attention_beside(first, second, blocks, meta, query_t, pair_t, mixed_grad_t, logs, cosine, sine, normed_t, out):
+        moved, out = blocks_to(blocks), step("c", out)
         query_back, pair_back, pair_blocks = attend_backward(
             meta, query_t, pair_t, mixed_grad_t, logs, cosine, sine, seqs
         )
-        send, keep = project_sums(meta, normed_t, query_back, pair_back, seqs, (Z, Q), split)
-        keep, moved = lax.optimization_barrier((keep, moved))
+        sums = project_sums(meta, normed_t, query_back, pair_back, seqs, (Z, Q), split)
+        sums, moved, out = lax.optimization_barrier((tuple(sums), moved, out))
         out_rows = total(in_f32(first) + in_f32(second), moved).astype(BF)
-        return out_rows, query_back, pair_blocks, send, keep
-
-    out_rows, query_back, pair_blocks, send, keep = window(
+        return out_rows, query_back, pair_blocks, sums, out
+
+    out_rows, query_back, pair_blocks, sums, out_other = window(
         attention_beside, out_keep[0], out_send[0], blocks, meta, query_t, pair_t, mixed_grad_t, logs,
-        cosine, sine, normed_t,
+        cosine, sine, normed_t, outs[1],
     )
     grad_ffn, pair_blocks = lax.optimization_barrier((grad_ffn, pair_blocks))
     pair_own = sum_z(pair_blocks)
-    send, keep = pieces_for(send, keep)
-    send = step("c", send)
-    rows_of = total(in_f32(keep[0]) + in_f32(send[0]), blocks_to(to_send(keep, send))).astype(BF)
+    pair_send, pair_keep = pieces_for(*sums[:2])
+    query_send, query_keep = pieces_for(*sums[2:])
+    pair_send, query_send = step("c", pair_send), step("c", query_send)
+    pair_blocks_out = blocks_to(to_send(pair_keep, pair_send))
+    query_blocks_out = blocks_to(to_send(query_keep, query_send))
+    pair_rows = total(in_f32(pair_keep[0]) + in_f32(pair_send[0]), pair_blocks_out).astype(BF)
+    query_rows = total(in_f32(query_keep[0]) + in_f32(query_send[0]), query_blocks_out).astype(BF)
+    rows_of = jnp.concatenate([pair_rows, query_rows], axis=-1)
     out, out_other = halves((outs[0], out_other))
     blocks = [after(block, rows_of) for block in to_send(out, out_other)]
     rows_of, pair_own = lax.optimization_barrier((jnp.concatenate([rows_of, out_rows], axis=-1), pair_own))

time: 472 us -> 464 us (0.983)
  waiting for transfers between devices: 220 us -> 208 us
  starting transfers between devices: 46.6 us -> 51.5 us
    ppermute x22 -> x26, waiting for transfers between devices: 18.5 us -> 11.6 us  [step(): return lax.ppermute(value, 'dp', [(n, n ^ 1) for n in range(self.DP)])]
    ppermute x27 -> x30, waiting for transfers between devices: 153 us -> 148 us  [step(): lax.ppermute(value, 'dp', [(n, n % 4 ^ 2 * i | 4 * ((n // 4 + j) % self.Q...]
    ppermute x27 -> x30, starting transfers between devices: 33.2 us -> 36.9 us  [step(): lax.ppermute(value, 'dp', [(n, n % 4 ^ 2 * i | 4 * ((n // 4 + j) % self.Q...]
    convert_element_type x4 -> x7, other arithmetic: 13.8 us -> 12.7 us  [to_send(): (in_f32(own[n]) + in_f32(other[n])).astype(BF)]
  transfers between devices with their start and end apart: 60 -> 67, of which waited for: 29 -> 32; matrix products, arithmetic and copies ran while one was open for 9% -> 9% of each run, Pallas kernels for 19% -> 20%
where the time goes in v7:
time: 464 us; the launch traced here: 456 us
  waiting for transfers between devices  208 us (45%)
  Pallas kernels  126 us (27%)
  starting transfers between devices  51.5 us (11%)
  other arithmetic  40.9 us (9%)
  between operations  14.5 us (3%)
  local copies, waits for them, and re-layouts  14 us (3%)
    ppermute x30, waiting for transfers between devices, step(): lax.ppermute(value, 'dp', [(n, n % 4 ^ 2 * i | 4 * ((n // 4 + j) % self.Q...  148 us
    pallas_call x9, Pallas kernels, kernel_call(): pl.pallas_call(body, out_shape=out_shape, in_specs=in_specs, out_specs=ou...  126 us
    ppermute x6, waiting for transfers between devices, around(): lax.ppermute(value, 'seq', [(n, (n + hop) % self.Z) for n in range(self.Z)])  43.1 us
    ppermute x30, starting transfers between devices, step(): lax.ppermute(value, 'dp', [(n, n % 4 ^ 2 * i | 4 * ((n // 4 + j) % self.Q...  36.9 us
    convert_element_type x7, other arithmetic, to_send(): (in_f32(own[n]) + in_f32(other[n])).astype(BF)  12.7 us
    ppermute x26, waiting for transfers between devices, step(): return lax.ppermute(value, 'dp', [(n, n ^ 1) for n in range(self.DP)])  11.6 us
  transfers between devices with their start and end apart: 67, of which 32 were waited for; matrix products, arithmetic and copies ran while one was open for 9% of the time, Pallas kernels for 20%

profile of v7, /device:TPU:0, one launch (start us, length us, event | category | flops | bytes accessed | tf_op | source)
XLA Modules:
  0.0 455.5 jit_solution(3257747919449239245)
XLA Ops:
  10.1 2.4 pad_maximum_fusion.4
  12.5 22.1 %conditional.7 = (bf16[48,3200]{1,0:T(8,128)(2,1)}, bf16[48,3200]{1,0:T(8,128)(2,1)}, bf16[256,1536]{1,0:T(8,128)(2,1)}, bf16[256,1536]{1,0:T(8,128)(2,1)}) conditional(s32[]{:T(128)} %convert_element_type.316, () %tuple.84, (bf16[48,3200]{1,0:T(8,128)(2,1)S(1)}, bf16[256,1536]{1,0:T(8,128)(2,1)S(1)}) %tuple.151), branch_computations={%region_0.1_spmd, %region_1.2_spmd} | conditional | bytes 8749248 | solution.py:673
  12.5 3.0 collective-permute-start.3
  16.9 3.6 collective-permute-start.1
  20.5 7.7 %collective-permute-done.1 = bf16[48,3200]{1,0:T(8,128)(2,1)} collective-permute-done((bf16[48,3200]{1,0:T(8,128)(2,1)S(1)}, bf16[48,3200]{1,0:T(8,128)(2,1)}, u32[]{:S(2)}, u32[]{:S(2)}) %collective-permute-start.1) | collective-permute-done | bytes 307232 | tf_op jit(solution)/shard_map/cond/branch_1_fun/ppermute | solution.py:64
  28.3 5.8 %collective-permute-done = bf16[48,3200]{1,0:T(8,128)(2,1)} collective-permute-done((bf16[48,3200]{1,0:T(8,128)(2,1)S(1)}, bf16[48,3200]{1,0:T(8,128)(2,1)}, u32[]{:S(2)}, u32[]{:S(2)}) %collective-permute-start) | collective-permute-done | bytes 307232 | tf_op jit(solution)/shard_map/cond/branch_1_fun/ppermute | solution.py:64
  35.4 13.6 %conditional.8 = (bf16[4,48,3200]{2,1,0:T(8,128)(2,1)S(1)}, bf16[256,1536]{1,0:T(8,128)(2,1)S(1)}) conditional(s32[]{:T(128)} %convert_element_type.316, () %tuple.83, (bf16[48,3200]{1,0:T(8,128)(2,1)S(1)}, bf16[48,3200]{1,0:T(8,128)(2,1)}, bf16[48,3200]{1,0:T(8,128)(2,1)}, bf16[256,1536]{1,0:T(8,128)(2,1)}, bf16[256,1536]{1,0:T(8,128)(2,1)}) %tuple.87), branch_computations={%region_2.3_spmd, %region_3.4_spmd} | conditional | flops 3416064 | bytes 9977992 | solution.py:673
  41.2 4.1 collective-permute-done.16
  49.8 30.7 %conditional.9 = (bf16[4,48,3200]{2,1,0:T(8,128)(2,1)}, bf16[4,48,3200]{2,1,0:T(8,128)(2,1)}, bf16[4,48,3200]{2,1,0:T(8,128)(2,1)}, bf16[48,1536]{1,0:T(8,128)(2,1)}, bf16[48,1536]{1,0:T(8,128)(2,1)}) conditional(s32[]{:T(128)} %convert_element_type.316, () %tuple.82, (bf16[4,48,3200]{2,1,0:T(8,128)(2,1)S(1)}, bf16[48,1536]{1,0:T(8,128)(2,1)S(1)}) %tuple.154), branch_computations={%region_4.5_spmd, %region_5.6_spmd} | conditional | bytes 15925488 | solution.py:673
  52.8 2.3 collective-permute-start.8
  55.1 11.4 %collective-permute-done.8 = bf16[48,1536]{1,0:T(8,128)(2,1)} collective-permute-done((bf16[48,1536]{1,0:T(8,128)(2,1)S(1)}, bf16[48,1536]{1,0:T(8,128)(2,1)}, u32[]{:S(2)}, u32[]{:S(2)}) %collective-permute-start.8) | collective-permute-done | bytes 147488 | tf_op jit(solution)/shard_map/cond/branch_1_fun/ppermute | solution.py:64
  66.5 4.2 collective-permute-done.7
  70.8 8.6 %collective-permute-done.5 = bf16[4,48,3200]{2,1,0:T(8,128)(2,1)} collective-permute-done((bf16[4,48,3200]{2,1,0:T(8,128)(2,1)S(1)}, bf16[4,48,3200]{2,1,0:T(8,128)(2,1)}, u32[]{:S(2)}, u32[]{:S(2)}) %collective-permute-start.5) | collective-permute-done | bytes 1228832 | tf_op jit(solution)/shard_map/cond/branch_1_fun/ppermute | solution.py:70
  80.5 19.1 %conditional.10 = (bf16[2,48,3200]{2,1,0:T(8,128)(2,1)}, bf16[2,48,3200]{2,1,0:T(8,128)(2,1)}, bf16[4,48,3200]{2,1,0:T(8,128)(2,1)}, bf16[4,48,3200]{2,1,0:T(8,128)(2,1)}, bf16[4,48,1536]{2,1,0:T(8,128)(2,1)}) conditional(s32[]{:T(128)} %convert_element_type.316, () %tuple.81, (bf16[4,48,3200]{2,1,0:T(8,128)(2,1)}, bf16[4,48,3200]{2,1,0:T(8,128)(2,1)}, ...), branch_computations={%region_6.7_spmd, %region_7.8_spmd} | conditional | flops 884736 | bytes 18972912 | solution.py:673
  87.1 9.8 %collective-permute-done.23 = bf16[48,1536]{1,0:T(8,128)(2,1)S(1)} collective-permute-done((bf16[48,1536]{1,0:T(8,128)(2,1)}, bf16[48,1536]{1,0:T(8,128)(2,1)S(1)}, u32[]{:S(2)}, u32[]{:S(2)}) %collective-permute-start.23) | collective-permute-done | bytes 147488 | tf_op jit(solution)/shard_map/cond/branch_1_fun/ppermute | solution.py:64
  102.7 5.1 %all-gather.5.cloned.1.call-done = bf16[8,128,1536]{2,1,0:T(8,128)(2,1)} async-done(((bf16[2,128,1536]{2,1,0:T(8,128)(2,1)}), bf16[8,128,1536]{2,1,0:T(8,128)(2,1)}) %all-gather.5.cloned.1.call-update) | async-done | bytes 3145744 | tf_op jit(solution)/shard_map/all_gather | solution.py:681
  107.8 20.1 %conditional.11 = (bf16[4,48,1536]{2,1,0:T(8,128)(2,1)}, bf16[4,48,1536]{2,1,0:T(8,128)(2,1)}, bf16[1536,256]{1,0:T(8,128)(2,1)}, bf16[1536,1024]{1,0:T(8,128)(2...) conditional(s32[]{:T(128)} %convert_element_type.316, () %tuple.80, ...), branch_computations={%region_9.10_spmd, %region_10.11_spmd} | conditional | flops 6039797760 | bytes 35520724 | solution.py:673
  110.9 17.0 %branch_1_fun.4 = (bf16[1536,256]{1,0:T(8,128)(2,1)}, bf16[1536,1024]{1,0:T(8,128)(2,1)S(1)}, bf16[1536,1024]{1,0:T(8,128)(2,1)}, f32[8,1536]{1,0:T(8,128)S(1)}) custom-call(s32[4]{0:T(128)S(1)} %get-tuple-element.117.meta, bf16[4,2,128,1536]{3,2,1,0:T(8,128)(2,1)} %bitcast.89, f32[48,1024]{1,0:T(8,128)} %get-tuple-element.119.cosine, ...), custom_call_target="tpu_custom_call" | custom-call | flops 6039797760 | bytes 20971520 | tf_op jit(solution)/shard_map/cond/branch_1_fun/pallas_call | solution.py:85
  129.6 15.5 %conditional.12 = (bf16[2,48,1536]{2,1,0:T(8,128)(2,1)}, bf16[2,48,1536]{2,1,0:T(8,128)(2,1)}, bf16[4,48,1536]{2,1,0:T(8,128)(2,1)}, bf16[4,48,1536]{2,1,0:T(8,1...) conditional(s32[]{:T(128)} %convert_element_type.316, () %tuple.79, ...), branch_computations={%region_11.12_spmd, %region_12.13_spmd} | conditional | flops 805306368 | bytes 16908552 | solution.py:673
  132.8 12.2 %branch_1_fun.5 = (bf16[256,1536]{1,0:T(8,128)(2,1)}, bf16[1536,256]{1,0:T(8,128)(2,1)}, f32[8,2,1,256]{3,2,1,0:T(1,128)}) custom-call(s32[4]{0:T(128)S(1)} %get-tuple-element.138.meta, bf16[1536,256]{1,0:T(8,128)(2,1)} %get-tuple-element.139.query_t, bf16[1536,1024]{1,0:T(8,128)(2,1)S(1)} %get-tuple-element.140.pair_t), custom_call_target="tpu_custom_call" | custom-call | flops 805306368 | bytes 6291456 | tf_op jit(solution)/shard_map/cond/branch_1_fun/pallas_call | solution.py:85
  146.2 2.2 collective-permute-done.30.refs_7_
  150.0 7.0 %shard_map.203 = (f32[256,1536]{1,0:T(8,128)}, bf16[256,1536]{1,0:T(8,128)(2,1)}) custom-call(s32[4]{0:T(128)S(1)} %pad_add_fusion.meta, bf16[256,1536]{1,0:T(8,128)(2,1)} %bitcast.70, bf16[256,1536]{1,0:T(8,128)(2,1)} %get-tuple-element.281.mixed, f32[8,1536]{1,0:T(8,128)S(1)} %get-tuple-element.282.gain, bf16[4,48,1536]{2,1,0:T(8,128)(2,1)} %get-tuple-element.270.refs_0_, ...), custom_call_target="tpu_custom_call" | custom-call | flops 1207959552 | bytes 10485760 | tf_op jit(solution)/shard_map/pallas_call | solution.py:85
  157.0 2.9 collective-permute-start.34
  161.2 17.4 %collective-permute-done.34.refs_3_ = bf16[256,1536]{1,0:T(8,128)(2,1)S(1)} collective-permute-done((bf16[256,1536]{1,0:T(8,128)(2,1)}, bf16[256,1536]{1,0:T(8,128)(2,1)S(1)}, u32[]{:S(2)}, u32[]{:S(2)}) %collective-permute-start.34) | collective-permute-done | bytes 786464 | tf_op jit(solution)/shard_map/ppermute | solution.py:70
  178.6 16.3 %collective-permute-done.33.refs_2_ = bf16[256,1536]{1,0:T(8,128)(2,1)S(1)} collective-permute-done((bf16[256,1536]{1,0:T(8,128)(2,1)}, bf16[256,1536]{1,0:T(8,128)(2,1)S(1)}, u32[]{:S(2)}, u32[]{:S(2)}) %collective-permute-start.33) | collective-permute-done | bytes 786464 | tf_op jit(solution)/shard_map/ppermute | solution.py:70
  198.4 37.0 %shard_map.204 = (bf16[1024,1536]{1,0:T(8,128)(2,1)}, bf16[1024,1536]{1,0:T(8,128)(2,1)}, bf16[256,1536]{1,0:T(8,128)(2,1)}, bf16[256,1536]{1,0:T(8,128)(2,1)}, ...) custom-call(bf16[256,1536]{1,0:T(8,128)(2,1)} %get-tuple-element.289, ...), custom_call_target="tpu_custom_call" | custom-call | flops 28991029248 | bytes 35651584 | tf_op jit(solution)/shard_map/pallas_call | solution.py:85
  243.5 16.4 %collective-permute-done.45 = bf16[256,1536]{1,0:T(8,128)(2,1)} collective-permute-done((bf16[256,1536]{1,0:T(8,128)(2,1)S(1)}, bf16[256,1536]{1,0:T(8,128)(2,1)}, u32[]{:S(2)}, u32[]{:S(2)}) %collective-permute-start.45) | collective-permute-done | bytes 786464 | tf_op jit(solution)/shard_map/ppermute | solution.py:70
  259.9 17.4 %collective-permute-done.47 = bf16[256,1536]{1,0:T(8,128)(2,1)} collective-permute-done((bf16[256,1536]{1,0:T(8,128)(2,1)S(1)}, bf16[256,1536]{1,0:T(8,128)(2,1)}, u32[]{:S(2)}, u32[]{:S(2)}) %collective-permute-start.47) | collective-permute-done | bytes 786464 | tf_op jit(solution)/shard_map/ppermute | solution.py:70
  277.3 3.7 convert_add_fusion.second_grad
  281.0 7.0 %shard_map.205 = (f32[256,1536]{1,0:T(8,128)}, bf16[256,1536]{1,0:T(8,128)(2,1)}, bf16[4,4,48,1664]{3,2,1,0:T(8,128)(2,1)}, bf16[4,4,48,1664]{3,2,1,0:T(8,128)(2,1)}) custom-call(bf16[256,1536]{1,0:T(8,128)(2,1)S(1)} %bitcast.79, f32[256,1536]{1,0:T(8,128)} %get-tuple-element.288.total, f32[256,1536]{1,0:T(8,128)} %convert_add_fusion.second_grad, ...), custom_call_target="tpu_custom_call" | custom-call | flops 1207959552 | bytes 14680064 | tf_op jit(solution)/shard_map/pallas_call | solution.py:85
  287.9 6.2 %shard_map.206 = bf16[1536,256]{1,0:T(8,128)(2,1)} custom-call(s32[4]{0:T(128)S(1)} %pad_add_fusion.meta, bf16[256,1536]{1,0:T(8,128)(2,1)} %get-tuple-element.308.da, bf16[4,48,1536]{2,1,0:T(8,128)(2,1)} %get-tuple-element.270.refs_0_, bf16[4,48,1536]{2,1,0:T(8,128)(2,1)} %get-tuple-element.283.refs_1_, bf16[4,48,1536]{2,1,0:T(8,128)(2,1)} %get-tuple-element.278.refs_2_, ...), custom_call_target="tpu_custom_call" | custom-call | flops 999999995904 | bytes 8388608 | tf_op jit(solution)/shard_map/pallas_call | solution.py:85
  294.2 3.7 add_convert_fusion.7
  297.9 35.6 %conditional.13 = (bf16[4,48,1664]{2,1,0:T(8,128)(2,1)}, bf16[1536,256]{1,0:T(8,128)(2,1)}, bf16[4,1536,256]{2,1,0:T(8,128)(2,1)}, bf16[4,4,48,1536]{3,2,1,0:T(8...) conditional(s32[]{:T(128)} %convert_element_type.316, () %tuple.96, ...), branch_computations={%region_13.14_spmd, %region_14.15_spmd} | conditional | flops 1000003207168 | bytes 63930592 | solution.py:673
  301.5 15.9 %branch_1_fun.6 = (bf16[1536,256]{1,0:T(8,128)(2,1)}, bf16[1536,1024]{1,0:T(8,128)(2,1)}, bf16[4,1536,256]{2,1,0:T(8,128)(2,1)}) custom-call(s32[4]{0:T(128)S(1)} %get-tuple-element.146.meta, bf16[1536,256]{1,0:T(8,128)(2,1)} %get-tuple-element.148.query_t, bf16[1536,1024]{1,0:T(8,128)(2,1)S(1)} %get-tuple-element.149.pair_t, ...), custom_call_target="tpu_custom_call" | custom-call | flops 999999995904 | bytes 12582912 | tf_op jit(solution)/shard_map/cond/branch_1_fun/pallas_call | solution.py:85
  317.4 13.0 %branch_1_fun.7 = (bf16[4,4,48,1536]{3,2,1,0:T(8,128)(2,1)}, bf16[4,4,48,1536]{3,2,1,0:T(8,128)(2,1)}, bf16[4,4,48,1536]{3,2,1,0:T(8,128)(2,1)}, bf16[4,4,48,1536]{3,2,1,0:T(8,128)(2,1)}) custom-call(s32[4]{0:T(128)S(1)} %get-tuple-element.146.meta, bf16[1536,1024]{1,0:T(8,128)(2,1)} %get-tuple-element.147.normed_t, ...), custom_call_target="tpu_custom_call" | custom-call | flops 1 | bytes 27262976 | tf_op jit(solution)/shard_map/cond/branch_1_fun/pallas_call | solution.py:85
  330.4 3.1 fusion.2
  334.3 4.3 collective-permute-done.51
  348.6 8.2 %collective-permute-done.52 = bf16[4,48,1536]{2,1,0:T(8,128)(2,1)S(1)} collective-permute-done((bf16[4,48,1536]{2,1,0:T(8,128)(2,1)S(1)}, bf16[4,48,1536]{2,1,0:T(8,128)(2,1)S(1)}, u32[]{:S(2)}, u32[]{:S(2)}) %collective-permute-start.52) | collective-permute-done | bytes 589856 | tf_op jit(solution)/shard_map/ppermute | solution.py:70
  357.8 12.1 %collective-permute-done.54 = bf16[4,48,1536]{2,1,0:T(8,128)(2,1)S(1)} collective-permute-done((bf16[4,48,1536]{2,1,0:T(8,128)(2,1)S(1)}, bf16[4,48,1536]{2,1,0:T(8,128)(2,1)S(1)}, u32[]{:S(2)}, u32[]{:S(2)}) %collective-permute-start.54) | collective-permute-done | bytes 589856 | tf_op jit(solution)/shard_map/ppermute | solution.py:70
  369.9 2.1 collective-permute-done.53
  372.0 10.1 %collective-permute-done.56 = bf16[4,48,1536]{2,1,0:T(8,128)(2,1)S(1)} collective-permute-done((bf16[4,48,1536]{2,1,0:T(8,128)(2,1)S(1)}, bf16[4,48,1536]{2,1,0:T(8,128)(2,1)S(1)}, u32[]{:S(2)}, u32[]{:S(2)}) %collective-permute-start.56) | collective-permute-done | bytes 589856 | tf_op jit(solution)/shard_map/ppermute | solution.py:70
  382.1 12.6 %collective-permute-done.58 = bf16[4,48,1536]{2,1,0:T(8,128)(2,1)S(1)} collective-permute-done((bf16[4,48,1536]{2,1,0:T(8,128)(2,1)S(1)}, bf16[4,48,1536]{2,1,0:T(8,128)(2,1)S(1)}, u32[]{:S(2)}, u32[]{:S(2)}) %collective-permute-start.58) | collective-permute-done | bytes 589856 | tf_op jit(solution)/shard_map/ppermute | solution.py:70
  398.9 2.6 pad_maximum_fusion.3
  401.6 3.4 add_convert_fusion.3
  410.0 11.0 %shard_map.207 = bf16[256,1536]{1,0:T(8,128)(2,1)} custom-call(s32[4]{0:T(128)S(1)} %pad_add_fusion.meta, bf16[256,1536]{1,0:T(8,128)(2,1)} %bitcast.71, f32[8,1536]{1,0:T(8,128)S(1)} %copy-done.9, f32[256,1536]{1,0:T(8,128)} %get-tuple-element.320.first_grad, bf16[1536,256]{1,0:T(8,128)(2,1)} %get-tuple-element.321.query_back, bf16[1536,256]{1,0:T(8,128)(2,1)} %bitcast.74, ...), custom_call_target="tpu_custom_call" | custom-call | flops 2415919104 | bytes 14680064 | tf_op jit(solution)/shard_map/pallas_call | solution.py:85
  421.1 4.7 %collective-permute-done.59 = bf16[256,1536]{1,0:T(8,128)(2,1)S(1)} collective-permute-done((bf16[256,1536]{1,0:T(8,128)(2,1)}, bf16[256,1536]{1,0:T(8,128)(2,1)S(1)}, u32[]{:S(2)}, u32[]{:S(2)}) %collective-permute-start.59) | collective-permute-done | bytes 786464 | tf_op jit(solution)/shard_map/ppermute | solution.py:70
  425.7 15.5 %collective-permute-done.60 = bf16[256,1536]{1,0:T(8,128)(2,1)} collective-permute-done((bf16[256,1536]{1,0:T(8,128)(2,1)}, bf16[256,1536]{1,0:T(8,128)(2,1)}, u32[]{:S(2)}, u32[]{:S(2)}) %collective-permute-start.60) | collective-permute-done | bytes 786464 | tf_op jit(solution)/shard_map/ppermute | solution.py:70
  441.3 3.3 add_convert_fusion
  (236 shorter events, 84.3 us)
Async XLA Ops:
  7.2 100.6 %all-gather.5.cloned.1.call-start = ((), (), s32[]{:S(2)}) async-start(), calls=%async_computation.6 | async-start | bytes 3932160 | tf_op jit(solution)/shard_map/all_gather | solution.py:681
  12.5 21.6 %collective-permute-start.3 = (bf16[256,1536]{1,0:T(8,128)(2,1)S(1)}, bf16[256,1536]{1,0:T(8,128)(2,1)}, u32[]{:S(2)}, u32[]{:S(2)}) collective-permute-start(bf16[256,1536]{1,0:T(8,128)(2,1)S(1)} %get-tuple-element.103), channel_id=1, source_target_pairs={{0,4},{1,5},{2,6},{3,7},{4,0},{5,1},{6,2},{7,3},{8,12},{9,13},{10,... | collective-permute-start | bytes 2359304 | tf_op jit(solution)/shard_map/cond/branch_1_fun/ppermute | solution.py:70
  15.4 19.1 %collective-permute-start.2 = (bf16[256,1536]{1,0:T(8,128)(2,1)S(1)}, bf16[256,1536]{1,0:T(8,128)(2,1)}, u32[]{:S(2)}, u32[]{:S(2)}) collective-permute-start(bf16[256,1536]{1,0:T(8,128)(2,1)S(1)} %get-tuple-element.103), channel_id=1, source_target_pairs={{0,2},{1,3},{2,0},{3,1},{4,6},{5,7},{6,4},{7,5},{8,10},{9,11},{10,... | collective-permute-start | bytes 2359304 | tf_op jit(solution)/shard_map/cond/branch_1_fun/ppermute | solution.py:70
  34.6 163.9 %all-gather.7.cloned.1.call-start = ((), (), s32[]{:S(2)}) async-start(), calls=%async_computation.7 | async-start | bytes 5898240 | tf_op jit(solution)/shard_map/all_gather | solution.py:681
  35.3 298.2 %reduce-scatter.4.cloned.1.call-start = ((), (), s32[]{:S(2)}) async-start(), calls=%async_computation.3 | async-start | bytes 5898240 | tf_op jit(solution)/shard_map/reduce_scatter | solution.py:684
  49.8 20.9 %collective-permute-start.6 = (bf16[4,48,3200]{2,1,0:T(8,128)(2,1)S(1)}, bf16[4,48,3200]{2,1,0:T(8,128)(2,1)}, u32[]{:S(2)}, u32[]{:S(2)}) collective-permute-start(bf16[4,48,3200]{2,1,0:T(8,128)(2,1)S(1)} %get-tuple-element.109), channel_id=1, source_target_pairs={{0,1},{1,0},{2,3},{3,2},{4,5},{5,4},{6,7},{7,6},{8,9},{9,8},{10,11... | collective-permute-start | bytes 3686408 | tf_op jit(solution)/shard_map/cond/branch_1_fun/ppermute | solution.py:68
  49.8 29.5 %collective-permute-start.5 = (bf16[4,48,3200]{2,1,0:T(8,128)(2,1)S(1)}, bf16[4,48,3200]{2,1,0:T(8,128)(2,1)}, u32[]{:S(2)}, u32[]{:S(2)}) collective-permute-start(bf16[4,48,3200]{2,1,0:T(8,128)(2,1)S(1)} %get-tuple-element.109), channel_id=1, source_target_pairs={{0,4},{1,5},{2,6},{3,7},{4,0},{5,1},{6,2},{7,3},{8,12},{9,13},{10,... | collective-permute-start | bytes 3686408 | tf_op jit(solution)/shard_map/cond/branch_1_fun/ppermute | solution.py:70
  51.3 29.3 %collective-permute-start.4 = (bf16[4,48,3200]{2,1,0:T(8,128)(2,1)S(1)}, bf16[4,48,3200]{2,1,0:T(8,128)(2,1)}, u32[]{:S(2)}, u32[]{:S(2)}) collective-permute-start(bf16[4,48,3200]{2,1,0:T(8,128)(2,1)S(1)} %get-tuple-element.109), channel_id=1, source_target_pairs={{0,2},{1,3},{2,0},{3,1},{4,6},{5,7},{6,4},{7,5},{8,10},{9,11},{10,... | collective-permute-start | bytes 3686408 | tf_op jit(solution)/shard_map/cond/branch_1_fun/ppermute | solution.py:70
  52.8 13.8 %collective-permute-start.8 = (bf16[48,1536]{1,0:T(8,128)(2,1)S(1)}, bf16[48,1536]{1,0:T(8,128)(2,1)}, u32[]{:S(2)}, u32[]{:S(2)}) collective-permute-start(bf16[48,1536]{1,0:T(8,128)(2,1)S(1)} %get-tuple-element.110), channel_id=1, source_target_pairs={{0,24},{8,0},{16,8},{24,16},{1,25},{9,1},{17,9},{25,17},{2,26},{10... | collective-permute-start | bytes 442376 | tf_op jit(solution)/shard_map/cond/branch_1_fun/ppermute | solution.py:64
  55.1 15.7 %collective-permute-start.7 = (bf16[48,1536]{1,0:T(8,128)(2,1)S(1)}, bf16[48,1536]{1,0:T(8,128)(2,1)}, u32[]{:S(2)}, u32[]{:S(2)}) collective-permute-start(bf16[48,1536]{1,0:T(8,128)(2,1)S(1)} %get-tuple-element.110), channel_id=1, source_target_pairs={{0,8},{8,16},{16,24},{24,0},{1,9},{9,17},{17,25},{25,1},{2,10},{10... | collective-permute-start | bytes 442376 | tf_op jit(solution)/shard_map/cond/branch_1_fun/ppermute | solution.py:64
  80.5 19.1 %collective-permute-start.22 = (bf16[4,48,3200]{2,1,0:T(8,128)(2,1)}, bf16[4,48,3200]{2,1,0:T(8,128)(2,1)}, u32[]{:S(2)}, u32[]{:S(2)}) collective-permute-start(bf16[4,48,3200]{2,1,0:T(8,128)(2,1)} %get-tuple-element.111), channel_id=1, source_target_pairs={{0,1},{1,0},{2,3},{3,2},{4,5},{5,4},{6,7},{7,6},{8,9},{9,8},{10,11... | collective-permute-start | bytes 3686408 | tf_op jit(solution)/shard_map/cond/branch_1_fun/ppermute | solution.py:68
  80.5 19.1 %collective-permute-start.21 = (bf16[4,48,3200]{2,1,0:T(8,128)(2,1)}, bf16[4,48,3200]{2,1,0:T(8,128)(2,1)}, u32[]{:S(2)}, u32[]{:S(2)}) collective-permute-start(bf16[4,48,3200]{2,1,0:T(8,128)(2,1)} %get-tuple-element.112), channel_id=1, source_target_pairs={{0,1},{1,0},{2,3},{3,2},{4,5},{5,4},{6,7},{7,6},{8,9},{9,8},{10,11... | collective-permute-start | bytes 3686408 | tf_op jit(solution)/shard_map/cond/branch_1_fun/ppermute | solution.py:68
  82.2 16.6 %collective-permute-start.20 = (bf16[2,48,3200]{2,1,0:T(8,128)(2,1)S(1)}, bf16[2,48,3200]{2,1,0:T(8,128)(2,1)}, u32[]{:S(2)}, u32[]{:S(2)}) collective-permute-start(bf16[2,48,3200]{2,1,0:T(8,128)(2,1)S(1)} %slice.116), channel_id=1, source_target_pairs={{0,4},{1,5},{2,6},{3,7},{4,0},{5,1},{6,2},{7,3},{8,12},{9,13},{10,... | collective-permute-start | bytes 1843208 | tf_op jit(solution)/shard_map/cond/branch_1_fun/ppermute | solution.py:70
  83.9 15.7 %collective-permute-start.19 = (bf16[2,48,3200]{2,1,0:T(8,128)(2,1)S(1)}, bf16[2,48,3200]{2,1,0:T(8,128)(2,1)}, u32[]{:S(2)}, u32[]{:S(2)}) collective-permute-start(bf16[2,48,3200]{2,1,0:T(8,128)(2,1)S(1)} %slice.115), channel_id=1, source_target_pairs={{0,2},{1,3},{2,0},{3,1},{4,6},{5,7},{6,4},{7,5},{8,10},{9,11},{10,... | collective-permute-start | bytes 1843208 | tf_op jit(solution)/shard_map/cond/branch_1_fun/ppermute | solution.py:70
  107.9 20.1 %collective-permute-start.10 = (bf16[4,48,1536]{2,1,0:T(8,128)(2,1)}, bf16[4,48,1536]{2,1,0:T(8,128)(2,1)}, u32[]{:S(2)}, u32[]{:S(2)}) collective-permute-start(bf16[4,48,1536]{2,1,0:T(8,128)(2,1)} %get-tuple-element.116), channel_id=1, source_target_pairs={{0,4},{1,5},{2,6},{3,7},{4,0},{5,1},{6,2},{7,3},{8,12},{9,13},{10,... | collective-permute-start | bytes 1769480 | tf_op jit(solution)/shard_map/cond/branch_1_fun/ppermute | solution.py:70
  109.4 18.5 %collective-permute-start.9 = (bf16[4,48,1536]{2,1,0:T(8,128)(2,1)}, bf16[4,48,1536]{2,1,0:T(8,128)(2,1)}, u32[]{:S(2)}, u32[]{:S(2)}) collective-permute-start(bf16[4,48,1536]{2,1,0:T(8,128)(2,1)} %get-tuple-element.116), channel_id=1, source_target_pairs={{0,2},{1,3},{2,0},{3,1},{4,6},{5,7},{6,4},{7,5},{8,10},{9,11},{10,... | collective-permute-start | bytes 1769480 | tf_op jit(solution)/shard_map/cond/branch_1_fun/ppermute | solution.py:70
  129.6 15.5 %collective-permute-start.13 = (bf16[4,48,1536]{2,1,0:T(8,128)(2,1)}, bf16[4,48,1536]{2,1,0:T(8,128)(2,1)}, u32[]{:S(2)}, u32[]{:S(2)}) collective-permute-start(bf16[4,48,1536]{2,1,0:T(8,128)(2,1)} %get-tuple-element.137), channel_id=1, source_target_pairs={{0,1},{1,0},{2,3},{3,2},{4,5},{5,4},{6,7},{7,6},{8,9},{9,8},{10,11... | collective-permute-start | bytes 1769480 | tf_op jit(solution)/shard_map/cond/branch_1_fun/ppermute | solution.py:68
  129.6 15.5 %collective-permute-start.15 = (bf16[4,48,1536]{2,1,0:T(8,128)(2,1)}, bf16[4,48,1536]{2,1,0:T(8,128)(2,1)}, u32[]{:S(2)}, u32[]{:S(2)}) collective-permute-start(bf16[4,48,1536]{2,1,0:T(8,128)(2,1)} %get-tuple-element.135), channel_id=1, source_target_pairs={{0,1},{1,0},{2,3},{3,2},{4,5},{5,4},{6,7},{7,6},{8,9},{9,8},{10,11... | collective-permute-start | bytes 1769480 | tf_op jit(solution)/shard_map/cond/branch_1_fun/ppermute | solution.py:68
  130.1 15.0 %collective-permute-start.14 = (bf16[4,48,1536]{2,1,0:T(8,128)(2,1)}, bf16[4,48,1536]{2,1,0:T(8,128)(2,1)}, u32[]{:S(2)}, u32[]{:S(2)}) collective-permute-start(bf16[4,48,1536]{2,1,0:T(8,128)(2,1)} %get-tuple-element.136), channel_id=1, source_target_pairs={{0,1},{1,0},{2,3},{3,2},{4,5},{5,4},{6,7},{7,6},{8,9},{9,8},{10,11... | collective-permute-start | bytes 1769480 | tf_op jit(solution)/shard_map/cond/branch_1_fun/ppermute | solution.py:68
  131.1 13.9 %collective-permute-start.12 = (bf16[2,48,1536]{2,1,0:T(8,128)(2,1)S(1)}, bf16[2,48,1536]{2,1,0:T(8,128)(2,1)}, u32[]{:S(2)}, u32[]{:S(2)}) collective-permute-start(bf16[2,48,1536]{2,1,0:T(8,128)(2,1)S(1)} %slice.118), channel_id=1, source_target_pairs={{0,4},{1,5},{2,6},{3,7},{4,0},{5,1},{6,2},{7,3},{8,12},{9,13},{10,... | collective-permute-start | bytes 884744 | tf_op jit(solution)/shard_map/cond/branch_1_fun/ppermute | solution.py:70
  145.0 15.1 %collective-permute-start.39 = (bf16[256,1536]{1,0:T(8,128)(2,1)}, bf16[256,1536]{1,0:T(8,128)(2,1)S(1)}, u32[]{:S(2)}, u32[]{:S(2)}) collective-permute-start(bf16[256,1536]{1,0:T(8,128)(2,1)} %bitcast.76), channel_id=1, source_target_pairs={{0,1},{1,0},{2,3},{3,2},{4,5},{5,4},{6,7},{7,6},{8,9},{9,8},{10,11... | collective-permute-start | bytes 2359304 | tf_op jit(solution)/shard_map/ppermute | solution.py:68
  145.7 14.9 %collective-permute-start.40 = (bf16[256,1536]{1,0:T(8,128)(2,1)}, bf16[256,1536]{1,0:T(8,128)(2,1)S(1)}, u32[]{:S(2)}, u32[]{:S(2)}) collective-permute-start(bf16[256,1536]{1,0:T(8,128)(2,1)} %get-tuple-element.291.refs_9_), channel_id=1, source_target_pairs={{0,1},{1,0},{2,3},{3,2},{4,5},{5,4},{6,7},{7,6},{8,9},{9,8},{10,11... | collective-permute-start | bytes 2359304 | tf_op jit(solution)/shard_map/ppermute | solution.py:68
  146.1 14.6 %collective-permute-start.41 = (bf16[256,1536]{1,0:T(8,128)(2,1)}, bf16[256,1536]{1,0:T(8,128)(2,1)}, u32[]{:S(2)}, u32[]{:S(2)}) collective-permute-start(bf16[256,1536]{1,0:T(8,128)(2,1)} %get-tuple-element.292.refs_10_), channel_id=1, source_target_pairs={{0,1},{1,0},{2,3},{3,2},{4,5},{5,4},{6,7},{7,6},{8,9},{9,8},{10,11... | collective-permute-start | bytes 2359304 | tf_op jit(solution)/shard_map/ppermute | solution.py:68
  157.0 21.6 %collective-permute-start.34 = (bf16[256,1536]{1,0:T(8,128)(2,1)}, bf16[256,1536]{1,0:T(8,128)(2,1)S(1)}, u32[]{:S(2)}, u32[]{:S(2)}) collective-permute-start(bf16[256,1536]{1,0:T(8,128)(2,1)} %get-tuple-element.289.refs_0_), channel_id=1, source_target_pairs={{0,6},{1,7},{2,4},{3,5},{4,2},{5,3},{6,0},{7,1},{8,14},{9,15},{10,... | collective-permute-start | bytes 2359304 | tf_op jit(solution)/shard_map/ppermute | solution.py:70
  160.0 34.9 %collective-permute-start.33 = (bf16[256,1536]{1,0:T(8,128)(2,1)}, bf16[256,1536]{1,0:T(8,128)(2,1)S(1)}, u32[]{:S(2)}, u32[]{:S(2)}) collective-permute-start(bf16[256,1536]{1,0:T(8,128)(2,1)} %get-tuple-element.289.refs_0_), channel_id=1, source_target_pairs={{0,4},{1,5},{2,6},{3,7},{4,0},{5,1},{6,2},{7,3},{8,12},{9,13},{10,... | collective-permute-start | bytes 2359304 | tf_op jit(solution)/shard_map/ppermute | solution.py:70
  160.1 34.9 %collective-permute-start.32 = (bf16[256,1536]{1,0:T(8,128)(2,1)}, bf16[256,1536]{1,0:T(8,128)(2,1)S(1)}, u32[]{:S(2)}, u32[]{:S(2)}) collective-permute-start(bf16[256,1536]{1,0:T(8,128)(2,1)} %get-tuple-element.289.refs_0_), channel_id=1, source_target_pairs={{0,2},{1,3},{2,0},{3,1},{4,6},{5,7},{6,4},{7,5},{8,10},{9,11},{10,... | collective-permute-start | bytes 2359304 | tf_op jit(solution)/shard_map/ppermute | solution.py:70
  160.6 34.8 %collective-permute-start.42 = (bf16[256,1536]{1,0:T(8,128)(2,1)S(1)}, bf16[256,1536]{1,0:T(8,128)(2,1)S(1)}, u32[]{:S(2)}, u32[]{:S(2)}) collective-permute-start(bf16[256,1536]{1,0:T(8,128)(2,1)S(1)} %copy-done.13), channel_id=1, source_target_pairs={{0,1},{1,0},{2,3},{3,2},{4,5},{5,4},{6,7},{7,6},{8,9},{9,8},{10,11... | collective-permute-start | bytes 2359304 | tf_op jit(solution)/shard_map/ppermute | solution.py:68
  160.7 34.7 %collective-permute-start.35 = (bf16[256,1536]{1,0:T(8,128)(2,1)}, bf16[256,1536]{1,0:T(8,128)(2,1)S(1)}, u32[]{:S(2)}, u32[]{:S(2)}) collective-permute-start(bf16[256,1536]{1,0:T(8,128)(2,1)} %get-tuple-element.289.refs_0_), channel_id=1, source_target_pairs={{0,1},{1,0},{2,3},{3,2},{4,5},{5,4},{6,7},{7,6},{8,9},{9,8},{10,11... | collective-permute-start | bytes 2359304 | tf_op jit(solution)/shard_map/ppermute | solution.py:68
  178.6 16.8 %collective-permute-start.38 = (bf16[256,1536]{1,0:T(8,128)(2,1)S(1)}, bf16[256,1536]{1,0:T(8,128)(2,1)S(1)}, u32[]{:S(2)}, u32[]{:S(2)}) collective-permute-start(bf16[256,1536]{1,0:T(8,128)(2,1)S(1)} %collective-permute-done.34.refs_3_), channel_id=1, source_target_pairs={{0,1},{1,0},{2,3},{3,2},{4,5},{5,4},{6,7},{7,6},{8,9},{9,8},{10,11... | collective-permute-start | bytes 2359304 | tf_op jit(solution)/shard_map/ppermute | solution.py:68
  239.3 20.6 %collective-permute-start.45 = (bf16[256,1536]{1,0:T(8,128)(2,1)S(1)}, bf16[256,1536]{1,0:T(8,128)(2,1)}, u32[]{:S(2)}, u32[]{:S(2)}) collective-permute-start(bf16[256,1536]{1,0:T(8,128)(2,1)S(1)} %add_convert_fusion.6), channel_id=1, source_target_pairs={{0,2},{1,3},{2,0},{3,1},{4,6},{5,7},{6,4},{7,5},{8,10},{9,11},{10,... | collective-permute-start | bytes 2359304 | tf_op jit(solution)/shard_map/ppermute | solution.py:70
  240.9 36.3 %collective-permute-start.47 = (bf16[256,1536]{1,0:T(8,128)(2,1)S(1)}, bf16[256,1536]{1,0:T(8,128)(2,1)}, u32[]{:S(2)}, u32[]{:S(2)}) collective-permute-start(bf16[256,1536]{1,0:T(8,128)(2,1)S(1)} %add_convert_fusion.5), channel_id=1, source_target_pairs={{0,4},{1,5},{2,6},{3,7},{4,0},{5,1},{6,2},{7,3},{8,12},{9,13},{10,... | collective-permute-start | bytes 2359304 | tf_op jit(solution)/shard_map/ppermute | solution.py:70
  242.3 35.0 %collective-permute-start.49 = (bf16[256,1536]{1,0:T(8,128)(2,1)S(1)}, bf16[256,1536]{1,0:T(8,128)(2,1)}, u32[]{:S(2)}, u32[]{:S(2)}) collective-permute-start(bf16[256,1536]{1,0:T(8,128)(2,1)S(1)} %add_convert_fusion.4), channel_id=1, source_target_pairs={{0,6},{1,7},{2,4},{3,5},{4,2},{5,3},{6,0},{7,1},{8,14},{9,15},{10,... | collective-permute-start | bytes 2359304 | tf_op jit(solution)/shard_map/ppermute | solution.py:70
  243.4 33.9 %collective-permute-start.43 = (bf16[256,1536]{1,0:T(8,128)(2,1)}, bf16[256,1536]{1,0:T(8,128)(2,1)}, u32[]{:S(2)}, u32[]{:S(2)}) collective-permute-start(bf16[256,1536]{1,0:T(8,128)(2,1)} %get-tuple-element.298), channel_id=1, source_target_pairs={{0,1},{1,0},{2,3},{3,2},{4,5},{5,4},{6,7},{7,6},{8,9},{9,8},{10,11... | collective-permute-start | bytes 2359304 | tf_op jit(solution)/shard_map/ppermute | solution.py:68
  243.5 158.1 %reduce-scatter.6.cloned.1.call-start = ((), (), s32[]{:S(2)}) async-start(), calls=%async_computation.4 | async-start | bytes 3932160 | tf_op jit(solution)/shard_map/reduce_scatter | solution.py:684
  297.9 32.5 %collective-permute-start.24 = (bf16[4,48,1664]{2,1,0:T(8,128)(2,1)}, bf16[4,48,1664]{2,1,0:T(8,128)(2,1)}, u32[]{:S(2)}, u32[]{:S(2)}) collective-permute-start(bf16[4,48,1664]{2,1,0:T(8,128)(2,1)} %bitcast.10), channel_id=1, source_target_pairs={{0,2},{1,3},{2,0},{3,1},{4,6},{5,7},{6,4},{7,5},{8,10},{9,11},{10,... | collective-permute-start | bytes 1916936 | tf_op jit(solution)/shard_map/cond/branch_1_fun/ppermute | solution.py:70
  298.7 31.7 %collective-permute-start.25 = (bf16[4,48,1664]{2,1,0:T(8,128)(2,1)}, bf16[4,48,1664]{2,1,0:T(8,128)(2,1)}, u32[]{:S(2)}, u32[]{:S(2)}) collective-permute-start(bf16[4,48,1664]{2,1,0:T(8,128)(2,1)} %bitcast.11), channel_id=1, source_target_pairs={{0,4},{1,5},{2,6},{3,7},{4,0},{5,1},{6,2},{7,3},{8,12},{9,13},{10,... | collective-permute-start | bytes 1916936 | tf_op jit(solution)/shard_map/cond/branch_1_fun/ppermute | solution.py:70
  300.0 30.4 %collective-permute-start.26 = (bf16[4,48,1664]{2,1,0:T(8,128)(2,1)}, bf16[4,48,1664]{2,1,0:T(8,128)(2,1)}, u32[]{:S(2)}, u32[]{:S(2)}) collective-permute-start(bf16[4,48,1664]{2,1,0:T(8,128)(2,1)} %bitcast.12), channel_id=1, source_target_pairs={{0,6},{1,7},{2,4},{3,5},{4,2},{5,3},{6,0},{7,1},{8,14},{9,15},{10,... | collective-permute-start | bytes 1916936 | tf_op jit(solution)/shard_map/cond/branch_1_fun/ppermute | solution.py:70
  301.5 29.0 %collective-permute-start.27 = (bf16[1024,1536]{1,0:T(8,128)(2,1)}, bf16[1024,1536]{1,0:T(8,128)(2,1)}, u32[]{:S(2)}, u32[]{:S(2)}) collective-permute-start(bf16[1024,1536]{1,0:T(8,128)(2,1)} %get-tuple-element.163), channel_id=1, source_target_pairs={{0,1},{1,0},{2,3},{3,2},{4,5},{5,4},{6,7},{7,6},{8,9},{9,8},{10,11... | collective-permute-start | bytes 9437192 | tf_op jit(solution)/shard_map/cond/branch_1_fun/ppermute | solution.py:68
  333.5 111.1 %reduce-scatter.8.cloned.1.call-start = ((), (), s32[]{:S(2)}) async-start(), calls=%async_computation.5 | async-start | bytes 2273280 | tf_op jit(solution)/shard_map/reduce_scatter | solution.py:684
  340.5 16.2 %collective-permute-start.52 = (bf16[4,48,1536]{2,1,0:T(8,128)(2,1)S(1)}, bf16[4,48,1536]{2,1,0:T(8,128)(2,1)S(1)}, u32[]{:S(2)}, u32[]{:S(2)}) collective-permute-start(bf16[4,48,1536]{2,1,0:T(8,128)(2,1)S(1)} %get-tuple-element.350), channel_id=1, source_target_pairs={{0,2},{1,3},{2,0},{3,1},{4,6},{5,7},{6,4},{7,5},{8,10},{9,11},{10,... | collective-permute-start | bytes 1769480 | tf_op jit(solution)/shard_map/ppermute | solution.py:70
  341.3 28.6 %collective-permute-start.54 = (bf16[4,48,1536]{2,1,0:T(8,128)(2,1)S(1)}, bf16[4,48,1536]{2,1,0:T(8,128)(2,1)S(1)}, u32[]{:S(2)}, u32[]{:S(2)}) collective-permute-start(bf16[4,48,1536]{2,1,0:T(8,128)(2,1)S(1)} %get-tuple-element.351), channel_id=1, source_target_pairs={{0,6},{1,7},{2,4},{3,5},{4,2},{5,3},{6,0},{7,1},{8,14},{9,15},{10,... | collective-permute-start | bytes 1769480 | tf_op jit(solution)/shard_map/ppermute | solution.py:70
  343.1 28.9 %collective-permute-start.53 = (bf16[4,48,1536]{2,1,0:T(8,128)(2,1)S(1)}, bf16[4,48,1536]{2,1,0:T(8,128)(2,1)S(1)}, u32[]{:S(2)}, u32[]{:S(2)}) collective-permute-start(bf16[4,48,1536]{2,1,0:T(8,128)(2,1)S(1)} %get-tuple-element.352), channel_id=1, source_target_pairs={{0,4},{1,5},{2,6},{3,7},{4,0},{5,1},{6,2},{7,3},{8,12},{9,13},{10,... | collective-permute-start | bytes 1769480 | tf_op jit(solution)/shard_map/ppermute | solution.py:70
  346.1 36.0 %collective-permute-start.56 = (bf16[4,48,1536]{2,1,0:T(8,128)(2,1)S(1)}, bf16[4,48,1536]{2,1,0:T(8,128)(2,1)S(1)}, u32[]{:S(2)}, u32[]{:S(2)}) collective-permute-start(bf16[4,48,1536]{2,1,0:T(8,128)(2,1)S(1)} %get-tuple-element.353), channel_id=1, source_target_pairs={{0,2},{1,3},{2,0},{3,1},{4,6},{5,7},{6,4},{7,5},{8,10},{9,11},{10,... | collective-permute-start | bytes 1769480 | tf_op jit(solution)/shard_map/ppermute | solution.py:70
  346.8 47.9 %collective-permute-start.58 = (bf16[4,48,1536]{2,1,0:T(8,128)(2,1)S(1)}, bf16[4,48,1536]{2,1,0:T(8,128)(2,1)S(1)}, u32[]{:S(2)}, u32[]{:S(2)}) collective-permute-start(bf16[4,48,1536]{2,1,0:T(8,128)(2,1)S(1)} %get-tuple-element.354), channel_id=1, source_target_pairs={{0,6},{1,7},{2,4},{3,5},{4,2},{5,3},{6,0},{7,1},{8,14},{9,15},{10,... | collective-permute-start | bytes 1769480 | tf_op jit(solution)/shard_map/ppermute | solution.py:70
  356.8 39.3 %collective-permute-start.57 = (bf16[4,48,1536]{2,1,0:T(8,128)(2,1)S(1)}, bf16[4,48,1536]{2,1,0:T(8,128)(2,1)S(1)}, u32[]{:S(2)}, u32[]{:S(2)}) collective-permute-start(bf16[4,48,1536]{2,1,0:T(8,128)(2,1)S(1)} %get-tuple-element.355), channel_id=1, source_target_pairs={{0,4},{1,5},{2,6},{3,7},{4,0},{5,1},{6,2},{7,3},{8,12},{9,13},{10,... | collective-permute-start | bytes 1769480 | tf_op jit(solution)/shard_map/ppermute | solution.py:70
  405.0 20.7 %collective-permute-start.59 = (bf16[256,1536]{1,0:T(8,128)(2,1)}, bf16[256,1536]{1,0:T(8,128)(2,1)S(1)}, u32[]{:S(2)}, u32[]{:S(2)}) collective-permute-start(bf16[256,1536]{1,0:T(8,128)(2,1)} %get-tuple-element.319), channel_id=1, source_target_pairs={{0,2},{1,3},{2,0},{3,1},{4,6},{5,7},{6,4},{7,5},{8,10},{9,11},{10,... | collective-permute-start | bytes 2359304 | tf_op jit(solution)/shard_map/ppermute | solution.py:70
  406.1 35.2 %collective-permute-start.60 = (bf16[256,1536]{1,0:T(8,128)(2,1)}, bf16[256,1536]{1,0:T(8,128)(2,1)}, u32[]{:S(2)}, u32[]{:S(2)}) collective-permute-start(bf16[256,1536]{1,0:T(8,128)(2,1)} %get-tuple-element.328), channel_id=1, source_target_pairs={{0,4},{1,5},{2,6},{3,7},{4,0},{5,1},{6,2},{7,3},{8,12},{9,13},{10,... | collective-permute-start | bytes 2359304 | tf_op jit(solution)/shard_map/ppermute | solution.py:70
  406.7 34.5 %collective-permute-start.61 = (bf16[256,1536]{1,0:T(8,128)(2,1)}, bf16[256,1536]{1,0:T(8,128)(2,1)}, u32[]{:S(2)}, u32[]{:S(2)}) collective-permute-start(bf16[256,1536]{1,0:T(8,128)(2,1)} %get-tuple-element.330), channel_id=1, source_target_pairs={{0,6},{1,7},{2,4},{3,5},{4,2},{5,3},{6,0},{7,1},{8,14},{9,15},{10,... | collective-permute-start | bytes 2359304 | tf_op jit(solution)/shard_map/ppermute | solution.py:70
  (59 other events, 681.8 us)
Sparse Core Ops, SparseCore 0:
  34.7 73.0 all-gather.4
  109.4 88.0 all-gather.6
  243.6 83.1 reduce-scatter.3
  333.7 57.9 reduce-scatter.5
  401.7 36.7 reduce-scatter.7

commit v8 on v7

--- a/solution.py
+++ b/solution.py
@@ -793,23 +793,23 @@
     if rounds:
 
         def round4(meta, cosine, sine, out_pack, tokens_all, arrays):
-            moved = step((0, 1), out_pack), step((1, 0), out_pack)
+            moved = step((0, 1), out_pack), step((1, 0), out_pack), step("c", out_pack)
             found = [(array,) + piece[1:] for array, piece in zip(arrays, pieces)]
             return moved + tuple(
                 project_forward(meta, tokens_all, cosine, sine, found, Q, width, seqs, rows)
             )
 
-        out_x, out_q, query_t, pair_t, normed_t, gains = window(
+        out_x, out_q, out_packc, query_t, pair_t, normed_t, gains = window(
             round4, meta, cosine, sine, out_pack, tokens_all, arrays_of(pieces)
         )
 
-        def round5(meta, query_t, pair_t, out_pack, out_x, out_q):
+        def round5(meta, query_t, pair_t, out_x, out_q):
             corner = step((0, 1), out_q[:2]), step((1, 0), out_x[2:])
-            cores_of = step("c", out_pack), step("c", out_x), step("c", out_q)
+            cores_of = step("c", out_x), step("c", out_q)
             return corner + cores_of + tuple(attend_forward(meta, query_t, pair_t, seqs))
 
-        corner_a, corner_b, out_packc, out_xc, out_qc, mixed, mixed_t, logs = window(
-            round5, meta, query_t, pair_t, out_pack, out_x, out_q
+        corner_a, corner_b, out_xc, out_qc, mixed, mixed_t, logs = window(
+            round5, meta, query_t, pair_t, out_x, out_q
         )
         out_pieces = [
             (out_pack, 0, 0, 0, 0), (out_packc, 0, 0, 1, 0), (out_x, 0, 1, 0, 0), (out_xc, 0, 1, 1, 0),

time: 464 us -> 465 us (level)
  no operation moved by 1% of the time
where the time goes in v8:
time: 465 us; the launch traced here: 456 us
  waiting for transfers between devices  208 us (45%)
  Pallas kernels  126 us (27%)
  starting transfers between devices  51.5 us (11%)
  other arithmetic  40.9 us (9%)
  between operations  14.5 us (3%)
  local copies, waits for them, and re-layouts  14.1 us (3%)
    ppermute x30, waiting for transfers between devices, step(): lax.ppermute(value, 'dp', [(n, n % 4 ^ 2 * i | 4 * ((n // 4 + j) % self.Q...  147 us
    pallas_call x9, Pallas kernels, kernel_call(): pl.pallas_call(body, out_shape=out_shape, in_specs=in_specs, out_specs=ou...  126 us
    ppermute x6, waiting for transfers between devices, around(): lax.ppermute(value, 'seq', [(n, (n + hop) % self.Z) for n in range(self.Z)])  43.1 us
    ppermute x30, starting transfers between devices, step(): lax.ppermute(value, 'dp', [(n, n % 4 ^ 2 * i | 4 * ((n // 4 + j) % self.Q...  36.9 us
    convert_element_type x7, other arithmetic, to_send(): (in_f32(own[n]) + in_f32(other[n])).astype(BF)  12.7 us
    ppermute x26, waiting for transfers between devices, step(): return lax.ppermute(value, 'dp', [(n, n ^ 1) for n in range(self.DP)])  11.6 us
  transfers between devices with their start and end apart: 67, of which 32 were waited for; matrix products, arithmetic and copies ran while one was open for 9% of the time, Pallas kernels for 20%

profile of v8, /device:TPU:0, one launch (start us, length us, event | category | flops | bytes accessed | tf_op | source)
XLA Modules:
  0.0 455.6 jit_solution(17019563499350281812)
XLA Ops:
  10.1 2.3 pad_maximum_fusion.4
  12.4 22.1 %conditional.7 = (bf16[48,3200]{1,0:T(8,128)(2,1)}, bf16[48,3200]{1,0:T(8,128)(2,1)}, bf16[256,1536]{1,0:T(8,128)(2,1)}, bf16[256,1536]{1,0:T(8,128)(2,1)}) conditional(s32[]{:T(128)} %convert_element_type.316, () %tuple.84, (bf16[48,3200]{1,0:T(8,128)(2,1)S(1)}, bf16[256,1536]{1,0:T(8,128)(2,1)S(1)}) %tuple.151), branch_computations={%region_0.1_spmd, %region_1.2_spmd} | conditional | bytes 8749248 | solution.py:673
  12.4 3.0 collective-permute-start.3
  16.9 3.6 collective-permute-start.1
  20.5 7.7 %collective-permute-done.1 = bf16[48,3200]{1,0:T(8,128)(2,1)} collective-permute-done((bf16[48,3200]{1,0:T(8,128)(2,1)S(1)}, bf16[48,3200]{1,0:T(8,128)(2,1)}, u32[]{:S(2)}, u32[]{:S(2)}) %collective-permute-start.1) | collective-permute-done | bytes 307232 | tf_op jit(solution)/shard_map/cond/branch_1_fun/ppermute | solution.py:64
  28.2 5.8 %collective-permute-done = bf16[48,3200]{1,0:T(8,128)(2,1)} collective-permute-done((bf16[48,3200]{1,0:T(8,128)(2,1)S(1)}, bf16[48,3200]{1,0:T(8,128)(2,1)}, u32[]{:S(2)}, u32[]{:S(2)}) %collective-permute-start) | collective-permute-done | bytes 307232 | tf_op jit(solution)/shard_map/cond/branch_1_fun/ppermute | solution.py:64
  35.3 13.6 %conditional.8 = (bf16[4,48,3200]{2,1,0:T(8,128)(2,1)S(1)}, bf16[256,1536]{1,0:T(8,128)(2,1)S(1)}) conditional(s32[]{:T(128)} %convert_element_type.316, () %tuple.83, (bf16[48,3200]{1,0:T(8,128)(2,1)S(1)}, bf16[48,3200]{1,0:T(8,128)(2,1)}, bf16[48,3200]{1,0:T(8,128)(2,1)}, bf16[256,1536]{1,0:T(8,128)(2,1)}, bf16[256,1536]{1,0:T(8,128)(2,1)}) %tuple.87), branch_computations={%region_2.3_spmd, %region_3.4_spmd} | conditional | flops 3416064 | bytes 9977992 | solution.py:673
  41.1 4.1 collective-permute-done.16
  49.8 30.7 %conditional.9 = (bf16[4,48,3200]{2,1,0:T(8,128)(2,1)}, bf16[4,48,3200]{2,1,0:T(8,128)(2,1)}, bf16[4,48,3200]{2,1,0:T(8,128)(2,1)}, bf16[48,1536]{1,0:T(8,128)(2,1)}, bf16[48,1536]{1,0:T(8,128)(2,1)}) conditional(s32[]{:T(128)} %convert_element_type.316, () %tuple.82, (bf16[4,48,3200]{2,1,0:T(8,128)(2,1)S(1)}, bf16[48,1536]{1,0:T(8,128)(2,1)S(1)}) %tuple.154), branch_computations={%region_4.5_spmd, %region_5.6_spmd} | conditional | bytes 15925488 | solution.py:673
  52.7 2.3 collective-permute-start.8
  55.0 11.4 %collective-permute-done.8 = bf16[48,1536]{1,0:T(8,128)(2,1)} collective-permute-done((bf16[48,1536]{1,0:T(8,128)(2,1)S(1)}, bf16[48,1536]{1,0:T(8,128)(2,1)}, u32[]{:S(2)}, u32[]{:S(2)}) %collective-permute-start.8) | collective-permute-done | bytes 147488 | tf_op jit(solution)/shard_map/cond/branch_1_fun/ppermute | solution.py:64
  66.5 4.2 collective-permute-done.7
  70.7 8.6 %collective-permute-done.5 = bf16[4,48,3200]{2,1,0:T(8,128)(2,1)} collective-permute-done((bf16[4,48,3200]{2,1,0:T(8,128)(2,1)S(1)}, bf16[4,48,3200]{2,1,0:T(8,128)(2,1)}, u32[]{:S(2)}, u32[]{:S(2)}) %collective-permute-start.5) | collective-permute-done | bytes 1228832 | tf_op jit(solution)/shard_map/cond/branch_1_fun/ppermute | solution.py:70
  80.5 19.1 %conditional.10 = (bf16[2,48,3200]{2,1,0:T(8,128)(2,1)}, bf16[2,48,3200]{2,1,0:T(8,128)(2,1)}, bf16[4,48,3200]{2,1,0:T(8,128)(2,1)}, bf16[4,48,3200]{2,1,0:T(8,128)(2,1)}, bf16[4,48,1536]{2,1,0:T(8,128)(2,1)}) conditional(s32[]{:T(128)} %convert_element_type.316, () %tuple.81, (bf16[4,48,3200]{2,1,0:T(8,128)(2,1)}, bf16[4,48,3200]{2,1,0:T(8,128)(2,1)}, ...), branch_computations={%region_6.7_spmd, %region_7.8_spmd} | conditional | flops 884736 | bytes 18972912 | solution.py:673
  87.0 9.8 %collective-permute-done.23 = bf16[48,1536]{1,0:T(8,128)(2,1)S(1)} collective-permute-done((bf16[48,1536]{1,0:T(8,128)(2,1)}, bf16[48,1536]{1,0:T(8,128)(2,1)S(1)}, u32[]{:S(2)}, u32[]{:S(2)}) %collective-permute-start.23) | collective-permute-done | bytes 147488 | tf_op jit(solution)/shard_map/cond/branch_1_fun/ppermute | solution.py:64
  102.7 5.1 %all-gather.5.cloned.1.call-done = bf16[8,128,1536]{2,1,0:T(8,128)(2,1)} async-done(((bf16[2,128,1536]{2,1,0:T(8,128)(2,1)}), bf16[8,128,1536]{2,1,0:T(8,128)(2,1)}) %all-gather.5.cloned.1.call-update) | async-done | bytes 3145744 | tf_op jit(solution)/shard_map/all_gather | solution.py:681
  107.8 20.2 %conditional.11 = (bf16[4,48,1536]{2,1,0:T(8,128)(2,1)}, bf16[4,48,1536]{2,1,0:T(8,128)(2,1)}, bf16[4,48,1536]{2,1,0:T(8,128)(2,1)}, bf16[1536,256]{1,0:T(8,128)...) conditional(s32[]{:T(128)} %convert_element_type.316, () %tuple.80, ...), branch_computations={%region_9.10_spmd, %region_10.11_spmd} | conditional | flops 6039797760 | bytes 37880068 | solution.py:673
  110.9 17.0 %branch_1_fun.4 = (bf16[1536,256]{1,0:T(8,128)(2,1)}, bf16[1536,1024]{1,0:T(8,128)(2,1)S(1)}, bf16[1536,1024]{1,0:T(8,128)(2,1)}, f32[8,1536]{1,0:T(8,128)S(1)}) custom-call(s32[4]{0:T(128)S(1)} %get-tuple-element.115.meta, bf16[4,2,128,1536]{3,2,1,0:T(8,128)(2,1)} %bitcast.89, f32[48,1024]{1,0:T(8,128)} %get-tuple-element.117.cosine, ...), custom_call_target="tpu_custom_call" | custom-call | flops 6039797760 | bytes 20971520 | tf_op jit(solution)/shard_map/cond/branch_1_fun/pallas_call | solution.py:85
  129.6 15.4 %conditional.12 = (bf16[2,48,1536]{2,1,0:T(8,128)(2,1)}, bf16[2,48,1536]{2,1,0:T(8,128)(2,1)}, bf16[4,48,1536]{2,1,0:T(8,128)(2,1)}, bf16[4,48,1536]{2,1,0:T(8,1...) conditional(s32[]{:T(128)} %convert_element_type.316, () %tuple.79, ...), branch_computations={%region_11.12_spmd, %region_12.13_spmd} | conditional | flops 805306368 | bytes 14549208 | solution.py:673
  132.8 12.2 %branch_1_fun.5 = (bf16[256,1536]{1,0:T(8,128)(2,1)}, bf16[1536,256]{1,0:T(8,128)(2,1)}, f32[8,2,1,256]{3,2,1,0:T(1,128)}) custom-call(s32[4]{0:T(128)S(1)} %get-tuple-element.135.meta, bf16[1536,256]{1,0:T(8,128)(2,1)} %get-tuple-element.136.query_t, bf16[1536,1024]{1,0:T(8,128)(2,1)S(1)} %get-tuple-element.137.pair_t), custom_call_target="tpu_custom_call" | custom-call | flops 805306368 | bytes 6291456 | tf_op jit(solution)/shard_map/cond/branch_1_fun/pallas_call | solution.py:85
  146.2 2.2 collective-permute-done.30.refs_7_
  150.0 7.0 %shard_map.203 = (f32[256,1536]{1,0:T(8,128)}, bf16[256,1536]{1,0:T(8,128)(2,1)}) custom-call(s32[4]{0:T(128)S(1)} %pad_add_fusion.meta, bf16[256,1536]{1,0:T(8,128)(2,1)} %bitcast.70, bf16[256,1536]{1,0:T(8,128)(2,1)} %get-tuple-element.278.mixed, f32[8,1536]{1,0:T(8,128)S(1)} %get-tuple-element.279.gain, bf16[4,48,1536]{2,1,0:T(8,128)(2,1)} %get-tuple-element.267.refs_0_, ...), custom_call_target="tpu_custom_call" | custom-call | flops 1207959552 | bytes 10485760 | tf_op jit(solution)/shard_map/pallas_call | solution.py:85
  157.0 3.0 collective-permute-start.34
  161.3 17.3 %collective-permute-done.34.refs_3_ = bf16[256,1536]{1,0:T(8,128)(2,1)S(1)} collective-permute-done((bf16[256,1536]{1,0:T(8,128)(2,1)}, bf16[256,1536]{1,0:T(8,128)(2,1)S(1)}, u32[]{:S(2)}, u32[]{:S(2)}) %collective-permute-start.34) | collective-permute-done | bytes 786464 | tf_op jit(solution)/shard_map/ppermute | solution.py:70
  178.6 16.3 %collective-permute-done.33.refs_2_ = bf16[256,1536]{1,0:T(8,128)(2,1)S(1)} collective-permute-done((bf16[256,1536]{1,0:T(8,128)(2,1)}, bf16[256,1536]{1,0:T(8,128)(2,1)S(1)}, u32[]{:S(2)}, u32[]{:S(2)}) %collective-permute-start.33) | collective-permute-done | bytes 786464 | tf_op jit(solution)/shard_map/ppermute | solution.py:70
  198.5 37.0 %shard_map.204 = (bf16[1024,1536]{1,0:T(8,128)(2,1)}, bf16[1024,1536]{1,0:T(8,128)(2,1)}, bf16[256,1536]{1,0:T(8,128)(2,1)}, bf16[256,1536]{1,0:T(8,128)(2,1)}, ...) custom-call(bf16[256,1536]{1,0:T(8,128)(2,1)} %get-tuple-element.286, ...), custom_call_target="tpu_custom_call" | custom-call | flops 28991029248 | bytes 35651584 | tf_op jit(solution)/shard_map/pallas_call | solution.py:85
  243.6 16.4 %collective-permute-done.45 = bf16[256,1536]{1,0:T(8,128)(2,1)} collective-permute-done((bf16[256,1536]{1,0:T(8,128)(2,1)S(1)}, bf16[256,1536]{1,0:T(8,128)(2,1)}, u32[]{:S(2)}, u32[]{:S(2)}) %collective-permute-start.45) | collective-permute-done | bytes 786464 | tf_op jit(solution)/shard_map/ppermute | solution.py:70
  260.0 17.4 %collective-permute-done.47 = bf16[256,1536]{1,0:T(8,128)(2,1)} collective-permute-done((bf16[256,1536]{1,0:T(8,128)(2,1)S(1)}, bf16[256,1536]{1,0:T(8,128)(2,1)}, u32[]{:S(2)}, u32[]{:S(2)}) %collective-permute-start.47) | collective-permute-done | bytes 786464 | tf_op jit(solution)/shard_map/ppermute | solution.py:70
  277.3 3.7 convert_add_fusion.second_grad
  281.1 7.0 %shard_map.205 = (f32[256,1536]{1,0:T(8,128)}, bf16[256,1536]{1,0:T(8,128)(2,1)}, bf16[4,4,48,1664]{3,2,1,0:T(8,128)(2,1)}, bf16[4,4,48,1664]{3,2,1,0:T(8,128)(2,1)}) custom-call(bf16[256,1536]{1,0:T(8,128)(2,1)S(1)} %bitcast.79, f32[256,1536]{1,0:T(8,128)} %get-tuple-element.285.total, f32[256,1536]{1,0:T(8,128)} %convert_add_fusion.second_grad, ...), custom_call_target="tpu_custom_call" | custom-call | flops 1207959552 | bytes 14680064 | tf_op jit(solution)/shard_map/pallas_call | solution.py:85
  288.0 6.2 %shard_map.206 = bf16[1536,256]{1,0:T(8,128)(2,1)} custom-call(s32[4]{0:T(128)S(1)} %pad_add_fusion.meta, bf16[256,1536]{1,0:T(8,128)(2,1)} %get-tuple-element.305.da, bf16[4,48,1536]{2,1,0:T(8,128)(2,1)} %get-tuple-element.267.refs_0_, bf16[4,48,1536]{2,1,0:T(8,128)(2,1)} %get-tuple-element.280.refs_1_, bf16[4,48,1536]{2,1,0:T(8,128)(2,1)} %get-tuple-element.275.refs_2_, ...), custom_call_target="tpu_custom_call" | custom-call | flops 999999995904 | bytes 8388608 | tf_op jit(solution)/shard_map/pallas_call | solution.py:85
  294.2 3.7 add_convert_fusion.7
  298.0 35.7 %conditional.13 = (bf16[4,48,1664]{2,1,0:T(8,128)(2,1)}, bf16[1536,256]{1,0:T(8,128)(2,1)}, bf16[4,1536,256]{2,1,0:T(8,128)(2,1)}, bf16[4,4,48,1536]{3,2,1,0:T(8...) conditional(s32[]{:T(128)} %convert_element_type.316, () %tuple.96, ...), branch_computations={%region_13.14_spmd, %region_14.15_spmd} | conditional | flops 1000003207168 | bytes 63930592 | solution.py:673
  301.5 16.0 %branch_1_fun.6 = (bf16[1536,256]{1,0:T(8,128)(2,1)}, bf16[1536,1024]{1,0:T(8,128)(2,1)}, bf16[4,1536,256]{2,1,0:T(8,128)(2,1)}) custom-call(s32[4]{0:T(128)S(1)} %get-tuple-element.143.meta, bf16[1536,256]{1,0:T(8,128)(2,1)} %get-tuple-element.145.query_t, bf16[1536,1024]{1,0:T(8,128)(2,1)S(1)} %get-tuple-element.146.pair_t, ...), custom_call_target="tpu_custom_call" | custom-call | flops 999999995904 | bytes 12582912 | tf_op jit(solution)/shard_map/cond/branch_1_fun/pallas_call | solution.py:85
  317.5 13.0 %branch_1_fun.7 = (bf16[4,4,48,1536]{3,2,1,0:T(8,128)(2,1)}, bf16[4,4,48,1536]{3,2,1,0:T(8,128)(2,1)}, bf16[4,4,48,1536]{3,2,1,0:T(8,128)(2,1)}, bf16[4,4,48,1536]{3,2,1,0:T(8,128)(2,1)}) custom-call(s32[4]{0:T(128)S(1)} %get-tuple-element.143.meta, bf16[1536,1024]{1,0:T(8,128)(2,1)} %get-tuple-element.144.normed_t, ...), custom_call_target="tpu_custom_call" | custom-call | flops 1 | bytes 27262976 | tf_op jit(solution)/shard_map/cond/branch_1_fun/pallas_call | solution.py:85
  330.6 3.1 fusion.2
  334.5 4.3 collective-permute-done.51
  348.7 8.2 %collective-permute-done.52 = bf16[4,48,1536]{2,1,0:T(8,128)(2,1)S(1)} collective-permute-done((bf16[4,48,1536]{2,1,0:T(8,128)(2,1)S(1)}, bf16[4,48,1536]{2,1,0:T(8,128)(2,1)S(1)}, u32[]{:S(2)}, u32[]{:S(2)}) %collective-permute-start.52) | collective-permute-done | bytes 589856 | tf_op jit(solution)/shard_map/ppermute | solution.py:70
  357.9 12.1 %collective-permute-done.54 = bf16[4,48,1536]{2,1,0:T(8,128)(2,1)S(1)} collective-permute-done((bf16[4,48,1536]{2,1,0:T(8,128)(2,1)S(1)}, bf16[4,48,1536]{2,1,0:T(8,128)(2,1)S(1)}, u32[]{:S(2)}, u32[]{:S(2)}) %collective-permute-start.54) | collective-permute-done | bytes 589856 | tf_op jit(solution)/shard_map/ppermute | solution.py:70
  370.0 2.1 collective-permute-done.53
  372.1 10.1 %collective-permute-done.56 = bf16[4,48,1536]{2,1,0:T(8,128)(2,1)S(1)} collective-permute-done((bf16[4,48,1536]{2,1,0:T(8,128)(2,1)S(1)}, bf16[4,48,1536]{2,1,0:T(8,128)(2,1)S(1)}, u32[]{:S(2)}, u32[]{:S(2)}) %collective-permute-start.56) | collective-permute-done | bytes 589856 | tf_op jit(solution)/shard_map/ppermute | solution.py:70
  382.2 12.6 %collective-permute-done.58 = bf16[4,48,1536]{2,1,0:T(8,128)(2,1)S(1)} collective-permute-done((bf16[4,48,1536]{2,1,0:T(8,128)(2,1)S(1)}, bf16[4,48,1536]{2,1,0:T(8,128)(2,1)S(1)}, u32[]{:S(2)}, u32[]{:S(2)}) %collective-permute-start.58) | collective-permute-done | bytes 589856 | tf_op jit(solution)/shard_map/ppermute | solution.py:70
  399.1 2.6 pad_maximum_fusion.3
  401.7 3.4 add_convert_fusion.3
  410.1 11.0 %shard_map.207 = bf16[256,1536]{1,0:T(8,128)(2,1)} custom-call(s32[4]{0:T(128)S(1)} %pad_add_fusion.meta, bf16[256,1536]{1,0:T(8,128)(2,1)} %bitcast.71, f32[8,1536]{1,0:T(8,128)S(1)} %copy-done.9, f32[256,1536]{1,0:T(8,128)} %get-tuple-element.317.first_grad, bf16[1536,256]{1,0:T(8,128)(2,1)} %get-tuple-element.318.query_back, bf16[1536,256]{1,0:T(8,128)(2,1)} %bitcast.74, ...), custom_call_target="tpu_custom_call" | custom-call | flops 2415919104 | bytes 14680064 | tf_op jit(solution)/shard_map/pallas_call | solution.py:85
  421.2 4.7 %collective-permute-done.59 = bf16[256,1536]{1,0:T(8,128)(2,1)S(1)} collective-permute-done((bf16[256,1536]{1,0:T(8,128)(2,1)}, bf16[256,1536]{1,0:T(8,128)(2,1)S(1)}, u32[]{:S(2)}, u32[]{:S(2)}) %collective-permute-start.59) | collective-permute-done | bytes 786464 | tf_op jit(solution)/shard_map/ppermute | solution.py:70
  425.8 15.5 %collective-permute-done.60 = bf16[256,1536]{1,0:T(8,128)(2,1)} collective-permute-done((bf16[256,1536]{1,0:T(8,128)(2,1)}, bf16[256,1536]{1,0:T(8,128)(2,1)}, u32[]{:S(2)}, u32[]{:S(2)}) %collective-permute-start.60) | collective-permute-done | bytes 786464 | tf_op jit(solution)/shard_map/ppermute | solution.py:70
  441.3 3.3 add_convert_fusion
  (236 shorter events, 84.3 us)
Async XLA Ops:
  7.2 100.6 %all-gather.5.cloned.1.call-start = ((), (), s32[]{:S(2)}) async-start(), calls=%async_computation.6 | async-start | bytes 3932160 | tf_op jit(solution)/shard_map/all_gather | solution.py:681
  12.4 21.6 %collective-permute-start.3 = (bf16[256,1536]{1,0:T(8,128)(2,1)S(1)}, bf16[256,1536]{1,0:T(8,128)(2,1)}, u32[]{:S(2)}, u32[]{:S(2)}) collective-permute-start(bf16[256,1536]{1,0:T(8,128)(2,1)S(1)} %get-tuple-element.101), channel_id=1, source_target_pairs={{0,4},{1,5},{2,6},{3,7},{4,0},{5,1},{6,2},{7,3},{8,12},{9,13},{10,... | collective-permute-start | bytes 2359304 | tf_op jit(solution)/shard_map/cond/branch_1_fun/ppermute | solution.py:70
  15.4 19.1 %collective-permute-start.2 = (bf16[256,1536]{1,0:T(8,128)(2,1)S(1)}, bf16[256,1536]{1,0:T(8,128)(2,1)}, u32[]{:S(2)}, u32[]{:S(2)}) collective-permute-start(bf16[256,1536]{1,0:T(8,128)(2,1)S(1)} %get-tuple-element.101), channel_id=1, source_target_pairs={{0,2},{1,3},{2,0},{3,1},{4,6},{5,7},{6,4},{7,5},{8,10},{9,11},{10,... | collective-permute-start | bytes 2359304 | tf_op jit(solution)/shard_map/cond/branch_1_fun/ppermute | solution.py:70
  34.5 164.0 %all-gather.7.cloned.1.call-start = ((), (), s32[]{:S(2)}) async-start(), calls=%async_computation.7 | async-start | bytes 5898240 | tf_op jit(solution)/shard_map/all_gather | solution.py:681
  35.3 298.4 %reduce-scatter.4.cloned.1.call-start = ((), (), s32[]{:S(2)}) async-start(), calls=%async_computation.3 | async-start | bytes 5898240 | tf_op jit(solution)/shard_map/reduce_scatter | solution.py:684
  49.8 20.9 %collective-permute-start.6 = (bf16[4,48,3200]{2,1,0:T(8,128)(2,1)S(1)}, bf16[4,48,3200]{2,1,0:T(8,128)(2,1)}, u32[]{:S(2)}, u32[]{:S(2)}) collective-permute-start(bf16[4,48,3200]{2,1,0:T(8,128)(2,1)S(1)} %get-tuple-element.107), channel_id=1, source_target_pairs={{0,1},{1,0},{2,3},{3,2},{4,5},{5,4},{6,7},{7,6},{8,9},{9,8},{10,11... | collective-permute-start | bytes 3686408 | tf_op jit(solution)/shard_map/cond/branch_1_fun/ppermute | solution.py:68
  49.8 29.5 %collective-permute-start.5 = (bf16[4,48,3200]{2,1,0:T(8,128)(2,1)S(1)}, bf16[4,48,3200]{2,1,0:T(8,128)(2,1)}, u32[]{:S(2)}, u32[]{:S(2)}) collective-permute-start(bf16[4,48,3200]{2,1,0:T(8,128)(2,1)S(1)} %get-tuple-element.107), channel_id=1, source_target_pairs={{0,4},{1,5},{2,6},{3,7},{4,0},{5,1},{6,2},{7,3},{8,12},{9,13},{10,... | collective-permute-start | bytes 3686408 | tf_op jit(solution)/shard_map/cond/branch_1_fun/ppermute | solution.py:70
  51.2 29.3 %collective-permute-start.4 = (bf16[4,48,3200]{2,1,0:T(8,128)(2,1)S(1)}, bf16[4,48,3200]{2,1,0:T(8,128)(2,1)}, u32[]{:S(2)}, u32[]{:S(2)}) collective-permute-start(bf16[4,48,3200]{2,1,0:T(8,128)(2,1)S(1)} %get-tuple-element.107), channel_id=1, source_target_pairs={{0,2},{1,3},{2,0},{3,1},{4,6},{5,7},{6,4},{7,5},{8,10},{9,11},{10,... | collective-permute-start | bytes 3686408 | tf_op jit(solution)/shard_map/cond/branch_1_fun/ppermute | solution.py:70
  52.7 13.8 %collective-permute-start.8 = (bf16[48,1536]{1,0:T(8,128)(2,1)S(1)}, bf16[48,1536]{1,0:T(8,128)(2,1)}, u32[]{:S(2)}, u32[]{:S(2)}) collective-permute-start(bf16[48,1536]{1,0:T(8,128)(2,1)S(1)} %get-tuple-element.108), channel_id=1, source_target_pairs={{0,24},{8,0},{16,8},{24,16},{1,25},{9,1},{17,9},{25,17},{2,26},{10... | collective-permute-start | bytes 442376 | tf_op jit(solution)/shard_map/cond/branch_1_fun/ppermute | solution.py:64
  55.0 15.7 %collective-permute-start.7 = (bf16[48,1536]{1,0:T(8,128)(2,1)S(1)}, bf16[48,1536]{1,0:T(8,128)(2,1)}, u32[]{:S(2)}, u32[]{:S(2)}) collective-permute-start(bf16[48,1536]{1,0:T(8,128)(2,1)S(1)} %get-tuple-element.108), channel_id=1, source_target_pairs={{0,8},{8,16},{16,24},{24,0},{1,9},{9,17},{17,25},{25,1},{2,10},{10... | collective-permute-start | bytes 442376 | tf_op jit(solution)/shard_map/cond/branch_1_fun/ppermute | solution.py:64
  80.5 19.1 %collective-permute-start.22 = (bf16[4,48,3200]{2,1,0:T(8,128)(2,1)}, bf16[4,48,3200]{2,1,0:T(8,128)(2,1)}, u32[]{:S(2)}, u32[]{:S(2)}) collective-permute-start(bf16[4,48,3200]{2,1,0:T(8,128)(2,1)} %get-tuple-element.109), channel_id=1, source_target_pairs={{0,1},{1,0},{2,3},{3,2},{4,5},{5,4},{6,7},{7,6},{8,9},{9,8},{10,11... | collective-permute-start | bytes 3686408 | tf_op jit(solution)/shard_map/cond/branch_1_fun/ppermute | solution.py:68
  80.5 19.1 %collective-permute-start.21 = (bf16[4,48,3200]{2,1,0:T(8,128)(2,1)}, bf16[4,48,3200]{2,1,0:T(8,128)(2,1)}, u32[]{:S(2)}, u32[]{:S(2)}) collective-permute-start(bf16[4,48,3200]{2,1,0:T(8,128)(2,1)} %get-tuple-element.110), channel_id=1, source_target_pairs={{0,1},{1,0},{2,3},{3,2},{4,5},{5,4},{6,7},{7,6},{8,9},{9,8},{10,11... | collective-permute-start | bytes 3686408 | tf_op jit(solution)/shard_map/cond/branch_1_fun/ppermute | solution.py:68
  82.1 16.6 %collective-permute-start.20 = (bf16[2,48,3200]{2,1,0:T(8,128)(2,1)S(1)}, bf16[2,48,3200]{2,1,0:T(8,128)(2,1)}, u32[]{:S(2)}, u32[]{:S(2)}) collective-permute-start(bf16[2,48,3200]{2,1,0:T(8,128)(2,1)S(1)} %slice.116), channel_id=1, source_target_pairs={{0,4},{1,5},{2,6},{3,7},{4,0},{5,1},{6,2},{7,3},{8,12},{9,13},{10,... | collective-permute-start | bytes 1843208 | tf_op jit(solution)/shard_map/cond/branch_1_fun/ppermute | solution.py:70
  83.9 15.7 %collective-permute-start.19 = (bf16[2,48,3200]{2,1,0:T(8,128)(2,1)S(1)}, bf16[2,48,3200]{2,1,0:T(8,128)(2,1)}, u32[]{:S(2)}, u32[]{:S(2)}) collective-permute-start(bf16[2,48,3200]{2,1,0:T(8,128)(2,1)S(1)} %slice.115), channel_id=1, source_target_pairs={{0,2},{1,3},{2,0},{3,1},{4,6},{5,7},{6,4},{7,5},{8,10},{9,11},{10,... | collective-permute-start | bytes 1843208 | tf_op jit(solution)/shard_map/cond/branch_1_fun/ppermute | solution.py:70
  107.8 20.1 %collective-permute-start.11 = (bf16[4,48,1536]{2,1,0:T(8,128)(2,1)}, bf16[4,48,1536]{2,1,0:T(8,128)(2,1)}, u32[]{:S(2)}, u32[]{:S(2)}) collective-permute-start(bf16[4,48,1536]{2,1,0:T(8,128)(2,1)} %get-tuple-element.114), channel_id=1, source_target_pairs={{0,1},{1,0},{2,3},{3,2},{4,5},{5,4},{6,7},{7,6},{8,9},{9,8},{10,11... | collective-permute-start | bytes 1769480 | tf_op jit(solution)/shard_map/cond/branch_1_fun/ppermute | solution.py:68
  107.9 20.1 %collective-permute-start.10 = (bf16[4,48,1536]{2,1,0:T(8,128)(2,1)}, bf16[4,48,1536]{2,1,0:T(8,128)(2,1)}, u32[]{:S(2)}, u32[]{:S(2)}) collective-permute-start(bf16[4,48,1536]{2,1,0:T(8,128)(2,1)} %get-tuple-element.114), channel_id=1, source_target_pairs={{0,4},{1,5},{2,6},{3,7},{4,0},{5,1},{6,2},{7,3},{8,12},{9,13},{10,... | collective-permute-start | bytes 1769480 | tf_op jit(solution)/shard_map/cond/branch_1_fun/ppermute | solution.py:70
  109.5 18.5 %collective-permute-start.9 = (bf16[4,48,1536]{2,1,0:T(8,128)(2,1)}, bf16[4,48,1536]{2,1,0:T(8,128)(2,1)}, u32[]{:S(2)}, u32[]{:S(2)}) collective-permute-start(bf16[4,48,1536]{2,1,0:T(8,128)(2,1)} %get-tuple-element.114), channel_id=1, source_target_pairs={{0,2},{1,3},{2,0},{3,1},{4,6},{5,7},{6,4},{7,5},{8,10},{9,11},{10,... | collective-permute-start | bytes 1769480 | tf_op jit(solution)/shard_map/cond/branch_1_fun/ppermute | solution.py:70
  129.6 15.4 %collective-permute-start.15 = (bf16[4,48,1536]{2,1,0:T(8,128)(2,1)}, bf16[4,48,1536]{2,1,0:T(8,128)(2,1)}, u32[]{:S(2)}, u32[]{:S(2)}) collective-permute-start(bf16[4,48,1536]{2,1,0:T(8,128)(2,1)} %get-tuple-element.133), channel_id=1, source_target_pairs={{0,1},{1,0},{2,3},{3,2},{4,5},{5,4},{6,7},{7,6},{8,9},{9,8},{10,11... | collective-permute-start | bytes 1769480 | tf_op jit(solution)/shard_map/cond/branch_1_fun/ppermute | solution.py:68
  129.6 15.4 %collective-permute-start.14 = (bf16[4,48,1536]{2,1,0:T(8,128)(2,1)}, bf16[4,48,1536]{2,1,0:T(8,128)(2,1)}, u32[]{:S(2)}, u32[]{:S(2)}) collective-permute-start(bf16[4,48,1536]{2,1,0:T(8,128)(2,1)} %get-tuple-element.134), channel_id=1, source_target_pairs={{0,1},{1,0},{2,3},{3,2},{4,5},{5,4},{6,7},{7,6},{8,9},{9,8},{10,11... | collective-permute-start | bytes 1769480 | tf_op jit(solution)/shard_map/cond/branch_1_fun/ppermute | solution.py:68
  131.1 13.9 %collective-permute-start.13 = (bf16[2,48,1536]{2,1,0:T(8,128)(2,1)S(1)}, bf16[2,48,1536]{2,1,0:T(8,128)(2,1)}, u32[]{:S(2)}, u32[]{:S(2)}) collective-permute-start(bf16[2,48,1536]{2,1,0:T(8,128)(2,1)S(1)} %slice.118), channel_id=1, source_target_pairs={{0,4},{1,5},{2,6},{3,7},{4,0},{5,1},{6,2},{7,3},{8,12},{9,13},{10,... | collective-permute-start | bytes 884744 | tf_op jit(solution)/shard_map/cond/branch_1_fun/ppermute | solution.py:70
  145.0 15.2 %collective-permute-start.39 = (bf16[256,1536]{1,0:T(8,128)(2,1)}, bf16[256,1536]{1,0:T(8,128)(2,1)S(1)}, u32[]{:S(2)}, u32[]{:S(2)}) collective-permute-start(bf16[256,1536]{1,0:T(8,128)(2,1)} %bitcast.76), channel_id=1, source_target_pairs={{0,1},{1,0},{2,3},{3,2},{4,5},{5,4},{6,7},{7,6},{8,9},{9,8},{10,11... | collective-permute-start | bytes 2359304 | tf_op jit(solution)/shard_map/ppermute | solution.py:68
  145.7 15.0 %collective-permute-start.40 = (bf16[256,1536]{1,0:T(8,128)(2,1)}, bf16[256,1536]{1,0:T(8,128)(2,1)S(1)}, u32[]{:S(2)}, u32[]{:S(2)}) collective-permute-start(bf16[256,1536]{1,0:T(8,128)(2,1)} %get-tuple-element.288.refs_9_), channel_id=1, source_target_pairs={{0,1},{1,0},{2,3},{3,2},{4,5},{5,4},{6,7},{7,6},{8,9},{9,8},{10,11... | collective-permute-start | bytes 2359304 | tf_op jit(solution)/shard_map/ppermute | solution.py:68
  146.1 14.7 %collective-permute-start.41 = (bf16[256,1536]{1,0:T(8,128)(2,1)}, bf16[256,1536]{1,0:T(8,128)(2,1)}, u32[]{:S(2)}, u32[]{:S(2)}) collective-permute-start(bf16[256,1536]{1,0:T(8,128)(2,1)} %get-tuple-element.289.refs_10_), channel_id=1, source_target_pairs={{0,1},{1,0},{2,3},{3,2},{4,5},{5,4},{6,7},{7,6},{8,9},{9,8},{10,11... | collective-permute-start | bytes 2359304 | tf_op jit(solution)/shard_map/ppermute | solution.py:68
  157.0 21.6 %collective-permute-start.34 = (bf16[256,1536]{1,0:T(8,128)(2,1)}, bf16[256,1536]{1,0:T(8,128)(2,1)S(1)}, u32[]{:S(2)}, u32[]{:S(2)}) collective-permute-start(bf16[256,1536]{1,0:T(8,128)(2,1)} %get-tuple-element.286.refs_0_), channel_id=1, source_target_pairs={{0,6},{1,7},{2,4},{3,5},{4,2},{5,3},{6,0},{7,1},{8,14},{9,15},{10,... | collective-permute-start | bytes 2359304 | tf_op jit(solution)/shard_map/ppermute | solution.py:70
  160.0 34.9 %collective-permute-start.33 = (bf16[256,1536]{1,0:T(8,128)(2,1)}, bf16[256,1536]{1,0:T(8,128)(2,1)S(1)}, u32[]{:S(2)}, u32[]{:S(2)}) collective-permute-start(bf16[256,1536]{1,0:T(8,128)(2,1)} %get-tuple-element.286.refs_0_), channel_id=1, source_target_pairs={{0,4},{1,5},{2,6},{3,7},{4,0},{5,1},{6,2},{7,3},{8,12},{9,13},{10,... | collective-permute-start | bytes 2359304 | tf_op jit(solution)/shard_map/ppermute | solution.py:70
  160.2 34.9 %collective-permute-start.32 = (bf16[256,1536]{1,0:T(8,128)(2,1)}, bf16[256,1536]{1,0:T(8,128)(2,1)S(1)}, u32[]{:S(2)}, u32[]{:S(2)}) collective-permute-start(bf16[256,1536]{1,0:T(8,128)(2,1)} %get-tuple-element.286.refs_0_), channel_id=1, source_target_pairs={{0,2},{1,3},{2,0},{3,1},{4,6},{5,7},{6,4},{7,5},{8,10},{9,11},{10,... | collective-permute-start | bytes 2359304 | tf_op jit(solution)/shard_map/ppermute | solution.py:70
  160.7 34.8 %collective-permute-start.42 = (bf16[256,1536]{1,0:T(8,128)(2,1)S(1)}, bf16[256,1536]{1,0:T(8,128)(2,1)S(1)}, u32[]{:S(2)}, u32[]{:S(2)}) collective-permute-start(bf16[256,1536]{1,0:T(8,128)(2,1)S(1)} %copy-done.13), channel_id=1, source_target_pairs={{0,1},{1,0},{2,3},{3,2},{4,5},{5,4},{6,7},{7,6},{8,9},{9,8},{10,11... | collective-permute-start | bytes 2359304 | tf_op jit(solution)/shard_map/ppermute | solution.py:68
  160.8 34.7 %collective-permute-start.35 = (bf16[256,1536]{1,0:T(8,128)(2,1)}, bf16[256,1536]{1,0:T(8,128)(2,1)S(1)}, u32[]{:S(2)}, u32[]{:S(2)}) collective-permute-start(bf16[256,1536]{1,0:T(8,128)(2,1)} %get-tuple-element.286.refs_0_), channel_id=1, source_target_pairs={{0,1},{1,0},{2,3},{3,2},{4,5},{5,4},{6,7},{7,6},{8,9},{9,8},{10,11... | collective-permute-start | bytes 2359304 | tf_op jit(solution)/shard_map/ppermute | solution.py:68
  178.6 16.9 %collective-permute-start.38 = (bf16[256,1536]{1,0:T(8,128)(2,1)S(1)}, bf16[256,1536]{1,0:T(8,128)(2,1)S(1)}, u32[]{:S(2)}, u32[]{:S(2)}) collective-permute-start(bf16[256,1536]{1,0:T(8,128)(2,1)S(1)} %collective-permute-done.34.refs_3_), channel_id=1, source_target_pairs={{0,1},{1,0},{2,3},{3,2},{4,5},{5,4},{6,7},{7,6},{8,9},{9,8},{10,11... | collective-permute-start | bytes 2359304 | tf_op jit(solution)/shard_map/ppermute | solution.py:68
  239.4 20.6 %collective-permute-start.45 = (bf16[256,1536]{1,0:T(8,128)(2,1)S(1)}, bf16[256,1536]{1,0:T(8,128)(2,1)}, u32[]{:S(2)}, u32[]{:S(2)}) collective-permute-start(bf16[256,1536]{1,0:T(8,128)(2,1)S(1)} %add_convert_fusion.6), channel_id=1, source_target_pairs={{0,2},{1,3},{2,0},{3,1},{4,6},{5,7},{6,4},{7,5},{8,10},{9,11},{10,... | collective-permute-start | bytes 2359304 | tf_op jit(solution)/shard_map/ppermute | solution.py:70
  241.0 36.3 %collective-permute-start.47 = (bf16[256,1536]{1,0:T(8,128)(2,1)S(1)}, bf16[256,1536]{1,0:T(8,128)(2,1)}, u32[]{:S(2)}, u32[]{:S(2)}) collective-permute-start(bf16[256,1536]{1,0:T(8,128)(2,1)S(1)} %add_convert_fusion.5), channel_id=1, source_target_pairs={{0,4},{1,5},{2,6},{3,7},{4,0},{5,1},{6,2},{7,3},{8,12},{9,13},{10,... | collective-permute-start | bytes 2359304 | tf_op jit(solution)/shard_map/ppermute | solution.py:70
  242.3 35.0 %collective-permute-start.49 = (bf16[256,1536]{1,0:T(8,128)(2,1)S(1)}, bf16[256,1536]{1,0:T(8,128)(2,1)}, u32[]{:S(2)}, u32[]{:S(2)}) collective-permute-start(bf16[256,1536]{1,0:T(8,128)(2,1)S(1)} %add_convert_fusion.4), channel_id=1, source_target_pairs={{0,6},{1,7},{2,4},{3,5},{4,2},{5,3},{6,0},{7,1},{8,14},{9,15},{10,... | collective-permute-start | bytes 2359304 | tf_op jit(solution)/shard_map/ppermute | solution.py:70
  243.5 33.9 %collective-permute-start.43 = (bf16[256,1536]{1,0:T(8,128)(2,1)}, bf16[256,1536]{1,0:T(8,128)(2,1)}, u32[]{:S(2)}, u32[]{:S(2)}) collective-permute-start(bf16[256,1536]{1,0:T(8,128)(2,1)} %get-tuple-element.295), channel_id=1, source_target_pairs={{0,1},{1,0},{2,3},{3,2},{4,5},{5,4},{6,7},{7,6},{8,9},{9,8},{10,11... | collective-permute-start | bytes 2359304 | tf_op jit(solution)/shard_map/ppermute | solution.py:68
  243.5 158.1 %reduce-scatter.6.cloned.1.call-start = ((), (), s32[]{:S(2)}) async-start(), calls=%async_computation.4 | async-start | bytes 3932160 | tf_op jit(solution)/shard_map/reduce_scatter | solution.py:684
  298.0 32.6 %collective-permute-start.24 = (bf16[4,48,1664]{2,1,0:T(8,128)(2,1)}, bf16[4,48,1664]{2,1,0:T(8,128)(2,1)}, u32[]{:S(2)}, u32[]{:S(2)}) collective-permute-start(bf16[4,48,1664]{2,1,0:T(8,128)(2,1)} %bitcast.10), channel_id=1, source_target_pairs={{0,2},{1,3},{2,0},{3,1},{4,6},{5,7},{6,4},{7,5},{8,10},{9,11},{10,... | collective-permute-start | bytes 1916936 | tf_op jit(solution)/shard_map/cond/branch_1_fun/ppermute | solution.py:70
  298.8 31.8 %collective-permute-start.25 = (bf16[4,48,1664]{2,1,0:T(8,128)(2,1)}, bf16[4,48,1664]{2,1,0:T(8,128)(2,1)}, u32[]{:S(2)}, u32[]{:S(2)}) collective-permute-start(bf16[4,48,1664]{2,1,0:T(8,128)(2,1)} %bitcast.11), channel_id=1, source_target_pairs={{0,4},{1,5},{2,6},{3,7},{4,0},{5,1},{6,2},{7,3},{8,12},{9,13},{10,... | collective-permute-start | bytes 1916936 | tf_op jit(solution)/shard_map/cond/branch_1_fun/ppermute | solution.py:70
  300.1 30.5 %collective-permute-start.26 = (bf16[4,48,1664]{2,1,0:T(8,128)(2,1)}, bf16[4,48,1664]{2,1,0:T(8,128)(2,1)}, u32[]{:S(2)}, u32[]{:S(2)}) collective-permute-start(bf16[4,48,1664]{2,1,0:T(8,128)(2,1)} %bitcast.12), channel_id=1, source_target_pairs={{0,6},{1,7},{2,4},{3,5},{4,2},{5,3},{6,0},{7,1},{8,14},{9,15},{10,... | collective-permute-start | bytes 1916936 | tf_op jit(solution)/shard_map/cond/branch_1_fun/ppermute | solution.py:70
  301.5 29.0 %collective-permute-start.27 = (bf16[1024,1536]{1,0:T(8,128)(2,1)}, bf16[1024,1536]{1,0:T(8,128)(2,1)}, u32[]{:S(2)}, u32[]{:S(2)}) collective-permute-start(bf16[1024,1536]{1,0:T(8,128)(2,1)} %get-tuple-element.160), channel_id=1, source_target_pairs={{0,1},{1,0},{2,3},{3,2},{4,5},{5,4},{6,7},{7,6},{8,9},{9,8},{10,11... | collective-permute-start | bytes 9437192 | tf_op jit(solution)/shard_map/cond/branch_1_fun/ppermute | solution.py:68
  333.7 111.0 %reduce-scatter.8.cloned.1.call-start = ((), (), s32[]{:S(2)}) async-start(), calls=%async_computation.5 | async-start | bytes 2273280 | tf_op jit(solution)/shard_map/reduce_scatter | solution.py:684
  340.7 16.2 %collective-permute-start.52 = (bf16[4,48,1536]{2,1,0:T(8,128)(2,1)S(1)}, bf16[4,48,1536]{2,1,0:T(8,128)(2,1)S(1)}, u32[]{:S(2)}, u32[]{:S(2)}) collective-permute-start(bf16[4,48,1536]{2,1,0:T(8,128)(2,1)S(1)} %get-tuple-element.347), channel_id=1, source_target_pairs={{0,2},{1,3},{2,0},{3,1},{4,6},{5,7},{6,4},{7,5},{8,10},{9,11},{10,... | collective-permute-start | bytes 1769480 | tf_op jit(solution)/shard_map/ppermute | solution.py:70
  341.5 28.6 %collective-permute-start.54 = (bf16[4,48,1536]{2,1,0:T(8,128)(2,1)S(1)}, bf16[4,48,1536]{2,1,0:T(8,128)(2,1)S(1)}, u32[]{:S(2)}, u32[]{:S(2)}) collective-permute-start(bf16[4,48,1536]{2,1,0:T(8,128)(2,1)S(1)} %get-tuple-element.348), channel_id=1, source_target_pairs={{0,6},{1,7},{2,4},{3,5},{4,2},{5,3},{6,0},{7,1},{8,14},{9,15},{10,... | collective-permute-start | bytes 1769480 | tf_op jit(solution)/shard_map/ppermute | solution.py:70
  343.2 28.9 %collective-permute-start.53 = (bf16[4,48,1536]{2,1,0:T(8,128)(2,1)S(1)}, bf16[4,48,1536]{2,1,0:T(8,128)(2,1)S(1)}, u32[]{:S(2)}, u32[]{:S(2)}) collective-permute-start(bf16[4,48,1536]{2,1,0:T(8,128)(2,1)S(1)} %get-tuple-element.349), channel_id=1, source_target_pairs={{0,4},{1,5},{2,6},{3,7},{4,0},{5,1},{6,2},{7,3},{8,12},{9,13},{10,... | collective-permute-start | bytes 1769480 | tf_op jit(solution)/shard_map/ppermute | solution.py:70
  346.2 36.0 %collective-permute-start.56 = (bf16[4,48,1536]{2,1,0:T(8,128)(2,1)S(1)}, bf16[4,48,1536]{2,1,0:T(8,128)(2,1)S(1)}, u32[]{:S(2)}, u32[]{:S(2)}) collective-permute-start(bf16[4,48,1536]{2,1,0:T(8,128)(2,1)S(1)} %get-tuple-element.350), channel_id=1, source_target_pairs={{0,2},{1,3},{2,0},{3,1},{4,6},{5,7},{6,4},{7,5},{8,10},{9,11},{10,... | collective-permute-start | bytes 1769480 | tf_op jit(solution)/shard_map/ppermute | solution.py:70
  346.9 47.9 %collective-permute-start.58 = (bf16[4,48,1536]{2,1,0:T(8,128)(2,1)S(1)}, bf16[4,48,1536]{2,1,0:T(8,128)(2,1)S(1)}, u32[]{:S(2)}, u32[]{:S(2)}) collective-permute-start(bf16[4,48,1536]{2,1,0:T(8,128)(2,1)S(1)} %get-tuple-element.351), channel_id=1, source_target_pairs={{0,6},{1,7},{2,4},{3,5},{4,2},{5,3},{6,0},{7,1},{8,14},{9,15},{10,... | collective-permute-start | bytes 1769480 | tf_op jit(solution)/shard_map/ppermute | solution.py:70
  356.9 39.3 %collective-permute-start.57 = (bf16[4,48,1536]{2,1,0:T(8,128)(2,1)S(1)}, bf16[4,48,1536]{2,1,0:T(8,128)(2,1)S(1)}, u32[]{:S(2)}, u32[]{:S(2)}) collective-permute-start(bf16[4,48,1536]{2,1,0:T(8,128)(2,1)S(1)} %get-tuple-element.352), channel_id=1, source_target_pairs={{0,4},{1,5},{2,6},{3,7},{4,0},{5,1},{6,2},{7,3},{8,12},{9,13},{10,... | collective-permute-start | bytes 1769480 | tf_op jit(solution)/shard_map/ppermute | solution.py:70
  405.1 20.7 %collective-permute-start.59 = (bf16[256,1536]{1,0:T(8,128)(2,1)}, bf16[256,1536]{1,0:T(8,128)(2,1)S(1)}, u32[]{:S(2)}, u32[]{:S(2)}) collective-permute-start(bf16[256,1536]{1,0:T(8,128)(2,1)} %get-tuple-element.316), channel_id=1, source_target_pairs={{0,2},{1,3},{2,0},{3,1},{4,6},{5,7},{6,4},{7,5},{8,10},{9,11},{10,... | collective-permute-start | bytes 2359304 | tf_op jit(solution)/shard_map/ppermute | solution.py:70
  406.1 35.2 %collective-permute-start.60 = (bf16[256,1536]{1,0:T(8,128)(2,1)}, bf16[256,1536]{1,0:T(8,128)(2,1)}, u32[]{:S(2)}, u32[]{:S(2)}) collective-permute-start(bf16[256,1536]{1,0:T(8,128)(2,1)} %get-tuple-element.325), channel_id=1, source_target_pairs={{0,4},{1,5},{2,6},{3,7},{4,0},{5,1},{6,2},{7,3},{8,12},{9,13},{10,... | collective-permute-start | bytes 2359304 | tf_op jit(solution)/shard_map/ppermute | solution.py:70
  406.8 34.5 %collective-permute-start.61 = (bf16[256,1536]{1,0:T(8,128)(2,1)}, bf16[256,1536]{1,0:T(8,128)(2,1)}, u32[]{:S(2)}, u32[]{:S(2)}) collective-permute-start(bf16[256,1536]{1,0:T(8,128)(2,1)} %get-tuple-element.327), channel_id=1, source_target_pairs={{0,6},{1,7},{2,4},{3,5},{4,2},{5,3},{6,0},{7,1},{8,14},{9,15},{10,... | collective-permute-start | bytes 2359304 | tf_op jit(solution)/shard_map/ppermute | solution.py:70
  (59 other events, 682.0 us)
Sparse Core Ops, SparseCore 0:
  34.6 73.0 all-gather.4
  109.3 88.0 all-gather.6
  243.6 82.9 reduce-scatter.3
  333.8 57.8 reduce-scatter.5
  401.8 36.6 reduce-scatter.7
